TPU v7x, 512 devices: a whole 4x8x8 slice. The times are simulated.
512 devices in a mesh: tm: 64 (over x, z, core), panel: 8 (over y).
Axes of the slice: x: 4, y: 8, z: 8, core: 2. Of those that a mesh axis runs over, the one named last changes fastest.
Arguments:
- transition: bfloat16 [64, 1024, 1024], P('tm', None, 'panel'), may hold values from -1 to 1
- drift: bfloat16 [64, 1024], P('tm'), may hold values from -6 to 6
- spread: bfloat16 [64, 1024, 1024], P('tm', None, 'panel'), may hold values from -1 to 1, as said below
- belief: bfloat16 [64, 1024], P('tm'), may hold values from -6 to 6
- precision: bfloat16 [64, 1024, 1024], P('tm', None, 'panel'), may hold values from -1 to 1, as said below
- probe_hosts: int32 [64, 256], P('tm'), may hold values from 0 to 511
- probe_values: float32 [64, 256], P('tm'), may hold values from -6 to 6
Outputs:
- sum_transition: bfloat16 [64, 1024, 1024], P('tm', None, 'panel')
- sum_drift: bfloat16 [64, 1024], P('tm')
- sum_spread: bfloat16 [64, 1024, 1024], P('tm', None, 'panel')
- sum_belief: bfloat16 [64, 1024], P('tm')
- sum_precision: bfloat16 [64, 1024, 1024], P('tm', None, 'panel')
Inputs may be any that keep to these rules, and one draw needn't show every extreme that they name: `spread`: every 1024 x 1024 block is symmetric. `precision`: every 1024 x 1024 block is symmetric.
All inputs are finite; a program needn't handle non-finite values.
Results may differ from a plain program's by a relative error of at most 0.012.
The roundings to bfloat16 on the way count: a program that leaves them out, or rounds other values in their place, can miss the bound.
Values may be sent and summed in bfloat16 or wider, within the bound.
No kernel may reach another device: no remote copies, remote signals or barrier semaphores. Data moves between devices by JAX's collectives and lax.ppermute only.
A program may use at most 64 MiB of HBM per device.

v0:
```python
import jax
import jax.numpy as jnp
from jax import lax
from jax.sharding import PartitionSpec as P

NS = 2
LEVELS = 2


def sent_to_all(shard, axis):
    length = lax.axis_size(axis)
    return lax.all_to_all(
        jnp.broadcast_to(shard[None], (length, *shard.shape)), axis, 0, 0, tiled=True
    )


def joined_along(parts, dim):
    dims = list(parts.shape[1:])
    dims[dim] *= parts.shape[0]
    return jnp.moveaxis(parts, 0, dim).reshape(dims)


def gathered_copies(shard, axis, dim):
    parts = sent_to_all(shard, axis)
    return joined_along(parts, dim)


def partner(shard, axis, stride):
    return lax.ppermute(shard, axis, [(i, i ^ 1 << stride) for i in range(lax.axis_size(axis))])


def mat_vector(matrix, vector):
    return jnp.dot(matrix, vector.astype(jnp.bfloat16), preferred_element_type=jnp.float32)


def tmat_vector(matrix, vector):
    return jnp.dot(vector.astype(jnp.bfloat16), matrix, preferred_element_type=jnp.float32)


def series_panel(cov_full, info_full, anchor, series_terms):
    current = anchor
    for repeat in range(series_terms):
        inside = jnp.dot(info_full, current, preferred_element_type=jnp.float32).astype(
            jnp.bfloat16
        )
        outside = jnp.dot(cov_full, inside, preferred_element_type=jnp.float32)
        current = (anchor.astype(jnp.float32) - outside).astype(jnp.bfloat16)
    return current


def series_forward(cov_full, info_full, anchor, series_terms):
    current = anchor
    for repeat in range(series_terms):
        current = anchor - mat_vector(cov_full, mat_vector(info_full, current))
    return current


def series_backward(cov_full, info_full, anchor, series_terms):
    current = anchor
    for repeat in range(series_terms):
        current = anchor - mat_vector(info_full, mat_vector(cov_full, current))
    return current


def local(transition, drift, spread, belief, precision, probe_hosts, probe_values):
    series_terms = 2**NS - 1
    states = transition.shape[1]
    width = transition.shape[2]
    host_count = states // 2
    panel_index = lax.axis_index("panel")
    time_index = lax.axis_index("tm")
    own_move = transition[0]
    own_spread = spread[0]
    own_weight = precision[0]
    own_drift = drift[0]
    chooser = (probe_hosts[0][:, None] == jnp.arange(host_count, dtype=jnp.int32)[None, :]).astype(
        jnp.float32
    )
    offsets = jnp.dot(probe_values[0], chooser, precision=lax.Precision.HIGHEST)
    paired = jnp.stack([offsets, jnp.zeros_like(offsets)], axis=1).reshape(states)
    own_belief = (belief[0].astype(jnp.float32) + paired).astype(jnp.bfloat16)
    for height in range(LEVELS):
        earlier_side = time_index >> height & 1 == 0
        role_panel = jnp.where(earlier_side, own_spread, own_weight)
        other_panel = jnp.where(earlier_side, own_weight, own_spread)
        own_full = gathered_copies(role_panel, "panel", 1)
        their_move, their_other, their_drift, their_belief = partner(
            (own_move, other_panel, own_drift, own_belief), "tm", height
        )
        their_full = partner(own_full, "tm", height)
        their_move_full = lax.all_gather(their_move, "panel", axis=1, tiled=True)
        first_col = 0

        def early_work():
            row_block = lax.dynamic_slice_in_dim(
                their_move_full, panel_index * width + first_col, width, 0
            )
            crossed = lax.dot_general(
                own_full, row_block, (((1,), (1,)), ((), ())), preferred_element_type=jnp.float32
            ).astype(jnp.bfloat16)
            product = series_panel(own_full, their_full, crossed, series_terms)
            forward = own_drift.astype(jnp.float32) + mat_vector(own_full, their_belief)
            forward = series_forward(own_full, their_full, forward, series_terms)
            fresh = (mat_vector(their_move_full, forward) + their_drift.astype(jnp.float32)).astype(
                jnp.bfloat16
            )
            return (product, fresh)

        def late_work():
            product = series_panel(their_full, own_full, their_move, series_terms)
            backward = own_belief.astype(jnp.float32) - mat_vector(own_full, their_drift)
            backward = series_backward(their_full, own_full, backward, series_terms)
            fresh = (
                tmat_vector(their_move_full, backward) + their_belief.astype(jnp.float32)
            ).astype(jnp.bfloat16)
            return (product, fresh)

        product, fresh_vector = lax.cond(earlier_side, early_work, late_work)
        other_cols = their_other

        def early_spread():
            return (
                jnp.dot(their_move_full, product, preferred_element_type=jnp.float32)
                + other_cols.astype(jnp.float32)
            ).astype(jnp.bfloat16)

        def late_keep():
            return product

        outgoing = lax.cond(earlier_side, early_spread, late_keep)
        received = partner(outgoing, "tm", height)

        def early_finish():
            return jnp.dot(their_move_full, received, preferred_element_type=jnp.float32).astype(
                jnp.bfloat16
            )

        def late_finish():
            weighted = jnp.dot(own_full, product, preferred_element_type=jnp.float32).astype(
                jnp.bfloat16
            )
            return (
                lax.dot_general(
                    their_move_full,
                    weighted,
                    (((0,), (0,)), ((), ())),
                    preferred_element_type=jnp.float32,
                )
                + other_cols.astype(jnp.float32)
            ).astype(jnp.bfloat16)

        first_block = lax.cond(earlier_side, early_finish, late_finish)
        their_first, their_vector = partner((first_block, fresh_vector), "tm", height)
        move_cols = jnp.where(earlier_side, first_block, their_first)
        weight_cols = jnp.where(earlier_side, their_first, first_block)
        spread_cols = jnp.where(earlier_side, outgoing, received)
        own_drift = jnp.where(earlier_side, fresh_vector, their_vector)
        own_belief = jnp.where(earlier_side, their_vector, fresh_vector)
        own_move = move_cols
        own_spread = spread_cols
        own_weight = weight_cols
    return (own_move[None], own_drift[None], own_spread[None], own_belief[None], own_weight[None])


def solution(mesh):
    in_specs = (
        P("tm", None, "panel"),
        P("tm", None),
        P("tm", None, "panel"),
        P("tm", None),
        P("tm", None, "panel"),
        P("tm", None),
        P("tm", None),
    )
    out_specs = (
        P("tm", None, "panel"),
        P("tm", None),
        P("tm", None, "panel"),
        P("tm", None),
        P("tm", None, "panel"),
    )
    return jax.shard_map(local, mesh=mesh, in_specs=in_specs, out_specs=out_specs, check_vma=False)
```

profile of v0, /device:TPU:1, one launch (start us, length us, event | category | flops | bytes accessed | tf_op | source)
XLA Modules:
  0.0 294.4 jit_solution(15901596718605557430)
XLA Ops:
  7.2 1.1 copy.85
  8.3 1.1 copy.86
  9.4 0.7 select_bitcast_fusion.3
  10.3 1.6 broadcast_in_dim.31
  11.9 7.8 %all-to-all-start = ((bf16[8,1024,128]{2,1,0:T(8,128)(2,1)}), bf16[8,1024,128]{2,1,0:T(8,128)(2,1)}, u32[]{:S(2)}, u32[]{:S(2)}) async-start(bf16[8,1024,128]{2,1,0:T(8,128)(2,1)} %broadcast_in_dim.31), calls=%async_computation | async-start | bytes 4194304 | tf_op jit(solution)/shard_map/all_to_all | solution.py:12
  19.8 5.5 %collective-permute-start = (bf16[1024,128]{1,0:T(8,128)(2,1)S(1)}, bf16[1024,128]{1,0:T(8,128)(2,1)S(1)}, u32[]{:S(2)}, u32[]{:S(2)}) collective-permute-start(bf16[1024,128]{1,0:T(8,128)(2,1)S(1)} %bitcast.293), channel_id=1, source_target_pairs={{0,8},{8,0},{16,24},{24,16},{32,40},{40,32},{48,56},{56,48},{64,72... | collective-permute-start | bytes 786440 | tf_op jit(solution)/shard_map/ppermute | solution.py:29
  25.2 1.1 collective-permute-done
  26.4 0.7 copy-done.7
  27.2 51.3 %all-to-all-done = bf16[8,1024,128]{2,1,0:T(8,128)(2,1)} async-done(((bf16[8,1024,128]{2,1,0:T(8,128)(2,1)}), bf16[8,1024,128]{2,1,0:T(8,128)(2,1)}, u32[]{:S(2)}, u32[]{:S(2)}) %all-to-all-start) | async-done | bytes 2097184 | tf_op jit(solution)/shard_map/all_to_all | solution.py:12
  78.4 2.9 copy.88
  81.3 3.1 %collective-permute-start.1 = (bf16[1024,1024]{0,1:T(8,128)(2,1)S(1)}, bf16[1024,1024]{0,1:T(8,128)(2,1)}, u32[]{:S(2)}, u32[]{:S(2)}) collective-permute-start(bf16[1024,1024]{0,1:T(8,128)(2,1)S(1)} %bitcast.243), channel_id=1, source_target_pairs={{0,8},{8,0},{16,24},{24,16},{32,40},{40,32},{48,56},{56,48},{64,72... | collective-permute-start | bytes 6291464 | tf_op jit(solution)/shard_map/ppermute | solution.py:29
  84.4 1.9 collective-permute-start.4
  87.2 2.4 collective-permute-start.3
  89.7 1.9 collective-permute-start.2
  91.6 1.1 collective-permute-done.2
  92.8 1.5 all-gather.3.cloned.1.call-done
  94.2 16.3 %conditional.40 = (bf16[1024,128]{0,1:T(8,128)(2,1)S(1)}, bf16[1024,128]{1,0:T(8,128)(2,1)S(1)}, bf16[1024]{0:T(1024)(128)(2,1)S(1)}) conditional(s32[]{:T(128)} %convert_element_type.335, (bf16[1024,128]{1,0:T(8,128)(2,1)S(1)}, bf16[1024,1024]{0,1:T(8,128)(2,1)S(1)}, bf16[1024,1024]{0,1:T(8,128)(2,1)}, bf16[1024]{0:T(1024)(128)(2,1)S(1)}, ...), branch_computations={%region_0.1_spmd.clone, %region_1.2_spmd.clone} | conditional | flops 1897550848 | bytes 46028956
  94.6 2.0 fusion.45
  97.0 2.0 fusion.47
  99.5 2.1 fusion.49
  102.4 0.8 convolution_convert_fusion.6
  103.3 2.4 convolution_convert_fusion.5
  105.8 2.4 convolution_convert_fusion.4
  108.1 2.1 fusion.9
  110.6 9.9 %collective-permute-start.5 = (bf16[1024,128]{1,0:T(8,128)(2,1)S(1)}, bf16[1024,128]{1,0:T(8,128)(2,1)S(1)}, u32[]{:S(2)}, u32[]{:S(2)}) collective-permute-start(bf16[1024,128]{1,0:T(8,128)(2,1)S(1)} %get-tuple-element.411), channel_id=1, source_target_pairs={{0,8},{8,0},{16,24},{24,16},{32,40},{40,32},{48,56},{56,48},{64,72... | collective-permute-start | bytes 786440 | tf_op jit(solution)/shard_map/ppermute | solution.py:29
  120.5 1.1 collective-permute-done.5
  121.7 3.3 %conditional.17 = (bf16[1024,128]{1,0:T(8,128)(2,1)S(1)}) conditional(s32[]{:T(128)} %convert_element_type.335, (bf16[1024,1024]{0,1:T(8,128)(2,1)S(1)}, bf16[1024,128]{0,1:T(8,128)(2,1)S(1)}, bf16[1024,1024]{1,0:T(8,128)(2,1)}, bf16[1024,128]{0,1:T(8,128)(2,1)S(1)}) %tuple.189, (bf16[1024,1024]{1,0:T(8,128)(2,1)}, ...), branch_computations={%region_4.5_spmd, %region_5.6_spmd} | conditional | flops 537395200 | bytes 5505032
  121.7 3.1 %fusion.2 = bf16[1024,128]{0,1:T(8,128)(2,1)S(1)} fusion(bf16[1024,1024]{1,0:T(8,128)(2,1)} %get-tuple-element.165, bf16[1024,1024]{0,1:T(8,128)(2,1)S(1)} %get-tuple-element.354, bf16[1024,128]{0,1:T(8,128)(2,1)S(1)} %get-tuple-element.355, bf16[1024,128]{0,1:T(8,128)(2,1)S(1)} %get-tuple-element.166), kind=kOutput, calls=%fused_computation.5 | convolution fusion | flops 537395200 | bytes 4980736 | tf_op jit(solution)/shard_map/cond/branch_0_fun/dot_general | solution.py:143
  124.9 1.9 collective-permute-start.6
  126.9 1.5 collective-permute-done.6
  128.4 0.8 broadcast_select_fusion.3
  129.1 1.6 broadcast_in_dim.32
  130.8 4.4 %all-to-all-start.1 = ((bf16[8,1024,128]{2,1,0:T(8,128)(2,1)}), bf16[8,1024,128]{2,1,0:T(8,128)(2,1)}, u32[]{:S(2)}, u32[]{:S(2)}) async-start(bf16[8,1024,128]{2,1,0:T(8,128)(2,1)} %broadcast_in_dim.32), calls=%async_computation.1 | async-start | bytes 4194304 | tf_op jit(solution)/shard_map/all_to_all | solution.py:12
  135.2 3.1 %collective-permute-start.7 = (bf16[1024,128]{1,0:T(8,128)(2,1)S(1)}, bf16[1024,128]{1,0:T(8,128)(2,1)S(1)}, u32[]{:S(2)}, u32[]{:S(2)}) collective-permute-start(bf16[1024,128]{1,0:T(8,128)(2,1)S(1)} %get-tuple-element.390), channel_id=1, source_target_pairs={{0,16},{8,24},{16,0},{24,8},{32,48},{40,56},{48,32},{56,40},{64,80... | collective-permute-start | bytes 786440 | tf_op jit(solution)/shard_map/ppermute | solution.py:29
  138.3 6.5 %collective-permute-done.7 = bf16[1024,128]{1,0:T(8,128)(2,1)S(1)} collective-permute-done((bf16[1024,128]{1,0:T(8,128)(2,1)S(1)}, bf16[1024,128]{1,0:T(8,128)(2,1)S(1)}, u32[]{:S(2)}, u32[]{:S(2)}) %collective-permute-start.7) | collective-permute-done | bytes 262176 | tf_op jit(solution)/shard_map/ppermute | solution.py:29
  144.8 0.7 copy-done.9
  145.5 44.7 %all-to-all-done.1 = bf16[8,1024,128]{2,1,0:T(8,128)(2,1)} async-done(((bf16[8,1024,128]{2,1,0:T(8,128)(2,1)}), bf16[8,1024,128]{2,1,0:T(8,128)(2,1)}, u32[]{:S(2)}, u32[]{:S(2)}) %all-to-all-start.1) | async-done | bytes 2097184 | tf_op jit(solution)/shard_map/all_to_all | solution.py:12
  190.3 2.9 copy.104
  193.1 4.3 %collective-permute-start.8 = (bf16[1024,1024]{0,1:T(8,128)(2,1)S(1)}, bf16[1024,1024]{0,1:T(8,128)(2,1)}, u32[]{:S(2)}, u32[]{:S(2)}) collective-permute-start(bf16[1024,1024]{0,1:T(8,128)(2,1)S(1)} %bitcast.239), channel_id=1, source_target_pairs={{0,16},{8,24},{16,0},{24,8},{32,48},{40,56},{48,32},{56,40},{64,80... | collective-permute-start | bytes 6291464 | tf_op jit(solution)/shard_map/ppermute | solution.py:29
  197.5 1.9 collective-permute-start.12
  199.4 2.8 collective-permute-start.9
  202.2 0.8 collective-permute-done.9
  203.0 3.6 %collective-permute-start.10 = (bf16[1024]{0:T(1024)(128)(2,1)S(1)}, bf16[1024]{0:T(1024)(128)(2,1)S(1)}, u32[]{:S(2)}, u32[]{:S(2)}) collective-permute-start(bf16[1024]{0:T(1024)(128)(2,1)S(1)} %get-tuple-element.395), channel_id=1, source_target_pairs={{0,16},{8,24},{16,0},{24,8},{32,48},{40,56},{48,32},{56,40},{64,80... | collective-permute-start | bytes 6152 | tf_op jit(solution)/shard_map/ppermute | solution.py:29
  206.6 1.9 collective-permute-start.11
  208.6 39.9 %collective-permute-done.10 = bf16[1024]{0:T(1024)(128)(2,1)S(1)} collective-permute-done((bf16[1024]{0:T(1024)(128)(2,1)S(1)}, bf16[1024]{0:T(1024)(128)(2,1)S(1)}, u32[]{:S(2)}, u32[]{:S(2)}) %collective-permute-start.10) | collective-permute-done | bytes 2080 | tf_op jit(solution)/shard_map/ppermute | solution.py:29
  248.5 17.3 %conditional.41 = (bf16[1024,128]{0,1:T(8,128)(2,1)S(1)}, bf16[1024]{0:T(1024)(128)(2,1)S(1)}) conditional(s32[]{:T(128)} %convert_element_type.334, (bf16[1024,128]{1,0:T(8,128)(2,1)S(1)}, bf16[1024,1024]{0,1:T(8,128)(2,1)S(1)}, bf16[1024,1024]{0,1:T(8,128)(2,1)}, bf16[1024]{0:T(1024)(128)(2,1)S(1)}, bf16[1024]{0:T(1024)(128)(2,1)S(1)}, ...), branch_computations={%region_6.7_spmd.clone, %region_7.8_spmd.clone} | conditional | flops 1897550848 | bytes 43407456
  248.8 1.4 convolution_convert_fusion.17
  250.2 2.1 convolution_convert_fusion.16
  252.3 2.4 convolution_convert_fusion.15
  254.6 2.4 convolution_convert_fusion.14
  257.9 2.0 fusion.69
  260.2 2.0 fusion.71
  262.7 2.1 fusion.73
  265.9 2.3 conditional.20
  265.9 2.3 fusion.3
  268.2 1.9 collective-permute-start.13
  270.1 3.4 %collective-permute-start.15 = (bf16[1024]{0:T(1024)(128)(2,1)S(1)}, bf16[1024]{0:T(1024)(128)(2,1)S(1)}, u32[]{:S(2)}, u32[]{:S(2)}) collective-permute-start(bf16[1024]{0:T(1024)(128)(2,1)S(1)} %get-tuple-element.382), channel_id=1, source_target_pairs={{0,16},{8,24},{16,0},{24,8},{32,48},{40,56},{48,32},{56,40},{64,80... | collective-permute-start | bytes 6152 | tf_op jit(solution)/shard_map/ppermute | solution.py:29
  273.5 3.3 %collective-permute-done.13 = bf16[1024,128]{1,0:T(8,128)(2,1)S(1)} collective-permute-done((bf16[1024,128]{1,0:T(8,128)(2,1)S(1)}, bf16[1024,128]{1,0:T(8,128)(2,1)S(1)}, u32[]{:S(2)}, u32[]{:S(2)}) %collective-permute-start.13) | collective-permute-done | bytes 262176 | tf_op jit(solution)/shard_map/ppermute | solution.py:29
  276.8 2.3 conditional.21
  276.8 2.3 convolution_convert_fusion.3
  279.1 3.3 %collective-permute-start.14 = (bf16[1024,128]{1,0:T(8,128)(2,1)S(1)}, bf16[1024,128]{1,0:T(8,128)(2,1)S(1)}, u32[]{:S(2)}, u32[]{:S(2)}) collective-permute-start(bf16[1024,128]{1,0:T(8,128)(2,1)S(1)} %get-tuple-element.385), channel_id=1, source_target_pairs={{0,16},{8,24},{16,0},{24,8},{32,48},{40,56},{48,32},{56,40},{64,80... | collective-permute-start | bytes 786440 | tf_op jit(solution)/shard_map/ppermute | solution.py:29
  283.6 0.7 select_bitcast_fusion.1
  284.4 2.4 collective-permute-done.14
  286.8 0.8 select_bitcast_fusion
  (92 shorter events, 7.8 us)
Async XLA Ops:
  7.2 79.1 %copy-start = (f32[1,256]{1,0:T(1,128)S(1)}, f32[1,256]{1,0:T(1,128)}, u32[]{:S(2)}) copy-start(f32[1,256]{1,0:T(1,128)} %param.25) | copy-start | bytes 3076
  11.9 7.8 %copy-start.15 = (bf16[1,1024,128]{2,1,0:T(8,128)(2,1)S(1)}, bf16[1,1024,128]{2,1,0:T(8,128)(2,1)}, u32[]{:S(2)}) copy-start(bf16[1,1024,128]{2,1,0:T(8,128)(2,1)} %param.19) | copy-start | bytes 786436
  11.9 66.5 %all-to-all-start = ((bf16[8,1024,128]{2,1,0:T(8,128)(2,1)}), bf16[8,1024,128]{2,1,0:T(8,128)(2,1)}, u32[]{:S(2)}, u32[]{:S(2)}) async-start(bf16[8,1024,128]{2,1,0:T(8,128)(2,1)} %broadcast_in_dim.31), calls=%async_computation | async-start | bytes 4194304 | tf_op jit(solution)/shard_map/all_to_all | solution.py:12
  19.7 74.5 %all-gather.3.cloned.1.call-start = ((), (), s32[]{:S(2)}) async-start(), calls=%async_computation.2 | async-start | bytes 2359296 | tf_op jit(solution)/shard_map/all_gather | solution.py:91
  19.8 6.6 %collective-permute-start = (bf16[1024,128]{1,0:T(8,128)(2,1)S(1)}, bf16[1024,128]{1,0:T(8,128)(2,1)S(1)}, u32[]{:S(2)}, u32[]{:S(2)}) collective-permute-start(bf16[1024,128]{1,0:T(8,128)(2,1)S(1)} %bitcast.293), channel_id=1, source_target_pairs={{0,8},{8,0},{16,24},{24,16},{32,40},{40,32},{48,56},{56,48},{64,72... | collective-permute-start | bytes 786440 | tf_op jit(solution)/shard_map/ppermute | solution.py:29
  26.4 0.7 copy-start.7
  27.1 59.2 %copy-start.14 = (s32[1,256]{1,0:T(1,128)S(1)}, s32[1,256]{1,0:T(1,128)}, u32[]{:S(2)}) copy-start(s32[1,256]{1,0:T(1,128)} %param.24) | copy-start | bytes 3076
  27.1 60.1 %copy-start.12 = (bf16[1,1024]{1,0:T(2,128)(2,1)S(1)}, bf16[1,1024]{1,0:T(2,128)(2,1)}, u32[]{:S(2)}) copy-start(bf16[1,1024]{1,0:T(2,128)(2,1)} %param.22) | copy-start | bytes 6148
  27.1 62.5 %copy-start.13 = (bf16[1,1024]{1,0:T(2,128)(2,1)S(1)}, bf16[1,1024]{1,0:T(2,128)(2,1)}, u32[]{:S(2)}) copy-start(bf16[1,1024]{1,0:T(2,128)(2,1)} %param.20) | copy-start | bytes 6148
  27.2 67.1 %copy-start.8 = (bf16[1024,128]{1,0:T(8,128)(2,1)S(1)}, bf16[1024,128]{1,0:T(8,128)(2,1)}, u32[]{:S(2)}) copy-start(bf16[1024,128]{1,0:T(8,128)(2,1)} %copy-done.7) | copy-start | bytes 786436
  81.3 12.9 %collective-permute-start.1 = (bf16[1024,1024]{0,1:T(8,128)(2,1)S(1)}, bf16[1024,1024]{0,1:T(8,128)(2,1)}, u32[]{:S(2)}, u32[]{:S(2)}) collective-permute-start(bf16[1024,1024]{0,1:T(8,128)(2,1)S(1)} %bitcast.243), channel_id=1, source_target_pairs={{0,8},{8,0},{16,24},{24,16},{32,40},{40,32},{48,56},{56,48},{64,72... | collective-permute-start | bytes 6291464 | tf_op jit(solution)/shard_map/ppermute | solution.py:29
  84.4 26.2 %collective-permute-start.4 = (bf16[1024,128]{0,1:T(8,128)(2,1)}, bf16[1024,128]{0,1:T(8,128)(2,1)S(1)}, u32[]{:S(2)}, u32[]{:S(2)}) collective-permute-start(bf16[1024,128]{0,1:T(8,128)(2,1)} %get-tuple-element.391), channel_id=1, source_target_pairs={{0,8},{8,0},{16,24},{24,16},{32,40},{40,32},{48,56},{56,48},{64,72... | collective-permute-start | bytes 786440 | tf_op jit(solution)/shard_map/ppermute | solution.py:29
  87.2 4.4 %collective-permute-start.3 = (bf16[1024]{0:T(1024)(128)(2,1)S(1)}, bf16[1024]{0:T(1024)(128)(2,1)S(1)}, u32[]{:S(2)}, u32[]{:S(2)}) collective-permute-start(bf16[1024]{0:T(1024)(128)(2,1)S(1)} %add_convert_fusion.4), channel_id=1, source_target_pairs={{0,8},{8,0},{16,24},{24,16},{32,40},{40,32},{48,56},{56,48},{64,72... | collective-permute-start | bytes 6152 | tf_op jit(solution)/shard_map/ppermute | solution.py:29
  89.7 3.1 %collective-permute-start.2 = (bf16[1024]{0:T(1024)(128)(2,1)S(1)}, bf16[1024]{0:T(1024)(128)(2,1)S(1)}, u32[]{:S(2)}, u32[]{:S(2)}) collective-permute-start(bf16[1024]{0:T(1024)(128)(2,1)S(1)} %reduce), channel_id=1, source_target_pairs={{0,8},{8,0},{16,24},{24,16},{32,40},{40,32},{48,56},{56,48},{64,72... | collective-permute-start | bytes 6152 | tf_op jit(solution)/shard_map/ppermute | solution.py:29
  99.4 2.6 copy-start.3
  110.6 11.1 %collective-permute-start.5 = (bf16[1024,128]{1,0:T(8,128)(2,1)S(1)}, bf16[1024,128]{1,0:T(8,128)(2,1)S(1)}, u32[]{:S(2)}, u32[]{:S(2)}) collective-permute-start(bf16[1024,128]{1,0:T(8,128)(2,1)S(1)} %get-tuple-element.411), channel_id=1, source_target_pairs={{0,8},{8,0},{16,24},{24,16},{32,40},{40,32},{48,56},{56,48},{64,72... | collective-permute-start | bytes 786440 | tf_op jit(solution)/shard_map/ppermute | solution.py:29
  124.9 3.4 %collective-permute-start.6 = (bf16[1024,128]{1,0:T(8,128)(2,1)S(1)}, bf16[1024,128]{1,0:T(8,128)(2,1)S(1)}, u32[]{:S(2)}, u32[]{:S(2)}) collective-permute-start(bf16[1024,128]{1,0:T(8,128)(2,1)S(1)} %get-tuple-element.381), channel_id=1, source_target_pairs={{0,8},{8,0},{16,24},{24,16},{32,40},{40,32},{48,56},{56,48},{64,72... | collective-permute-start | bytes 786440 | tf_op jit(solution)/shard_map/ppermute | solution.py:29
  130.8 59.5 %all-to-all-start.1 = ((bf16[8,1024,128]{2,1,0:T(8,128)(2,1)}), bf16[8,1024,128]{2,1,0:T(8,128)(2,1)}, u32[]{:S(2)}, u32[]{:S(2)}) async-start(bf16[8,1024,128]{2,1,0:T(8,128)(2,1)} %broadcast_in_dim.32), calls=%async_computation.1 | async-start | bytes 4194304 | tf_op jit(solution)/shard_map/all_to_all | solution.py:12
  135.1 113.4 %all-gather.5.cloned.1.call-start = ((), (), s32[]{:S(2)}) async-start(), calls=%async_computation.3 | async-start | bytes 2359296 | tf_op jit(solution)/shard_map/all_gather | solution.py:91
  135.2 9.6 %collective-permute-start.7 = (bf16[1024,128]{1,0:T(8,128)(2,1)S(1)}, bf16[1024,128]{1,0:T(8,128)(2,1)S(1)}, u32[]{:S(2)}, u32[]{:S(2)}) collective-permute-start(bf16[1024,128]{1,0:T(8,128)(2,1)S(1)} %get-tuple-element.390), channel_id=1, source_target_pairs={{0,16},{8,24},{16,0},{24,8},{32,48},{40,56},{48,32},{56,40},{64,80... | collective-permute-start | bytes 786440 | tf_op jit(solution)/shard_map/ppermute | solution.py:29
  144.8 0.7 copy-start.9
  145.5 51.9 %copy-start.11 = (bf16[1024,128]{1,0:T(8,128)(2,1)S(1)}, bf16[1024,128]{1,0:T(8,128)(2,1)}, u32[]{:S(2)}) copy-start(bf16[1024,128]{1,0:T(8,128)(2,1)} %get-tuple-element.386) | copy-start | bytes 786436
  145.5 103.0 %copy-start.10 = (bf16[1024,128]{1,0:T(8,128)(2,1)S(1)}, bf16[1024,128]{1,0:T(8,128)(2,1)}, u32[]{:S(2)}) copy-start(bf16[1024,128]{1,0:T(8,128)(2,1)} %copy-done.9) | copy-start | bytes 786436
  193.1 55.4 %collective-permute-start.8 = (bf16[1024,1024]{0,1:T(8,128)(2,1)S(1)}, bf16[1024,1024]{0,1:T(8,128)(2,1)}, u32[]{:S(2)}, u32[]{:S(2)}) collective-permute-start(bf16[1024,1024]{0,1:T(8,128)(2,1)S(1)} %bitcast.239), channel_id=1, source_target_pairs={{0,16},{8,24},{16,0},{24,8},{32,48},{40,56},{48,32},{56,40},{64,80... | collective-permute-start | bytes 6291464 | tf_op jit(solution)/shard_map/ppermute | solution.py:29
  197.5 68.4 %collective-permute-start.12 = (bf16[1024,128]{1,0:T(8,128)(2,1)S(1)}, bf16[1024,128]{1,0:T(8,128)(2,1)S(1)}, u32[]{:S(2)}, u32[]{:S(2)}) collective-permute-start(bf16[1024,128]{1,0:T(8,128)(2,1)S(1)} %copy-done.11), channel_id=1, source_target_pairs={{0,16},{8,24},{16,0},{24,8},{32,48},{40,56},{48,32},{56,40},{64,80... | collective-permute-start | bytes 786440 | tf_op jit(solution)/shard_map/ppermute | solution.py:29
  199.4 3.6 %collective-permute-start.9 = (bf16[1024]{0:T(1024)(128)(2,1)S(1)}, bf16[1024]{0:T(1024)(128)(2,1)S(1)}, u32[]{:S(2)}, u32[]{:S(2)}) collective-permute-start(bf16[1024]{0:T(1024)(128)(2,1)S(1)} %get-tuple-element.380), channel_id=1, source_target_pairs={{0,8},{8,0},{16,24},{24,16},{32,40},{40,32},{48,56},{56,48},{64,72... | collective-permute-start | bytes 6152 | tf_op jit(solution)/shard_map/ppermute | solution.py:29
  203.0 45.5 %collective-permute-start.10 = (bf16[1024]{0:T(1024)(128)(2,1)S(1)}, bf16[1024]{0:T(1024)(128)(2,1)S(1)}, u32[]{:S(2)}, u32[]{:S(2)}) collective-permute-start(bf16[1024]{0:T(1024)(128)(2,1)S(1)} %get-tuple-element.395), channel_id=1, source_target_pairs={{0,16},{8,24},{16,0},{24,8},{32,48},{40,56},{48,32},{56,40},{64,80... | collective-permute-start | bytes 6152 | tf_op jit(solution)/shard_map/ppermute | solution.py:29
  206.6 41.9 %collective-permute-start.11 = (bf16[1024]{0:T(1024)(128)(2,1)S(1)}, bf16[1024]{0:T(1024)(128)(2,1)S(1)}, u32[]{:S(2)}, u32[]{:S(2)}) collective-permute-start(bf16[1024]{0:T(1024)(128)(2,1)S(1)} %get-tuple-element.396), channel_id=1, source_target_pairs={{0,16},{8,24},{16,0},{24,8},{32,48},{40,56},{48,32},{56,40},{64,80... | collective-permute-start | bytes 6152 | tf_op jit(solution)/shard_map/ppermute | solution.py:29
  262.6 2.6 copy-start.2
  268.2 8.6 %collective-permute-start.13 = (bf16[1024,128]{1,0:T(8,128)(2,1)S(1)}, bf16[1024,128]{1,0:T(8,128)(2,1)S(1)}, u32[]{:S(2)}, u32[]{:S(2)}) collective-permute-start(bf16[1024,128]{1,0:T(8,128)(2,1)S(1)} %get-tuple-element.412), channel_id=1, source_target_pairs={{0,16},{8,24},{16,0},{24,8},{32,48},{40,56},{48,32},{56,40},{64,80... | collective-permute-start | bytes 786440 | tf_op jit(solution)/shard_map/ppermute | solution.py:29
  270.1 12.3 %collective-permute-start.15 = (bf16[1024]{0:T(1024)(128)(2,1)S(1)}, bf16[1024]{0:T(1024)(128)(2,1)S(1)}, u32[]{:S(2)}, u32[]{:S(2)}) collective-permute-start(bf16[1024]{0:T(1024)(128)(2,1)S(1)} %get-tuple-element.382), channel_id=1, source_target_pairs={{0,16},{8,24},{16,0},{24,8},{32,48},{40,56},{48,32},{56,40},{64,80... | collective-permute-start | bytes 6152 | tf_op jit(solution)/shard_map/ppermute | solution.py:29
  279.1 7.7 %collective-permute-start.14 = (bf16[1024,128]{1,0:T(8,128)(2,1)S(1)}, bf16[1024,128]{1,0:T(8,128)(2,1)S(1)}, u32[]{:S(2)}, u32[]{:S(2)}) collective-permute-start(bf16[1024,128]{1,0:T(8,128)(2,1)S(1)} %get-tuple-element.385), channel_id=1, source_target_pairs={{0,16},{8,24},{16,0},{24,8},{32,48},{40,56},{48,32},{56,40},{64,80... | collective-permute-start | bytes 786440 | tf_op jit(solution)/shard_map/ppermute | solution.py:29
Sparse Core Ops, SparseCore 0:
  27.2 66.9 all-gather.2
  145.6 65.3 all-gather.4
where the time goes:
time: 298 us; the launch traced here: 294 us
  waiting for transfers between devices  155 us (52%)
  starting transfers between devices  65.2 us (22%)
  matrix products  40.9 us (14%)
  local copies, waits for them, and re-layouts  14.8 us (5%)
  between operations  14.5 us (5%)
  other arithmetic  3.23 us (1%)
    all_to_all x2, waiting for transfers between devices, sent_to_all(): lax.all_to_all(jnp.broadcast_to(shard[None], (length, *shard.shape)), axi...  96 us
    ppermute x16, waiting for transfers between devices, partner(): lax.ppermute(shard, axis, [(i, i ^ 1 << stride) for i in range(lax.axis_s...  57.8 us
    ppermute x16, starting transfers between devices, partner(): lax.ppermute(shard, axis, [(i, i ^ 1 << stride) for i in range(lax.axis_s...  53 us
    dot_general x15, matrix products, mat_vector(): jnp.dot(matrix, vector.astype(jnp.bfloat16), preferred_element_type=jnp.f...  15.9 us
    dot_general x6, matrix products, series_panel(): jnp.dot(info_full, current, preferred_element_type=jnp.float32)  12.3 us
    all_to_all x2, starting transfers between devices, sent_to_all(): lax.all_to_all(jnp.broadcast_to(shard[None], (length, *shard.shape)), axi...  12.1 us
  transfers between devices with their start and end apart: 20, of which 12 were waited for; matrix products, arithmetic and copies ran while one was open for 15% of the time, Pallas kernels for 0%

commit v1 on v0

v1 whole, which is shorter than its diff:
```python
import jax
import jax.numpy as jnp
from jax import lax
from jax.experimental import pallas as pl
from jax.experimental.pallas import tpu as pltpu
from jax.sharding import PartitionSpec as P

NS = 2
LEVELS = 2
W = 128
N = 8
D = W * N
RING = 1664
HALF = 768
INTERPRET = False

f32 = jnp.float32
bf16 = jnp.bfloat16


def dot(a, b):
    return jnp.dot(a, b, preferred_element_type=f32)


def eye_mask():
    return lax.broadcasted_iota(jnp.int32, (W, W), 0) == lax.broadcasted_iota(jnp.int32, (W, W), 1)


def as_column(row, eye):
    col = jnp.sum(jnp.where(eye, jnp.broadcast_to(row, (W, W)), 0.0), axis=1, keepdims=True)
    return jnp.broadcast_to(col, (W, W))


def as_row(block, eye):
    return jnp.sum(jnp.where(eye, block, 0.0), axis=0, keepdims=True)


def call(kernel, out_shape, scratch, scalars, *args):
    outs = out_shape if isinstance(out_shape, (list, tuple)) else [out_shape]
    vm = pl.BlockSpec(memory_space=pltpu.VMEM)
    res = pl.pallas_call(
        kernel,
        out_shape=list(outs),
        in_specs=[pl.BlockSpec(memory_space=pltpu.SMEM)] + [vm] * len(args),
        out_specs=[vm] * len(outs),
        scratch_shapes=list(scratch),
        compiler_params=pltpu.CompilerParams(vmem_limit_bytes=56 * 2**20),
        interpret=INTERPRET,
    )(scalars, *args)
    return res


def struct(*shape):
    return jax.ShapeDtypeStruct(shape, bf16)


def blk(index):
    return pl.ds(pl.multiple_of(index * W, W), W)


def start_kernel(s, spread, weight, drift, belief, hosts, values, msg, own_vec):
    role = s[0]

    @pl.when(role == 0)
    def _():
        msg[0:D, :] = weight[...]

    @pl.when(role == 1)
    def _():
        msg[0:D, :] = spread[...]

    state = lax.broadcasted_iota(jnp.int32, (hosts.shape[0], D), 1)
    hit = jnp.where(2 * hosts[...] == state, values[...], 0.0)
    eta = (belief[...].astype(f32) + jnp.sum(hit, axis=0, keepdims=True)).astype(bf16).astype(f32)
    b = drift[...].astype(f32)
    rows = [b[:, k * W : (k + 1) * W] for k in range(N)] + [
        eta[:, k * W : (k + 1) * W] for k in range(N)
    ]
    vec = jnp.concatenate(rows, axis=0).astype(bf16)
    msg[D : D + 2 * N, :] = vec
    own_vec[...] = vec


def ring_kernel(s, xa, xb, aa, ab, msg):
    q = s[1]

    def put_x(src):
        for d in range(4):
            msg[512 + d * W : 512 + (d + 1) * W, :] = src[blk((q + d) % N), :]
        msg[1536:1664, :] = src[blk((q + 4) % N), :]

    def put_a(src):
        msg[0:512, :] = src[0:512, :]
        msg[1024:1536, :] = src[512:1024, :]

    pl.when(s[2] == 0)(lambda: put_x(xa))
    pl.when(s[2] == 1)(lambda: put_x(xb))
    pl.when(s[3] == 0)(lambda: put_a(aa))
    pl.when(s[3] == 1)(lambda: put_a(ab))


def assemble_kernel(s, xa, xb, msg, m1, m2, m3, p1, p2, p3, m4, p4, x_out, a_out):
    q = s[1]

    def put(l, d, block):
        r = (l + d) % N
        x_out[r * W : (r + 1) * W, l * W : (l + 1) * W] = block
        if d:
            x_out[l * W : (l + 1) * W, r * W : (r + 1) * W] = block.T

    def own(src):
        for d in range(N):
            put(0, d, src[blk((q + d) % N), :])

    pl.when(s[2] == 0)(lambda: own(xa))
    pl.when(s[2] == 1)(lambda: own(xb))
    for l, src in ((1, m1), (2, m2), (3, m3), (7, p1), (6, p2), (5, p3)):
        for d in range(5 if l < 4 else 4):
            if (l + d) % N == 0:
                continue
            row = 1536 if d == 4 else 512 + d * W
            put(l, d, src[row : row + W, :])
    for d in (0, 1):
        put(4, d, m4[512 + d * W : 512 + (d + 1) * W, :])
        put(4, d + 2, p4[d * W : (d + 1) * W, :])
    for l, src in ((0, msg), (1, m1), (2, m2), (3, m3), (7, p1), (6, p2), (5, p3)):
        a_out[0:512, l * W : (l + 1) * W] = src[0:512, :]
        a_out[512:1024, l * W : (l + 1) * W] = src[1024:1536, :]
    a_out[0:512, 4 * W : 5 * W] = m4[0:512, :]
    a_out[512:1024, 4 * W : 5 * W] = p4[256:768, :]


def combine_kernel(
    s, x_own, x_other, a_full, aia, aib, adda, addb, vec_i, vec_j, out1, out2, r, t, base, acc, vecs
):
    role = s[0]
    q = s[1]
    terms = 2**NS - 1
    eye = eye_mask()
    vi = vec_i[...].astype(f32)
    vj = vec_j[...].astype(f32)

    def rotated_move(dst, col):
        def put(src):
            for l in range(N):
                dst[l * W : (l + 1) * W, col : col + W] = src[blk((q + l) % N), :]

        pl.when(s[2] == 0)(lambda: put(aia))
        pl.when(s[2] == 1)(lambda: put(aib))

    def rotated_vector(rows, first, dst, col):
        vecs[...] = rows
        for l in range(N):
            row = vecs[pl.ds(first + (q + l) % N, 1), :]
            dst[l * W : (l + 1) * W, col : col + W] = as_column(row, eye).astype(dst.dtype)

    @pl.when(role == 0)
    def _():
        cov, info = x_own, x_other
        a_row = a_full[blk(q), :]
        for l in range(N):
            r[l * W : (l + 1) * W, 0:W] = a_row[:, l * W : (l + 1) * W].T
        rotated_vector(vj, N, r, 2 * W)
        rotated_vector(vi, 0, acc, 0)
        v = dot(cov[...], r[:, 0:W]).astype(bf16)
        w = acc[:, 0:W] + dot(cov[...], r[:, 2 * W : 3 * W])
        acc[:, 0:W] = w
        base[:, 0:W] = v
        rotated_move(base, W)
        r[:, 0 : 2 * W] = base[...]
        r[:, 2 * W : 3 * W] = w.astype(bf16)
        for _ in range(terms):
            t[...] = dot(info[...], r[...]).astype(bf16)
            out = dot(cov[...], t[...])
            r[:, 0 : 2 * W] = (base[...].astype(f32) - out[:, 0 : 2 * W]).astype(bf16)
            r[:, 2 * W : 3 * W] = (acc[:, 0:W] - out[:, 2 * W : 3 * W]).astype(bf16)
        res = dot(a_full[...], r[...])

        def put_c(src):
            out1[0:D, :] = (res[:, 0:W] + src[0:D, :].astype(f32)).astype(bf16)

        pl.when(s[3] == 0)(lambda: put_c(adda))
        pl.when(s[3] == 1)(lambda: put_c(addb))
        out2[...] = res[:, W : 2 * W].astype(bf16)
        rows = [
            as_row(res[l * W : (l + 1) * W, 2 * W : 3 * W], eye) + vj[l : l + 1, :] for l in range(N)
        ]
        rows = rows + [jnp.zeros((1, W), f32)] * N
        out1[D : D + 2 * N, :] = jnp.concatenate(rows, axis=0).astype(bf16)

    @pl.when(role == 1)
    def _():
        info, cov = x_own, x_other
        rotated_move(base, 0)
        rotated_vector(vi, 0, r, W)
        rotated_vector(vj, N, acc, 0)
        r[:, 0:W] = base[:, 0:W]
        out = dot(info[...], r[:, 0 : 2 * W])
        back = acc[:, 0:W] - out[:, W : 2 * W]
        acc[:, 0:W] = back
        t[:, 0:W] = out[:, 0:W].astype(bf16)
        t[:, W : 2 * W] = back.astype(bf16)
        for _ in range(terms):
            out = dot(cov[...], t[:, 0 : 2 * W])
            r[:, 0:W] = (base[:, 0:W].astype(f32) - out[:, 0:W]).astype(bf16)
            r[:, W : 2 * W] = out[:, W : 2 * W].astype(bf16)
            out = dot(info[...], r[:, 0 : 2 * W])
            t[:, 0:W] = out[:, 0:W].astype(bf16)
            t[:, W : 2 * W] = (acc[:, 0:W] - out[:, W : 2 * W]).astype(bf16)
        for l in range(N):
            r[blk((q + l) % N), 0 : 2 * W] = t[l * W : (l + 1) * W, 0 : 2 * W]
        res = dot(r[:, 0 : 2 * W].T, a_full[...])
        acc[0 : 2 * W, :] = res

        def put_j(src):
            for l in range(N):
                rows = blk((q + l) % N)
                out1[rows, :] = (
                    acc[0:W, l * W : (l + 1) * W].T + src[rows, :].astype(f32)
                ).astype(bf16)

        pl.when(s[3] == 0)(lambda: put_j(adda))
        pl.when(s[3] == 1)(lambda: put_j(addb))
        vecs[...] = vi
        for l in range(N):
            spot = pl.ds(N + (q + l) % N, 1)
            vecs[spot, :] = vecs[spot, :] + acc[W : W + 1, l * W : (l + 1) * W]
        rows = lax.broadcasted_iota(jnp.int32, (2 * N, W), 0)
        out1[D : D + 2 * N, :] = jnp.where(rows < N, 0.0, vecs[...]).astype(bf16)
        out2[...] = jnp.zeros((D, W), bf16)


def finish_kernel(s, own1, own2, got1, got2, move, spread, weight, drift, belief):
    def put(first, second_move, last):
        spread[...] = first[0:D, :]
        move[...] = second_move[...]
        weight[...] = last[0:D, :]
        b = first[D : D + 2 * N, :].astype(f32)
        e = last[D : D + 2 * N, :].astype(f32)
        for l in range(N):
            drift[:, l * W : (l + 1) * W] = b[l : l + 1, :].astype(bf16)
            belief[:, l * W : (l + 1) * W] = e[N + l : N + l + 1, :].astype(bf16)

    pl.when(s[0] == 0)(lambda: put(own1, own2, got1))
    pl.when(s[0] == 1)(lambda: put(got1, got2, own1))


def swap(x, axis_bit):
    return lax.ppermute(x, "tm", [(i, i ^ (1 << axis_bit)) for i in range(lax.axis_size("tm"))])


def swap_early(x, axis_bit):
    return lax.ppermute(x, "tm", [(i, i ^ (1 << axis_bit)) for i in range(0, lax.axis_size("tm"), 2)])


def send_early(x):
    return lax.ppermute(x, "tm", [(i, i + 1) for i in range(0, lax.axis_size("tm"), 2)])


def shift(x, by):
    return lax.ppermute(x, "panel", [(i, (i + by) % N) for i in range(N)])


def gathered(msg):
    up, down = msg, msg
    got_m, got_p = [], []
    for _ in range(3):
        up = shift(up, 1)
        down = shift(down, -1)
        got_p.append(up)
        got_m.append(down)
    m4 = shift(down[0:HALF], -1)
    p4 = shift(up[HALF : 2 * HALF], 1)
    return got_m + got_p + [m4, p4]


def combined(role, q, x_pair, x_pick, ring_pair, ring_pick, ai_pair, ai_pick, add_pair, add_pick, vec_i, vec_j):
    ring_scalars = jnp.stack([role, q, x_pick, ring_pick])
    (msg,) = call(ring_kernel, [struct(RING, W)], (), ring_scalars, *x_pair, *ring_pair)
    parts = gathered(msg)
    x_full, a_full = call(
        assemble_kernel, [struct(D, D), struct(D, D)], (), ring_scalars, *x_pair, msg, *parts
    )
    x_other = swap(x_full, 0)
    return call(
        combine_kernel,
        [struct(D + 2 * N, W), struct(D, W)],
        (
            pltpu.VMEM((D, 3 * W), bf16),
            pltpu.VMEM((D, 3 * W), bf16),
            pltpu.VMEM((D, 2 * W), bf16),
            pltpu.VMEM((D, D), f32),
            pltpu.VMEM((2 * N, W), f32),
        ),
        jnp.stack([role, q, ai_pick, add_pick]),
        x_full,
        x_other,
        a_full,
        *ai_pair,
        *add_pair,
        vec_i,
        vec_j,
    )


def local(transition, drift, spread, belief, precision, probe_hosts, probe_values):
    q = lax.axis_index("panel").astype(jnp.int32)
    t = lax.axis_index("tm").astype(jnp.int32)
    role = t & 1
    odd = (t >> 1) & 1
    zero = jnp.zeros((), jnp.int32)
    move, cov, info = transition[0], spread[0], precision[0]
    first, own_vec = call(
        start_kernel,
        [struct(D + 2 * N, W), struct(2 * N, W)],
        (),
        jnp.stack([role, q]),
        cov,
        info,
        drift,
        belief,
        probe_hosts.reshape(-1, 1),
        probe_values.reshape(-1, 1),
    )
    got_move = swap(move, 0)
    got = swap(first, 0)
    got_vec = got[D:]
    vec_i = jnp.where(role == 0, own_vec, got_vec)
    vec_j = jnp.where(role == 0, got_vec, own_vec)
    out1, out2 = combined(
        role, q, (cov, info), role, (got_move, got_move), zero, (move, got_move), role,
        (got, got), zero, vec_i, vec_j,
    )
    far1 = swap(out1, 1)
    far2 = swap_early(out2, 1)
    near = odd == 0
    pair_i = jnp.where(near, out1[D:], far1[D:])
    pair_j = jnp.where(near, far1[D:], out1[D:])
    early_move = jnp.where(near, out2, far2)
    bundle = swap(jnp.concatenate([early_move, pair_i, pair_j], axis=0), 0)
    vec_i = pair_i + bundle[D : D + 2 * N]
    vec_j = pair_j + bundle[D + 2 * N :]
    late_move = jnp.where(near, far2, out2)
    out1, out2 = combined(
        role, q, (out1, far1), role ^ odd, (late_move, bundle), role, (early_move, bundle), role,
        (far1, out1), role ^ odd, vec_i, vec_j,
    )
    got1 = swap(out1, 0)
    got2 = send_early(out2)
    panel = struct(D, W)
    row = struct(1, D)
    move, cov, info, drift, belief = call(
        finish_kernel, [panel, panel, panel, row, row], (), jnp.stack([role, q]), out1, out2, got1, got2
    )
    return move[None], drift, cov[None], belief, info[None]


def solution(mesh):
    in_specs = (
        P("tm", None, "panel"),
        P("tm", None),
        P("tm", None, "panel"),
        P("tm", None),
        P("tm", None, "panel"),
        P("tm", None),
        P("tm", None),
    )
    out_specs = (
        P("tm", None, "panel"),
        P("tm", None),
        P("tm", None, "panel"),
        P("tm", None),
        P("tm", None, "panel"),
    )
    return jax.shard_map(local, mesh=mesh, in_specs=in_specs, out_specs=out_specs, check_vma=False)
```

time: 298 us -> 211 us (0.71)
  waiting for transfers between devices: 155 us -> 61.2 us
  Pallas kernels: 0 us -> 45.2 us
  matrix products: 40.9 us -> 0 us
  starting transfers between devices: 65.2 us -> 86.3 us
  between operations: 14.5 us -> 1.11 us
  local copies, waits for them, and re-layouts: 14.8 us -> 8.69 us
  other arithmetic: 3.23 us -> 7.4 us
    all_to_all x2 -> x0, waiting for transfers between devices: 96 us -> none  [sent_to_all(): lax.all_to_all(jnp.broadcast_to(shard[None], (length, *shard.shape)), axi...]
    pallas_call x0 -> x8, Pallas kernels: none -> 45.2 us  [call(): pl.pallas_call(kernel, out_shape=list(outs), in_specs=[pl.BlockSpec(memor...]
    dot_general x29 -> x0, matrix products: 40.9 us -> none  [the longest x15 15.9 us: mat_vector(): jnp.dot(matrix, vector.astype(jnp.bfloat16), preferred_element_type=jnp.f...]
    ppermute x16 -> x25, starting transfers between devices: 53 us -> 86.3 us  [the longest x16 52.9 us: shift(): return lax.ppermute(x, 'panel', [(i, (i + by) % N) for i in range(N)])]
    all_to_all x2 -> x0, starting transfers between devices: 12.1 us -> none  [sent_to_all(): lax.all_to_all(jnp.broadcast_to(shard[None], (length, *shard.shape)), axi...]
    all_to_all x2 -> x0, local copies, waits for them, and re-layouts: 5.71 us -> none  [sent_to_all(): lax.all_to_all(jnp.broadcast_to(shard[None], (length, *shard.shape)), axi...]
    broadcast_in_dim x5 -> x0, local copies, waits for them, and re-layouts: 4.62 us -> none  [the longest x3 3.43 us: sent_to_all(): jnp.broadcast_to(shard[None], (length, *shard.shape))]
    unnamed x26 -> x54, local copies, waits for them, and re-layouts: 3.63 us -> 7.04 us
  transfers between devices with their start and end apart: 20 -> 25, of which waited for: 12 -> 16; matrix products, arithmetic and copies ran while one was open for 15% -> 4% of each run, Pallas kernels for 0% -> 1%
where the time goes in v1:
time: 211 us; the launch traced here: 210 us
  starting transfers between devices  86.3 us (41%)
  waiting for transfers between devices  61.2 us (29%)
  Pallas kernels  45.2 us (21%)
  local copies, waits for them, and re-layouts  8.69 us (4%)
  other arithmetic  7.4 us (4%)
    ppermute x16, starting transfers between devices, shift(): return lax.ppermute(x, 'panel', [(i, (i + by) % N) for i in range(N)])  52.9 us
    ppermute x16, waiting for transfers between devices, shift(): return lax.ppermute(x, 'panel', [(i, (i + by) % N) for i in range(N)])  46.8 us
    pallas_call x8, Pallas kernels, call(): pl.pallas_call(kernel, out_shape=list(outs), in_specs=[pl.BlockSpec(memor...  45.2 us
    ppermute x7, starting transfers between devices, swap(): lax.ppermute(x, 'tm', [(i, i ^ 1 << axis_bit) for i in range(lax.axis_siz...  31.4 us
    ppermute x7, waiting for transfers between devices, swap(): lax.ppermute(x, 'tm', [(i, i ^ 1 << axis_bit) for i in range(lax.axis_siz...  12 us
    unnamed x54, local copies, waits for them, and re-layouts  7.04 us
  transfers between devices with their start and end apart: 25, of which 16 were waited for; matrix products, arithmetic and copies ran while one was open for 4% of the time, Pallas kernels for 1%

profile of v1, /device:TPU:1, one launch (start us, length us, event | category | flops | bytes accessed | tf_op | source)
XLA Modules:
  0.0 209.9 jit_solution(16634987913153063742)
XLA Ops:
  0.6 8.7 %collective-permute-start = (bf16[1024,128]{1,0:T(8,128)(2,1)}, bf16[1024,128]{1,0:T(8,128)(2,1)S(1)}, u32[]{:S(2)}, u32[]{:S(2)}) collective-permute-start(bf16[1024,128]{1,0:T(8,128)(2,1)} %bitcast.17), channel_id=1, source_target_pairs={{0,8},{8,0},{16,24},{24,16},{32,40},{40,32},{48,56},{56,48},{64,72... | collective-permute-start | bytes 786440 | tf_op jit(solution)/shard_map/ppermute | solution.py:249
  10.0 0.8 collective-permute-done.aa.ab.aib
  10.7 0.7 copy-done.2
  11.4 2.0 shard_map.110.msg
  13.5 1.9 collective-permute-start.4
  15.4 4.6 %collective-permute-start.1 = (bf16[1664,128]{1,0:T(8,128)(2,1)}, bf16[1664,128]{1,0:T(8,128)(2,1)S(1)}, u32[]{:S(2)}, u32[]{:S(2)}) collective-permute-start(bf16[1664,128]{1,0:T(8,128)(2,1)} %shard_map.110.msg), channel_id=1, source_target_pairs={{0,7},{1,0},{2,1},{3,2},{4,3},{5,4},{6,5},{7,6},{8,15},{9,8},{10,9... | collective-permute-start | bytes 1277960 | tf_op jit(solution)/shard_map/ppermute | solution.py:261
  20.0 7.8 %collective-permute-done.4.p1 = bf16[1664,128]{1,0:T(8,128)(2,1)S(1)} collective-permute-done((bf16[1664,128]{1,0:T(8,128)(2,1)}, bf16[1664,128]{1,0:T(8,128)(2,1)S(1)}, u32[]{:S(2)}, u32[]{:S(2)}) %collective-permute-start.4) | collective-permute-done | bytes 426016 | tf_op jit(solution)/shard_map/ppermute | solution.py:261
  27.8 1.9 collective-permute-start.5
  29.7 4.6 %collective-permute-start.2 = (bf16[1664,128]{1,0:T(8,128)(2,1)S(1)}, bf16[1664,128]{1,0:T(8,128)(2,1)S(1)}, u32[]{:S(2)}, u32[]{:S(2)}) collective-permute-start(bf16[1664,128]{1,0:T(8,128)(2,1)S(1)} %collective-permute-done.1.m1), channel_id=1, source_target_pairs={{0,7},{1,0},{2,1},{3,2},{4,3},{5,4},{6,5},{7,6},{8,15},{9,8},{10,9... | collective-permute-start | bytes 1277960 | tf_op jit(solution)/shard_map/ppermute | solution.py:261
  34.3 6.7 %collective-permute-done.5.p2 = bf16[1664,128]{1,0:T(8,128)(2,1)S(1)} collective-permute-done((bf16[1664,128]{1,0:T(8,128)(2,1)S(1)}, bf16[1664,128]{1,0:T(8,128)(2,1)S(1)}, u32[]{:S(2)}, u32[]{:S(2)}) %collective-permute-start.5) | collective-permute-done | bytes 426016 | tf_op jit(solution)/shard_map/ppermute | solution.py:261
  41.0 1.9 collective-permute-start.6
  43.0 4.6 %collective-permute-start.3 = (bf16[1664,128]{1,0:T(8,128)(2,1)S(1)}, bf16[1664,128]{1,0:T(8,128)(2,1)S(1)}, u32[]{:S(2)}, u32[]{:S(2)}) collective-permute-start(bf16[1664,128]{1,0:T(8,128)(2,1)S(1)} %collective-permute-done.2.m2), channel_id=1, source_target_pairs={{0,7},{1,0},{2,1},{3,2},{4,3},{5,4},{6,5},{7,6},{8,15},{9,8},{10,9... | collective-permute-start | bytes 1277960 | tf_op jit(solution)/shard_map/ppermute | solution.py:261
  47.5 5.9 %collective-permute-done.6.p3 = bf16[1664,128]{1,0:T(8,128)(2,1)S(1)} collective-permute-done((bf16[1664,128]{1,0:T(8,128)(2,1)S(1)}, bf16[1664,128]{1,0:T(8,128)(2,1)S(1)}, u32[]{:S(2)}, u32[]{:S(2)}) %collective-permute-start.6) | collective-permute-done | bytes 426016 | tf_op jit(solution)/shard_map/ppermute | solution.py:261
  53.4 2.1 collective-permute-start.8
  55.6 4.7 %collective-permute-start.7 = (bf16[768,128]{1,0:T(8,128)(2,1)S(1)}, bf16[768,128]{1,0:T(8,128)(2,1)S(1)}, u32[]{:S(2)}, u32[]{:S(2)}) collective-permute-start(bf16[768,128]{1,0:T(8,128)(2,1)S(1)} %slice.38), channel_id=1, source_target_pairs={{0,7},{1,0},{2,1},{3,2},{4,3},{5,4},{6,5},{7,6},{8,15},{9,8},{10,9... | collective-permute-start | bytes 589832 | tf_op jit(solution)/shard_map/ppermute | solution.py:261
  60.3 0.9 collective-permute-done.8.p4
  61.2 1.7 collective-permute-done.7.m4
  62.9 0.7 copy-done.24
  63.6 4.7 %shard_map.111 = (bf16[1024,1024]{1,0:T(8,128)(2,1)}, bf16[1024,1024]{1,0:T(8,128)(2,1)}) custom-call(s32[4]{0:T(128)} %get-tuple-element.35.s, bf16[1024,128]{1,0:T(8,128)(2,1)} %bitcast.12, bf16[1024,128]{1,0:T(8,128)(2,1)} %bitcast.15, bf16[1664,128]{1,0:T(8,128)(2,1)} %shard_map.110.msg, bf16[1664,128]{1,0:T(8,128)(2,1)} %copy-done.14, ...), custom_call_target="tpu_custom_call" | custom-call | tf_op jit(solution)/shard_map/pallas_call | solution.py:41
  68.3 6.0 %collective-permute-start.9 = (bf16[1024,1024]{1,0:T(8,128)(2,1)}, bf16[1024,1024]{1,0:T(8,128)(2,1)S(1)}, u32[]{:S(2)}, u32[]{:S(2)}) collective-permute-start(bf16[1024,1024]{1,0:T(8,128)(2,1)} %get-tuple-element.20.x_own), channel_id=1, source_target_pairs={{0,8},{8,0},{16,24},{24,16},{32,40},{40,32},{48,56},{56,48},{64,72... | collective-permute-start | bytes 6291464 | tf_op jit(solution)/shard_map/ppermute | solution.py:249
  74.3 0.8 copy.12.hosts
  75.1 0.8 copy.13.values
  75.9 0.7 pad_add_fusion.s
  76.5 2.1 %shard_map.112 = (bf16[1040,128]{1,0:T(8,128)(2,1)}, bf16[16,128]{1,0:T(8,128)(2,1)}) custom-call(s32[2]{0:T(128)} %pad_add_fusion.s, bf16[1024,128]{1,0:T(8,128)(2,1)} %bitcast.13, bf16[1024,128]{1,0:T(8,128)(2,1)} %bitcast.16, bf16[1,1024]{1,0:T(2,128)(2,1)} %drift.1, bf16[1,1024]{1,0:T(2,128)(2,1)} %belief.1, s32[256,1]{1,0:T(8,128)} %copy.12.hosts, ...), custom_call_target="tpu_custom_call" | custom-call | tf_op jit(solution)/shard_map/pallas_call | solution.py:41
  78.7 1.9 collective-permute-start.10
  80.6 1.7 collective-permute-done.10.adda.addb
  82.3 1.3 broadcast_select_fusion.4
  83.6 1.4 copy-done.4
  85.0 13.6 %shard_map.113 = (bf16[1040,128]{1,0:T(8,128)(2,1)}, bf16[1024,128]{1,0:T(8,128)(2,1)}) custom-call(s32[4]{0:T(128)} %get-tuple-element.35.s, bf16[1024,1024]{1,0:T(8,128)(2,1)} %get-tuple-element.20.x_own, bf16[1024,1024]{1,0:T(8,128)(2,1)} %copy-done.4, bf16[1024,1024]{1,0:T(8,128)(2,1)} %get-tuple-element.21.a_full, bf16[1024,128]{1,0:T(8,128)(2,1)} %bitcast.18, ...), custom_call_target="tpu_custom_call" | custom-call | tf_op jit(solution)/shard_map/pallas_call | solution.py:41
  98.6 0.7 collective-permute-start.12
  99.2 1.9 collective-permute-start.11
  101.2 1.7 broadcast_select_fusion
  102.9 6.8 %collective-permute-done.11.xb.adda = bf16[1040,128]{1,0:T(8,128)(2,1)S(1)} collective-permute-done((bf16[1040,128]{1,0:T(8,128)(2,1)}, bf16[1040,128]{1,0:T(8,128)(2,1)S(1)}, u32[]{:S(2)}, u32[]{:S(2)}) %collective-permute-start.11) | collective-permute-done | bytes 266272 | tf_op jit(solution)/shard_map/ppermute | solution.py:249
  109.8 0.7 broadcast_select_fusion.3
  110.5 5.1 %collective-permute-start.13 = (bf16[1056,128]{1,0:T(8,128)(2,1)S(1)}, bf16[1056,128]{1,0:T(8,128)(2,1)S(1)}, u32[]{:S(2)}, u32[]{:S(2)}) collective-permute-start(bf16[1056,128]{1,0:T(8,128)(2,1)S(1)} %pad_maximum_fusion), channel_id=1, source_target_pairs={{0,8},{8,0},{16,24},{24,16},{32,40},{40,32},{48,56},{56,48},{64,72... | collective-permute-start | bytes 811016 | tf_op jit(solution)/shard_map/ppermute | solution.py:249
  115.5 0.6 pad_add_fusion.4.s
  116.7 0.8 copy-done.5
  117.4 2.0 shard_map.114.msg
  119.5 1.9 collective-permute-start.17
  121.4 5.3 %collective-permute-start.14 = (bf16[1664,128]{1,0:T(8,128)(2,1)}, bf16[1664,128]{1,0:T(8,128)(2,1)S(1)}, u32[]{:S(2)}, u32[]{:S(2)}) collective-permute-start(bf16[1664,128]{1,0:T(8,128)(2,1)} %shard_map.114.msg), channel_id=1, source_target_pairs={{0,7},{1,0},{2,1},{3,2},{4,3},{5,4},{6,5},{7,6},{8,15},{9,8},{10,9... | collective-permute-start | bytes 1277960 | tf_op jit(solution)/shard_map/ppermute | solution.py:261
  126.7 8.1 %collective-permute-done.17.p1 = bf16[1664,128]{1,0:T(8,128)(2,1)S(1)} collective-permute-done((bf16[1664,128]{1,0:T(8,128)(2,1)}, bf16[1664,128]{1,0:T(8,128)(2,1)S(1)}, u32[]{:S(2)}, u32[]{:S(2)}) %collective-permute-start.17) | collective-permute-done | bytes 426016 | tf_op jit(solution)/shard_map/ppermute | solution.py:261
  134.8 1.9 collective-permute-start.18
  136.8 4.6 %collective-permute-start.15 = (bf16[1664,128]{1,0:T(8,128)(2,1)S(1)}, bf16[1664,128]{1,0:T(8,128)(2,1)S(1)}, u32[]{:S(2)}, u32[]{:S(2)}) collective-permute-start(bf16[1664,128]{1,0:T(8,128)(2,1)S(1)} %collective-permute-done.14.m1), channel_id=1, source_target_pairs={{0,7},{1,0},{2,1},{3,2},{4,3},{5,4},{6,5},{7,6},{8,15},{9,8},{10,9... | collective-permute-start | bytes 1277960 | tf_op jit(solution)/shard_map/ppermute | solution.py:261
  141.4 7.0 %collective-permute-done.18.p2 = bf16[1664,128]{1,0:T(8,128)(2,1)S(1)} collective-permute-done((bf16[1664,128]{1,0:T(8,128)(2,1)S(1)}, bf16[1664,128]{1,0:T(8,128)(2,1)S(1)}, u32[]{:S(2)}, u32[]{:S(2)}) %collective-permute-start.18) | collective-permute-done | bytes 426016 | tf_op jit(solution)/shard_map/ppermute | solution.py:261
  148.4 1.9 collective-permute-start.19
  150.3 4.6 %collective-permute-start.16 = (bf16[1664,128]{1,0:T(8,128)(2,1)S(1)}, bf16[1664,128]{1,0:T(8,128)(2,1)S(1)}, u32[]{:S(2)}, u32[]{:S(2)}) collective-permute-start(bf16[1664,128]{1,0:T(8,128)(2,1)S(1)} %collective-permute-done.15.m2), channel_id=1, source_target_pairs={{0,7},{1,0},{2,1},{3,2},{4,3},{5,4},{6,5},{7,6},{8,15},{9,8},{10,9... | collective-permute-start | bytes 1277960 | tf_op jit(solution)/shard_map/ppermute | solution.py:261
  154.9 6.1 %collective-permute-done.19.p3 = bf16[1664,128]{1,0:T(8,128)(2,1)S(1)} collective-permute-done((bf16[1664,128]{1,0:T(8,128)(2,1)S(1)}, bf16[1664,128]{1,0:T(8,128)(2,1)S(1)}, u32[]{:S(2)}, u32[]{:S(2)}) %collective-permute-start.19) | collective-permute-done | bytes 426016 | tf_op jit(solution)/shard_map/ppermute | solution.py:261
  161.0 1.9 collective-permute-start.21
  163.0 4.6 %collective-permute-start.20 = (bf16[768,128]{1,0:T(8,128)(2,1)S(1)}, bf16[768,128]{1,0:T(8,128)(2,1)S(1)}, u32[]{:S(2)}, u32[]{:S(2)}) collective-permute-start(bf16[768,128]{1,0:T(8,128)(2,1)S(1)} %slice.42), channel_id=1, source_target_pairs={{0,7},{1,0},{2,1},{3,2},{4,3},{5,4},{6,5},{7,6},{8,15},{9,8},{10,9... | collective-permute-start | bytes 589832 | tf_op jit(solution)/shard_map/ppermute | solution.py:261
  167.6 1.1 collective-permute-done.21.p4
  168.7 1.5 collective-permute-done.20.m4
  170.2 0.7 copy-done.23
  170.9 4.7 %shard_map.115 = (bf16[1024,1024]{1,0:T(8,128)(2,1)}, bf16[1024,1024]{1,0:T(8,128)(2,1)}) custom-call(s32[4]{0:T(128)} %pad_add_fusion.4.s, bf16[1040,128]{1,0:T(8,128)(2,1)} %get-tuple-element.24.xa.addb, bf16[1040,128]{1,0:T(8,128)(2,1)} %copy-done, bf16[1664,128]{1,0:T(8,128)(2,1)} %shard_map.114.msg, bf16[1664,128]{1,0:T(8,128)(2,1)} %copy-done.13, ...), custom_call_target="tpu_custom_call" | custom-call | tf_op jit(solution)/shard_map/pallas_call | solution.py:41
  175.6 5.7 %collective-permute-start.22 = (bf16[1024,1024]{1,0:T(8,128)(2,1)}, bf16[1024,1024]{1,0:T(8,128)(2,1)S(1)}, u32[]{:S(2)}, u32[]{:S(2)}) collective-permute-start(bf16[1024,1024]{1,0:T(8,128)(2,1)} %get-tuple-element.26.x_own), channel_id=1, source_target_pairs={{0,8},{8,0},{16,24},{24,16},{32,40},{40,32},{48,56},{56,48},{64,72... | collective-permute-start | bytes 6291464 | tf_op jit(solution)/shard_map/ppermute | solution.py:249
  181.9 1.3 slice_add_fusion
  183.2 2.1 %collective-permute-done.22.x_other = bf16[1024,1024]{1,0:T(8,128)(2,1)S(1)} collective-permute-done((bf16[1024,1024]{1,0:T(8,128)(2,1)}, bf16[1024,1024]{1,0:T(8,128)(2,1)S(1)}, u32[]{:S(2)}, u32[]{:S(2)}) %collective-permute-start.22) | collective-permute-done | bytes 2097184 | tf_op jit(solution)/shard_map/ppermute | solution.py:249
  185.3 1.4 copy-done.3
  186.6 13.8 %shard_map.116 = (bf16[1040,128]{1,0:T(8,128)(2,1)}, bf16[1024,128]{1,0:T(8,128)(2,1)}) custom-call(s32[4]{0:T(128)} %pad_add_fusion.1.s, bf16[1024,1024]{1,0:T(8,128)(2,1)} %get-tuple-element.26.x_own, bf16[1024,1024]{1,0:T(8,128)(2,1)} %copy-done.3, bf16[1024,1024]{1,0:T(8,128)(2,1)} %get-tuple-element.27.a_full, bf16[1024,128]{1,0:T(8,128)(2,1)} %copy-done.1, ...), custom_call_target="tpu_custom_call" | custom-call | tf_op jit(solution)/shard_map/pallas_call | solution.py:41
  200.5 2.2 %collective-permute-start.23 = (bf16[1040,128]{1,0:T(8,128)(2,1)}, bf16[1040,128]{1,0:T(8,128)(2,1)S(1)}, u32[]{:S(2)}, u32[]{:S(2)}) collective-permute-start(bf16[1040,128]{1,0:T(8,128)(2,1)} %get-tuple-element.28.own1), channel_id=1, source_target_pairs={{0,8},{8,0},{16,24},{24,16},{32,40},{40,32},{48,56},{56,48},{64,72... | collective-permute-start | bytes 798728 | tf_op jit(solution)/shard_map/ppermute | solution.py:249
  202.6 1.3 collective-permute-start.24
  203.9 2.3 %collective-permute-done.24.got2 = bf16[1024,128]{1,0:T(8,128)(2,1)S(1)} collective-permute-done((bf16[1024,128]{1,0:T(8,128)(2,1)}, bf16[1024,128]{1,0:T(8,128)(2,1)S(1)}, u32[]{:S(2)}, u32[]{:S(2)}) %collective-permute-start.24) | collective-permute-done | bytes 262176 | tf_op jit(solution)/shard_map/ppermute | solution.py:257
  206.3 0.7 copy-done.20
  207.0 0.7 copy-done.19
  207.7 2.1 %shard_map.117 = (bf16[1024,128]{1,0:T(8,128)(2,1)}, bf16[1024,128]{1,0:T(8,128)(2,1)}, bf16[1024,128]{1,0:T(8,128)(2,1)}, bf16[1,1024]{1,0:T(2,128)(2,1)}, bf16[1,1024]{1,0:T(2,128)(2,1)}) custom-call(s32[2]{0:T(128)} %pad_add_fusion.s, bf16[1040,128]{1,0:T(8,128)(2,1)} %get-tuple-element.28.own1, bf16[1024,128]{1,0:T(8,128)(2,1)} %get-tuple-element.29.own2, ...), custom_call_target="tpu_custom_call" | custom-call | tf_op jit(solution)/shard_map/pallas_call | solution.py:41
  (63 shorter events, 1.9 us)
Async XLA Ops:
  0.6 10.1 %collective-permute-start = (bf16[1024,128]{1,0:T(8,128)(2,1)}, bf16[1024,128]{1,0:T(8,128)(2,1)S(1)}, u32[]{:S(2)}, u32[]{:S(2)}) collective-permute-start(bf16[1024,128]{1,0:T(8,128)(2,1)} %bitcast.17), channel_id=1, source_target_pairs={{0,8},{8,0},{16,24},{24,16},{32,40},{40,32},{48,56},{56,48},{64,72... | collective-permute-start | bytes 786440 | tf_op jit(solution)/shard_map/ppermute | solution.py:249
  10.7 0.7 copy-start.2
  13.5 14.3 %collective-permute-start.4 = (bf16[1664,128]{1,0:T(8,128)(2,1)}, bf16[1664,128]{1,0:T(8,128)(2,1)S(1)}, u32[]{:S(2)}, u32[]{:S(2)}) collective-permute-start(bf16[1664,128]{1,0:T(8,128)(2,1)} %shard_map.110.msg), channel_id=1, source_target_pairs={{0,1},{1,2},{2,3},{3,4},{4,5},{5,6},{6,7},{7,0},{8,9},{9,10},{10,1... | collective-permute-start | bytes 1277960 | tf_op jit(solution)/shard_map/ppermute | solution.py:261
  15.4 14.3 %collective-permute-start.1 = (bf16[1664,128]{1,0:T(8,128)(2,1)}, bf16[1664,128]{1,0:T(8,128)(2,1)S(1)}, u32[]{:S(2)}, u32[]{:S(2)}) collective-permute-start(bf16[1664,128]{1,0:T(8,128)(2,1)} %shard_map.110.msg), channel_id=1, source_target_pairs={{0,7},{1,0},{2,1},{3,2},{4,3},{5,4},{6,5},{7,6},{8,15},{9,8},{10,9... | collective-permute-start | bytes 1277960 | tf_op jit(solution)/shard_map/ppermute | solution.py:261
  27.8 35.1 %copy-start.12 = (bf16[1664,128]{1,0:T(8,128)(2,1)}, bf16[1664,128]{1,0:T(8,128)(2,1)S(1)}, u32[]{:S(2)}) copy-start(bf16[1664,128]{1,0:T(8,128)(2,1)S(1)} %collective-permute-done.4.p1) | copy-start | bytes 1277956
  27.8 13.2 %collective-permute-start.5 = (bf16[1664,128]{1,0:T(8,128)(2,1)S(1)}, bf16[1664,128]{1,0:T(8,128)(2,1)S(1)}, u32[]{:S(2)}, u32[]{:S(2)}) collective-permute-start(bf16[1664,128]{1,0:T(8,128)(2,1)S(1)} %collective-permute-done.4.p1), channel_id=1, source_target_pairs={{0,1},{1,2},{2,3},{3,4},{4,5},{5,6},{6,7},{7,0},{8,9},{9,10},{10,1... | collective-permute-start | bytes 1277960 | tf_op jit(solution)/shard_map/ppermute | solution.py:261
  29.7 33.2 %copy-start.14 = (bf16[1664,128]{1,0:T(8,128)(2,1)}, bf16[1664,128]{1,0:T(8,128)(2,1)S(1)}, u32[]{:S(2)}) copy-start(bf16[1664,128]{1,0:T(8,128)(2,1)S(1)} %collective-permute-done.1.m1) | copy-start | bytes 1277956
  29.7 13.2 %collective-permute-start.2 = (bf16[1664,128]{1,0:T(8,128)(2,1)S(1)}, bf16[1664,128]{1,0:T(8,128)(2,1)S(1)}, u32[]{:S(2)}, u32[]{:S(2)}) collective-permute-start(bf16[1664,128]{1,0:T(8,128)(2,1)S(1)} %collective-permute-done.1.m1), channel_id=1, source_target_pairs={{0,7},{1,0},{2,1},{3,2},{4,3},{5,4},{6,5},{7,6},{8,15},{9,8},{10,9... | collective-permute-start | bytes 1277960 | tf_op jit(solution)/shard_map/ppermute | solution.py:261
  41.0 21.8 %copy-start.16 = (bf16[1664,128]{1,0:T(8,128)(2,1)}, bf16[1664,128]{1,0:T(8,128)(2,1)S(1)}, u32[]{:S(2)}) copy-start(bf16[1664,128]{1,0:T(8,128)(2,1)S(1)} %collective-permute-done.5.p2) | copy-start | bytes 1277956
  41.0 12.4 %collective-permute-start.6 = (bf16[1664,128]{1,0:T(8,128)(2,1)S(1)}, bf16[1664,128]{1,0:T(8,128)(2,1)S(1)}, u32[]{:S(2)}, u32[]{:S(2)}) collective-permute-start(bf16[1664,128]{1,0:T(8,128)(2,1)S(1)} %collective-permute-done.5.p2), channel_id=1, source_target_pairs={{0,1},{1,2},{2,3},{3,4},{4,5},{5,6},{6,7},{7,0},{8,9},{9,10},{10,1... | collective-permute-start | bytes 1277960 | tf_op jit(solution)/shard_map/ppermute | solution.py:261
  43.0 19.9 %copy-start.18 = (bf16[1664,128]{1,0:T(8,128)(2,1)}, bf16[1664,128]{1,0:T(8,128)(2,1)S(1)}, u32[]{:S(2)}) copy-start(bf16[1664,128]{1,0:T(8,128)(2,1)S(1)} %collective-permute-done.2.m2) | copy-start | bytes 1277956
  43.0 12.5 %collective-permute-start.3 = (bf16[1664,128]{1,0:T(8,128)(2,1)S(1)}, bf16[1664,128]{1,0:T(8,128)(2,1)S(1)}, u32[]{:S(2)}, u32[]{:S(2)}) collective-permute-start(bf16[1664,128]{1,0:T(8,128)(2,1)S(1)} %collective-permute-done.2.m2), channel_id=1, source_target_pairs={{0,7},{1,0},{2,1},{3,2},{4,3},{5,4},{6,5},{7,6},{8,15},{9,8},{10,9... | collective-permute-start | bytes 1277960 | tf_op jit(solution)/shard_map/ppermute | solution.py:261
  53.4 9.5 %copy-start.8 = (bf16[1664,128]{1,0:T(8,128)(2,1)}, bf16[1664,128]{1,0:T(8,128)(2,1)S(1)}, u32[]{:S(2)}) copy-start(bf16[1664,128]{1,0:T(8,128)(2,1)S(1)} %collective-permute-done.6.p3) | copy-start | bytes 1277956
  53.4 20.8 %copy-start.25 = (s32[1,256]{1,0:T(1,128)S(1)}, s32[1,256]{1,0:T(1,128)}, u32[]{:S(2)}) copy-start(s32[1,256]{1,0:T(1,128)} %param.12) | copy-start | bytes 3076
  53.4 7.8 %collective-permute-start.8 = (bf16[768,128]{1,0:T(8,128)(2,1)S(1)}, bf16[768,128]{1,0:T(8,128)(2,1)S(1)}, u32[]{:S(2)}, u32[]{:S(2)}) collective-permute-start(bf16[768,128]{1,0:T(8,128)(2,1)S(1)} %slice.39), channel_id=1, source_target_pairs={{0,1},{1,2},{2,3},{3,4},{4,5},{5,6},{6,7},{7,0},{8,9},{9,10},{10,1... | collective-permute-start | bytes 589832 | tf_op jit(solution)/shard_map/ppermute | solution.py:261
  55.5 7.4 %copy-start.10 = (bf16[1664,128]{1,0:T(8,128)(2,1)}, bf16[1664,128]{1,0:T(8,128)(2,1)S(1)}, u32[]{:S(2)}) copy-start(bf16[1664,128]{1,0:T(8,128)(2,1)S(1)} %collective-permute-done.3.m3) | copy-start | bytes 1277956
  55.5 19.5 %copy-start.26 = (f32[1,256]{1,0:T(1,128)S(1)}, f32[1,256]{1,0:T(1,128)}, u32[]{:S(2)}) copy-start(f32[1,256]{1,0:T(1,128)} %param.13) | copy-start | bytes 3076
  55.6 7.3 %collective-permute-start.7 = (bf16[768,128]{1,0:T(8,128)(2,1)S(1)}, bf16[768,128]{1,0:T(8,128)(2,1)S(1)}, u32[]{:S(2)}, u32[]{:S(2)}) collective-permute-start(bf16[768,128]{1,0:T(8,128)(2,1)S(1)} %slice.38), channel_id=1, source_target_pairs={{0,7},{1,0},{2,1},{3,2},{4,3},{5,4},{6,5},{7,6},{8,15},{9,8},{10,9... | collective-permute-start | bytes 589832 | tf_op jit(solution)/shard_map/ppermute | solution.py:261
  61.2 1.7 copy-start.22
  62.9 0.7 copy-start.24
  68.3 15.3 %collective-permute-start.9 = (bf16[1024,1024]{1,0:T(8,128)(2,1)}, bf16[1024,1024]{1,0:T(8,128)(2,1)S(1)}, u32[]{:S(2)}, u32[]{:S(2)}) collective-permute-start(bf16[1024,1024]{1,0:T(8,128)(2,1)} %get-tuple-element.20.x_own), channel_id=1, source_target_pairs={{0,8},{8,0},{16,24},{24,16},{32,40},{40,32},{48,56},{56,48},{64,72... | collective-permute-start | bytes 6291464 | tf_op jit(solution)/shard_map/ppermute | solution.py:249
  78.7 3.6 %collective-permute-start.10 = (bf16[1040,128]{1,0:T(8,128)(2,1)}, bf16[1040,128]{1,0:T(8,128)(2,1)S(1)}, u32[]{:S(2)}, u32[]{:S(2)}) collective-permute-start(bf16[1040,128]{1,0:T(8,128)(2,1)} %get-tuple-element.22), channel_id=1, source_target_pairs={{0,8},{8,0},{16,24},{24,16},{32,40},{40,32},{48,56},{56,48},{64,72... | collective-permute-start | bytes 798728 | tf_op jit(solution)/shard_map/ppermute | solution.py:249
  82.3 1.3 copy-start.6
  83.6 1.4 copy-start.4
  98.6 2.6 %collective-permute-start.12 = (bf16[1024,128]{1,0:T(8,128)(2,1)}, bf16[1024,128]{1,0:T(8,128)(2,1)S(1)}, u32[]{:S(2)}, u32[]{:S(2)}) collective-permute-start(bf16[1024,128]{1,0:T(8,128)(2,1)} %get-tuple-element.25), channel_id=1, source_target_pairs={{0,16},{16,0},{32,48},{48,32},{64,80},{80,64},{96,112},{112,96},{1... | collective-permute-start | bytes 786440 | tf_op jit(solution)/shard_map/ppermute | solution.py:253
  99.2 10.5 %collective-permute-start.11 = (bf16[1040,128]{1,0:T(8,128)(2,1)}, bf16[1040,128]{1,0:T(8,128)(2,1)S(1)}, u32[]{:S(2)}, u32[]{:S(2)}) collective-permute-start(bf16[1040,128]{1,0:T(8,128)(2,1)} %get-tuple-element.24.xa.addb), channel_id=1, source_target_pairs={{0,16},{8,24},{16,0},{24,8},{32,48},{40,56},{48,32},{56,40},{64,80... | collective-permute-start | bytes 798728 | tf_op jit(solution)/shard_map/ppermute | solution.py:249
  102.9 72.7 %copy-start.1 = (bf16[1024,128]{1,0:T(8,128)(2,1)}, bf16[1024,128]{1,0:T(8,128)(2,1)S(1)}, u32[]{:S(2)}) copy-start(bf16[1024,128]{1,0:T(8,128)(2,1)S(1)} %get-tuple-element.39.aia) | copy-start | bytes 786436
  109.8 6.9 %copy-start = (bf16[1040,128]{1,0:T(8,128)(2,1)}, bf16[1040,128]{1,0:T(8,128)(2,1)S(1)}, u32[]{:S(2)}) copy-start(bf16[1040,128]{1,0:T(8,128)(2,1)S(1)} %collective-permute-done.11.xb.adda) | copy-start | bytes 798724
  110.5 6.2 %collective-permute-start.13 = (bf16[1056,128]{1,0:T(8,128)(2,1)S(1)}, bf16[1056,128]{1,0:T(8,128)(2,1)S(1)}, u32[]{:S(2)}, u32[]{:S(2)}) collective-permute-start(bf16[1056,128]{1,0:T(8,128)(2,1)S(1)} %pad_maximum_fusion), channel_id=1, source_target_pairs={{0,8},{8,0},{16,24},{24,16},{32,40},{40,32},{48,56},{56,48},{64,72... | collective-permute-start | bytes 811016 | tf_op jit(solution)/shard_map/ppermute | solution.py:249
  116.7 0.8 copy-start.5
  119.5 15.3 %collective-permute-start.17 = (bf16[1664,128]{1,0:T(8,128)(2,1)}, bf16[1664,128]{1,0:T(8,128)(2,1)S(1)}, u32[]{:S(2)}, u32[]{:S(2)}) collective-permute-start(bf16[1664,128]{1,0:T(8,128)(2,1)} %shard_map.114.msg), channel_id=1, source_target_pairs={{0,1},{1,2},{2,3},{3,4},{4,5},{5,6},{6,7},{7,0},{8,9},{9,10},{10,1... | collective-permute-start | bytes 1277960 | tf_op jit(solution)/shard_map/ppermute | solution.py:261
  121.4 15.3 %collective-permute-start.14 = (bf16[1664,128]{1,0:T(8,128)(2,1)}, bf16[1664,128]{1,0:T(8,128)(2,1)S(1)}, u32[]{:S(2)}, u32[]{:S(2)}) collective-permute-start(bf16[1664,128]{1,0:T(8,128)(2,1)} %shard_map.114.msg), channel_id=1, source_target_pairs={{0,7},{1,0},{2,1},{3,2},{4,3},{5,4},{6,5},{7,6},{8,15},{9,8},{10,9... | collective-permute-start | bytes 1277960 | tf_op jit(solution)/shard_map/ppermute | solution.py:261
  134.8 35.4 %copy-start.11 = (bf16[1664,128]{1,0:T(8,128)(2,1)}, bf16[1664,128]{1,0:T(8,128)(2,1)S(1)}, u32[]{:S(2)}) copy-start(bf16[1664,128]{1,0:T(8,128)(2,1)S(1)} %collective-permute-done.17.p1) | copy-start | bytes 1277956
  134.8 13.5 %collective-permute-start.18 = (bf16[1664,128]{1,0:T(8,128)(2,1)S(1)}, bf16[1664,128]{1,0:T(8,128)(2,1)S(1)}, u32[]{:S(2)}, u32[]{:S(2)}) collective-permute-start(bf16[1664,128]{1,0:T(8,128)(2,1)S(1)} %collective-permute-done.17.p1), channel_id=1, source_target_pairs={{0,1},{1,2},{2,3},{3,4},{4,5},{5,6},{6,7},{7,0},{8,9},{9,10},{10,1... | collective-permute-start | bytes 1277960 | tf_op jit(solution)/shard_map/ppermute | solution.py:261
  136.8 33.4 %copy-start.13 = (bf16[1664,128]{1,0:T(8,128)(2,1)}, bf16[1664,128]{1,0:T(8,128)(2,1)S(1)}, u32[]{:S(2)}) copy-start(bf16[1664,128]{1,0:T(8,128)(2,1)S(1)} %collective-permute-done.14.m1) | copy-start | bytes 1277956
  136.8 13.5 %collective-permute-start.15 = (bf16[1664,128]{1,0:T(8,128)(2,1)S(1)}, bf16[1664,128]{1,0:T(8,128)(2,1)S(1)}, u32[]{:S(2)}, u32[]{:S(2)}) collective-permute-start(bf16[1664,128]{1,0:T(8,128)(2,1)S(1)} %collective-permute-done.14.m1), channel_id=1, source_target_pairs={{0,7},{1,0},{2,1},{3,2},{4,3},{5,4},{6,5},{7,6},{8,15},{9,8},{10,9... | collective-permute-start | bytes 1277960 | tf_op jit(solution)/shard_map/ppermute | solution.py:261
  148.4 21.8 %copy-start.15 = (bf16[1664,128]{1,0:T(8,128)(2,1)}, bf16[1664,128]{1,0:T(8,128)(2,1)S(1)}, u32[]{:S(2)}) copy-start(bf16[1664,128]{1,0:T(8,128)(2,1)S(1)} %collective-permute-done.18.p2) | copy-start | bytes 1277956
  148.4 12.7 %collective-permute-start.19 = (bf16[1664,128]{1,0:T(8,128)(2,1)S(1)}, bf16[1664,128]{1,0:T(8,128)(2,1)S(1)}, u32[]{:S(2)}, u32[]{:S(2)}) collective-permute-start(bf16[1664,128]{1,0:T(8,128)(2,1)S(1)} %collective-permute-done.18.p2), channel_id=1, source_target_pairs={{0,1},{1,2},{2,3},{3,4},{4,5},{5,6},{6,7},{7,0},{8,9},{9,10},{10,1... | collective-permute-start | bytes 1277960 | tf_op jit(solution)/shard_map/ppermute | solution.py:261
  150.3 19.9 %copy-start.17 = (bf16[1664,128]{1,0:T(8,128)(2,1)}, bf16[1664,128]{1,0:T(8,128)(2,1)S(1)}, u32[]{:S(2)}) copy-start(bf16[1664,128]{1,0:T(8,128)(2,1)S(1)} %collective-permute-done.15.m2) | copy-start | bytes 1277956
  150.3 12.7 %collective-permute-start.16 = (bf16[1664,128]{1,0:T(8,128)(2,1)S(1)}, bf16[1664,128]{1,0:T(8,128)(2,1)S(1)}, u32[]{:S(2)}, u32[]{:S(2)}) collective-permute-start(bf16[1664,128]{1,0:T(8,128)(2,1)S(1)} %collective-permute-done.15.m2), channel_id=1, source_target_pairs={{0,7},{1,0},{2,1},{3,2},{4,3},{5,4},{6,5},{7,6},{8,15},{9,8},{10,9... | collective-permute-start | bytes 1277960 | tf_op jit(solution)/shard_map/ppermute | solution.py:261
  161.0 9.2 %copy-start.7 = (bf16[1664,128]{1,0:T(8,128)(2,1)}, bf16[1664,128]{1,0:T(8,128)(2,1)S(1)}, u32[]{:S(2)}) copy-start(bf16[1664,128]{1,0:T(8,128)(2,1)S(1)} %collective-permute-done.19.p3) | copy-start | bytes 1277956
  161.0 7.6 %collective-permute-start.21 = (bf16[768,128]{1,0:T(8,128)(2,1)S(1)}, bf16[768,128]{1,0:T(8,128)(2,1)S(1)}, u32[]{:S(2)}, u32[]{:S(2)}) collective-permute-start(bf16[768,128]{1,0:T(8,128)(2,1)S(1)} %slice.43), channel_id=1, source_target_pairs={{0,1},{1,2},{2,3},{3,4},{4,5},{5,6},{6,7},{7,0},{8,9},{9,10},{10,1... | collective-permute-start | bytes 589832 | tf_op jit(solution)/shard_map/ppermute | solution.py:261
  163.0 7.2 %copy-start.9 = (bf16[1664,128]{1,0:T(8,128)(2,1)}, bf16[1664,128]{1,0:T(8,128)(2,1)S(1)}, u32[]{:S(2)}) copy-start(bf16[1664,128]{1,0:T(8,128)(2,1)S(1)} %collective-permute-done.16.m3) | copy-start | bytes 1277956
  163.0 7.2 %collective-permute-start.20 = (bf16[768,128]{1,0:T(8,128)(2,1)S(1)}, bf16[768,128]{1,0:T(8,128)(2,1)S(1)}, u32[]{:S(2)}, u32[]{:S(2)}) collective-permute-start(bf16[768,128]{1,0:T(8,128)(2,1)S(1)} %slice.42), channel_id=1, source_target_pairs={{0,7},{1,0},{2,1},{3,2},{4,3},{5,4},{6,5},{7,6},{8,15},{9,8},{10,9... | collective-permute-start | bytes 589832 | tf_op jit(solution)/shard_map/ppermute | solution.py:261
  168.7 1.6 copy-start.21
  170.2 0.7 copy-start.23
  175.6 9.7 %collective-permute-start.22 = (bf16[1024,1024]{1,0:T(8,128)(2,1)}, bf16[1024,1024]{1,0:T(8,128)(2,1)S(1)}, u32[]{:S(2)}, u32[]{:S(2)}) collective-permute-start(bf16[1024,1024]{1,0:T(8,128)(2,1)} %get-tuple-element.26.x_own), channel_id=1, source_target_pairs={{0,8},{8,0},{16,24},{24,16},{32,40},{40,32},{48,56},{56,48},{64,72... | collective-permute-start | bytes 6291464 | tf_op jit(solution)/shard_map/ppermute | solution.py:249
  185.3 1.4 copy-start.3
  200.5 5.8 %collective-permute-start.23 = (bf16[1040,128]{1,0:T(8,128)(2,1)}, bf16[1040,128]{1,0:T(8,128)(2,1)S(1)}, u32[]{:S(2)}, u32[]{:S(2)}) collective-permute-start(bf16[1040,128]{1,0:T(8,128)(2,1)} %get-tuple-element.28.own1), channel_id=1, source_target_pairs={{0,8},{8,0},{16,24},{24,16},{32,40},{40,32},{48,56},{56,48},{64,72... | collective-permute-start | bytes 798728 | tf_op jit(solution)/shard_map/ppermute | solution.py:249
  202.6 3.6 %collective-permute-start.24 = (bf16[1024,128]{1,0:T(8,128)(2,1)}, bf16[1024,128]{1,0:T(8,128)(2,1)S(1)}, u32[]{:S(2)}, u32[]{:S(2)}) collective-permute-start(bf16[1024,128]{1,0:T(8,128)(2,1)} %get-tuple-element.29.own2), channel_id=1, source_target_pairs={{0,8},{16,24},{32,40},{48,56},{64,72},{80,88},{96,104},{112,120},{... | collective-permute-start | bytes 786440 | tf_op jit(solution)/shard_map/ppermute | solution.py:257
  206.3 0.7 copy-start.20
  207.0 0.7 copy-start.19

commit v2 on v1

v2 whole, which is shorter than its diff:
```python
import jax
import jax.numpy as jnp
from jax import lax
from jax.experimental import pallas as pl
from jax.experimental.pallas import tpu as pltpu
from jax.sharding import PartitionSpec as P

NS = 2
LEVELS = 2
W = 128
N = 8
D = W * N
RING = 1664
HALF = 768
INTERPRET = False

f32 = jnp.float32
bf16 = jnp.bfloat16


def dot(a, b):
    return jnp.dot(a, b, preferred_element_type=f32)


def call(kernel, out_shape, scratch, scalars, *args, vmem=None, vmem_out=True):
    vm = pl.BlockSpec(memory_space=pltpu.VMEM)
    hbm = pl.BlockSpec(memory_space=pl.ANY)
    staged = len(args) if vmem is None else vmem
    outs = list(out_shape)
    flags = vmem_out if isinstance(vmem_out, (list, tuple)) else [vmem_out] * len(outs)
    return pl.pallas_call(
        kernel,
        out_shape=outs,
        in_specs=[pl.BlockSpec(memory_space=pltpu.SMEM)]
        + [vm] * staged
        + [hbm] * (len(args) - staged),
        out_specs=[vm if flag else hbm for flag in flags],
        scratch_shapes=list(scratch),
        compiler_params=pltpu.CompilerParams(vmem_limit_bytes=56 * 2**20),
        interpret=INTERPRET,
    )(scalars, *args)


def struct(*shape):
    return jax.ShapeDtypeStruct(shape, bf16)


def blk(index):
    return pl.ds(pl.multiple_of(index * W, W), W)


def start_kernel(s, spread, weight, drift, belief, hosts, values, msg, own_vec):
    role = s[0]

    @pl.when(role == 0)
    def _():
        msg[0:D, :] = weight[...]

    @pl.when(role == 1)
    def _():
        msg[0:D, :] = spread[...]

    state = lax.broadcasted_iota(jnp.int32, (hosts.shape[0], D), 1)
    hit = jnp.where(2 * hosts[...] == state, values[...], 0.0)
    eta = (belief[...].astype(f32) + jnp.sum(hit, axis=0, keepdims=True)).astype(bf16).astype(f32)
    b = drift[...].astype(f32)
    rows = [b[:, k * W : (k + 1) * W] for k in range(N)] + [
        eta[:, k * W : (k + 1) * W] for k in range(N)
    ]
    vec = jnp.concatenate(rows, axis=0).astype(bf16)
    msg[D : D + 2 * N, :] = vec
    own_vec[...] = vec


def run_copies(copies):
    for c in copies:
        c.start()
    for c in copies:
        c.wait()


def ring_kernel(s, xa, xb, aa, ab, msg, sems):
    q = s[1]

    def x_copies(src):
        out = [
            pltpu.make_async_copy(src.at[blk((q + d) % N)], msg.at[pl.ds(512 + d * W, W)], sems.at[d])
            for d in range(4)
        ]
        return out + [
            pltpu.make_async_copy(src.at[blk((q + 4) % N)], msg.at[pl.ds(1536, W)], sems.at[4])
        ]

    def a_copies(src):
        return [
            pltpu.make_async_copy(src.at[pl.ds(0, 512)], msg.at[pl.ds(0, 512)], sems.at[5]),
            pltpu.make_async_copy(src.at[pl.ds(512, 512)], msg.at[pl.ds(1024, 512)], sems.at[6]),
        ]

    for i, x in ((0, xa), (1, xb)):
        for j, a in ((0, aa), (1, ab)):
            pl.when((s[2] == i) & (s[3] == j))(lambda x=x, a=a: run_copies(x_copies(x) + a_copies(a)))


def assemble_kernel(s, xa, xb, m1, m2, m3, p1, p2, p3, m4, p4, x_out):
    q = s[1]

    def put(l, d, block):
        r = (l + d) % N
        x_out[r * W : (r + 1) * W, l * W : (l + 1) * W] = block
        if d:
            x_out[l * W : (l + 1) * W, r * W : (r + 1) * W] = block.T

    def own(src):
        for d in range(N):
            put(0, d, src[blk((q + d) % N), :])

    pl.when(s[2] == 0)(lambda: own(xa))
    pl.when(s[2] == 1)(lambda: own(xb))
    for l, src in ((1, m1), (2, m2), (3, m3), (7, p1), (6, p2), (5, p3)):
        for d in range(5 if l < 4 else 4):
            if (l + d) % N == 0:
                continue
            row = 1536 if d == 4 else 512 + d * W
            put(l, d, src[row : row + W, :])
    for d in (0, 1):
        put(4, d, m4[512 + d * W : 512 + (d + 1) * W, :])
        put(4, d + 2, p4[d * W : (d + 1) * W, :])


def combine_kernel(
    s, x_own, aia, aib, adda, addb, vec_i, vec_j, x_far, msg, m1, m2, m3, p1, p2, p3, m4, p4,
    out1, out2, x_other, a_full, r, t, base, vecs, sems,
):
    role = s[0]
    q = s[1]
    terms = 2**NS - 1
    far_copy = pltpu.make_async_copy(x_far, x_other, sems.at[0])
    far_copy.start()
    copies = []
    for l, src in ((0, msg), (1, m1), (2, m2), (3, m3), (7, p1), (6, p2), (5, p3)):
        for half in range(2):
            copies.append((src, 1024 * half, 512 * half, l))
    copies += [(m4, 0, 0, 4), (p4, 256, 512, 4)]
    copies = [
        pltpu.make_async_copy(
            src.at[pl.ds(first, 512)],
            a_full.at[pl.ds(to, 512), pl.ds(l * W, W)],
            sems.at[1 + i],
        )
        for i, (src, first, to, l) in enumerate(copies)
    ]
    for c in copies:
        c.start()
    vi = vec_i[...].astype(f32)
    vj = vec_j[...].astype(f32)

    def rotated_move(dst, row):
        def put(src):
            for l in range(N):
                dst[row : row + W, l * W : (l + 1) * W] = src[blk((q + l) % N), :].T

        pl.when(s[2] == 0)(lambda: put(aia))
        pl.when(s[2] == 1)(lambda: put(aib))

    def rotated_vector(rows, first):
        vecs[...] = rows
        return jnp.concatenate([vecs[pl.ds(first + (q + l) % N, 1), :] for l in range(N)], axis=1)

    def as_rows(vector):
        return jnp.broadcast_to(vector, (16, D)).astype(bf16)

    @pl.when(role == 0)
    def _():
        cov, info = x_own, x_other
        rotated_move(base, W)
        eta = rotated_vector(vj, N)
        w = rotated_vector(vi, 0)
        for c in copies:
            c.wait()
        r[0:W, :] = a_full[blk(q), :]
        r[W : W + 16, :] = as_rows(eta)
        out = dot(r[0 : W + 16, :], cov[...])
        base[0:W, :] = out[0:W].astype(bf16)
        w = w + out[W : W + 1]
        r[0 : 2 * W, :] = base[...]
        r[2 * W : 2 * W + 16, :] = as_rows(w)
        far_copy.wait()
        for _ in range(terms):
            t[...] = dot(r[...], info[...]).astype(bf16)
            out = dot(t[...], cov[...])
            r[0 : 2 * W, :] = (base[...].astype(f32) - out[0 : 2 * W]).astype(bf16)
            r[2 * W : 2 * W + 16, :] = as_rows(w - out[2 * W : 2 * W + 1])
        res = lax.dot_general(
            r[...], a_full[...], (((1,), (1,)), ((), ())), preferred_element_type=f32
        )

        def put_c(src):
            for l in range(N):
                rows = slice(l * W, (l + 1) * W)
                out1[rows, :] = (res[0:W, rows].T + src[rows, :].astype(f32)).astype(bf16)
                out2[rows, :] = res[W : 2 * W, rows].astype(bf16).T

        pl.when(s[3] == 0)(lambda: put_c(adda))
        pl.when(s[3] == 1)(lambda: put_c(addb))
        rows = [
            res[2 * W : 2 * W + 1, l * W : (l + 1) * W] + vj[l : l + 1, :] for l in range(N)
        ]
        rows = rows + [jnp.zeros((1, W), f32)] * N
        out2[D : D + 2 * N, :] = jnp.concatenate(rows, axis=0).astype(bf16)

    @pl.when(role == 1)
    def _():
        info, cov = x_own, x_other
        top = slice(0, W)
        low = slice(W, W + 16)
        both = slice(0, W + 16)
        rotated_move(base, 0)
        r[top, :] = base[top, :]
        r[low, :] = as_rows(rotated_vector(vi, 0))
        eta = rotated_vector(vj, N)
        out = dot(r[both, :], info[...])
        start = eta - out[W : W + 1]
        t[top, :] = out[top].astype(bf16)
        t[low, :] = as_rows(start)
        far_copy.wait()
        for _ in range(terms):
            out = dot(t[both, :], cov[...])
            r[top, :] = (base[top, :].astype(f32) - out[top]).astype(bf16)
            r[low, :] = out[low].astype(bf16)
            out = dot(r[both, :], info[...])
            t[top, :] = out[top].astype(bf16)
            t[low, :] = as_rows(start - out[W : W + 1])
        for c in copies:
            c.wait()
        for l in range(N):
            x_other[blk((q + l) % N), 0 : W + 16] = t[both, l * W : (l + 1) * W].T
        for l in range(N):
            r[both, l * W : (l + 1) * W] = x_other[l * W : (l + 1) * W, 0 : W + 16].T
        res = dot(r[both, :], a_full[...])

        def put_j(src):
            for l in range(N):
                rows = blk((q + l) % N)
                out1[rows, :] = (
                    res[top, l * W : (l + 1) * W].T + src[rows, :].astype(f32)
                ).astype(bf16)

        pl.when(s[3] == 0)(lambda: put_j(adda))
        pl.when(s[3] == 1)(lambda: put_j(addb))
        vecs[...] = vi
        for l in range(N):
            spot = pl.ds(N + (q + l) % N, 1)
            vecs[spot, :] = vecs[spot, :] + res[W : W + 1, l * W : (l + 1) * W]
        rows = lax.broadcasted_iota(jnp.int32, (2 * N, W), 0)
        out2[0:D, :] = jnp.zeros((D, W), bf16)
        out2[D : D + 2 * N, :] = jnp.where(rows < N, 0.0, vecs[...]).astype(bf16)


def pick_kernel(s, cov, move, info, got, msg, sem):
    def copy(src):
        c = pltpu.make_async_copy(src.at[pl.ds(0, D)], msg.at[pl.ds(0, D)], sem.at[0])
        c.start()
        c.wait()

    pl.when(s[0] == 0)(lambda: copy(cov))
    pl.when(s[0] == 1)(lambda: copy(move))
    pl.when(s[0] == 2)(lambda: copy(info))
    pl.when(s[0] == 3)(lambda: copy(got))


def finish_kernel(s, vec_own, vec_got, own1, own2, got1, got2, drift, belief, move, spread, weight, sems):
    def put(first, moved, last, b, e):
        copies = [
            pltpu.make_async_copy(first.at[pl.ds(0, D)], spread, sems.at[0]),
            pltpu.make_async_copy(moved.at[pl.ds(0, D)], move, sems.at[1]),
            pltpu.make_async_copy(last.at[pl.ds(0, D)], weight, sems.at[2]),
        ]
        for c in copies:
            c.start()
        b = b[...].astype(f32)
        e = e[...].astype(f32)
        for l in range(N):
            drift[:, l * W : (l + 1) * W] = b[l : l + 1, :].astype(bf16)
            belief[:, l * W : (l + 1) * W] = e[N + l : N + l + 1, :].astype(bf16)
        for c in copies:
            c.wait()

    pl.when(s[0] == 0)(lambda: put(own1, own2, got1, vec_own, vec_got))
    pl.when(s[0] == 1)(lambda: put(got1, got2, own1, vec_got, vec_own))


def swap(x, axis_bit):
    return lax.ppermute(x, "tm", [(i, i ^ (1 << axis_bit)) for i in range(lax.axis_size("tm"))])


def shift(x, by):
    return lax.ppermute(x, "panel", [(i, (i + by) % N) for i in range(N)])


def ring(msg, side):
    ups, downs = [shift(msg, 1)], [shift(msg, -1)]
    extra = side()
    first, second, extra = lax.optimization_barrier((ups[0], downs[0], extra))
    ups, downs = [first], [second]
    for _ in range(2):
        ups.append(shift(ups[-1], 1))
        downs.append(shift(downs[-1], -1))
    m4 = shift(downs[-1][0:HALF], -1)
    p4 = shift(ups[-1][HALF : 2 * HALF], 1)
    return downs + ups + [m4, p4], extra


def combined(role, q, x_pair, x_pick, ring_pair, ring_pick, side):
    ring_scalars = jnp.stack([role, q, x_pick, ring_pick])
    (msg,) = call(
        ring_kernel,
        [struct(RING, W)],
        (pltpu.SemaphoreType.DMA((7,)),),
        ring_scalars,
        *x_pair,
        *ring_pair,
        vmem=0,
        vmem_out=False,
    )
    parts, (ai_pair, ai_pick, add_pair, add_pick, vec_i, vec_j) = ring(msg, side)
    (x_full,) = call(assemble_kernel, [struct(D, D)], (), ring_scalars, *x_pair, *parts)
    x_far = swap(x_full, 0)
    return call(
        combine_kernel,
        [struct(D, W), struct(D + 2 * N, W)],
        (
            pltpu.VMEM((D, D), bf16),
            pltpu.VMEM((D, D), bf16),
            pltpu.VMEM((2 * W + 16, D), bf16),
            pltpu.VMEM((2 * W + 16, D), bf16),
            pltpu.VMEM((2 * W, D), bf16),
            pltpu.VMEM((2 * N, W), f32),
            pltpu.SemaphoreType.DMA((17,)),
        ),
        jnp.stack([role, q, ai_pick, add_pick]),
        x_full,
        *ai_pair,
        *add_pair,
        vec_i,
        vec_j,
        x_far,
        msg,
        *parts,
        vmem=7,
    )


def local(transition, drift, spread, belief, precision, probe_hosts, probe_values):
    q = lax.axis_index("panel").astype(jnp.int32)
    t = lax.axis_index("tm").astype(jnp.int32)
    role = t & 1
    odd = (t >> 1) & 1
    zero = jnp.zeros((), jnp.int32)
    move, cov, info = transition[0], spread[0], precision[0]
    got_move = swap(move, 0)

    def side0():
        first, own_vec = call(
            start_kernel,
            [struct(D + 2 * N, W), struct(2 * N, W)],
            (),
            jnp.stack([role, q]),
            cov,
            info,
            drift,
            belief,
            probe_hosts.reshape(-1, 1),
            probe_values.reshape(-1, 1),
        )
        got = swap(first, 0)
        got_vec = got[D:]
        vec_i = jnp.where(role == 0, own_vec, got_vec)
        vec_j = jnp.where(role == 0, got_vec, own_vec)
        return (move, got_move), role, (got, got), zero, vec_i, vec_j

    out1, out2 = combined(role, q, (cov, info), role, (got_move, got_move), zero, side0)
    near = odd == 0
    got2 = swap(out2, 0)
    own_vec = out2[D:] + got2[D:]
    choice = jnp.where(role == 0, odd, 3 - odd)
    (panel,) = call(
        pick_kernel,
        [struct(D, W)],
        (pltpu.SemaphoreType.DMA((1,)),),
        choice[None],
        out1,
        out2,
        out1,
        got2,
        vmem=0,
        vmem_out=False,
    )
    far = swap(panel, 1)

    def side1():
        rest = jnp.where(role == 0, jnp.where(near, out2[:D], out1), out1)
        bundle = swap(jnp.concatenate([rest, own_vec], axis=0), 1)
        far_vec = bundle[D:]
        vec_i = jnp.where(near, own_vec, far_vec)
        vec_j = jnp.where(near, far_vec, own_vec)
        early_move = jnp.where(
            role == 0,
            jnp.where(near, out2[:D], bundle[:D]),
            jnp.where(near, got2[:D], far),
        )
        return (early_move, early_move), zero, (bundle, out1), role ^ odd, vec_i, vec_j

    ring_a = jnp.where(role == 0, 1 - odd, odd)
    local_move = jnp.where(role == 0, out2[:D], got2[:D])
    out1, out2 = combined(role, q, (out1, far), role ^ odd, (local_move, far), ring_a, side1)
    got1 = swap(out1, 0)
    got2 = swap(out2, 0)
    panel = struct(D, W)
    row = struct(1, D)
    drift, belief, move, cov, info = call(
        finish_kernel,
        [row, row, panel, panel, panel],
        (pltpu.SemaphoreType.DMA((3,)),),
        role[None],
        out2[D:],
        got2[D:],
        out1,
        out2,
        got1,
        got2,
        vmem=2,
        vmem_out=[True, True, False, False, False],
    )
    return move[None], drift, cov[None], belief, info[None]


def solution(mesh):
    in_specs = (
        P("tm", None, "panel"),
        P("tm", None),
        P("tm", None, "panel"),
        P("tm", None),
        P("tm", None, "panel"),
        P("tm", None),
        P("tm", None),
    )
    out_specs = (
        P("tm", None, "panel"),
        P("tm", None),
        P("tm", None, "panel"),
        P("tm", None),
        P("tm", None, "panel"),
    )
    return jax.shard_map(local, mesh=mesh, in_specs=in_specs, out_specs=out_specs, check_vma=False)
```

time: 211 us -> 263 us (1.25)
  Pallas kernels: 45.2 us -> 89.5 us
  waiting for transfers between devices: 61.2 us -> 66.2 us
    pallas_call x8 -> x9, Pallas kernels: 45.2 us -> 89.5 us  [call(): pl.pallas_call(kernel, out_shape=outs, in_specs=[pl.BlockSpec(memory_spac...]
    ppermute x7 -> x9, starting transfers between devices: 31.4 us -> 40.5 us  [swap(): lax.ppermute(x, 'tm', [(i, i ^ 1 << axis_bit) for i in range(lax.axis_siz...]
    ppermute x16, starting transfers between devices: 52.9 us -> 45.6 us  [shift(): return lax.ppermute(x, 'panel', [(i, (i + by) % N) for i in range(N)])]
    ppermute x16, waiting for transfers between devices: 46.8 us -> 53.5 us  [shift(): return lax.ppermute(x, 'panel', [(i, (i + by) % N) for i in range(N)])]
    unnamed x54 -> x52, local copies, waits for them, and re-layouts: 7.04 us -> 5.63 us
    ppermute x7 -> x9, waiting for transfers between devices: 12 us -> 12.7 us  [swap(): lax.ppermute(x, 'tm', [(i, i ^ 1 << axis_bit) for i in range(lax.axis_siz...]
  transfers between devices with their start and end apart: 25 -> 25, of which waited for: 16 -> 16; matrix products, arithmetic and copies ran while one was open for 4% -> 4% of each run, Pallas kernels for 1% -> 10%
where the time goes in v2:
time: 263 us; the launch traced here: 262 us
  Pallas kernels  89.5 us (34%)
  starting transfers between devices  86.1 us (33%)
  waiting for transfers between devices  66.2 us (25%)
  local copies, waits for them, and re-layouts  10.5 us (4%)
  other arithmetic  8.66 us (3%)
    pallas_call x9, Pallas kernels, call(): pl.pallas_call(kernel, out_shape=outs, in_specs=[pl.BlockSpec(memory_spac...  89.5 us
    ppermute x16, waiting for transfers between devices, shift(): return lax.ppermute(x, 'panel', [(i, (i + by) % N) for i in range(N)])  53.5 us
    ppermute x16, starting transfers between devices, shift(): return lax.ppermute(x, 'panel', [(i, (i + by) % N) for i in range(N)])  45.6 us
    ppermute x9, starting transfers between devices, swap(): lax.ppermute(x, 'tm', [(i, i ^ 1 << axis_bit) for i in range(lax.axis_siz...  40.5 us
    ppermute x9, waiting for transfers between devices, swap(): lax.ppermute(x, 'tm', [(i, i ^ 1 << axis_bit) for i in range(lax.axis_siz...  12.7 us
    unnamed x52, local copies, waits for them, and re-layouts  5.63 us
  transfers between devices with their start and end apart: 25, of which 16 were waited for; matrix products, arithmetic and copies ran while one was open for 4% of the time, Pallas kernels for 10%

profile of v2, /device:TPU:1, one launch (start us, length us, event | category | flops | bytes accessed | tf_op | source)
XLA Modules:
  0.0 262.3 jit_solution(7564163098399571269)
XLA Ops:
  0.6 8.7 %collective-permute-start = (bf16[1024,128]{1,0:T(8,128)(2,1)}, bf16[1024,128]{1,0:T(8,128)(2,1)S(1)}, u32[]{:S(2)}, u32[]{:S(2)}) collective-permute-start(bf16[1024,128]{1,0:T(8,128)(2,1)} %bitcast.23), channel_id=1, source_target_pairs={{0,8},{8,0},{16,24},{24,16},{32,40},{40,32},{48,56},{56,48},{64,72... | collective-permute-start | bytes 786440 | tf_op jit(solution)/shard_map/ppermute | solution.py:294
  9.4 1.5 copy.12.hosts
  10.9 1.5 copy.13.values
  12.9 2.1 shard_map.111
  15.1 1.9 collective-permute-start.3
  17.6 0.7 copy-done.6
  18.3 14.8 %shard_map.110.msg = bf16[1664,128]{1,0:T(8,128)(2,1)} custom-call(s32[4]{0:T(128)} %pad_add_fusion.1.s, bf16[1024,128]{1,0:T(8,128)(2,1)} %bitcast.18, bf16[1024,128]{1,0:T(8,128)(2,1)} %bitcast.21, bf16[1024,128]{1,0:T(8,128)(2,1)} %copy-done.6, bf16[1024,128]{1,0:T(8,128)(2,1)} %copy-done.6), custom_call_target="tpu_custom_call" | custom-call | tf_op jit(solution)/shard_map/pallas_call | solution.py:31
  33.1 1.9 collective-permute-start.2
  35.0 3.4 %collective-permute-start.1 = (bf16[1664,128]{1,0:T(8,128)(2,1)}, bf16[1664,128]{1,0:T(8,128)(2,1)S(1)}, u32[]{:S(2)}, u32[]{:S(2)}) collective-permute-start(bf16[1664,128]{1,0:T(8,128)(2,1)} %shard_map.110.msg), channel_id=1, source_target_pairs={{0,1},{1,2},{2,3},{3,4},{4,5},{5,6},{6,7},{7,0},{8,9},{9,10},{10,1... | collective-permute-start | bytes 1277960 | tf_op jit(solution)/shard_map/ppermute | solution.py:298
  38.4 1.3 broadcast_select_fusion.3
  39.7 6.4 %collective-permute-done.2.m1 = bf16[1664,128]{1,0:T(8,128)(2,1)S(1)} collective-permute-done((bf16[1664,128]{1,0:T(8,128)(2,1)}, bf16[1664,128]{1,0:T(8,128)(2,1)S(1)}, u32[]{:S(2)}, u32[]{:S(2)}) %collective-permute-start.2) | collective-permute-done | bytes 426016 | tf_op jit(solution)/shard_map/ppermute | solution.py:298
  46.1 3.1 %collective-permute-done.1.p1 = bf16[1664,128]{1,0:T(8,128)(2,1)S(1)} collective-permute-done((bf16[1664,128]{1,0:T(8,128)(2,1)}, bf16[1664,128]{1,0:T(8,128)(2,1)S(1)}, u32[]{:S(2)}, u32[]{:S(2)}) %collective-permute-start.1) | collective-permute-done | bytes 426016 | tf_op jit(solution)/shard_map/ppermute | solution.py:298
  49.2 1.9 collective-permute-start.4
  51.1 3.4 %collective-permute-start.6 = (bf16[1664,128]{1,0:T(8,128)(2,1)S(1)}, bf16[1664,128]{1,0:T(8,128)(2,1)S(1)}, u32[]{:S(2)}, u32[]{:S(2)}) collective-permute-start(bf16[1664,128]{1,0:T(8,128)(2,1)S(1)} %collective-permute-done.1.p1), channel_id=1, source_target_pairs={{0,1},{1,2},{2,3},{3,4},{4,5},{5,6},{6,7},{7,0},{8,9},{9,10},{10,1... | collective-permute-start | bytes 1277960 | tf_op jit(solution)/shard_map/ppermute | solution.py:298
  54.5 6.7 %collective-permute-done.4.m2 = bf16[1664,128]{1,0:T(8,128)(2,1)S(1)} collective-permute-done((bf16[1664,128]{1,0:T(8,128)(2,1)S(1)}, bf16[1664,128]{1,0:T(8,128)(2,1)S(1)}, u32[]{:S(2)}, u32[]{:S(2)}) %collective-permute-start.4) | collective-permute-done | bytes 426016 | tf_op jit(solution)/shard_map/ppermute | solution.py:298
  61.2 3.4 %collective-permute-start.5 = (bf16[1664,128]{1,0:T(8,128)(2,1)S(1)}, bf16[1664,128]{1,0:T(8,128)(2,1)S(1)}, u32[]{:S(2)}, u32[]{:S(2)}) collective-permute-start(bf16[1664,128]{1,0:T(8,128)(2,1)S(1)} %collective-permute-done.4.m2), channel_id=1, source_target_pairs={{0,7},{1,0},{2,1},{3,2},{4,3},{5,4},{6,5},{7,6},{8,15},{9,8},{10,9... | collective-permute-start | bytes 1277960 | tf_op jit(solution)/shard_map/ppermute | solution.py:298
  64.6 1.9 collective-permute-start.7
  66.5 5.7 %collective-permute-done.5.m3 = bf16[1664,128]{1,0:T(8,128)(2,1)S(1)} collective-permute-done((bf16[1664,128]{1,0:T(8,128)(2,1)S(1)}, bf16[1664,128]{1,0:T(8,128)(2,1)S(1)}, u32[]{:S(2)}, u32[]{:S(2)}) %collective-permute-start.5) | collective-permute-done | bytes 426016 | tf_op jit(solution)/shard_map/ppermute | solution.py:298
  72.3 4.9 %collective-permute-start.8 = (bf16[768,128]{1,0:T(8,128)(2,1)S(1)}, bf16[768,128]{1,0:T(8,128)(2,1)S(1)}, u32[]{:S(2)}, u32[]{:S(2)}) collective-permute-start(bf16[768,128]{1,0:T(8,128)(2,1)S(1)} %slice.56), channel_id=1, source_target_pairs={{0,7},{1,0},{2,1},{3,2},{4,3},{5,4},{6,5},{7,6},{8,15},{9,8},{10,9... | collective-permute-start | bytes 589832 | tf_op jit(solution)/shard_map/ppermute | solution.py:298
  77.3 1.9 collective-permute-start.9
  79.2 0.6 collective-permute-done.8.m4
  79.8 5.1 %collective-permute-done.9.p4 = bf16[768,128]{1,0:T(8,128)(2,1)S(1)} collective-permute-done((bf16[768,128]{1,0:T(8,128)(2,1)S(1)}, bf16[768,128]{1,0:T(8,128)(2,1)S(1)}, u32[]{:S(2)}, u32[]{:S(2)}) %collective-permute-start.9) | collective-permute-done | bytes 196640 | tf_op jit(solution)/shard_map/ppermute | solution.py:298
  84.9 0.7 copy-done.23
  85.6 3.8 %shard_map.112.x_own = bf16[1024,1024]{1,0:T(8,128)(2,1)} custom-call(s32[4]{0:T(128)} %pad_add_fusion.1.s, bf16[1024,128]{1,0:T(8,128)(2,1)} %bitcast.19, bf16[1024,128]{1,0:T(8,128)(2,1)} %bitcast.22, bf16[1664,128]{1,0:T(8,128)(2,1)} %copy-done.10, bf16[1664,128]{1,0:T(8,128)(2,1)} %copy-done.15, bf16[1664,128]{1,0:T(8,128)(2,1)} %copy-done.2, ...), custom_call_target="tpu_custom_call" | custom-call | tf_op jit(solution)/shard_map/pallas_call | solution.py:31
  89.4 6.1 %collective-permute-start.10 = (bf16[1024,1024]{1,0:T(8,128)(2,1)}, bf16[1024,1024]{1,0:T(8,128)(2,1)S(1)}, u32[]{:S(2)}, u32[]{:S(2)}) collective-permute-start(bf16[1024,1024]{1,0:T(8,128)(2,1)} %shard_map.112.x_own), channel_id=1, source_target_pairs={{0,8},{8,0},{16,24},{24,16},{32,40},{40,32},{48,56},{56,48},{64,72... | collective-permute-start | bytes 6291464 | tf_op jit(solution)/shard_map/ppermute | solution.py:294
  96.0 3.4 %collective-permute-done.10.x_far = bf16[1024,1024]{1,0:T(8,128)(2,1)S(1)} collective-permute-done((bf16[1024,1024]{1,0:T(8,128)(2,1)}, bf16[1024,1024]{1,0:T(8,128)(2,1)S(1)}, u32[]{:S(2)}, u32[]{:S(2)}) %collective-permute-start.10) | collective-permute-done | bytes 2097184 | tf_op jit(solution)/shard_map/ppermute | solution.py:294
  99.4 1.4 copy-done.8
  100.8 7.4 %shard_map.113 = (bf16[1024,128]{1,0:T(8,128)(2,1)}, bf16[1040,128]{1,0:T(8,128)(2,1)}) custom-call(s32[4]{0:T(128)} %pad_add_fusion.3.s, bf16[1024,1024]{1,0:T(8,128)(2,1)} %shard_map.112.x_own, bf16[1024,128]{1,0:T(8,128)(2,1)} %bitcast.24, bf16[1024,128]{1,0:T(8,128)(2,1)} %copy-done.6, bf16[1040,128]{1,0:T(8,128)(2,1)} %copy-done.17, ...), custom_call_target="tpu_custom_call" | custom-call | tf_op jit(solution)/shard_map/pallas_call | solution.py:31
  108.2 5.0 %collective-permute-start.11 = (bf16[1040,128]{1,0:T(8,128)(2,1)}, bf16[1040,128]{1,0:T(8,128)(2,1)S(1)}, u32[]{:S(2)}, u32[]{:S(2)}) collective-permute-start(bf16[1040,128]{1,0:T(8,128)(2,1)} %get-tuple-element.49.move), channel_id=1, source_target_pairs={{0,8},{8,0},{16,24},{24,16},{32,40},{40,32},{48,56},{56,48},{64,72... | collective-permute-start | bytes 798728 | tf_op jit(solution)/shard_map/ppermute | solution.py:294
  113.2 1.1 select_select_fusion
  114.6 0.7 slice_add_fusion
  115.3 1.9 collective-permute-start.15
  117.2 9.1 %shard_map.114 = bf16[1024,128]{1,0:T(8,128)(2,1)} custom-call(s32[1]{0:T(128)} %bitcast.11.s, bf16[1024,128]{1,0:T(8,128)(2,1)} %get-tuple-element.57.cov.info.xa.addb, bf16[1040,128]{1,0:T(8,128)(2,1)} %get-tuple-element.49.move, bf16[1024,128]{1,0:T(8,128)(2,1)} %get-tuple-element.57.cov.info.xa.addb, bf16[1040,128]{1,0:T(8,128)(2,1)} %copy-done.19), custom_call_target="tpu_custom_call" | custom-call | tf_op jit(solution)/shard_map/pallas_call | solution.py:31
  126.3 3.4 %collective-permute-start.12 = (bf16[1024,128]{1,0:T(8,128)(2,1)}, bf16[1024,128]{1,0:T(8,128)(2,1)S(1)}, u32[]{:S(2)}, u32[]{:S(2)}) collective-permute-start(bf16[1024,128]{1,0:T(8,128)(2,1)} %shard_map.114), channel_id=1, source_target_pairs={{0,16},{8,24},{16,0},{24,8},{32,48},{40,56},{48,32},{56,40},{64,80... | collective-permute-start | bytes 786440 | tf_op jit(solution)/shard_map/ppermute | solution.py:294
  129.7 0.6 pad_add_fusion.s
  130.3 5.6 %collective-permute-done.12.xb.ab = bf16[1024,128]{1,0:T(8,128)(2,1)S(1)} collective-permute-done((bf16[1024,128]{1,0:T(8,128)(2,1)}, bf16[1024,128]{1,0:T(8,128)(2,1)S(1)}, u32[]{:S(2)}, u32[]{:S(2)}) %collective-permute-start.12) | collective-permute-done | bytes 262176 | tf_op jit(solution)/shard_map/ppermute | solution.py:294
  135.9 2.0 fusion
  137.9 14.8 %shard_map.115.msg = bf16[1664,128]{1,0:T(8,128)(2,1)} custom-call(s32[4]{0:T(128)} %pad_add_fusion.s, bf16[1024,128]{1,0:T(8,128)(2,1)} %get-tuple-element.57.cov.info.xa.addb, bf16[1024,128]{1,0:T(8,128)(2,1)} %copy-done, bf16[1024,128]{1,0:T(8,128)(2,1)} %get-tuple-element.68.aa, bf16[1024,128]{1,0:T(8,128)(2,1)} %copy-done), custom_call_target="tpu_custom_call" | custom-call | tf_op jit(solution)/shard_map/pallas_call | solution.py:31
  152.7 1.9 collective-permute-start.14
  154.7 3.4 %collective-permute-start.13 = (bf16[1664,128]{1,0:T(8,128)(2,1)}, bf16[1664,128]{1,0:T(8,128)(2,1)S(1)}, u32[]{:S(2)}, u32[]{:S(2)}) collective-permute-start(bf16[1664,128]{1,0:T(8,128)(2,1)} %shard_map.115.msg), channel_id=1, source_target_pairs={{0,1},{1,2},{2,3},{3,4},{4,5},{5,6},{6,7},{7,0},{8,9},{9,10},{10,1... | collective-permute-start | bytes 1277960 | tf_op jit(solution)/shard_map/ppermute | solution.py:298
  158.0 0.6 broadcast_select_fusion.1
  158.6 6.4 %collective-permute-done.14.m1 = bf16[1664,128]{1,0:T(8,128)(2,1)S(1)} collective-permute-done((bf16[1664,128]{1,0:T(8,128)(2,1)}, bf16[1664,128]{1,0:T(8,128)(2,1)S(1)}, u32[]{:S(2)}, u32[]{:S(2)}) %collective-permute-start.14) | collective-permute-done | bytes 426016 | tf_op jit(solution)/shard_map/ppermute | solution.py:298
  165.0 3.1 %collective-permute-done.13.p1 = bf16[1664,128]{1,0:T(8,128)(2,1)S(1)} collective-permute-done((bf16[1664,128]{1,0:T(8,128)(2,1)}, bf16[1664,128]{1,0:T(8,128)(2,1)S(1)}, u32[]{:S(2)}, u32[]{:S(2)}) %collective-permute-start.13) | collective-permute-done | bytes 426016 | tf_op jit(solution)/shard_map/ppermute | solution.py:298
  168.2 1.9 collective-permute-start.16
  170.1 3.4 %collective-permute-start.18 = (bf16[1664,128]{1,0:T(8,128)(2,1)S(1)}, bf16[1664,128]{1,0:T(8,128)(2,1)S(1)}, u32[]{:S(2)}, u32[]{:S(2)}) collective-permute-start(bf16[1664,128]{1,0:T(8,128)(2,1)S(1)} %collective-permute-done.13.p1), channel_id=1, source_target_pairs={{0,1},{1,2},{2,3},{3,4},{4,5},{5,6},{6,7},{7,0},{8,9},{9,10},{10,1... | collective-permute-start | bytes 1277960 | tf_op jit(solution)/shard_map/ppermute | solution.py:298
  173.4 5.9 %collective-permute-done.16.m2 = bf16[1664,128]{1,0:T(8,128)(2,1)S(1)} collective-permute-done((bf16[1664,128]{1,0:T(8,128)(2,1)S(1)}, bf16[1664,128]{1,0:T(8,128)(2,1)S(1)}, u32[]{:S(2)}, u32[]{:S(2)}) %collective-permute-start.16) | collective-permute-done | bytes 426016 | tf_op jit(solution)/shard_map/ppermute | solution.py:298
  179.3 3.4 %collective-permute-start.17 = (bf16[1664,128]{1,0:T(8,128)(2,1)S(1)}, bf16[1664,128]{1,0:T(8,128)(2,1)S(1)}, u32[]{:S(2)}, u32[]{:S(2)}) collective-permute-start(bf16[1664,128]{1,0:T(8,128)(2,1)S(1)} %collective-permute-done.16.m2), channel_id=1, source_target_pairs={{0,7},{1,0},{2,1},{3,2},{4,3},{5,4},{6,5},{7,6},{8,15},{9,8},{10,9... | collective-permute-start | bytes 1277960 | tf_op jit(solution)/shard_map/ppermute | solution.py:298
  182.8 1.9 collective-permute-start.19
  184.7 5.0 %collective-permute-done.17.m3 = bf16[1664,128]{1,0:T(8,128)(2,1)S(1)} collective-permute-done((bf16[1664,128]{1,0:T(8,128)(2,1)S(1)}, bf16[1664,128]{1,0:T(8,128)(2,1)S(1)}, u32[]{:S(2)}, u32[]{:S(2)}) %collective-permute-start.17) | collective-permute-done | bytes 426016 | tf_op jit(solution)/shard_map/ppermute | solution.py:298
  189.7 4.9 %collective-permute-start.20 = (bf16[768,128]{1,0:T(8,128)(2,1)S(1)}, bf16[768,128]{1,0:T(8,128)(2,1)S(1)}, u32[]{:S(2)}, u32[]{:S(2)}) collective-permute-start(bf16[768,128]{1,0:T(8,128)(2,1)S(1)} %slice.62), channel_id=1, source_target_pairs={{0,7},{1,0},{2,1},{3,2},{4,3},{5,4},{6,5},{7,6},{8,15},{9,8},{10,9... | collective-permute-start | bytes 589832 | tf_op jit(solution)/shard_map/ppermute | solution.py:298
  194.7 2.1 collective-permute-start.21
  197.2 5.1 %collective-permute-done.21.p4 = bf16[768,128]{1,0:T(8,128)(2,1)S(1)} collective-permute-done((bf16[768,128]{1,0:T(8,128)(2,1)S(1)}, bf16[768,128]{1,0:T(8,128)(2,1)S(1)}, u32[]{:S(2)}, u32[]{:S(2)}) %collective-permute-start.21) | collective-permute-done | bytes 196640 | tf_op jit(solution)/shard_map/ppermute | solution.py:298
  202.3 0.7 copy-done.22
  203.0 3.8 %shard_map.116.x_own = bf16[1024,1024]{1,0:T(8,128)(2,1)} custom-call(s32[4]{0:T(128)} %pad_add_fusion.s, bf16[1024,128]{1,0:T(8,128)(2,1)} %get-tuple-element.57.cov.info.xa.addb, bf16[1024,128]{1,0:T(8,128)(2,1)} %copy-done, bf16[1664,128]{1,0:T(8,128)(2,1)} %copy-done.9, bf16[1664,128]{1,0:T(8,128)(2,1)} %copy-done.13, bf16[1664,128]{1,0:T(8,128)(2,1)} %copy-done.1, ...), custom_call_target="tpu_custom_call" | custom-call | tf_op jit(solution)/shard_map/pallas_call | solution.py:31
  206.8 6.8 %collective-permute-start.22 = (bf16[1024,1024]{1,0:T(8,128)(2,1)}, bf16[1024,1024]{1,0:T(8,128)(2,1)S(1)}, u32[]{:S(2)}, u32[]{:S(2)}) collective-permute-start(bf16[1024,1024]{1,0:T(8,128)(2,1)} %shard_map.116.x_own), channel_id=1, source_target_pairs={{0,8},{8,0},{16,24},{24,16},{32,40},{40,32},{48,56},{56,48},{64,72... | collective-permute-start | bytes 6291464 | tf_op jit(solution)/shard_map/ppermute | solution.py:294
  214.2 3.4 %collective-permute-done.22.x_far = bf16[1024,1024]{1,0:T(8,128)(2,1)S(1)} collective-permute-done((bf16[1024,1024]{1,0:T(8,128)(2,1)}, bf16[1024,1024]{1,0:T(8,128)(2,1)S(1)}, u32[]{:S(2)}, u32[]{:S(2)}) %collective-permute-start.22) | collective-permute-done | bytes 2097184 | tf_op jit(solution)/shard_map/ppermute | solution.py:294
  217.6 1.4 copy-done.7
  219.0 7.5 %shard_map.117 = (bf16[1024,128]{1,0:T(8,128)(2,1)}, bf16[1040,128]{1,0:T(8,128)(2,1)}) custom-call(s32[4]{0:T(128)} %pad_add_fusion.4.s, bf16[1024,1024]{1,0:T(8,128)(2,1)} %shard_map.116.x_own, bf16[1024,128]{1,0:T(8,128)(2,1)} %get-tuple-element.55.aia.aib, bf16[1024,128]{1,0:T(8,128)(2,1)} %get-tuple-element.55.aia.aib, bf16[1040,128]{1,0:T(8,128)(2,1)} %copy-done.18, ...), custom_call_target="tpu_custom_call" | custom-call | tf_op jit(solution)/shard_map/pallas_call | solution.py:31
  226.5 4.8 %collective-permute-start.23 = (bf16[1040,128]{1,0:T(8,128)(2,1)}, bf16[1040,128]{1,0:T(8,128)(2,1)S(1)}, u32[]{:S(2)}, u32[]{:S(2)}) collective-permute-start(bf16[1040,128]{1,0:T(8,128)(2,1)} %get-tuple-element.60.own2), channel_id=1, source_target_pairs={{0,8},{8,0},{16,24},{24,16},{32,40},{40,32},{48,56},{56,48},{64,72... | collective-permute-start | bytes 798728 | tf_op jit(solution)/shard_map/ppermute | solution.py:294
  231.3 1.9 collective-permute-start.24
  233.2 1.3 slice.53.vec_own
  234.5 0.6 slice.64.vec_got
  235.2 0.7 copy-done.25
  235.9 26.2 %shard_map.118 = (bf16[1,1024]{1,0:T(2,128)(2,1)}, bf16[1,1024]{1,0:T(2,128)(2,1)}, bf16[1024,128]{1,0:T(8,128)(2,1)}, bf16[1024,128]{1,0:T(8,128)(2,1)}, bf16[1024,128]{1,0:T(8,128)(2,1)}) custom-call(s32[1]{0:T(128)} %bitcast.s, bf16[16,128]{1,0:T(8,128)(2,1)} %slice.53.vec_own, bf16[16,128]{1,0:T(8,128)(2,1)} %slice.64.vec_got, ...), custom_call_target="tpu_custom_call" | custom-call | tf_op jit(solution)/shard_map/pallas_call | solution.py:31
  (66 shorter events, 3.3 us)
Async XLA Ops:
  0.6 16.9 %collective-permute-start = (bf16[1024,128]{1,0:T(8,128)(2,1)}, bf16[1024,128]{1,0:T(8,128)(2,1)S(1)}, u32[]{:S(2)}, u32[]{:S(2)}) collective-permute-start(bf16[1024,128]{1,0:T(8,128)(2,1)} %bitcast.23), channel_id=1, source_target_pairs={{0,8},{8,0},{16,24},{24,16},{32,40},{40,32},{48,56},{56,48},{64,72... | collective-permute-start | bytes 786440 | tf_op jit(solution)/shard_map/ppermute | solution.py:294
  15.1 23.3 %collective-permute-start.3 = (bf16[1040,128]{1,0:T(8,128)(2,1)}, bf16[1040,128]{1,0:T(8,128)(2,1)S(1)}, u32[]{:S(2)}, u32[]{:S(2)}) collective-permute-start(bf16[1040,128]{1,0:T(8,128)(2,1)} %get-tuple-element.36), channel_id=1, source_target_pairs={{0,8},{8,0},{16,24},{24,16},{32,40},{40,32},{48,56},{56,48},{64,72... | collective-permute-start | bytes 798728 | tf_op jit(solution)/shard_map/ppermute | solution.py:294
  17.6 0.7 copy-start.6
  33.1 13.0 %collective-permute-start.2 = (bf16[1664,128]{1,0:T(8,128)(2,1)}, bf16[1664,128]{1,0:T(8,128)(2,1)S(1)}, u32[]{:S(2)}, u32[]{:S(2)}) collective-permute-start(bf16[1664,128]{1,0:T(8,128)(2,1)} %shard_map.110.msg), channel_id=1, source_target_pairs={{0,7},{1,0},{2,1},{3,2},{4,3},{5,4},{6,5},{7,6},{8,15},{9,8},{10,9... | collective-permute-start | bytes 1277960 | tf_op jit(solution)/shard_map/ppermute | solution.py:298
  35.0 14.2 %collective-permute-start.1 = (bf16[1664,128]{1,0:T(8,128)(2,1)}, bf16[1664,128]{1,0:T(8,128)(2,1)S(1)}, u32[]{:S(2)}, u32[]{:S(2)}) collective-permute-start(bf16[1664,128]{1,0:T(8,128)(2,1)} %shard_map.110.msg), channel_id=1, source_target_pairs={{0,1},{1,2},{2,3},{3,4},{4,5},{5,6},{6,7},{7,0},{8,9},{9,10},{10,1... | collective-permute-start | bytes 1277960 | tf_op jit(solution)/shard_map/ppermute | solution.py:298
  38.4 51.0 %copy-start.17 = (bf16[1040,128]{1,0:T(8,128)(2,1)}, bf16[1040,128]{1,0:T(8,128)(2,1)S(1)}, u32[]{:S(2)}) copy-start(bf16[1040,128]{1,0:T(8,128)(2,1)S(1)} %collective-permute-done.3.adda.addb) | copy-start | bytes 798724
  46.1 38.8 %copy-start.10 = (bf16[1664,128]{1,0:T(8,128)(2,1)}, bf16[1664,128]{1,0:T(8,128)(2,1)S(1)}, u32[]{:S(2)}) copy-start(bf16[1664,128]{1,0:T(8,128)(2,1)S(1)} %collective-permute-done.2.m1) | copy-start | bytes 1277956
  49.2 35.7 %copy-start.12 = (bf16[1664,128]{1,0:T(8,128)(2,1)}, bf16[1664,128]{1,0:T(8,128)(2,1)S(1)}, u32[]{:S(2)}) copy-start(bf16[1664,128]{1,0:T(8,128)(2,1)S(1)} %collective-permute-done.1.p1) | copy-start | bytes 1277956
  49.2 12.0 %collective-permute-start.4 = (bf16[1664,128]{1,0:T(8,128)(2,1)S(1)}, bf16[1664,128]{1,0:T(8,128)(2,1)S(1)}, u32[]{:S(2)}, u32[]{:S(2)}) collective-permute-start(bf16[1664,128]{1,0:T(8,128)(2,1)S(1)} %collective-permute-done.2.m1), channel_id=1, source_target_pairs={{0,7},{1,0},{2,1},{3,2},{4,3},{5,4},{6,5},{7,6},{8,15},{9,8},{10,9... | collective-permute-start | bytes 1277960 | tf_op jit(solution)/shard_map/ppermute | solution.py:298
  51.1 13.4 %collective-permute-start.6 = (bf16[1664,128]{1,0:T(8,128)(2,1)S(1)}, bf16[1664,128]{1,0:T(8,128)(2,1)S(1)}, u32[]{:S(2)}, u32[]{:S(2)}) collective-permute-start(bf16[1664,128]{1,0:T(8,128)(2,1)S(1)} %collective-permute-done.1.p1), channel_id=1, source_target_pairs={{0,1},{1,2},{2,3},{3,4},{4,5},{5,6},{6,7},{7,0},{8,9},{9,10},{10,1... | collective-permute-start | bytes 1277960 | tf_op jit(solution)/shard_map/ppermute | solution.py:298
  61.2 23.7 %copy-start.15 = (bf16[1664,128]{1,0:T(8,128)(2,1)}, bf16[1664,128]{1,0:T(8,128)(2,1)S(1)}, u32[]{:S(2)}) copy-start(bf16[1664,128]{1,0:T(8,128)(2,1)S(1)} %collective-permute-done.4.m2) | copy-start | bytes 1277956
  61.2 11.1 %collective-permute-start.5 = (bf16[1664,128]{1,0:T(8,128)(2,1)S(1)}, bf16[1664,128]{1,0:T(8,128)(2,1)S(1)}, u32[]{:S(2)}, u32[]{:S(2)}) collective-permute-start(bf16[1664,128]{1,0:T(8,128)(2,1)S(1)} %collective-permute-done.4.m2), channel_id=1, source_target_pairs={{0,7},{1,0},{2,1},{3,2},{4,3},{5,4},{6,5},{7,6},{8,15},{9,8},{10,9... | collective-permute-start | bytes 1277960 | tf_op jit(solution)/shard_map/ppermute | solution.py:298
  64.6 20.3 %copy-start.16 = (bf16[1664,128]{1,0:T(8,128)(2,1)}, bf16[1664,128]{1,0:T(8,128)(2,1)S(1)}, u32[]{:S(2)}) copy-start(bf16[1664,128]{1,0:T(8,128)(2,1)S(1)} %collective-permute-done.6.p2) | copy-start | bytes 1277956
  64.6 12.6 %collective-permute-start.7 = (bf16[1664,128]{1,0:T(8,128)(2,1)S(1)}, bf16[1664,128]{1,0:T(8,128)(2,1)S(1)}, u32[]{:S(2)}, u32[]{:S(2)}) collective-permute-start(bf16[1664,128]{1,0:T(8,128)(2,1)S(1)} %collective-permute-done.6.p2), channel_id=1, source_target_pairs={{0,1},{1,2},{2,3},{3,4},{4,5},{5,6},{6,7},{7,0},{8,9},{9,10},{10,1... | collective-permute-start | bytes 1277960 | tf_op jit(solution)/shard_map/ppermute | solution.py:298
  72.3 12.6 %copy-start.2 = (bf16[1664,128]{1,0:T(8,128)(2,1)}, bf16[1664,128]{1,0:T(8,128)(2,1)S(1)}, u32[]{:S(2)}) copy-start(bf16[1664,128]{1,0:T(8,128)(2,1)S(1)} %collective-permute-done.5.m3) | copy-start | bytes 1277956
  72.3 7.5 %collective-permute-start.8 = (bf16[768,128]{1,0:T(8,128)(2,1)S(1)}, bf16[768,128]{1,0:T(8,128)(2,1)S(1)}, u32[]{:S(2)}, u32[]{:S(2)}) collective-permute-start(bf16[768,128]{1,0:T(8,128)(2,1)S(1)} %slice.56), channel_id=1, source_target_pairs={{0,7},{1,0},{2,1},{3,2},{4,3},{5,4},{6,5},{7,6},{8,15},{9,8},{10,9... | collective-permute-start | bytes 589832 | tf_op jit(solution)/shard_map/ppermute | solution.py:298
  77.2 7.7 %copy-start.4 = (bf16[1664,128]{1,0:T(8,128)(2,1)}, bf16[1664,128]{1,0:T(8,128)(2,1)S(1)}, u32[]{:S(2)}) copy-start(bf16[1664,128]{1,0:T(8,128)(2,1)S(1)} %collective-permute-done.7.p3) | copy-start | bytes 1277956
  77.3 7.6 %collective-permute-start.9 = (bf16[768,128]{1,0:T(8,128)(2,1)S(1)}, bf16[768,128]{1,0:T(8,128)(2,1)S(1)}, u32[]{:S(2)}, u32[]{:S(2)}) collective-permute-start(bf16[768,128]{1,0:T(8,128)(2,1)S(1)} %slice.57), channel_id=1, source_target_pairs={{0,1},{1,2},{2,3},{3,4},{4,5},{5,6},{6,7},{7,0},{8,9},{9,10},{10,1... | collective-permute-start | bytes 589832 | tf_op jit(solution)/shard_map/ppermute | solution.py:298
  79.8 5.1 %copy-start.21 = (bf16[768,128]{1,0:T(8,128)(2,1)}, bf16[768,128]{1,0:T(8,128)(2,1)S(1)}, u32[]{:S(2)}) copy-start(bf16[768,128]{1,0:T(8,128)(2,1)S(1)} %collective-permute-done.8.m4) | copy-start | bytes 589828
  84.9 0.7 copy-start.23
  89.4 10.0 %collective-permute-start.10 = (bf16[1024,1024]{1,0:T(8,128)(2,1)}, bf16[1024,1024]{1,0:T(8,128)(2,1)S(1)}, u32[]{:S(2)}, u32[]{:S(2)}) collective-permute-start(bf16[1024,1024]{1,0:T(8,128)(2,1)} %shard_map.112.x_own), channel_id=1, source_target_pairs={{0,8},{8,0},{16,24},{24,16},{32,40},{40,32},{48,56},{56,48},{64,72... | collective-permute-start | bytes 6291464 | tf_op jit(solution)/shard_map/ppermute | solution.py:294
  99.4 1.4 copy-start.8
  108.2 27.7 %copy-start.5 = (bf16[1040,128]{1,0:T(8,128)(2,1)S(1)}, bf16[1040,128]{1,0:T(8,128)(2,1)}, u32[]{:S(2)}) copy-start(bf16[1040,128]{1,0:T(8,128)(2,1)} %get-tuple-element.49.move) | copy-start | bytes 798724
  108.2 6.3 %collective-permute-start.11 = (bf16[1040,128]{1,0:T(8,128)(2,1)}, bf16[1040,128]{1,0:T(8,128)(2,1)S(1)}, u32[]{:S(2)}, u32[]{:S(2)}) collective-permute-start(bf16[1040,128]{1,0:T(8,128)(2,1)} %get-tuple-element.49.move), channel_id=1, source_target_pairs={{0,8},{8,0},{16,24},{24,16},{32,40},{40,32},{48,56},{56,48},{64,72... | collective-permute-start | bytes 798728 | tf_op jit(solution)/shard_map/ppermute | solution.py:294
  114.6 2.6 %copy-start.19 = (bf16[1040,128]{1,0:T(8,128)(2,1)}, bf16[1040,128]{1,0:T(8,128)(2,1)S(1)}, u32[]{:S(2)}) copy-start(bf16[1040,128]{1,0:T(8,128)(2,1)S(1)} %collective-permute-done.11.got) | copy-start | bytes 798724
  115.3 20.6 %collective-permute-start.15 = (bf16[1040,128]{1,0:T(8,128)(2,1)S(1)}, bf16[1040,128]{1,0:T(8,128)(2,1)S(1)}, u32[]{:S(2)}, u32[]{:S(2)}) collective-permute-start(bf16[1040,128]{1,0:T(8,128)(2,1)S(1)} %pad_maximum_fusion), channel_id=1, source_target_pairs={{0,16},{8,24},{16,0},{24,8},{32,48},{40,56},{48,32},{56,40},{64,80... | collective-permute-start | bytes 798728 | tf_op jit(solution)/shard_map/ppermute | solution.py:294
  126.3 9.6 %collective-permute-start.12 = (bf16[1024,128]{1,0:T(8,128)(2,1)}, bf16[1024,128]{1,0:T(8,128)(2,1)S(1)}, u32[]{:S(2)}, u32[]{:S(2)}) collective-permute-start(bf16[1024,128]{1,0:T(8,128)(2,1)} %shard_map.114), channel_id=1, source_target_pairs={{0,16},{8,24},{16,0},{24,8},{32,48},{40,56},{48,32},{56,40},{64,80... | collective-permute-start | bytes 786440 | tf_op jit(solution)/shard_map/ppermute | solution.py:294
  135.9 2.0 copy-start
  135.9 70.9 %copy-start.18 = (bf16[1040,128]{1,0:T(8,128)(2,1)}, bf16[1040,128]{1,0:T(8,128)(2,1)S(1)}, u32[]{:S(2)}) copy-start(bf16[1040,128]{1,0:T(8,128)(2,1)S(1)} %collective-permute-done.15.adda) | copy-start | bytes 798724
  152.7 12.3 %collective-permute-start.14 = (bf16[1664,128]{1,0:T(8,128)(2,1)}, bf16[1664,128]{1,0:T(8,128)(2,1)S(1)}, u32[]{:S(2)}, u32[]{:S(2)}) collective-permute-start(bf16[1664,128]{1,0:T(8,128)(2,1)} %shard_map.115.msg), channel_id=1, source_target_pairs={{0,7},{1,0},{2,1},{3,2},{4,3},{5,4},{6,5},{7,6},{8,15},{9,8},{10,9... | collective-permute-start | bytes 1277960 | tf_op jit(solution)/shard_map/ppermute | solution.py:298
  154.7 13.5 %collective-permute-start.13 = (bf16[1664,128]{1,0:T(8,128)(2,1)}, bf16[1664,128]{1,0:T(8,128)(2,1)S(1)}, u32[]{:S(2)}, u32[]{:S(2)}) collective-permute-start(bf16[1664,128]{1,0:T(8,128)(2,1)} %shard_map.115.msg), channel_id=1, source_target_pairs={{0,1},{1,2},{2,3},{3,4},{4,5},{5,6},{6,7},{7,0},{8,9},{9,10},{10,1... | collective-permute-start | bytes 1277960 | tf_op jit(solution)/shard_map/ppermute | solution.py:298
  165.0 37.3 %copy-start.9 = (bf16[1664,128]{1,0:T(8,128)(2,1)}, bf16[1664,128]{1,0:T(8,128)(2,1)S(1)}, u32[]{:S(2)}) copy-start(bf16[1664,128]{1,0:T(8,128)(2,1)S(1)} %collective-permute-done.14.m1) | copy-start | bytes 1277956
  168.1 34.1 %copy-start.11 = (bf16[1664,128]{1,0:T(8,128)(2,1)}, bf16[1664,128]{1,0:T(8,128)(2,1)S(1)}, u32[]{:S(2)}) copy-start(bf16[1664,128]{1,0:T(8,128)(2,1)S(1)} %collective-permute-done.13.p1) | copy-start | bytes 1277956
  168.2 11.2 %collective-permute-start.16 = (bf16[1664,128]{1,0:T(8,128)(2,1)S(1)}, bf16[1664,128]{1,0:T(8,128)(2,1)S(1)}, u32[]{:S(2)}, u32[]{:S(2)}) collective-permute-start(bf16[1664,128]{1,0:T(8,128)(2,1)S(1)} %collective-permute-done.14.m1), channel_id=1, source_target_pairs={{0,7},{1,0},{2,1},{3,2},{4,3},{5,4},{6,5},{7,6},{8,15},{9,8},{10,9... | collective-permute-start | bytes 1277960 | tf_op jit(solution)/shard_map/ppermute | solution.py:298
  170.1 12.7 %collective-permute-start.18 = (bf16[1664,128]{1,0:T(8,128)(2,1)S(1)}, bf16[1664,128]{1,0:T(8,128)(2,1)S(1)}, u32[]{:S(2)}, u32[]{:S(2)}) collective-permute-start(bf16[1664,128]{1,0:T(8,128)(2,1)S(1)} %collective-permute-done.13.p1), channel_id=1, source_target_pairs={{0,1},{1,2},{2,3},{3,4},{4,5},{5,6},{6,7},{7,0},{8,9},{9,10},{10,1... | collective-permute-start | bytes 1277960 | tf_op jit(solution)/shard_map/ppermute | solution.py:298
  179.3 22.9 %copy-start.13 = (bf16[1664,128]{1,0:T(8,128)(2,1)}, bf16[1664,128]{1,0:T(8,128)(2,1)S(1)}, u32[]{:S(2)}) copy-start(bf16[1664,128]{1,0:T(8,128)(2,1)S(1)} %collective-permute-done.16.m2) | copy-start | bytes 1277956
  179.3 10.3 %collective-permute-start.17 = (bf16[1664,128]{1,0:T(8,128)(2,1)S(1)}, bf16[1664,128]{1,0:T(8,128)(2,1)S(1)}, u32[]{:S(2)}, u32[]{:S(2)}) collective-permute-start(bf16[1664,128]{1,0:T(8,128)(2,1)S(1)} %collective-permute-done.16.m2), channel_id=1, source_target_pairs={{0,7},{1,0},{2,1},{3,2},{4,3},{5,4},{6,5},{7,6},{8,15},{9,8},{10,9... | collective-permute-start | bytes 1277960 | tf_op jit(solution)/shard_map/ppermute | solution.py:298
  182.8 19.5 %copy-start.14 = (bf16[1664,128]{1,0:T(8,128)(2,1)}, bf16[1664,128]{1,0:T(8,128)(2,1)S(1)}, u32[]{:S(2)}) copy-start(bf16[1664,128]{1,0:T(8,128)(2,1)S(1)} %collective-permute-done.18.p2) | copy-start | bytes 1277956
  182.8 11.8 %collective-permute-start.19 = (bf16[1664,128]{1,0:T(8,128)(2,1)S(1)}, bf16[1664,128]{1,0:T(8,128)(2,1)S(1)}, u32[]{:S(2)}, u32[]{:S(2)}) collective-permute-start(bf16[1664,128]{1,0:T(8,128)(2,1)S(1)} %collective-permute-done.18.p2), channel_id=1, source_target_pairs={{0,1},{1,2},{2,3},{3,4},{4,5},{5,6},{6,7},{7,0},{8,9},{9,10},{10,1... | collective-permute-start | bytes 1277960 | tf_op jit(solution)/shard_map/ppermute | solution.py:298
  189.7 12.6 %copy-start.1 = (bf16[1664,128]{1,0:T(8,128)(2,1)}, bf16[1664,128]{1,0:T(8,128)(2,1)S(1)}, u32[]{:S(2)}) copy-start(bf16[1664,128]{1,0:T(8,128)(2,1)S(1)} %collective-permute-done.17.m3) | copy-start | bytes 1277956
  189.7 7.5 %collective-permute-start.20 = (bf16[768,128]{1,0:T(8,128)(2,1)S(1)}, bf16[768,128]{1,0:T(8,128)(2,1)S(1)}, u32[]{:S(2)}, u32[]{:S(2)}) collective-permute-start(bf16[768,128]{1,0:T(8,128)(2,1)S(1)} %slice.62), channel_id=1, source_target_pairs={{0,7},{1,0},{2,1},{3,2},{4,3},{5,4},{6,5},{7,6},{8,15},{9,8},{10,9... | collective-permute-start | bytes 589832 | tf_op jit(solution)/shard_map/ppermute | solution.py:298
  194.6 7.7 %copy-start.3 = (bf16[1664,128]{1,0:T(8,128)(2,1)}, bf16[1664,128]{1,0:T(8,128)(2,1)S(1)}, u32[]{:S(2)}) copy-start(bf16[1664,128]{1,0:T(8,128)(2,1)S(1)} %collective-permute-done.19.p3) | copy-start | bytes 1277956
  194.7 7.6 %collective-permute-start.21 = (bf16[768,128]{1,0:T(8,128)(2,1)S(1)}, bf16[768,128]{1,0:T(8,128)(2,1)S(1)}, u32[]{:S(2)}, u32[]{:S(2)}) collective-permute-start(bf16[768,128]{1,0:T(8,128)(2,1)S(1)} %slice.63), channel_id=1, source_target_pairs={{0,1},{1,2},{2,3},{3,4},{4,5},{5,6},{6,7},{7,0},{8,9},{9,10},{10,1... | collective-permute-start | bytes 589832 | tf_op jit(solution)/shard_map/ppermute | solution.py:298
  197.2 5.1 %copy-start.20 = (bf16[768,128]{1,0:T(8,128)(2,1)}, bf16[768,128]{1,0:T(8,128)(2,1)S(1)}, u32[]{:S(2)}) copy-start(bf16[768,128]{1,0:T(8,128)(2,1)S(1)} %collective-permute-done.20.m4) | copy-start | bytes 589828
  202.3 0.7 copy-start.22
  206.8 10.8 %collective-permute-start.22 = (bf16[1024,1024]{1,0:T(8,128)(2,1)}, bf16[1024,1024]{1,0:T(8,128)(2,1)S(1)}, u32[]{:S(2)}, u32[]{:S(2)}) collective-permute-start(bf16[1024,1024]{1,0:T(8,128)(2,1)} %shard_map.116.x_own), channel_id=1, source_target_pairs={{0,8},{8,0},{16,24},{24,16},{32,40},{40,32},{48,56},{56,48},{64,72... | collective-permute-start | bytes 6291464 | tf_op jit(solution)/shard_map/ppermute | solution.py:294
  217.6 1.4 copy-start.7
  226.5 8.0 %collective-permute-start.23 = (bf16[1040,128]{1,0:T(8,128)(2,1)}, bf16[1040,128]{1,0:T(8,128)(2,1)S(1)}, u32[]{:S(2)}, u32[]{:S(2)}) collective-permute-start(bf16[1040,128]{1,0:T(8,128)(2,1)} %get-tuple-element.60.own2), channel_id=1, source_target_pairs={{0,8},{8,0},{16,24},{24,16},{32,40},{40,32},{48,56},{56,48},{64,72... | collective-permute-start | bytes 798728 | tf_op jit(solution)/shard_map/ppermute | solution.py:294
  231.3 3.8 %collective-permute-start.24 = (bf16[1024,128]{1,0:T(8,128)(2,1)}, bf16[1024,128]{1,0:T(8,128)(2,1)S(1)}, u32[]{:S(2)}, u32[]{:S(2)}) collective-permute-start(bf16[1024,128]{1,0:T(8,128)(2,1)} %get-tuple-element.61.own1), channel_id=1, source_target_pairs={{0,8},{8,0},{16,24},{24,16},{32,40},{40,32},{48,56},{56,48},{64,72... | collective-permute-start | bytes 786440 | tf_op jit(solution)/shard_map/ppermute | solution.py:294
  234.5 0.7 copy-start.24
  235.2 0.7 copy-start.25

commit v3 on v2

--- a/solution.py
+++ b/solution.py
@@ -5,8 +5,8 @@
 from jax.experimental.pallas import tpu as pltpu
 from jax.sharding import PartitionSpec as P
 
+
 NS = 2
-LEVELS = 2
 W = 128
 N = 8
 D = W * N
@@ -22,19 +22,17 @@
     return jnp.dot(a, b, preferred_element_type=f32)
 
 
-def call(kernel, out_shape, scratch, scalars, *args, vmem=None, vmem_out=True):
+def call(kernel, out_shape, scratch, scalars, *args, vmem=None):
     vm = pl.BlockSpec(memory_space=pltpu.VMEM)
     hbm = pl.BlockSpec(memory_space=pl.ANY)
     staged = len(args) if vmem is None else vmem
-    outs = list(out_shape)
-    flags = vmem_out if isinstance(vmem_out, (list, tuple)) else [vmem_out] * len(outs)
     return pl.pallas_call(
         kernel,
-        out_shape=outs,
+        out_shape=list(out_shape),
         in_specs=[pl.BlockSpec(memory_space=pltpu.SMEM)]
         + [vm] * staged
         + [hbm] * (len(args) - staged),
-        out_specs=[vm if flag else hbm for flag in flags],
+        out_specs=[vm] * len(out_shape),
         scratch_shapes=list(scratch),
         compiler_params=pltpu.CompilerParams(vmem_limit_bytes=56 * 2**20),
         interpret=INTERPRET,
@@ -60,9 +58,22 @@
     def _():
         msg[0:D, :] = spread[...]
 
-    state = lax.broadcasted_iota(jnp.int32, (hosts.shape[0], D), 1)
-    hit = jnp.where(2 * hosts[...] == state, values[...], 0.0)
-    eta = (belief[...].astype(f32) + jnp.sum(hit, axis=0, keepdims=True)).astype(bf16).astype(f32)
+    eye = lax.broadcasted_iota(jnp.int32, (W, W), 0) == lax.broadcasted_iota(jnp.int32, (W, W), 1)
+
+    def column(row):
+        return jnp.sum(jnp.where(eye, row, 0.0), axis=1, keepdims=True)
+
+    lane = lax.broadcasted_iota(jnp.int32, (W, W), 1).astype(f32)
+    sums = [jnp.zeros((1, W), f32)] * N
+    for c in range(hosts.shape[1] // W):
+        part = slice(c * W, (c + 1) * W)
+        spot = column(2.0 * hosts[:, part].astype(f32))
+        value = column(values[:, part])
+        for k in range(N):
+            hit = jnp.where(spot == lane + k * W, value, 0.0)
+            sums[k] = sums[k] + jnp.sum(hit, axis=0, keepdims=True)
+    eta = belief[...].astype(f32) + jnp.concatenate(sums, axis=1)
+    eta = eta.astype(bf16).astype(f32)
     b = drift[...].astype(f32)
     rows = [b[:, k * W : (k + 1) * W] for k in range(N)] + [
         eta[:, k * W : (k + 1) * W] for k in range(N)
@@ -102,7 +113,7 @@
             pl.when((s[2] == i) & (s[3] == j))(lambda x=x, a=a: run_copies(x_copies(x) + a_copies(a)))
 
 
-def assemble_kernel(s, xa, xb, m1, m2, m3, p1, p2, p3, m4, p4, x_out):
+def assemble_kernel(s, xa, xb, m1, m2, m3, p1, p2, p3, x_out):
     q = s[1]
 
     def put(l, d, block):
@@ -123,20 +134,28 @@
                 continue
             row = 1536 if d == 4 else 512 + d * W
             put(l, d, src[row : row + W, :])
-    for d in (0, 1):
-        put(4, d, m4[512 + d * W : 512 + (d + 1) * W, :])
-        put(4, d + 2, p4[d * W : (d + 1) * W, :])
+    x_out[4 * W :, 4 * W : 5 * W] = jnp.zeros((4 * W, W), bf16)
+    x_out[4 * W : 5 * W, 5 * W :] = jnp.zeros((W, 3 * W), bf16)
+
+
+def patch(dst, last):
+    for d in range(4):
+        block = last[d * W : (d + 1) * W, :]
+        dst[(4 + d) * W : (5 + d) * W, 4 * W : 5 * W] = block
+        if d:
+            dst[4 * W : 5 * W, (4 + d) * W : (5 + d) * W] = block.T
 
 
 def combine_kernel(
-    s, x_own, aia, aib, adda, addb, vec_i, vec_j, x_far, msg, m1, m2, m3, p1, p2, p3, m4, p4,
-    out1, out2, x_other, a_full, r, t, base, vecs, sems,
+    s, last_own, last_far, aia, aib, adda, addb, vec_i, vec_j, x_here, x_far,
+    msg, m1, m2, m3, p1, p2, p3, m4, p4,
+    out1, out2, x_own, x_other, a_full, r, t, base, vecs, sems,
 ):
     role = s[0]
     q = s[1]
     terms = 2**NS - 1
-    far_copy = pltpu.make_async_copy(x_far, x_other, sems.at[0])
-    far_copy.start()
+    own_copy = pltpu.make_async_copy(x_here, x_own, sems.at[17])
+    own_copy.start()
     copies = []
     for l, src in ((0, msg), (1, m1), (2, m2), (3, m3), (7, p1), (6, p2), (5, p3)):
         for half in range(2):
@@ -152,6 +171,8 @@
     ]
     for c in copies:
         c.start()
+    far_copy = pltpu.make_async_copy(x_far, x_other, sems.at[0])
+    far_copy.start()
     vi = vec_i[...].astype(f32)
     vj = vec_j[...].astype(f32)
 
@@ -179,6 +200,8 @@
         for c in copies:
             c.wait()
         r[0:W, :] = a_full[blk(q), :]
+        own_copy.wait()
+        patch(x_own, last_own)
         r[W : W + 16, :] = as_rows(eta)
         out = dot(r[0 : W + 16, :], cov[...])
         base[0:W, :] = out[0:W].astype(bf16)
@@ -186,6 +209,7 @@
         r[0 : 2 * W, :] = base[...]
         r[2 * W : 2 * W + 16, :] = as_rows(w)
         far_copy.wait()
+        patch(x_other, last_far)
         for _ in range(terms):
             t[...] = dot(r[...], info[...]).astype(bf16)
             out = dot(t[...], cov[...])
@@ -219,11 +243,14 @@
         r[top, :] = base[top, :]
         r[low, :] = as_rows(rotated_vector(vi, 0))
         eta = rotated_vector(vj, N)
+        own_copy.wait()
+        patch(x_own, last_own)
         out = dot(r[both, :], info[...])
         start = eta - out[W : W + 1]
         t[top, :] = out[top].astype(bf16)
         t[low, :] = as_rows(start)
         far_copy.wait()
+        patch(x_other, last_far)
         for _ in range(terms):
             out = dot(t[both, :], cov[...])
             r[top, :] = (base[top, :].astype(f32) - out[top]).astype(bf16)
@@ -298,20 +325,7 @@
     return lax.ppermute(x, "panel", [(i, (i + by) % N) for i in range(N)])
 
 
-def ring(msg, side):
-    ups, downs = [shift(msg, 1)], [shift(msg, -1)]
-    extra = side()
-    first, second, extra = lax.optimization_barrier((ups[0], downs[0], extra))
-    ups, downs = [first], [second]
-    for _ in range(2):
-        ups.append(shift(ups[-1], 1))
-        downs.append(shift(downs[-1], -1))
-    m4 = shift(downs[-1][0:HALF], -1)
-    p4 = shift(ups[-1][HALF : 2 * HALF], 1)
-    return downs + ups + [m4, p4], extra
-
-
-def combined(role, q, x_pair, x_pick, ring_pair, ring_pick, side):
+def combined(role, q, x_pair, x_pick, ring_pair, ring_pick, gate, side):
     ring_scalars = jnp.stack([role, q, x_pick, ring_pick])
     (msg,) = call(
         ring_kernel,
@@ -321,33 +335,54 @@
         *x_pair,
         *ring_pair,
         vmem=0,
-        vmem_out=False,
-    )
-    parts, (ai_pair, ai_pick, add_pair, add_pick, vec_i, vec_j) = ring(msg, side)
-    (x_full,) = call(assemble_kernel, [struct(D, D)], (), ring_scalars, *x_pair, *parts)
-    x_far = swap(x_full, 0)
+    )
+    msg, gate = lax.optimization_barrier((msg, gate))
+    p1 = shift(msg, 1)
+    m1 = shift(msg, -1)
+    p1, m1, extra = lax.optimization_barrier((p1, m1, side(gate)))
+    ai_pair, ai_pick, add_pair, add_pick, vec_i, vec_j = extra
+    p2, m2 = shift(p1, 1), shift(m1, -1)
+    p3, m3 = shift(p2, 1), shift(m2, -1)
+    p4 = shift(p3[HALF : 2 * HALF], 1)
+    m4 = shift(m3[0:HALF], -1)
+    (x_here,) = call(
+        assemble_kernel, [struct(D, D)], (), ring_scalars, *x_pair, m1, m2, m3, p1, p2, p3
+    )
+    x_far = swap(x_here, 0)
+    last_own = jnp.concatenate([m4[512:768], p4[0:256]], axis=0)
+    last_far = swap(last_own, 0)
     return call(
         combine_kernel,
         [struct(D, W), struct(D + 2 * N, W)],
         (
             pltpu.VMEM((D, D), bf16),
             pltpu.VMEM((D, D), bf16),
+            pltpu.VMEM((D, D), bf16),
             pltpu.VMEM((2 * W + 16, D), bf16),
             pltpu.VMEM((2 * W + 16, D), bf16),
             pltpu.VMEM((2 * W, D), bf16),
             pltpu.VMEM((2 * N, W), f32),
-            pltpu.SemaphoreType.DMA((17,)),
+            pltpu.SemaphoreType.DMA((18,)),
         ),
         jnp.stack([role, q, ai_pick, add_pick]),
-        x_full,
+        last_own,
+        last_far,
         *ai_pair,
         *add_pair,
         vec_i,
         vec_j,
+        x_here,
         x_far,
         msg,
-        *parts,
-        vmem=7,
+        m1,
+        m2,
+        m3,
+        p1,
+        p2,
+        p3,
+        m4,
+        p4,
+        vmem=8,
     )
 
 
@@ -360,7 +395,7 @@
     move, cov, info = transition[0], spread[0], precision[0]
     got_move = swap(move, 0)
 
-    def side0():
+    def side0(drift):
         first, own_vec = call(
             start_kernel,
             [struct(D + 2 * N, W), struct(2 * N, W)],
@@ -370,8 +405,8 @@
             info,
             drift,
             belief,
-            probe_hosts.reshape(-1, 1),
-            probe_values.reshape(-1, 1),
+            probe_hosts,
+            probe_values,
         )
         got = swap(first, 0)
         got_vec = got[D:]
@@ -379,7 +414,9 @@
         vec_j = jnp.where(role == 0, got_vec, own_vec)
         return (move, got_move), role, (got, got), zero, vec_i, vec_j
 
-    out1, out2 = combined(role, q, (cov, info), role, (got_move, got_move), zero, side0)
+    out1, out2 = combined(
+        role, q, (cov, info), role, (got_move, got_move), zero, drift, side0
+    )
     near = odd == 0
     got2 = swap(out2, 0)
     own_vec = out2[D:] + got2[D:]
@@ -394,11 +431,10 @@
         out1,
         got2,
         vmem=0,
-        vmem_out=False,
     )
     far = swap(panel, 1)
 
-    def side1():
+    def side1(own_vec):
         rest = jnp.where(role == 0, jnp.where(near, out2[:D], out1), out1)
         bundle = swap(jnp.concatenate([rest, own_vec], axis=0), 1)
         far_vec = bundle[D:]
@@ -413,7 +449,9 @@
 
     ring_a = jnp.where(role == 0, 1 - odd, odd)
     local_move = jnp.where(role == 0, out2[:D], got2[:D])
-    out1, out2 = combined(role, q, (out1, far), role ^ odd, (local_move, far), ring_a, side1)
+    out1, out2 = combined(
+        role, q, (out1, far), role ^ odd, (local_move, far), ring_a, own_vec, side1
+    )
     got1 = swap(out1, 0)
     got2 = swap(out2, 0)
     panel = struct(D, W)
@@ -430,7 +468,6 @@
         got1,
         got2,
         vmem=2,
-        vmem_out=[True, True, False, False, False],
     )
     return move[None], drift, cov[None], belief, info[None]
 

time: 263 us -> 214 us (0.81)
  Pallas kernels: 89.5 us -> 35.6 us
  waiting for transfers between devices: 66.2 us -> 70.5 us
  local copies, waits for them, and re-layouts: 10.5 us -> 14.2 us
  starting transfers between devices: 86.1 us -> 82.9 us
    pallas_call x9, Pallas kernels: 89.5 us -> 35.6 us  [call(): pl.pallas_call(kernel, out_shape=list(out_shape), in_specs=[pl.BlockSpec(...]
    ppermute x16, waiting for transfers between devices: 53.5 us -> 62.7 us  [shift(): return lax.ppermute(x, 'panel', [(i, (i + by) % N) for i in range(N)])]
    ppermute x9 -> x11, waiting for transfers between devices: 12.7 us -> 7.82 us  [swap(): lax.ppermute(x, 'tm', [(i, i ^ 1 << axis_bit) for i in range(lax.axis_siz...]
    slice x4 -> x8, local copies, waits for them, and re-layouts: 0.06 us -> 3.79 us  [the longest x2 1.88 us: combined(): p4 = shift(p3[HALF:2 * HALF], 1)]
    ppermute x16, starting transfers between devices: 45.6 us -> 42.3 us  [shift(): return lax.ppermute(x, 'panel', [(i, (i + by) % N) for i in range(N)])]
    reshape x2 -> x0, local copies, waits for them, and re-layouts: 2.95 us -> none  [the longest x1 1.47 us: side0(): probe_hosts.reshape(-1, 1)]
    unnamed x52 -> x62, local copies, waits for them, and re-layouts: 5.63 us -> 8.53 us
    ppermute x9 -> x11, starting transfers between devices: 40.5 us -> 40.6 us  [swap(): lax.ppermute(x, 'tm', [(i, i ^ 1 << axis_bit) for i in range(lax.axis_siz...]
  transfers between devices with their start and end apart: 25 -> 27, of which waited for: 16 -> 20; matrix products, arithmetic and copies ran while one was open for 4% -> 7% of each run, Pallas kernels for 10% -> 0%
where the time goes in v3:
time: 214 us; the launch traced here: 213 us
  starting transfers between devices  82.9 us (39%)
  waiting for transfers between devices  70.5 us (33%)
  Pallas kernels  35.6 us (17%)
  local copies, waits for them, and re-layouts  14.2 us (7%)
  other arithmetic  8.42 us (4%)
    ppermute x16, waiting for transfers between devices, shift(): return lax.ppermute(x, 'panel', [(i, (i + by) % N) for i in range(N)])  62.7 us
    ppermute x16, starting transfers between devices, shift(): return lax.ppermute(x, 'panel', [(i, (i + by) % N) for i in range(N)])  42.3 us
    ppermute x11, starting transfers between devices, swap(): lax.ppermute(x, 'tm', [(i, i ^ 1 << axis_bit) for i in range(lax.axis_siz...  40.6 us
    pallas_call x9, Pallas kernels, call(): pl.pallas_call(kernel, out_shape=list(out_shape), in_specs=[pl.BlockSpec(...  35.6 us
    unnamed x62, local copies, waits for them, and re-layouts  8.53 us
    ppermute x11, waiting for transfers between devices, swap(): lax.ppermute(x, 'tm', [(i, i ^ 1 << axis_bit) for i in range(lax.axis_siz...  7.82 us
  transfers between devices with their start and end apart: 27, of which 20 were waited for; matrix products, arithmetic and copies ran while one was open for 7% of the time, Pallas kernels for 0%

profile of v3, /device:TPU:1, one launch (start us, length us, event | category | flops | bytes accessed | tf_op | source)
XLA Modules:
  0.0 212.9 jit_solution(11885679265409959399)
XLA Ops:
  0.6 8.7 %collective-permute-start = (bf16[1024,128]{1,0:T(8,128)(2,1)}, bf16[1024,128]{1,0:T(8,128)(2,1)S(1)}, u32[]{:S(2)}, u32[]{:S(2)}) collective-permute-start(bf16[1024,128]{1,0:T(8,128)(2,1)} %bitcast.21), channel_id=1, source_target_pairs={{0,8},{8,0},{16,24},{24,16},{32,40},{40,32},{48,56},{56,48},{64,72... | collective-permute-start | bytes 786440 | tf_op jit(solution)/shard_map/ppermute | solution.py:321
  11.4 2.6 %shard_map.110.msg = bf16[1664,128]{1,0:T(8,128)(2,1)} custom-call(s32[4]{0:T(128)} %pad_add_fusion.1.s, bf16[1024,128]{1,0:T(8,128)(2,1)} %bitcast.15, bf16[1024,128]{1,0:T(8,128)(2,1)} %bitcast.18, bf16[1024,128]{1,0:T(8,128)(2,1)} %copy-done.8, bf16[1024,128]{1,0:T(8,128)(2,1)} %copy-done.8), custom_call_target="tpu_custom_call" | custom-call | tf_op jit(solution)/shard_map/pallas_call | solution.py:29
  14.1 2.0 shard_map.111
  16.1 2.2 %collective-permute-start.3 = (bf16[1040,128]{1,0:T(8,128)(2,1)}, bf16[1040,128]{1,0:T(8,128)(2,1)S(1)}, u32[]{:S(2)}, u32[]{:S(2)}) collective-permute-start(bf16[1040,128]{1,0:T(8,128)(2,1)} %get-tuple-element.42), channel_id=1, source_target_pairs={{0,8},{8,0},{16,24},{24,16},{32,40},{40,32},{48,56},{56,48},{64,72... | collective-permute-start | bytes 798728 | tf_op jit(solution)/shard_map/ppermute | solution.py:321
  18.3 1.9 collective-permute-start.2
  20.2 3.4 %collective-permute-start.1 = (bf16[1664,128]{1,0:T(8,128)(2,1)}, bf16[1664,128]{1,0:T(8,128)(2,1)S(1)}, u32[]{:S(2)}, u32[]{:S(2)}) collective-permute-start(bf16[1664,128]{1,0:T(8,128)(2,1)} %shard_map.110.msg), channel_id=1, source_target_pairs={{0,1},{1,2},{2,3},{3,4},{4,5},{5,6},{6,7},{7,0},{8,9},{9,10},{10,1... | collective-permute-start | bytes 1277960 | tf_op jit(solution)/shard_map/ppermute | solution.py:325
  23.6 1.3 broadcast_select_fusion.3
  25.0 6.6 %collective-permute-done.2.m1 = bf16[1664,128]{1,0:T(8,128)(2,1)S(1)} collective-permute-done((bf16[1664,128]{1,0:T(8,128)(2,1)}, bf16[1664,128]{1,0:T(8,128)(2,1)S(1)}, u32[]{:S(2)}, u32[]{:S(2)}) %collective-permute-start.2) | collective-permute-done | bytes 426016 | tf_op jit(solution)/shard_map/ppermute | solution.py:325
  31.6 3.1 %collective-permute-done.1.p1 = bf16[1664,128]{1,0:T(8,128)(2,1)S(1)} collective-permute-done((bf16[1664,128]{1,0:T(8,128)(2,1)}, bf16[1664,128]{1,0:T(8,128)(2,1)S(1)}, u32[]{:S(2)}, u32[]{:S(2)}) %collective-permute-start.1) | collective-permute-done | bytes 426016 | tf_op jit(solution)/shard_map/ppermute | solution.py:325
  34.7 1.9 collective-permute-start.4
  36.7 3.4 %collective-permute-start.7 = (bf16[1664,128]{1,0:T(8,128)(2,1)S(1)}, bf16[1664,128]{1,0:T(8,128)(2,1)S(1)}, u32[]{:S(2)}, u32[]{:S(2)}) collective-permute-start(bf16[1664,128]{1,0:T(8,128)(2,1)S(1)} %collective-permute-done.1.p1), channel_id=1, source_target_pairs={{0,1},{1,2},{2,3},{3,4},{4,5},{5,6},{6,7},{7,0},{8,9},{9,10},{10,1... | collective-permute-start | bytes 1277960 | tf_op jit(solution)/shard_map/ppermute | solution.py:325
  40.0 6.9 %collective-permute-done.4.m2 = bf16[1664,128]{1,0:T(8,128)(2,1)S(1)} collective-permute-done((bf16[1664,128]{1,0:T(8,128)(2,1)S(1)}, bf16[1664,128]{1,0:T(8,128)(2,1)S(1)}, u32[]{:S(2)}, u32[]{:S(2)}) %collective-permute-start.4) | collective-permute-done | bytes 426016 | tf_op jit(solution)/shard_map/ppermute | solution.py:325
  47.0 3.4 %collective-permute-start.5 = (bf16[1664,128]{1,0:T(8,128)(2,1)S(1)}, bf16[1664,128]{1,0:T(8,128)(2,1)S(1)}, u32[]{:S(2)}, u32[]{:S(2)}) collective-permute-start(bf16[1664,128]{1,0:T(8,128)(2,1)S(1)} %collective-permute-done.4.m2), channel_id=1, source_target_pairs={{0,7},{1,0},{2,1},{3,2},{4,3},{5,4},{6,5},{7,6},{8,15},{9,8},{10,9... | collective-permute-start | bytes 1277960 | tf_op jit(solution)/shard_map/ppermute | solution.py:325
  50.4 1.9 collective-permute-start.8
  52.3 6.0 %collective-permute-done.5.m3 = bf16[1664,128]{1,0:T(8,128)(2,1)S(1)} collective-permute-done((bf16[1664,128]{1,0:T(8,128)(2,1)S(1)}, bf16[1664,128]{1,0:T(8,128)(2,1)S(1)}, u32[]{:S(2)}, u32[]{:S(2)}) %collective-permute-start.5) | collective-permute-done | bytes 426016 | tf_op jit(solution)/shard_map/ppermute | solution.py:325
  58.3 4.6 %collective-permute-done.8.p3 = bf16[1664,128]{1,0:T(8,128)(2,1)S(1)} collective-permute-done((bf16[1664,128]{1,0:T(8,128)(2,1)S(1)}, bf16[1664,128]{1,0:T(8,128)(2,1)S(1)}, u32[]{:S(2)}, u32[]{:S(2)}) %collective-permute-start.8) | collective-permute-done | bytes 426016 | tf_op jit(solution)/shard_map/ppermute | solution.py:325
  63.0 0.8 copy-done.4
  63.8 3.7 %shard_map.112.x_here = bf16[1024,1024]{1,0:T(8,128)(2,1)} custom-call(s32[4]{0:T(128)} %pad_add_fusion.1.s, bf16[1024,128]{1,0:T(8,128)(2,1)} %bitcast.17, bf16[1024,128]{1,0:T(8,128)(2,1)} %bitcast.20, bf16[1664,128]{1,0:T(8,128)(2,1)} %copy-done.13, bf16[1664,128]{1,0:T(8,128)(2,1)} %copy-done.17, bf16[1664,128]{1,0:T(8,128)(2,1)} %copy-done.2, ...), custom_call_target="tpu_custom_call" | custom-call | tf_op jit(solution)/shard_map/pallas_call | solution.py:29
  67.5 4.6 %collective-permute-start.11 = (bf16[1024,1024]{1,0:T(8,128)(2,1)}, bf16[1024,1024]{1,0:T(8,128)(2,1)S(1)}, u32[]{:S(2)}, u32[]{:S(2)}) collective-permute-start(bf16[1024,1024]{1,0:T(8,128)(2,1)} %shard_map.112.x_here), channel_id=1, source_target_pairs={{0,8},{8,0},{16,24},{24,16},{32,40},{40,32},{48,56},{56,48},{64,72... | collective-permute-start | bytes 6291464 | tf_op jit(solution)/shard_map/ppermute | solution.py:321
  72.1 0.9 slice.72
  73.1 1.9 collective-permute-start.6
  75.0 0.9 slice.74
  76.0 3.4 %collective-permute-start.9 = (bf16[768,128]{1,0:T(8,128)(2,1)S(1)}, bf16[768,128]{1,0:T(8,128)(2,1)S(1)}, u32[]{:S(2)}, u32[]{:S(2)}) collective-permute-start(bf16[768,128]{1,0:T(8,128)(2,1)S(1)} %slice.74), channel_id=1, source_target_pairs={{0,1},{1,2},{2,3},{3,4},{4,5},{5,6},{6,7},{7,0},{8,9},{9,10},{10,1... | collective-permute-start | bytes 589832 | tf_op jit(solution)/shard_map/ppermute | solution.py:325
  79.3 2.1 collective-permute-done.6.m4
  81.4 4.1 %collective-permute-done.9.p4 = bf16[768,128]{1,0:T(8,128)(2,1)S(1)} collective-permute-done((bf16[768,128]{1,0:T(8,128)(2,1)S(1)}, bf16[768,128]{1,0:T(8,128)(2,1)S(1)}, u32[]{:S(2)}, u32[]{:S(2)}) %collective-permute-start.9) | collective-permute-done | bytes 196640 | tf_op jit(solution)/shard_map/ppermute | solution.py:325
  85.5 2.8 %collective-permute-start.10 = (bf16[512,128]{1,0:T(8,128)(2,1)S(1)}, bf16[512,128]{1,0:T(8,128)(2,1)S(1)}, u32[]{:S(2)}, u32[]{:S(2)}) collective-permute-start(bf16[512,128]{1,0:T(8,128)(2,1)S(1)} %pad_maximum_fusion.1.last_own), channel_id=1, source_target_pairs={{0,8},{8,0},{16,24},{24,16},{32,40},{40,32},{48,56},{56,48},{64,72... | collective-permute-start | bytes 393224 | tf_op jit(solution)/shard_map/ppermute | solution.py:321
  89.9 1.4 copy-done.10
  91.3 8.2 %shard_map.113 = (bf16[1024,128]{1,0:T(8,128)(2,1)}, bf16[1040,128]{1,0:T(8,128)(2,1)}) custom-call(s32[4]{0:T(128)} %pad_add_fusion.3.s, bf16[512,128]{1,0:T(8,128)(2,1)} %copy-done.22, bf16[512,128]{1,0:T(8,128)(2,1)} %copy-done.30, bf16[1024,128]{1,0:T(8,128)(2,1)} %bitcast.22, bf16[1024,128]{1,0:T(8,128)(2,1)} %copy-done.8, ...), custom_call_target="tpu_custom_call" | custom-call | tf_op jit(solution)/shard_map/pallas_call | solution.py:29
  99.5 3.8 %collective-permute-start.12 = (bf16[1040,128]{1,0:T(8,128)(2,1)}, bf16[1040,128]{1,0:T(8,128)(2,1)S(1)}, u32[]{:S(2)}, u32[]{:S(2)}) collective-permute-start(bf16[1040,128]{1,0:T(8,128)(2,1)} %get-tuple-element.55.move), channel_id=1, source_target_pairs={{0,8},{8,0},{16,24},{24,16},{32,40},{40,32},{48,56},{56,48},{64,72... | collective-permute-start | bytes 798728 | tf_op jit(solution)/shard_map/ppermute | solution.py:321
  105.4 1.7 shard_map.114
  107.1 2.1 collective-permute-start.13
  109.8 1.9 select_select_fusion
  111.7 5.1 %collective-permute-done.13.xb.ab = bf16[1024,128]{1,0:T(8,128)(2,1)S(1)} collective-permute-done((bf16[1024,128]{1,0:T(8,128)(2,1)}, bf16[1024,128]{1,0:T(8,128)(2,1)S(1)}, u32[]{:S(2)}, u32[]{:S(2)}) %collective-permute-start.13) | collective-permute-done | bytes 262176 | tf_op jit(solution)/shard_map/ppermute | solution.py:321
  117.5 2.6 %shard_map.115.msg = bf16[1664,128]{1,0:T(8,128)(2,1)} custom-call(s32[4]{0:T(128)} %pad_add_fusion.s, bf16[1024,128]{1,0:T(8,128)(2,1)} %get-tuple-element.65.cov.info.xa.addb, bf16[1024,128]{1,0:T(8,128)(2,1)} %copy-done, bf16[1024,128]{1,0:T(8,128)(2,1)} %get-tuple-element.80.aa, bf16[1024,128]{1,0:T(8,128)(2,1)} %copy-done), custom_call_target="tpu_custom_call" | custom-call | tf_op jit(solution)/shard_map/pallas_call | solution.py:29
  120.2 2.2 %collective-permute-start.16 = (bf16[1040,128]{1,0:T(8,128)(2,1)S(1)}, bf16[1040,128]{1,0:T(8,128)(2,1)S(1)}, u32[]{:S(2)}, u32[]{:S(2)}) collective-permute-start(bf16[1040,128]{1,0:T(8,128)(2,1)S(1)} %pad_maximum_fusion), channel_id=1, source_target_pairs={{0,16},{8,24},{16,0},{24,8},{32,48},{40,56},{48,32},{56,40},{64,80... | collective-permute-start | bytes 798728 | tf_op jit(solution)/shard_map/ppermute | solution.py:321
  122.3 1.9 collective-permute-start.15
  124.3 3.4 %collective-permute-start.14 = (bf16[1664,128]{1,0:T(8,128)(2,1)}, bf16[1664,128]{1,0:T(8,128)(2,1)S(1)}, u32[]{:S(2)}, u32[]{:S(2)}) collective-permute-start(bf16[1664,128]{1,0:T(8,128)(2,1)} %shard_map.115.msg), channel_id=1, source_target_pairs={{0,1},{1,2},{2,3},{3,4},{4,5},{5,6},{6,7},{7,0},{8,9},{9,10},{10,1... | collective-permute-start | bytes 1277960 | tf_op jit(solution)/shard_map/ppermute | solution.py:325
  127.6 1.1 collective-permute-done.16.adda
  129.5 0.8 fusion.aia.aib
  130.2 4.4 %collective-permute-done.15.m1 = bf16[1664,128]{1,0:T(8,128)(2,1)S(1)} collective-permute-done((bf16[1664,128]{1,0:T(8,128)(2,1)}, bf16[1664,128]{1,0:T(8,128)(2,1)S(1)}, u32[]{:S(2)}, u32[]{:S(2)}) %collective-permute-start.15) | collective-permute-done | bytes 426016 | tf_op jit(solution)/shard_map/ppermute | solution.py:325
  134.6 3.1 %collective-permute-done.14.p1 = bf16[1664,128]{1,0:T(8,128)(2,1)S(1)} collective-permute-done((bf16[1664,128]{1,0:T(8,128)(2,1)}, bf16[1664,128]{1,0:T(8,128)(2,1)S(1)}, u32[]{:S(2)}, u32[]{:S(2)}) %collective-permute-start.14) | collective-permute-done | bytes 426016 | tf_op jit(solution)/shard_map/ppermute | solution.py:325
  137.7 1.9 collective-permute-start.17
  139.6 3.4 %collective-permute-start.20 = (bf16[1664,128]{1,0:T(8,128)(2,1)S(1)}, bf16[1664,128]{1,0:T(8,128)(2,1)S(1)}, u32[]{:S(2)}, u32[]{:S(2)}) collective-permute-start(bf16[1664,128]{1,0:T(8,128)(2,1)S(1)} %collective-permute-done.14.p1), channel_id=1, source_target_pairs={{0,1},{1,2},{2,3},{3,4},{4,5},{5,6},{6,7},{7,0},{8,9},{9,10},{10,1... | collective-permute-start | bytes 1277960 | tf_op jit(solution)/shard_map/ppermute | solution.py:325
  143.0 5.9 %collective-permute-done.17.m2 = bf16[1664,128]{1,0:T(8,128)(2,1)S(1)} collective-permute-done((bf16[1664,128]{1,0:T(8,128)(2,1)S(1)}, bf16[1664,128]{1,0:T(8,128)(2,1)S(1)}, u32[]{:S(2)}, u32[]{:S(2)}) %collective-permute-start.17) | collective-permute-done | bytes 426016 | tf_op jit(solution)/shard_map/ppermute | solution.py:325
  148.9 3.4 %collective-permute-start.18 = (bf16[1664,128]{1,0:T(8,128)(2,1)S(1)}, bf16[1664,128]{1,0:T(8,128)(2,1)S(1)}, u32[]{:S(2)}, u32[]{:S(2)}) collective-permute-start(bf16[1664,128]{1,0:T(8,128)(2,1)S(1)} %collective-permute-done.17.m2), channel_id=1, source_target_pairs={{0,7},{1,0},{2,1},{3,2},{4,3},{5,4},{6,5},{7,6},{8,15},{9,8},{10,9... | collective-permute-start | bytes 1277960 | tf_op jit(solution)/shard_map/ppermute | solution.py:325
  152.3 1.9 collective-permute-start.21
  154.2 4.9 %collective-permute-done.18.m3 = bf16[1664,128]{1,0:T(8,128)(2,1)S(1)} collective-permute-done((bf16[1664,128]{1,0:T(8,128)(2,1)S(1)}, bf16[1664,128]{1,0:T(8,128)(2,1)S(1)}, u32[]{:S(2)}, u32[]{:S(2)}) %collective-permute-start.18) | collective-permute-done | bytes 426016 | tf_op jit(solution)/shard_map/ppermute | solution.py:325
  159.2 4.6 %collective-permute-done.21.p3 = bf16[1664,128]{1,0:T(8,128)(2,1)S(1)} collective-permute-done((bf16[1664,128]{1,0:T(8,128)(2,1)S(1)}, bf16[1664,128]{1,0:T(8,128)(2,1)S(1)}, u32[]{:S(2)}, u32[]{:S(2)}) %collective-permute-start.21) | collective-permute-done | bytes 426016 | tf_op jit(solution)/shard_map/ppermute | solution.py:325
  163.9 0.8 copy-done.3
  164.6 3.9 %shard_map.116.x_here = bf16[1024,1024]{1,0:T(8,128)(2,1)} custom-call(s32[4]{0:T(128)} %pad_add_fusion.s, bf16[1024,128]{1,0:T(8,128)(2,1)} %get-tuple-element.65.cov.info.xa.addb, bf16[1024,128]{1,0:T(8,128)(2,1)} %copy-done, bf16[1664,128]{1,0:T(8,128)(2,1)} %copy-done.11, bf16[1664,128]{1,0:T(8,128)(2,1)} %copy-done.15, bf16[1664,128]{1,0:T(8,128)(2,1)} %copy-done.1, ...), custom_call_target="tpu_custom_call" | custom-call | tf_op jit(solution)/shard_map/pallas_call | solution.py:29
  168.5 5.7 %collective-permute-start.24 = (bf16[1024,1024]{1,0:T(8,128)(2,1)}, bf16[1024,1024]{1,0:T(8,128)(2,1)S(1)}, u32[]{:S(2)}, u32[]{:S(2)}) collective-permute-start(bf16[1024,1024]{1,0:T(8,128)(2,1)} %shard_map.116.x_here), channel_id=1, source_target_pairs={{0,8},{8,0},{16,24},{24,16},{32,40},{40,32},{48,56},{56,48},{64,72... | collective-permute-start | bytes 6291464 | tf_op jit(solution)/shard_map/ppermute | solution.py:321
  174.2 0.9 slice.80
  175.2 1.9 collective-permute-start.19
  177.1 0.9 slice.82
  178.1 3.4 %collective-permute-start.22 = (bf16[768,128]{1,0:T(8,128)(2,1)S(1)}, bf16[768,128]{1,0:T(8,128)(2,1)S(1)}, u32[]{:S(2)}, u32[]{:S(2)}) collective-permute-start(bf16[768,128]{1,0:T(8,128)(2,1)S(1)} %slice.82), channel_id=1, source_target_pairs={{0,1},{1,2},{2,3},{3,4},{4,5},{5,6},{6,7},{7,0},{8,9},{9,10},{10,1... | collective-permute-start | bytes 589832 | tf_op jit(solution)/shard_map/ppermute | solution.py:325
  181.4 2.1 collective-permute-done.19.m4
  183.5 4.1 %collective-permute-done.22.p4 = bf16[768,128]{1,0:T(8,128)(2,1)S(1)} collective-permute-done((bf16[768,128]{1,0:T(8,128)(2,1)S(1)}, bf16[768,128]{1,0:T(8,128)(2,1)S(1)}, u32[]{:S(2)}, u32[]{:S(2)}) %collective-permute-start.22) | collective-permute-done | bytes 196640 | tf_op jit(solution)/shard_map/ppermute | solution.py:325
  187.6 2.8 %collective-permute-start.23 = (bf16[512,128]{1,0:T(8,128)(2,1)S(1)}, bf16[512,128]{1,0:T(8,128)(2,1)S(1)}, u32[]{:S(2)}, u32[]{:S(2)}) collective-permute-start(bf16[512,128]{1,0:T(8,128)(2,1)S(1)} %pad_maximum_fusion.2.last_own), channel_id=1, source_target_pairs={{0,8},{8,0},{16,24},{24,16},{32,40},{40,32},{48,56},{56,48},{64,72... | collective-permute-start | bytes 393224 | tf_op jit(solution)/shard_map/ppermute | solution.py:321
  192.0 1.4 copy-done.9
  193.4 8.2 %shard_map.117 = (bf16[1024,128]{1,0:T(8,128)(2,1)}, bf16[1040,128]{1,0:T(8,128)(2,1)}) custom-call(s32[4]{0:T(128)} %pad_add_fusion.4.s, bf16[512,128]{1,0:T(8,128)(2,1)} %copy-done.21, bf16[512,128]{1,0:T(8,128)(2,1)} %copy-done.29, bf16[1024,128]{1,0:T(8,128)(2,1)} %fusion.aia.aib, bf16[1024,128]{1,0:T(8,128)(2,1)} %fusion.aia.aib, ...), custom_call_target="tpu_custom_call" | custom-call | tf_op jit(solution)/shard_map/pallas_call | solution.py:29
  201.6 3.8 %collective-permute-start.25 = (bf16[1040,128]{1,0:T(8,128)(2,1)}, bf16[1040,128]{1,0:T(8,128)(2,1)S(1)}, u32[]{:S(2)}, u32[]{:S(2)}) collective-permute-start(bf16[1040,128]{1,0:T(8,128)(2,1)} %get-tuple-element.68.own2), channel_id=1, source_target_pairs={{0,8},{8,0},{16,24},{24,16},{32,40},{40,32},{48,56},{56,48},{64,72... | collective-permute-start | bytes 798728 | tf_op jit(solution)/shard_map/ppermute | solution.py:321
  205.4 1.9 collective-permute-start.26
  207.3 1.3 slice.69.vec_own
  210.0 2.7 %shard_map.118 = (bf16[1,1024]{1,0:T(2,128)(2,1)}, bf16[1,1024]{1,0:T(2,128)(2,1)}, bf16[1024,128]{1,0:T(8,128)(2,1)}, bf16[1024,128]{1,0:T(8,128)(2,1)}, bf16[1024,128]{1,0:T(8,128)(2,1)}) custom-call(s32[1]{0:T(128)} %bitcast.s, bf16[16,128]{1,0:T(8,128)(2,1)} %slice.69.vec_own, bf16[16,128]{1,0:T(8,128)(2,1)} %slice.84.vec_got, ...), custom_call_target="tpu_custom_call" | custom-call | tf_op jit(solution)/shard_map/pallas_call | solution.py:29
  (84 shorter events, 10.9 us)
Async XLA Ops:
  0.6 10.1 %collective-permute-start = (bf16[1024,128]{1,0:T(8,128)(2,1)}, bf16[1024,128]{1,0:T(8,128)(2,1)S(1)}, u32[]{:S(2)}, u32[]{:S(2)}) collective-permute-start(bf16[1024,128]{1,0:T(8,128)(2,1)} %bitcast.21), channel_id=1, source_target_pairs={{0,8},{8,0},{16,24},{24,16},{32,40},{40,32},{48,56},{56,48},{64,72... | collective-permute-start | bytes 786440 | tf_op jit(solution)/shard_map/ppermute | solution.py:321
  10.7 0.7 copy-start.8
  16.1 7.5 %collective-permute-start.3 = (bf16[1040,128]{1,0:T(8,128)(2,1)}, bf16[1040,128]{1,0:T(8,128)(2,1)S(1)}, u32[]{:S(2)}, u32[]{:S(2)}) collective-permute-start(bf16[1040,128]{1,0:T(8,128)(2,1)} %get-tuple-element.42), channel_id=1, source_target_pairs={{0,8},{8,0},{16,24},{24,16},{32,40},{40,32},{48,56},{56,48},{64,72... | collective-permute-start | bytes 798728 | tf_op jit(solution)/shard_map/ppermute | solution.py:321
  18.3 13.3 %collective-permute-start.2 = (bf16[1664,128]{1,0:T(8,128)(2,1)}, bf16[1664,128]{1,0:T(8,128)(2,1)S(1)}, u32[]{:S(2)}, u32[]{:S(2)}) collective-permute-start(bf16[1664,128]{1,0:T(8,128)(2,1)} %shard_map.110.msg), channel_id=1, source_target_pairs={{0,7},{1,0},{2,1},{3,2},{4,3},{5,4},{6,5},{7,6},{8,15},{9,8},{10,9... | collective-permute-start | bytes 1277960 | tf_op jit(solution)/shard_map/ppermute | solution.py:325
  20.2 14.5 %collective-permute-start.1 = (bf16[1664,128]{1,0:T(8,128)(2,1)}, bf16[1664,128]{1,0:T(8,128)(2,1)S(1)}, u32[]{:S(2)}, u32[]{:S(2)}) collective-permute-start(bf16[1664,128]{1,0:T(8,128)(2,1)} %shard_map.110.msg), channel_id=1, source_target_pairs={{0,1},{1,2},{2,3},{3,4},{4,5},{5,6},{6,7},{7,0},{8,9},{9,10},{10,1... | collective-permute-start | bytes 1277960 | tf_op jit(solution)/shard_map/ppermute | solution.py:325
  23.6 65.7 %copy-start.19 = (bf16[1040,128]{1,0:T(8,128)(2,1)}, bf16[1040,128]{1,0:T(8,128)(2,1)S(1)}, u32[]{:S(2)}) copy-start(bf16[1040,128]{1,0:T(8,128)(2,1)S(1)} %collective-permute-done.3.adda.addb) | copy-start | bytes 798724
  31.6 31.4 %copy-start.13 = (bf16[1664,128]{1,0:T(8,128)(2,1)}, bf16[1664,128]{1,0:T(8,128)(2,1)S(1)}, u32[]{:S(2)}) copy-start(bf16[1664,128]{1,0:T(8,128)(2,1)S(1)} %collective-permute-done.2.m1) | copy-start | bytes 1277956
  34.7 28.2 %copy-start.14 = (bf16[1664,128]{1,0:T(8,128)(2,1)}, bf16[1664,128]{1,0:T(8,128)(2,1)S(1)}, u32[]{:S(2)}) copy-start(bf16[1664,128]{1,0:T(8,128)(2,1)S(1)} %collective-permute-done.1.p1) | copy-start | bytes 1277956
  34.7 12.2 %collective-permute-start.4 = (bf16[1664,128]{1,0:T(8,128)(2,1)S(1)}, bf16[1664,128]{1,0:T(8,128)(2,1)S(1)}, u32[]{:S(2)}, u32[]{:S(2)}) collective-permute-start(bf16[1664,128]{1,0:T(8,128)(2,1)S(1)} %collective-permute-done.2.m1), channel_id=1, source_target_pairs={{0,7},{1,0},{2,1},{3,2},{4,3},{5,4},{6,5},{7,6},{8,15},{9,8},{10,9... | collective-permute-start | bytes 1277960 | tf_op jit(solution)/shard_map/ppermute | solution.py:325
  36.7 13.7 %collective-permute-start.7 = (bf16[1664,128]{1,0:T(8,128)(2,1)S(1)}, bf16[1664,128]{1,0:T(8,128)(2,1)S(1)}, u32[]{:S(2)}, u32[]{:S(2)}) collective-permute-start(bf16[1664,128]{1,0:T(8,128)(2,1)S(1)} %collective-permute-done.1.p1), channel_id=1, source_target_pairs={{0,1},{1,2},{2,3},{3,4},{4,5},{5,6},{6,7},{7,0},{8,9},{9,10},{10,1... | collective-permute-start | bytes 1277960 | tf_op jit(solution)/shard_map/ppermute | solution.py:325
  47.0 16.0 %copy-start.17 = (bf16[1664,128]{1,0:T(8,128)(2,1)}, bf16[1664,128]{1,0:T(8,128)(2,1)S(1)}, u32[]{:S(2)}) copy-start(bf16[1664,128]{1,0:T(8,128)(2,1)S(1)} %collective-permute-done.4.m2) | copy-start | bytes 1277956
  47.0 11.4 %collective-permute-start.5 = (bf16[1664,128]{1,0:T(8,128)(2,1)S(1)}, bf16[1664,128]{1,0:T(8,128)(2,1)S(1)}, u32[]{:S(2)}, u32[]{:S(2)}) collective-permute-start(bf16[1664,128]{1,0:T(8,128)(2,1)S(1)} %collective-permute-done.4.m2), channel_id=1, source_target_pairs={{0,7},{1,0},{2,1},{3,2},{4,3},{5,4},{6,5},{7,6},{8,15},{9,8},{10,9... | collective-permute-start | bytes 1277960 | tf_op jit(solution)/shard_map/ppermute | solution.py:325
  50.4 12.6 %copy-start.18 = (bf16[1664,128]{1,0:T(8,128)(2,1)}, bf16[1664,128]{1,0:T(8,128)(2,1)S(1)}, u32[]{:S(2)}) copy-start(bf16[1664,128]{1,0:T(8,128)(2,1)S(1)} %collective-permute-done.7.p2) | copy-start | bytes 1277956
  50.4 12.6 %collective-permute-start.8 = (bf16[1664,128]{1,0:T(8,128)(2,1)S(1)}, bf16[1664,128]{1,0:T(8,128)(2,1)S(1)}, u32[]{:S(2)}, u32[]{:S(2)}) collective-permute-start(bf16[1664,128]{1,0:T(8,128)(2,1)S(1)} %collective-permute-done.7.p2), channel_id=1, source_target_pairs={{0,1},{1,2},{2,3},{3,4},{4,5},{5,6},{6,7},{7,0},{8,9},{9,10},{10,1... | collective-permute-start | bytes 1277960 | tf_op jit(solution)/shard_map/ppermute | solution.py:325
  58.3 4.7 %copy-start.2 = (bf16[1664,128]{1,0:T(8,128)(2,1)}, bf16[1664,128]{1,0:T(8,128)(2,1)S(1)}, u32[]{:S(2)}) copy-start(bf16[1664,128]{1,0:T(8,128)(2,1)S(1)} %collective-permute-done.5.m3) | copy-start | bytes 1277956
  63.0 0.8 copy-start.4
  67.5 21.8 %collective-permute-start.11 = (bf16[1024,1024]{1,0:T(8,128)(2,1)}, bf16[1024,1024]{1,0:T(8,128)(2,1)S(1)}, u32[]{:S(2)}, u32[]{:S(2)}) collective-permute-start(bf16[1024,1024]{1,0:T(8,128)(2,1)} %shard_map.112.x_here), channel_id=1, source_target_pairs={{0,8},{8,0},{16,24},{24,16},{32,40},{40,32},{48,56},{56,48},{64,72... | collective-permute-start | bytes 6291464 | tf_op jit(solution)/shard_map/ppermute | solution.py:321
  73.1 8.3 %collective-permute-start.6 = (bf16[768,128]{1,0:T(8,128)(2,1)S(1)}, bf16[768,128]{1,0:T(8,128)(2,1)S(1)}, u32[]{:S(2)}, u32[]{:S(2)}) collective-permute-start(bf16[768,128]{1,0:T(8,128)(2,1)S(1)} %slice.72), channel_id=1, source_target_pairs={{0,7},{1,0},{2,1},{3,2},{4,3},{5,4},{6,5},{7,6},{8,15},{9,8},{10,9... | collective-permute-start | bytes 589832 | tf_op jit(solution)/shard_map/ppermute | solution.py:325
  76.0 9.5 %collective-permute-start.9 = (bf16[768,128]{1,0:T(8,128)(2,1)S(1)}, bf16[768,128]{1,0:T(8,128)(2,1)S(1)}, u32[]{:S(2)}, u32[]{:S(2)}) collective-permute-start(bf16[768,128]{1,0:T(8,128)(2,1)S(1)} %slice.74), channel_id=1, source_target_pairs={{0,1},{1,2},{2,3},{3,4},{4,5},{5,6},{6,7},{7,0},{8,9},{9,10},{10,1... | collective-permute-start | bytes 589832 | tf_op jit(solution)/shard_map/ppermute | solution.py:325
  81.4 7.9 %copy-start.24 = (bf16[768,128]{1,0:T(8,128)(2,1)}, bf16[768,128]{1,0:T(8,128)(2,1)S(1)}, u32[]{:S(2)}) copy-start(bf16[768,128]{1,0:T(8,128)(2,1)S(1)} %collective-permute-done.6.m4) | copy-start | bytes 589828
  85.5 3.8 %copy-start.26 = (bf16[768,128]{1,0:T(8,128)(2,1)}, bf16[768,128]{1,0:T(8,128)(2,1)S(1)}, u32[]{:S(2)}) copy-start(bf16[768,128]{1,0:T(8,128)(2,1)S(1)} %collective-permute-done.9.p4) | copy-start | bytes 589828
  85.5 3.8 %copy-start.22 = (bf16[512,128]{1,0:T(8,128)(2,1)}, bf16[512,128]{1,0:T(8,128)(2,1)S(1)}, u32[]{:S(2)}) copy-start(bf16[512,128]{1,0:T(8,128)(2,1)S(1)} %pad_maximum_fusion.1.last_own) | copy-start | bytes 393220
  85.5 3.8 %collective-permute-start.10 = (bf16[512,128]{1,0:T(8,128)(2,1)S(1)}, bf16[512,128]{1,0:T(8,128)(2,1)S(1)}, u32[]{:S(2)}, u32[]{:S(2)}) collective-permute-start(bf16[512,128]{1,0:T(8,128)(2,1)S(1)} %pad_maximum_fusion.1.last_own), channel_id=1, source_target_pairs={{0,8},{8,0},{16,24},{24,16},{32,40},{40,32},{48,56},{56,48},{64,72... | collective-permute-start | bytes 393224 | tf_op jit(solution)/shard_map/ppermute | solution.py:321
  89.3 0.7 copy-start.30
  89.9 1.4 copy-start.10
  99.5 5.2 %collective-permute-start.12 = (bf16[1040,128]{1,0:T(8,128)(2,1)}, bf16[1040,128]{1,0:T(8,128)(2,1)S(1)}, u32[]{:S(2)}, u32[]{:S(2)}) collective-permute-start(bf16[1040,128]{1,0:T(8,128)(2,1)} %get-tuple-element.55.move), channel_id=1, source_target_pairs={{0,8},{8,0},{16,24},{24,16},{32,40},{40,32},{48,56},{56,48},{64,72... | collective-permute-start | bytes 798728 | tf_op jit(solution)/shard_map/ppermute | solution.py:321
  104.6 0.7 copy-start.6
  105.4 24.1 %copy-start.5 = (bf16[1040,128]{1,0:T(8,128)(2,1)S(1)}, bf16[1040,128]{1,0:T(8,128)(2,1)}, u32[]{:S(2)}) copy-start(bf16[1040,128]{1,0:T(8,128)(2,1)} %get-tuple-element.55.move) | copy-start | bytes 798724
  107.1 22.4 %copy-start.7 = (bf16[1040,128]{1,0:T(8,128)(2,1)S(1)}, bf16[1040,128]{1,0:T(8,128)(2,1)}, u32[]{:S(2)}) copy-start(bf16[1040,128]{1,0:T(8,128)(2,1)} %copy-done.6) | copy-start | bytes 798724
  107.1 9.7 %collective-permute-start.13 = (bf16[1024,128]{1,0:T(8,128)(2,1)}, bf16[1024,128]{1,0:T(8,128)(2,1)S(1)}, u32[]{:S(2)}, u32[]{:S(2)}) collective-permute-start(bf16[1024,128]{1,0:T(8,128)(2,1)} %shard_map.114), channel_id=1, source_target_pairs={{0,16},{8,24},{16,0},{24,8},{32,48},{40,56},{48,32},{56,40},{64,80... | collective-permute-start | bytes 786440 | tf_op jit(solution)/shard_map/ppermute | solution.py:321
  116.8 0.7 copy-start
  120.2 8.6 %collective-permute-start.16 = (bf16[1040,128]{1,0:T(8,128)(2,1)S(1)}, bf16[1040,128]{1,0:T(8,128)(2,1)S(1)}, u32[]{:S(2)}, u32[]{:S(2)}) collective-permute-start(bf16[1040,128]{1,0:T(8,128)(2,1)S(1)} %pad_maximum_fusion), channel_id=1, source_target_pairs={{0,16},{8,24},{16,0},{24,8},{32,48},{40,56},{48,32},{56,40},{64,80... | collective-permute-start | bytes 798728 | tf_op jit(solution)/shard_map/ppermute | solution.py:321
  122.3 12.2 %collective-permute-start.15 = (bf16[1664,128]{1,0:T(8,128)(2,1)}, bf16[1664,128]{1,0:T(8,128)(2,1)S(1)}, u32[]{:S(2)}, u32[]{:S(2)}) collective-permute-start(bf16[1664,128]{1,0:T(8,128)(2,1)} %shard_map.115.msg), channel_id=1, source_target_pairs={{0,7},{1,0},{2,1},{3,2},{4,3},{5,4},{6,5},{7,6},{8,15},{9,8},{10,9... | collective-permute-start | bytes 1277960 | tf_op jit(solution)/shard_map/ppermute | solution.py:325
  124.3 13.4 %collective-permute-start.14 = (bf16[1664,128]{1,0:T(8,128)(2,1)}, bf16[1664,128]{1,0:T(8,128)(2,1)S(1)}, u32[]{:S(2)}, u32[]{:S(2)}) collective-permute-start(bf16[1664,128]{1,0:T(8,128)(2,1)} %shard_map.115.msg), channel_id=1, source_target_pairs={{0,1},{1,2},{2,3},{3,4},{4,5},{5,6},{6,7},{7,0},{8,9},{9,10},{10,1... | collective-permute-start | bytes 1277960 | tf_op jit(solution)/shard_map/ppermute | solution.py:325
  128.8 39.7 %copy-start.20 = (bf16[1040,128]{1,0:T(8,128)(2,1)}, bf16[1040,128]{1,0:T(8,128)(2,1)S(1)}, u32[]{:S(2)}) copy-start(bf16[1040,128]{1,0:T(8,128)(2,1)S(1)} %collective-permute-done.16.adda) | copy-start | bytes 798724
  134.6 29.3 %copy-start.11 = (bf16[1664,128]{1,0:T(8,128)(2,1)}, bf16[1664,128]{1,0:T(8,128)(2,1)S(1)}, u32[]{:S(2)}) copy-start(bf16[1664,128]{1,0:T(8,128)(2,1)S(1)} %collective-permute-done.15.m1) | copy-start | bytes 1277956
  137.7 26.1 %copy-start.12 = (bf16[1664,128]{1,0:T(8,128)(2,1)}, bf16[1664,128]{1,0:T(8,128)(2,1)S(1)}, u32[]{:S(2)}) copy-start(bf16[1664,128]{1,0:T(8,128)(2,1)S(1)} %collective-permute-done.14.p1) | copy-start | bytes 1277956
  137.7 11.2 %collective-permute-start.17 = (bf16[1664,128]{1,0:T(8,128)(2,1)S(1)}, bf16[1664,128]{1,0:T(8,128)(2,1)S(1)}, u32[]{:S(2)}, u32[]{:S(2)}) collective-permute-start(bf16[1664,128]{1,0:T(8,128)(2,1)S(1)} %collective-permute-done.15.m1), channel_id=1, source_target_pairs={{0,7},{1,0},{2,1},{3,2},{4,3},{5,4},{6,5},{7,6},{8,15},{9,8},{10,9... | collective-permute-start | bytes 1277960 | tf_op jit(solution)/shard_map/ppermute | solution.py:325
  139.6 12.7 %collective-permute-start.20 = (bf16[1664,128]{1,0:T(8,128)(2,1)S(1)}, bf16[1664,128]{1,0:T(8,128)(2,1)S(1)}, u32[]{:S(2)}, u32[]{:S(2)}) collective-permute-start(bf16[1664,128]{1,0:T(8,128)(2,1)S(1)} %collective-permute-done.14.p1), channel_id=1, source_target_pairs={{0,1},{1,2},{2,3},{3,4},{4,5},{5,6},{6,7},{7,0},{8,9},{9,10},{10,1... | collective-permute-start | bytes 1277960 | tf_op jit(solution)/shard_map/ppermute | solution.py:325
  148.9 15.0 %copy-start.15 = (bf16[1664,128]{1,0:T(8,128)(2,1)}, bf16[1664,128]{1,0:T(8,128)(2,1)S(1)}, u32[]{:S(2)}) copy-start(bf16[1664,128]{1,0:T(8,128)(2,1)S(1)} %collective-permute-done.17.m2) | copy-start | bytes 1277956
  148.9 10.3 %collective-permute-start.18 = (bf16[1664,128]{1,0:T(8,128)(2,1)S(1)}, bf16[1664,128]{1,0:T(8,128)(2,1)S(1)}, u32[]{:S(2)}, u32[]{:S(2)}) collective-permute-start(bf16[1664,128]{1,0:T(8,128)(2,1)S(1)} %collective-permute-done.17.m2), channel_id=1, source_target_pairs={{0,7},{1,0},{2,1},{3,2},{4,3},{5,4},{6,5},{7,6},{8,15},{9,8},{10,9... | collective-permute-start | bytes 1277960 | tf_op jit(solution)/shard_map/ppermute | solution.py:325
  152.3 11.5 %copy-start.16 = (bf16[1664,128]{1,0:T(8,128)(2,1)}, bf16[1664,128]{1,0:T(8,128)(2,1)S(1)}, u32[]{:S(2)}) copy-start(bf16[1664,128]{1,0:T(8,128)(2,1)S(1)} %collective-permute-done.20.p2) | copy-start | bytes 1277956
  152.3 11.5 %collective-permute-start.21 = (bf16[1664,128]{1,0:T(8,128)(2,1)S(1)}, bf16[1664,128]{1,0:T(8,128)(2,1)S(1)}, u32[]{:S(2)}, u32[]{:S(2)}) collective-permute-start(bf16[1664,128]{1,0:T(8,128)(2,1)S(1)} %collective-permute-done.20.p2), channel_id=1, source_target_pairs={{0,1},{1,2},{2,3},{3,4},{4,5},{5,6},{6,7},{7,0},{8,9},{9,10},{10,1... | collective-permute-start | bytes 1277960 | tf_op jit(solution)/shard_map/ppermute | solution.py:325
  159.2 4.7 %copy-start.1 = (bf16[1664,128]{1,0:T(8,128)(2,1)}, bf16[1664,128]{1,0:T(8,128)(2,1)S(1)}, u32[]{:S(2)}) copy-start(bf16[1664,128]{1,0:T(8,128)(2,1)S(1)} %collective-permute-done.18.m3) | copy-start | bytes 1277956
  163.9 0.8 copy-start.3
  168.5 22.9 %collective-permute-start.24 = (bf16[1024,1024]{1,0:T(8,128)(2,1)}, bf16[1024,1024]{1,0:T(8,128)(2,1)S(1)}, u32[]{:S(2)}, u32[]{:S(2)}) collective-permute-start(bf16[1024,1024]{1,0:T(8,128)(2,1)} %shard_map.116.x_here), channel_id=1, source_target_pairs={{0,8},{8,0},{16,24},{24,16},{32,40},{40,32},{48,56},{56,48},{64,72... | collective-permute-start | bytes 6291464 | tf_op jit(solution)/shard_map/ppermute | solution.py:321
  175.2 8.3 %collective-permute-start.19 = (bf16[768,128]{1,0:T(8,128)(2,1)S(1)}, bf16[768,128]{1,0:T(8,128)(2,1)S(1)}, u32[]{:S(2)}, u32[]{:S(2)}) collective-permute-start(bf16[768,128]{1,0:T(8,128)(2,1)S(1)} %slice.80), channel_id=1, source_target_pairs={{0,7},{1,0},{2,1},{3,2},{4,3},{5,4},{6,5},{7,6},{8,15},{9,8},{10,9... | collective-permute-start | bytes 589832 | tf_op jit(solution)/shard_map/ppermute | solution.py:325
  178.1 9.5 %collective-permute-start.22 = (bf16[768,128]{1,0:T(8,128)(2,1)S(1)}, bf16[768,128]{1,0:T(8,128)(2,1)S(1)}, u32[]{:S(2)}, u32[]{:S(2)}) collective-permute-start(bf16[768,128]{1,0:T(8,128)(2,1)S(1)} %slice.82), channel_id=1, source_target_pairs={{0,1},{1,2},{2,3},{3,4},{4,5},{5,6},{6,7},{7,0},{8,9},{9,10},{10,1... | collective-permute-start | bytes 589832 | tf_op jit(solution)/shard_map/ppermute | solution.py:325
  183.5 7.9 %copy-start.23 = (bf16[768,128]{1,0:T(8,128)(2,1)}, bf16[768,128]{1,0:T(8,128)(2,1)S(1)}, u32[]{:S(2)}) copy-start(bf16[768,128]{1,0:T(8,128)(2,1)S(1)} %collective-permute-done.19.m4) | copy-start | bytes 589828
  187.6 3.8 %copy-start.25 = (bf16[768,128]{1,0:T(8,128)(2,1)}, bf16[768,128]{1,0:T(8,128)(2,1)S(1)}, u32[]{:S(2)}) copy-start(bf16[768,128]{1,0:T(8,128)(2,1)S(1)} %collective-permute-done.22.p4) | copy-start | bytes 589828
  187.6 3.8 %copy-start.21 = (bf16[512,128]{1,0:T(8,128)(2,1)}, bf16[512,128]{1,0:T(8,128)(2,1)S(1)}, u32[]{:S(2)}) copy-start(bf16[512,128]{1,0:T(8,128)(2,1)S(1)} %pad_maximum_fusion.2.last_own) | copy-start | bytes 393220
  187.6 3.8 %collective-permute-start.23 = (bf16[512,128]{1,0:T(8,128)(2,1)S(1)}, bf16[512,128]{1,0:T(8,128)(2,1)S(1)}, u32[]{:S(2)}, u32[]{:S(2)}) collective-permute-start(bf16[512,128]{1,0:T(8,128)(2,1)S(1)} %pad_maximum_fusion.2.last_own), channel_id=1, source_target_pairs={{0,8},{8,0},{16,24},{24,16},{32,40},{40,32},{48,56},{56,48},{64,72... | collective-permute-start | bytes 393224 | tf_op jit(solution)/shard_map/ppermute | solution.py:321
  191.4 0.6 copy-start.29
  192.0 1.4 copy-start.9
  201.6 7.0 %collective-permute-start.25 = (bf16[1040,128]{1,0:T(8,128)(2,1)}, bf16[1040,128]{1,0:T(8,128)(2,1)S(1)}, u32[]{:S(2)}, u32[]{:S(2)}) collective-permute-start(bf16[1040,128]{1,0:T(8,128)(2,1)} %get-tuple-element.68.own2), channel_id=1, source_target_pairs={{0,8},{8,0},{16,24},{24,16},{32,40},{40,32},{48,56},{56,48},{64,72... | collective-permute-start | bytes 798728 | tf_op jit(solution)/shard_map/ppermute | solution.py:321
  205.4 3.8 %collective-permute-start.26 = (bf16[1024,128]{1,0:T(8,128)(2,1)}, bf16[1024,128]{1,0:T(8,128)(2,1)S(1)}, u32[]{:S(2)}, u32[]{:S(2)}) collective-permute-start(bf16[1024,128]{1,0:T(8,128)(2,1)} %get-tuple-element.69.own1), channel_id=1, source_target_pairs={{0,8},{8,0},{16,24},{24,16},{32,40},{40,32},{48,56},{56,48},{64,72... | collective-permute-start | bytes 786440 | tf_op jit(solution)/shard_map/ppermute | solution.py:321
  208.6 0.7 copy-start.27
  209.3 0.7 copy-start.28

commit v4 on v3

v4 whole, which is shorter than its diff:
```python
import functools

import jax
import jax.numpy as jnp
from jax import lax
from jax.experimental import pallas as pl
from jax.experimental.pallas import tpu as pltpu
from jax.sharding import PartitionSpec as P


NS = 2
W = 128
N = 8
D = W * N
RING = 1664
HALF = 768
INTERPRET = False

f32 = jnp.float32
bf16 = jnp.bfloat16


def dot(a, b):
    return jnp.dot(a, b, preferred_element_type=f32)


def call(kernel, out_shape, scratch, *args, vmem=None, vmem_out=True):
    vm = pl.BlockSpec(memory_space=pltpu.VMEM)
    hbm = pl.BlockSpec(memory_space=pl.ANY)
    staged = len(args) if vmem is None else vmem
    flags = vmem_out if isinstance(vmem_out, list) else [vmem_out] * len(out_shape)
    return pl.pallas_call(
        kernel,
        out_shape=list(out_shape),
        in_specs=[vm] * staged + [hbm] * (len(args) - staged),
        out_specs=[vm if flag else hbm for flag in flags],
        scratch_shapes=list(scratch),
        compiler_params=pltpu.CompilerParams(vmem_limit_bytes=56 * 2**20),
        interpret=INTERPRET,
    )(*args)


def place():
    t = lax.axis_index("tm").astype(jnp.int32)
    return t & 1, (t >> 1) & 1, lax.axis_index("panel").astype(jnp.int32)


def each_state(run):
    core, odd, _ = place()
    for i in (0, 1):
        for j in (0, 1):
            pl.when((core == i) & (odd == j))(lambda i=i, j=j: run(i, j))


def stream(pieces, buf, sems_in, sems_out):
    ins = [
        pltpu.make_async_copy(src.at[pl.ds(a, W)], buf.at[pl.ds(k * W, W)], sems_in.at[k])
        for k, (src, a, _, _) in enumerate(pieces)
    ]
    outs = [
        pltpu.make_async_copy(buf.at[pl.ds(k * W, W)], dst.at[pl.ds(b, W)], sems_out.at[k])
        for k, (_, _, dst, b) in enumerate(pieces)
    ]
    for c in ins:
        c.start()
    for c, o in zip(ins, outs):
        c.wait()
        o.start()
    for o in outs:
        o.wait()


def streaming(pieces):
    return (
        pltpu.VMEM((pieces * W, W), bf16),
        pltpu.SemaphoreType.DMA((pieces,)),
        pltpu.SemaphoreType.DMA((pieces,)),
    )


def struct(*shape):
    return jax.ShapeDtypeStruct(shape, bf16)


def at(index):
    return pl.multiple_of(index * W, W)


def blk(index):
    return pl.ds(at(index), W)


def start_kernel(move, drift, belief, hosts, values, msg, own_vec):
    msg[0:D, :] = move[...]
    eye = lax.broadcasted_iota(jnp.int32, (W, W), 0) == lax.broadcasted_iota(jnp.int32, (W, W), 1)

    def column(row):
        return jnp.sum(jnp.where(eye, row, 0.0), axis=1, keepdims=True)

    lane = lax.broadcasted_iota(jnp.int32, (W, W), 1).astype(f32)
    sums = [jnp.zeros((1, W), f32)] * N
    for c in range(hosts.shape[1] // W):
        part = slice(c * W, (c + 1) * W)
        spot = column(2.0 * hosts[:, part].astype(f32))
        value = column(values[:, part])
        for k in range(N):
            hit = jnp.where(spot == lane + k * W, value, 0.0)
            sums[k] = sums[k] + jnp.sum(hit, axis=0, keepdims=True)
    eta = belief[...].astype(f32) + jnp.concatenate(sums, axis=1)
    eta = eta.astype(bf16).astype(f32)
    b = drift[...].astype(f32)
    rows = [b[:, k * W : (k + 1) * W] for k in range(N)] + [
        eta[:, k * W : (k + 1) * W] for k in range(N)
    ]
    vec = jnp.concatenate(rows, axis=0).astype(bf16)
    msg[D : D + 2 * N, :] = vec
    own_vec[...] = vec


def ring_kernel(sources, *refs):
    *inputs, msg, buf, sems_in, sems_out = refs
    q = place()[2]

    def run(core, odd):
        x, a = (inputs[k] for k in sources(core, odd))
        pieces = [(x, at((q + d) % N), msg, 512 + d * W if d < 4 else 1536) for d in range(5)]
        pieces += [(a, k * W, msg, k * W if k < 4 else 512 + k * W) for k in range(N)]
        stream(pieces, buf, sems_in, sems_out)

    each_state(run)


def assemble_kernel(pick, xa, xb, m1, m2, m3, p1, p2, p3, x_out):
    core, odd, q = place()

    def put(l, d, block):
        r = (l + d) % N
        x_out[r * W : (r + 1) * W, l * W : (l + 1) * W] = block
        if d:
            x_out[l * W : (l + 1) * W, r * W : (r + 1) * W] = block.T

    def own(src):
        for d in range(N):
            put(0, d, src[blk((q + d) % N), :])

    pl.when(pick(core, odd) == 0)(lambda: own(xa))
    pl.when(pick(core, odd) == 1)(lambda: own(xb))
    for l, src in ((1, m1), (2, m2), (3, m3), (7, p1), (6, p2), (5, p3)):
        for d in range(5 if l < 4 else 4):
            if (l + d) % N == 0:
                continue
            row = 1536 if d == 4 else 512 + d * W
            put(l, d, src[row : row + W, :])
    x_out[4 * W :, 4 * W : 5 * W] = jnp.zeros((4 * W, W), bf16)
    x_out[4 * W : 5 * W, 5 * W :] = jnp.zeros((W, 3 * W), bf16)


def patch(dst, last):
    for d in range(4):
        block = last[d * W : (d + 1) * W, :]
        dst[(4 + d) * W : (5 + d) * W, 4 * W : 5 * W] = block
        if d:
            dst[4 * W : 5 * W, (4 + d) * W : (5 + d) * W] = block.T


def combine_kernel(own_is_cov, sides, count, last_own, last_far, vec_i, vec_j, *refs):
    side_refs = refs[:count]
    (x_here, x_far, msg, m1, m2, m3, p1, p2, p3, m4, p4, out1, out2,
     x_own, x_other, a_full, r, t, base, vecs, ai, add, sems) = refs[count:]
    core, _, q = place()
    terms = 2**NS - 1

    def whole(src, dst, first):
        return [
            pltpu.make_async_copy(
                src.at[pl.ds(k * 256, 256)], dst.at[pl.ds(k * 256, 256)], sems.at[first + k]
            )
            for k in range(4)
        ]

    own_copies = whole(x_here, x_own, 18)
    far_copies = whole(x_far, x_other, 22)
    copies = []
    for l, src in ((0, msg), (1, m1), (2, m2), (3, m3), (7, p1), (6, p2), (5, p3)):
        for half in range(2):
            copies.append((src, 1024 * half, 512 * half, l))
    copies += [(m4, 0, 0, 4), (p4, 256, 512, 4)]
    copies = [
        pltpu.make_async_copy(
            src.at[pl.ds(first, 512)], a_full.at[pl.ds(to, 512), pl.ds(l * W, W)], sems.at[2 + i]
        )
        for i, (src, first, to, l) in enumerate(copies)
    ]
    side_copies = [
        pltpu.make_async_copy(side_refs[0].at[pl.ds(0, D)], dst, sems.at[k])
        for k, dst in enumerate((ai, add))
    ]

    def start_sides(i, j):
        for k, dst in zip(sides(i, j), (ai, add)):
            sem = sems.at[0] if dst is ai else sems.at[1]
            pltpu.make_async_copy(side_refs[k].at[pl.ds(0, D)], dst, sem).start()

    each_state(start_sides)

    def start(group):
        for c in group:
            c.start()

    def wait(group):
        for c in group:
            c.wait()

    @pl.when(core == 1)
    def _():
        start(copies)
        start(own_copies if own_is_cov else far_copies)
        start(far_copies if own_is_cov else own_copies)

    @pl.when(core == 0)
    def _():
        start(own_copies if own_is_cov else far_copies)
        start(far_copies if own_is_cov else own_copies)
        start(copies)

    vi = vec_i[...].astype(f32)
    vj = vec_j[...].astype(f32)

    def ready_own():
        wait(own_copies)
        patch(x_own, last_own)

    def ready_far():
        wait(far_copies)
        patch(x_other, last_far)

    first_ready, then_ready = (ready_own, ready_far) if own_is_cov else (ready_far, ready_own)
    first_x, then_x = (x_own, x_other) if own_is_cov else (x_other, x_own)

    def rotated_move(dst, row):
        for l in range(N):
            dst[row : row + W, l * W : (l + 1) * W] = ai[blk((q + l) % N), :].T

    def rotated_vector(rows, first):
        vecs[...] = rows
        return jnp.concatenate([vecs[pl.ds(first + (q + l) % N, 1), :] for l in range(N)], axis=1)

    def as_rows(vector):
        return jnp.broadcast_to(vector, (16, D)).astype(bf16)

    @pl.when(core == 1)
    def _():
        cov, info = first_x, then_x
        eta = rotated_vector(vj, N)
        w = rotated_vector(vi, 0)
        side_copies[0].wait()
        rotated_move(base, W)
        r[W : W + 16, :] = as_rows(eta)
        wait(copies)
        r[0:W, :] = a_full[blk(q), :]
        first_ready()
        out = dot(r[0 : W + 16, :], cov[...])
        base[0:W, :] = out[0:W].astype(bf16)
        w = w + out[W : W + 1]
        r[0 : 2 * W, :] = base[...]
        r[2 * W : 2 * W + 16, :] = as_rows(w)
        then_ready()
        for _ in range(terms):
            t[...] = dot(r[...], info[...]).astype(bf16)
            out = dot(t[...], cov[...])
            r[0 : 2 * W, :] = (base[...].astype(f32) - out[0 : 2 * W]).astype(bf16)
            r[2 * W : 2 * W + 16, :] = as_rows(w - out[2 * W : 2 * W + 1])
        res = lax.dot_general(
            r[...], a_full[...], (((1,), (1,)), ((), ())), preferred_element_type=f32
        )
        side_copies[1].wait()
        for l in range(N):
            rows = slice(l * W, (l + 1) * W)
            out1[rows, :] = (res[0:W, rows].T + add[rows, :].astype(f32)).astype(bf16)
            out2[rows, :] = res[W : 2 * W, rows].astype(bf16).T
        rows = [res[2 * W : 2 * W + 1, l * W : (l + 1) * W] + vj[l : l + 1, :] for l in range(N)]
        rows = rows + [jnp.zeros((1, W), f32)] * N
        out2[D : D + 2 * N, :] = jnp.concatenate(rows, axis=0).astype(bf16)

    @pl.when(core == 0)
    def _():
        info, cov = first_x, then_x
        top = slice(0, W)
        low = slice(W, W + 16)
        both = slice(0, W + 16)
        eta = rotated_vector(vj, N)
        side_copies[0].wait()
        rotated_move(base, 0)
        r[top, :] = base[top, :]
        r[low, :] = as_rows(rotated_vector(vi, 0))
        first_ready()
        out = dot(r[both, :], info[...])
        start_vec = eta - out[W : W + 1]
        t[top, :] = out[top].astype(bf16)
        t[low, :] = as_rows(start_vec)
        then_ready()
        for _ in range(terms):
            out = dot(t[both, :], cov[...])
            r[top, :] = (base[top, :].astype(f32) - out[top]).astype(bf16)
            r[low, :] = out[low].astype(bf16)
            out = dot(r[both, :], info[...])
            t[top, :] = out[top].astype(bf16)
            t[low, :] = as_rows(start_vec - out[W : W + 1])
        wait(copies)
        side_copies[1].wait()
        for l in range(N):
            x_other[blk((q + l) % N), 0 : W + 16] = t[both, l * W : (l + 1) * W].T
        for l in range(N):
            r[both, l * W : (l + 1) * W] = x_other[l * W : (l + 1) * W, 0 : W + 16].T
        res = dot(r[both, :], a_full[...])
        for l in range(N):
            rows = blk((q + l) % N)
            out1[rows, :] = (res[top, l * W : (l + 1) * W].T + add[rows, :].astype(f32)).astype(bf16)
        vecs[...] = vi
        for l in range(N):
            spot = pl.ds(N + (q + l) % N, 1)
            vecs[spot, :] = vecs[spot, :] + res[W : W + 1, l * W : (l + 1) * W]
        rows = lax.broadcasted_iota(jnp.int32, (2 * N, W), 0)
        out2[0:D, :] = jnp.zeros((D, W), bf16)
        out2[D : D + 2 * N, :] = jnp.where(rows < N, 0.0, vecs[...]).astype(bf16)


def pick_kernel(out1, out2, got2, msg, buf, sems_in, sems_out):
    def run(core, odd):
        src = out2 if (core, odd) == (1, 1) else got2 if (core, odd) == (0, 0) else out1
        stream([(src, k * W, msg, k * W) for k in range(N)], buf, sems_in, sems_out)

    each_state(run)


def finish_kernel(
    own1, own2, got1, got2, drift, belief, move, spread, weight, buf, sems_in, sems_out, vec, sems
):
    core = place()[0]

    def put(first, moved, last, b, e):
        tails = [
            pltpu.make_async_copy(
                src.at[pl.ds(D, 2 * N)], vec.at[pl.ds(k * 2 * N, 2 * N)], sems.at[k]
            )
            for k, src in enumerate((b, e))
        ]
        for c in tails:
            c.start()
        pieces = []
        for src, dst in ((first, spread), (moved, move), (last, weight)):
            pieces += [(src, k * W, dst, k * W) for k in range(N)]
        stream(pieces, buf, sems_in, sems_out)
        for c in tails:
            c.wait()
        rows = vec[...].astype(f32)
        for l in range(N):
            drift[:, l * W : (l + 1) * W] = rows[l : l + 1, :].astype(bf16)
            belief[:, l * W : (l + 1) * W] = rows[3 * N + l : 3 * N + l + 1, :].astype(bf16)

    pl.when(core == 1)(lambda: put(own1, own2, got1, own2, got2))
    pl.when(core == 0)(lambda: put(got1, got2, own1, got2, own2))


def swap(x, axis_bit):
    return lax.ppermute(x, "tm", [(i, i ^ (1 << axis_bit)) for i in range(lax.axis_size("tm"))])


def shift(x, by):
    return lax.ppermute(x, "panel", [(i, (i + by) % N) for i in range(N)])


def combined(own_is_cov, x_pair, x_pick, ring_refs, sources, gate, side, sides):
    (msg,) = call(
        functools.partial(ring_kernel, sources),
        [struct(RING, W)],
        streaming(RING // W),
        *ring_refs,
        vmem=0,
        vmem_out=False,
    )
    msg, gate = lax.optimization_barrier((msg, gate))
    p1 = shift(msg, 1)
    m1 = shift(msg, -1)
    p1, m1, (vec_i, vec_j, side_refs) = lax.optimization_barrier((p1, m1, side(gate)))
    p2, m2 = shift(p1, 1), shift(m1, -1)
    p3, m3 = shift(p2, 1), shift(m2, -1)
    p4 = shift(p3[HALF : 2 * HALF], 1)
    m4 = shift(m3[0:HALF], -1)
    (x_here,) = call(
        functools.partial(assemble_kernel, x_pick),
        [struct(D, D)],
        (),
        *x_pair,
        m1,
        m2,
        m3,
        p1,
        p2,
        p3,
    )
    x_far = swap(x_here, 0)
    last_own = jnp.concatenate([m4[512:768], p4[0:256]], axis=0)
    last_far = swap(last_own, 0)
    return call(
        functools.partial(combine_kernel, own_is_cov, sides, len(side_refs)),
        [struct(D, W), struct(D + 2 * N, W)],
        (
            pltpu.VMEM((D, D), bf16),
            pltpu.VMEM((D, D), bf16),
            pltpu.VMEM((D, D), bf16),
            pltpu.VMEM((2 * W + 16, D), bf16),
            pltpu.VMEM((2 * W + 16, D), bf16),
            pltpu.VMEM((2 * W, D), bf16),
            pltpu.VMEM((2 * N, W), f32),
            pltpu.VMEM((D, W), bf16),
            pltpu.VMEM((D, W), bf16),
            pltpu.SemaphoreType.DMA((26,)),
        ),
        last_own,
        last_far,
        vec_i,
        vec_j,
        *side_refs,
        x_here,
        x_far,
        msg,
        m1,
        m2,
        m3,
        p1,
        p2,
        p3,
        m4,
        p4,
        vmem=4,
    )


def local(transition, drift, spread, belief, precision, probe_hosts, probe_values):
    core, odd, _ = place()
    near = odd == 0
    move, cov, info = transition[0], spread[0], precision[0]

    def side0(drift):
        first, own_vec = call(
            start_kernel,
            [struct(D + 2 * N, W), struct(2 * N, W)],
            (),
            move,
            drift,
            belief,
            probe_hosts,
            probe_values,
        )
        got = swap(first, 0)
        got_vec = got[D:]
        vec_i = jnp.where(core == 0, own_vec, got_vec)
        vec_j = jnp.where(core == 0, got_vec, own_vec)
        return vec_i, vec_j, (move, got, cov, info)

    out1, out2 = combined(
        False,
        (cov, info),
        lambda core, odd: core,
        (cov, info, move),
        lambda core, odd: (core, 2),
        drift,
        side0,
        lambda core, odd: (core, 3 - core),
    )
    got2 = swap(out2, 0)
    own_vec = out2[D:] + got2[D:]
    (panel,) = call(
        pick_kernel, [struct(D, W)], streaming(N), out1, out2, got2, vmem=0, vmem_out=False
    )
    far = swap(panel, 1)

    def side1(own_vec):
        rest = jnp.where((core == 1) & near, out2[:D], out1)
        bundle = swap(jnp.concatenate([rest, own_vec], axis=0), 1)
        far_vec = bundle[D:]
        vec_i = jnp.where(near, own_vec, far_vec)
        vec_j = jnp.where(near, far_vec, own_vec)
        return vec_i, vec_j, (out1, out2, got2, far, bundle)

    sources = {(1, 0): (0, 3), (1, 1): (3, 1), (0, 0): (3, 2), (0, 1): (0, 3)}
    sides = {(1, 0): (1, 4), (1, 1): (4, 0), (0, 0): (2, 0), (0, 1): (3, 4)}
    out1, out2 = combined(
        True,
        (out1, far),
        lambda core, odd: 1 ^ core ^ odd,
        (out1, out2, got2, far),
        lambda core, odd: sources[core, odd],
        own_vec,
        side1,
        lambda core, odd: sides[core, odd],
    )
    got1 = swap(out1, 0)
    got2 = swap(out2, 0)
    panel = struct(D, W)
    row = struct(1, D)
    drift, belief, move, cov, info = call(
        finish_kernel,
        [row, row, panel, panel, panel],
        streaming(3 * N) + (pltpu.VMEM((4 * N, W), bf16), pltpu.SemaphoreType.DMA((2,))),
        out1,
        out2,
        got1,
        got2,
        vmem=0,
        vmem_out=[True, True, False, False, False],
    )
    return move[None], drift, cov[None], belief, info[None]


def solution(mesh):
    in_specs = (
        P("tm", None, "panel"),
        P("tm", None),
        P("tm", None, "panel"),
        P("tm", None),
        P("tm", None, "panel"),
        P("tm", None),
        P("tm", None),
    )
    out_specs = (
        P("tm", None, "panel"),
        P("tm", None),
        P("tm", None, "panel"),
        P("tm", None),
        P("tm", None, "panel"),
    )
    return jax.shard_map(local, mesh=mesh, in_specs=in_specs, out_specs=out_specs, check_vma=False)
```

time: 214 us -> 209 us (0.977)
  waiting for transfers between devices: 70.5 us -> 77.1 us
  starting transfers between devices: 82.9 us -> 76.7 us
  other arithmetic: 8.42 us -> 3.71 us
    ppermute x11 -> x10, starting transfers between devices: 40.6 us -> 34.4 us  [swap(): lax.ppermute(x, 'tm', [(i, i ^ 1 << axis_bit) for i in range(lax.axis_siz...]
    ppermute x11 -> x10, waiting for transfers between devices: 7.82 us -> 12.6 us  [swap(): lax.ppermute(x, 'tm', [(i, i ^ 1 << axis_bit) for i in range(lax.axis_siz...]
    another operation x5 -> x0, other arithmetic: 3.07 us -> none  [the longest x2 1.26 us: combined(): jnp.stack([role, q, ai_pick, add_pick])]
    unnamed x62 -> x56, local copies, waits for them, and re-layouts: 8.53 us -> 8.39 us
  transfers between devices with their start and end apart: 27 -> 26, of which waited for: 20 -> 20; matrix products, arithmetic and copies ran while one was open for 7% -> 4% of each run, Pallas kernels for 0% -> 0%
where the time goes in v4:
time: 209 us; the launch traced here: 207 us
  waiting for transfers between devices  77.1 us (37%)
  starting transfers between devices  76.7 us (37%)
  Pallas kernels  36.3 us (17%)
  local copies, waits for them, and re-layouts  12.2 us (6%)
  other arithmetic  3.71 us (2%)
    ppermute x16, waiting for transfers between devices, shift(): return lax.ppermute(x, 'panel', [(i, (i + by) % N) for i in range(N)])  64.5 us
    ppermute x16, starting transfers between devices, shift(): return lax.ppermute(x, 'panel', [(i, (i + by) % N) for i in range(N)])  42.3 us
    pallas_call x9, Pallas kernels, call(): pl.pallas_call(kernel, out_shape=list(out_shape), in_specs=[vm] * staged...  36.3 us
    ppermute x10, starting transfers between devices, swap(): lax.ppermute(x, 'tm', [(i, i ^ 1 << axis_bit) for i in range(lax.axis_siz...  34.4 us
    ppermute x10, waiting for transfers between devices, swap(): lax.ppermute(x, 'tm', [(i, i ^ 1 << axis_bit) for i in range(lax.axis_siz...  12.6 us
    unnamed x56, local copies, waits for them, and re-layouts  8.39 us
  transfers between devices with their start and end apart: 26, of which 20 were waited for; matrix products, arithmetic and copies ran while one was open for 4% of the time, Pallas kernels for 0%

profile of v4, /device:TPU:1, one launch (start us, length us, event | category | flops | bytes accessed | tf_op | source)
XLA Modules:
  0.0 207.3 jit_solution(10913203395383847061)
XLA Ops:
  0.6 1.8 shard_map.110.refs_6_
  2.5 1.9 shard_map.111
  4.4 8.7 %collective-permute-start.2 = (bf16[1040,128]{1,0:T(8,128)(2,1)}, bf16[1040,128]{1,0:T(8,128)(2,1)S(1)}, u32[]{:S(2)}, u32[]{:S(2)}) collective-permute-start(bf16[1040,128]{1,0:T(8,128)(2,1)} %get-tuple-element.40), channel_id=1, source_target_pairs={{0,8},{8,0},{16,24},{24,16},{32,40},{40,32},{48,56},{56,48},{64,72... | collective-permute-start | bytes 798728 | tf_op jit(solution)/shard_map/ppermute | solution.py:366
  13.1 1.9 collective-permute-start.1
  15.0 3.4 %collective-permute-start = (bf16[1664,128]{1,0:T(8,128)(2,1)}, bf16[1664,128]{1,0:T(8,128)(2,1)S(1)}, u32[]{:S(2)}, u32[]{:S(2)}) collective-permute-start(bf16[1664,128]{1,0:T(8,128)(2,1)} %shard_map.110.refs_6_), channel_id=1, source_target_pairs={{0,1},{1,2},{2,3},{3,4},{4,5},{5,6},{6,7},{7,0},{8,9},{9,10},{10,1... | collective-permute-start | bytes 1277960 | tf_op jit(solution)/shard_map/ppermute | solution.py:370
  18.4 1.3 broadcast_select_fusion.2
  19.8 6.8 %collective-permute-done.1.m1.refs_7_ = bf16[1664,128]{1,0:T(8,128)(2,1)S(1)} collective-permute-done((bf16[1664,128]{1,0:T(8,128)(2,1)}, bf16[1664,128]{1,0:T(8,128)(2,1)S(1)}, u32[]{:S(2)}, u32[]{:S(2)}) %collective-permute-start.1) | collective-permute-done | bytes 426016 | tf_op jit(solution)/shard_map/ppermute | solution.py:370
  26.6 3.1 %collective-permute-done.p1.refs_10_ = bf16[1664,128]{1,0:T(8,128)(2,1)S(1)} collective-permute-done((bf16[1664,128]{1,0:T(8,128)(2,1)}, bf16[1664,128]{1,0:T(8,128)(2,1)S(1)}, u32[]{:S(2)}, u32[]{:S(2)}) %collective-permute-start) | collective-permute-done | bytes 426016 | tf_op jit(solution)/shard_map/ppermute | solution.py:370
  29.7 1.9 collective-permute-start.3
  31.6 3.4 %collective-permute-start.6 = (bf16[1664,128]{1,0:T(8,128)(2,1)S(1)}, bf16[1664,128]{1,0:T(8,128)(2,1)S(1)}, u32[]{:S(2)}, u32[]{:S(2)}) collective-permute-start(bf16[1664,128]{1,0:T(8,128)(2,1)S(1)} %collective-permute-done.p1.refs_10_), channel_id=1, source_target_pairs={{0,1},{1,2},{2,3},{3,4},{4,5},{5,6},{6,7},{7,0},{8,9},{9,10},{10,1... | collective-permute-start | bytes 1277960 | tf_op jit(solution)/shard_map/ppermute | solution.py:370
  35.0 7.1 %collective-permute-done.3.m2.refs_8_ = bf16[1664,128]{1,0:T(8,128)(2,1)S(1)} collective-permute-done((bf16[1664,128]{1,0:T(8,128)(2,1)S(1)}, bf16[1664,128]{1,0:T(8,128)(2,1)S(1)}, u32[]{:S(2)}, u32[]{:S(2)}) %collective-permute-start.3) | collective-permute-done | bytes 426016 | tf_op jit(solution)/shard_map/ppermute | solution.py:370
  42.1 3.4 %collective-permute-start.4 = (bf16[1664,128]{1,0:T(8,128)(2,1)S(1)}, bf16[1664,128]{1,0:T(8,128)(2,1)S(1)}, u32[]{:S(2)}, u32[]{:S(2)}) collective-permute-start(bf16[1664,128]{1,0:T(8,128)(2,1)S(1)} %collective-permute-done.3.m2.refs_8_), channel_id=1, source_target_pairs={{0,7},{1,0},{2,1},{3,2},{4,3},{5,4},{6,5},{7,6},{8,15},{9,8},{10,9... | collective-permute-start | bytes 1277960 | tf_op jit(solution)/shard_map/ppermute | solution.py:370
  45.5 1.9 collective-permute-start.7
  47.5 6.2 %collective-permute-done.4.m3.refs_9_ = bf16[1664,128]{1,0:T(8,128)(2,1)S(1)} collective-permute-done((bf16[1664,128]{1,0:T(8,128)(2,1)S(1)}, bf16[1664,128]{1,0:T(8,128)(2,1)S(1)}, u32[]{:S(2)}, u32[]{:S(2)}) %collective-permute-start.4) | collective-permute-done | bytes 426016 | tf_op jit(solution)/shard_map/ppermute | solution.py:370
  53.6 4.6 %collective-permute-done.7.p3.refs_12_ = bf16[1664,128]{1,0:T(8,128)(2,1)S(1)} collective-permute-done((bf16[1664,128]{1,0:T(8,128)(2,1)S(1)}, bf16[1664,128]{1,0:T(8,128)(2,1)S(1)}, u32[]{:S(2)}, u32[]{:S(2)}) %collective-permute-start.7) | collective-permute-done | bytes 426016 | tf_op jit(solution)/shard_map/ppermute | solution.py:370
  58.3 0.8 copy-done.3
  59.1 3.7 %shard_map.112.refs_4_ = bf16[1024,1024]{1,0:T(8,128)(2,1)} custom-call(bf16[1024,128]{1,0:T(8,128)(2,1)} %bitcast.7, bf16[1024,128]{1,0:T(8,128)(2,1)} %bitcast.10, bf16[1664,128]{1,0:T(8,128)(2,1)} %copy-done.8, bf16[1664,128]{1,0:T(8,128)(2,1)} %copy-done.14, bf16[1664,128]{1,0:T(8,128)(2,1)} %copy-done.1, bf16[1664,128]{1,0:T(8,128)(2,1)} %copy-done.9, ...), custom_call_target="tpu_custom_call" | custom-call | tf_op jit(solution)/shard_map/pallas_call | solution.py:32
  62.8 4.5 %collective-permute-start.10 = (bf16[1024,1024]{1,0:T(8,128)(2,1)}, bf16[1024,1024]{1,0:T(8,128)(2,1)S(1)}, u32[]{:S(2)}, u32[]{:S(2)}) collective-permute-start(bf16[1024,1024]{1,0:T(8,128)(2,1)} %shard_map.112.refs_4_), channel_id=1, source_target_pairs={{0,8},{8,0},{16,24},{24,16},{32,40},{40,32},{48,56},{56,48},{64,72... | collective-permute-start | bytes 6291464 | tf_op jit(solution)/shard_map/ppermute | solution.py:366
  67.3 0.9 slice.53
  68.2 1.9 collective-permute-start.5
  70.1 0.9 slice.55
  71.1 3.4 %collective-permute-start.8 = (bf16[768,128]{1,0:T(8,128)(2,1)S(1)}, bf16[768,128]{1,0:T(8,128)(2,1)S(1)}, u32[]{:S(2)}, u32[]{:S(2)}) collective-permute-start(bf16[768,128]{1,0:T(8,128)(2,1)S(1)} %slice.55), channel_id=1, source_target_pairs={{0,1},{1,2},{2,3},{3,4},{4,5},{5,6},{6,7},{7,0},{8,9},{9,10},{10,1... | collective-permute-start | bytes 589832 | tf_op jit(solution)/shard_map/ppermute | solution.py:370
  74.4 2.1 %collective-permute-done.5.refs_13_ = bf16[768,128]{1,0:T(8,128)(2,1)S(1)} collective-permute-done((bf16[768,128]{1,0:T(8,128)(2,1)S(1)}, bf16[768,128]{1,0:T(8,128)(2,1)S(1)}, u32[]{:S(2)}, u32[]{:S(2)}) %collective-permute-start.5) | collective-permute-done | bytes 196640 | tf_op jit(solution)/shard_map/ppermute | solution.py:370
  76.5 4.1 %collective-permute-done.8.refs_14_ = bf16[768,128]{1,0:T(8,128)(2,1)S(1)} collective-permute-done((bf16[768,128]{1,0:T(8,128)(2,1)S(1)}, bf16[768,128]{1,0:T(8,128)(2,1)S(1)}, u32[]{:S(2)}, u32[]{:S(2)}) %collective-permute-start.8) | collective-permute-done | bytes 196640 | tf_op jit(solution)/shard_map/ppermute | solution.py:370
  80.7 2.8 %collective-permute-start.9 = (bf16[512,128]{1,0:T(8,128)(2,1)S(1)}, bf16[512,128]{1,0:T(8,128)(2,1)S(1)}, u32[]{:S(2)}, u32[]{:S(2)}) collective-permute-start(bf16[512,128]{1,0:T(8,128)(2,1)S(1)} %pad_maximum_fusion.1.last_own), channel_id=1, source_target_pairs={{0,8},{8,0},{16,24},{24,16},{32,40},{40,32},{48,56},{56,48},{64,72... | collective-permute-start | bytes 393224 | tf_op jit(solution)/shard_map/ppermute | solution.py:366
  83.5 1.0 collective-permute-done.9.last_far
  85.1 1.4 copy-done.6
  86.4 9.5 %shard_map.113 = (bf16[1024,128]{1,0:T(8,128)(2,1)}, bf16[1040,128]{1,0:T(8,128)(2,1)}) custom-call(bf16[512,128]{1,0:T(8,128)(2,1)} %copy-done.17, bf16[512,128]{1,0:T(8,128)(2,1)} %copy-done.27, bf16[16,128]{1,0:T(8,128)(2,1)} %get-tuple-element.43.vec_i, bf16[16,128]{1,0:T(8,128)(2,1)} %get-tuple-element.44.vec_j, bf16[1024,128]{1,0:T(8,128)(2,1)} %bitcast.14, ...), custom_call_target="tpu_custom_call" | custom-call | tf_op jit(solution)/shard_map/pallas_call | solution.py:32
  95.9 1.9 collective-permute-start.11
  97.8 1.7 collective-permute-done.11.got2.refs_2_
  100.3 1.6 shard_map.114
  101.9 1.9 collective-permute-start.12
  103.8 1.0 slice_select_fusion
  105.5 6.2 %collective-permute-done.12.refs_3_.xb = bf16[1024,128]{1,0:T(8,128)(2,1)S(1)} collective-permute-done((bf16[1024,128]{1,0:T(8,128)(2,1)}, bf16[1024,128]{1,0:T(8,128)(2,1)S(1)}, u32[]{:S(2)}, u32[]{:S(2)}) %collective-permute-start.12) | collective-permute-done | bytes 262176 | tf_op jit(solution)/shard_map/ppermute | solution.py:366
  112.4 1.8 shard_map.115.refs_7_
  114.2 2.2 %collective-permute-start.15 = (bf16[1040,128]{1,0:T(8,128)(2,1)S(1)}, bf16[1040,128]{1,0:T(8,128)(2,1)S(1)}, u32[]{:S(2)}, u32[]{:S(2)}) collective-permute-start(bf16[1040,128]{1,0:T(8,128)(2,1)S(1)} %pad_maximum_fusion), channel_id=1, source_target_pairs={{0,16},{8,24},{16,0},{24,8},{32,48},{40,56},{48,32},{56,40},{64,80... | collective-permute-start | bytes 798728 | tf_op jit(solution)/shard_map/ppermute | solution.py:366
  116.5 1.9 collective-permute-start.14
  118.4 3.4 %collective-permute-start.13 = (bf16[1664,128]{1,0:T(8,128)(2,1)}, bf16[1664,128]{1,0:T(8,128)(2,1)S(1)}, u32[]{:S(2)}, u32[]{:S(2)}) collective-permute-start(bf16[1664,128]{1,0:T(8,128)(2,1)} %shard_map.115.refs_7_), channel_id=1, source_target_pairs={{0,1},{1,2},{2,3},{3,4},{4,5},{5,6},{6,7},{7,0},{8,9},{9,10},{10,1... | collective-permute-start | bytes 1277960 | tf_op jit(solution)/shard_map/ppermute | solution.py:370
  121.8 1.3 collective-permute-done.15.refs_4_
  123.8 5.2 %collective-permute-done.14.m1.refs_8_ = bf16[1664,128]{1,0:T(8,128)(2,1)S(1)} collective-permute-done((bf16[1664,128]{1,0:T(8,128)(2,1)}, bf16[1664,128]{1,0:T(8,128)(2,1)S(1)}, u32[]{:S(2)}, u32[]{:S(2)}) %collective-permute-start.14) | collective-permute-done | bytes 426016 | tf_op jit(solution)/shard_map/ppermute | solution.py:370
  128.9 3.1 %collective-permute-done.13.p1.refs_11_ = bf16[1664,128]{1,0:T(8,128)(2,1)S(1)} collective-permute-done((bf16[1664,128]{1,0:T(8,128)(2,1)}, bf16[1664,128]{1,0:T(8,128)(2,1)S(1)}, u32[]{:S(2)}, u32[]{:S(2)}) %collective-permute-start.13) | collective-permute-done | bytes 426016 | tf_op jit(solution)/shard_map/ppermute | solution.py:370
  132.1 1.9 collective-permute-start.16
  134.0 3.4 %collective-permute-start.19 = (bf16[1664,128]{1,0:T(8,128)(2,1)S(1)}, bf16[1664,128]{1,0:T(8,128)(2,1)S(1)}, u32[]{:S(2)}, u32[]{:S(2)}) collective-permute-start(bf16[1664,128]{1,0:T(8,128)(2,1)S(1)} %collective-permute-done.13.p1.refs_11_), channel_id=1, source_target_pairs={{0,1},{1,2},{2,3},{3,4},{4,5},{5,6},{6,7},{7,0},{8,9},{9,10},{10,1... | collective-permute-start | bytes 1277960 | tf_op jit(solution)/shard_map/ppermute | solution.py:370
  137.4 6.1 %collective-permute-done.16.m2.refs_9_ = bf16[1664,128]{1,0:T(8,128)(2,1)S(1)} collective-permute-done((bf16[1664,128]{1,0:T(8,128)(2,1)S(1)}, bf16[1664,128]{1,0:T(8,128)(2,1)S(1)}, u32[]{:S(2)}, u32[]{:S(2)}) %collective-permute-start.16) | collective-permute-done | bytes 426016 | tf_op jit(solution)/shard_map/ppermute | solution.py:370
  143.5 3.4 %collective-permute-start.17 = (bf16[1664,128]{1,0:T(8,128)(2,1)S(1)}, bf16[1664,128]{1,0:T(8,128)(2,1)S(1)}, u32[]{:S(2)}, u32[]{:S(2)}) collective-permute-start(bf16[1664,128]{1,0:T(8,128)(2,1)S(1)} %collective-permute-done.16.m2.refs_9_), channel_id=1, source_target_pairs={{0,7},{1,0},{2,1},{3,2},{4,3},{5,4},{6,5},{7,6},{8,15},{9,8},{10,9... | collective-permute-start | bytes 1277960 | tf_op jit(solution)/shard_map/ppermute | solution.py:370
  146.9 1.9 collective-permute-start.20
  148.9 5.2 %collective-permute-done.17.m3.refs_10_ = bf16[1664,128]{1,0:T(8,128)(2,1)S(1)} collective-permute-done((bf16[1664,128]{1,0:T(8,128)(2,1)S(1)}, bf16[1664,128]{1,0:T(8,128)(2,1)S(1)}, u32[]{:S(2)}, u32[]{:S(2)}) %collective-permute-start.17) | collective-permute-done | bytes 426016 | tf_op jit(solution)/shard_map/ppermute | solution.py:370
  154.1 4.6 %collective-permute-done.20.p3.refs_13_ = bf16[1664,128]{1,0:T(8,128)(2,1)S(1)} collective-permute-done((bf16[1664,128]{1,0:T(8,128)(2,1)S(1)}, bf16[1664,128]{1,0:T(8,128)(2,1)S(1)}, u32[]{:S(2)}, u32[]{:S(2)}) %collective-permute-start.20) | collective-permute-done | bytes 426016 | tf_op jit(solution)/shard_map/ppermute | solution.py:370
  159.5 3.9 %shard_map.116.refs_5_ = bf16[1024,1024]{1,0:T(8,128)(2,1)} custom-call(bf16[1024,128]{1,0:T(8,128)(2,1)} %get-tuple-element.57.out1.refs_0_.xa, bf16[1024,128]{1,0:T(8,128)(2,1)} %copy-done.5, bf16[1664,128]{1,0:T(8,128)(2,1)} %copy-done.10, bf16[1664,128]{1,0:T(8,128)(2,1)} %copy-done.12, bf16[1664,128]{1,0:T(8,128)(2,1)} %copy-done, ...), custom_call_target="tpu_custom_call" | custom-call | tf_op jit(solution)/shard_map/pallas_call | solution.py:32
  163.4 5.3 %collective-permute-start.23 = (bf16[1024,1024]{1,0:T(8,128)(2,1)}, bf16[1024,1024]{1,0:T(8,128)(2,1)S(1)}, u32[]{:S(2)}, u32[]{:S(2)}) collective-permute-start(bf16[1024,1024]{1,0:T(8,128)(2,1)} %shard_map.116.refs_5_), channel_id=1, source_target_pairs={{0,8},{8,0},{16,24},{24,16},{32,40},{40,32},{48,56},{56,48},{64,72... | collective-permute-start | bytes 6291464 | tf_op jit(solution)/shard_map/ppermute | solution.py:366
  168.6 0.9 slice.59
  169.6 1.9 collective-permute-start.18
  171.5 0.9 slice.61
  172.5 3.4 %collective-permute-start.21 = (bf16[768,128]{1,0:T(8,128)(2,1)S(1)}, bf16[768,128]{1,0:T(8,128)(2,1)S(1)}, u32[]{:S(2)}, u32[]{:S(2)}) collective-permute-start(bf16[768,128]{1,0:T(8,128)(2,1)S(1)} %slice.61), channel_id=1, source_target_pairs={{0,1},{1,2},{2,3},{3,4},{4,5},{5,6},{6,7},{7,0},{8,9},{9,10},{10,1... | collective-permute-start | bytes 589832 | tf_op jit(solution)/shard_map/ppermute | solution.py:370
  175.8 2.1 %collective-permute-done.18.refs_14_ = bf16[768,128]{1,0:T(8,128)(2,1)S(1)} collective-permute-done((bf16[768,128]{1,0:T(8,128)(2,1)S(1)}, bf16[768,128]{1,0:T(8,128)(2,1)S(1)}, u32[]{:S(2)}, u32[]{:S(2)}) %collective-permute-start.18) | collective-permute-done | bytes 196640 | tf_op jit(solution)/shard_map/ppermute | solution.py:370
  177.9 4.1 %collective-permute-done.21.refs_15_ = bf16[768,128]{1,0:T(8,128)(2,1)S(1)} collective-permute-done((bf16[768,128]{1,0:T(8,128)(2,1)S(1)}, bf16[768,128]{1,0:T(8,128)(2,1)S(1)}, u32[]{:S(2)}, u32[]{:S(2)}) %collective-permute-start.21) | collective-permute-done | bytes 196640 | tf_op jit(solution)/shard_map/ppermute | solution.py:370
  182.1 2.8 %collective-permute-start.22 = (bf16[512,128]{1,0:T(8,128)(2,1)S(1)}, bf16[512,128]{1,0:T(8,128)(2,1)S(1)}, u32[]{:S(2)}, u32[]{:S(2)}) collective-permute-start(bf16[512,128]{1,0:T(8,128)(2,1)S(1)} %pad_maximum_fusion.2.last_own), channel_id=1, source_target_pairs={{0,8},{8,0},{16,24},{24,16},{32,40},{40,32},{48,56},{56,48},{64,72... | collective-permute-start | bytes 393224 | tf_op jit(solution)/shard_map/ppermute | solution.py:366
  184.8 1.0 collective-permute-done.22.last_far
  186.5 1.4 copy-done.7
  187.8 9.4 %shard_map.117 = (bf16[1024,128]{1,0:T(8,128)(2,1)}, bf16[1040,128]{1,0:T(8,128)(2,1)}) custom-call(bf16[512,128]{1,0:T(8,128)(2,1)} %copy-done.16, bf16[512,128]{1,0:T(8,128)(2,1)} %copy-done.26, bf16[16,128]{1,0:T(8,128)(2,1)} %get-tuple-element.55.vec_i, bf16[16,128]{1,0:T(8,128)(2,1)} %get-tuple-element.56.vec_j, ...), custom_call_target="tpu_custom_call" | custom-call | tf_op jit(solution)/shard_map/pallas_call | solution.py:32
  197.3 1.9 collective-permute-start.25
  199.2 2.4 %collective-permute-start.24 = (bf16[1024,128]{1,0:T(8,128)(2,1)}, bf16[1024,128]{1,0:T(8,128)(2,1)S(1)}, u32[]{:S(2)}, u32[]{:S(2)}) collective-permute-start(bf16[1024,128]{1,0:T(8,128)(2,1)} %get-tuple-element.62.own1), channel_id=1, source_target_pairs={{0,8},{8,0},{16,24},{24,16},{32,40},{40,32},{48,56},{56,48},{64,72... | collective-permute-start | bytes 786440 | tf_op jit(solution)/shard_map/ppermute | solution.py:366
  201.6 1.4 collective-permute-done.24.got1
  204.4 2.8 %shard_map.118 = (bf16[1,1024]{1,0:T(2,128)(2,1)}, bf16[1,1024]{1,0:T(2,128)(2,1)}, bf16[1024,128]{1,0:T(8,128)(2,1)}, bf16[1024,128]{1,0:T(8,128)(2,1)}, bf16[1024,128]{1,0:T(8,128)(2,1)}) custom-call(bf16[1024,128]{1,0:T(8,128)(2,1)} %get-tuple-element.62.own1, bf16[1040,128]{1,0:T(8,128)(2,1)} %get-tuple-element.63.own2, bf16[1024,128]{1,0:T(8,128)(2,1)} %copy-done.25, ...), custom_call_target="tpu_custom_call" | custom-call | tf_op jit(solution)/shard_map/pallas_call | solution.py:32
  (68 shorter events, 6.3 us)
Async XLA Ops:
  4.4 14.0 %collective-permute-start.2 = (bf16[1040,128]{1,0:T(8,128)(2,1)}, bf16[1040,128]{1,0:T(8,128)(2,1)S(1)}, u32[]{:S(2)}, u32[]{:S(2)}) collective-permute-start(bf16[1040,128]{1,0:T(8,128)(2,1)} %get-tuple-element.40), channel_id=1, source_target_pairs={{0,8},{8,0},{16,24},{24,16},{32,40},{40,32},{48,56},{56,48},{64,72... | collective-permute-start | bytes 798728 | tf_op jit(solution)/shard_map/ppermute | solution.py:366
  13.1 13.5 %collective-permute-start.1 = (bf16[1664,128]{1,0:T(8,128)(2,1)}, bf16[1664,128]{1,0:T(8,128)(2,1)S(1)}, u32[]{:S(2)}, u32[]{:S(2)}) collective-permute-start(bf16[1664,128]{1,0:T(8,128)(2,1)} %shard_map.110.refs_6_), channel_id=1, source_target_pairs={{0,7},{1,0},{2,1},{3,2},{4,3},{5,4},{6,5},{7,6},{8,15},{9,8},{10,9... | collective-permute-start | bytes 1277960 | tf_op jit(solution)/shard_map/ppermute | solution.py:370
  15.0 14.7 %collective-permute-start = (bf16[1664,128]{1,0:T(8,128)(2,1)}, bf16[1664,128]{1,0:T(8,128)(2,1)S(1)}, u32[]{:S(2)}, u32[]{:S(2)}) collective-permute-start(bf16[1664,128]{1,0:T(8,128)(2,1)} %shard_map.110.refs_6_), channel_id=1, source_target_pairs={{0,1},{1,2},{2,3},{3,4},{4,5},{5,6},{6,7},{7,0},{8,9},{9,10},{10,1... | collective-permute-start | bytes 1277960 | tf_op jit(solution)/shard_map/ppermute | solution.py:370
  18.4 66.0 %copy-start.22 = (bf16[1040,128]{1,0:T(8,128)(2,1)}, bf16[1040,128]{1,0:T(8,128)(2,1)S(1)}, u32[]{:S(2)}) copy-start(bf16[1040,128]{1,0:T(8,128)(2,1)S(1)} %collective-permute-done.2.refs_1_) | copy-start | bytes 798724
  26.6 31.7 %copy-start.8 = (bf16[1664,128]{1,0:T(8,128)(2,1)}, bf16[1664,128]{1,0:T(8,128)(2,1)S(1)}, u32[]{:S(2)}) copy-start(bf16[1664,128]{1,0:T(8,128)(2,1)S(1)} %collective-permute-done.1.m1.refs_7_) | copy-start | bytes 1277956
  29.7 28.6 %copy-start.9 = (bf16[1664,128]{1,0:T(8,128)(2,1)}, bf16[1664,128]{1,0:T(8,128)(2,1)S(1)}, u32[]{:S(2)}) copy-start(bf16[1664,128]{1,0:T(8,128)(2,1)S(1)} %collective-permute-done.p1.refs_10_) | copy-start | bytes 1277956
  29.7 12.4 %collective-permute-start.3 = (bf16[1664,128]{1,0:T(8,128)(2,1)S(1)}, bf16[1664,128]{1,0:T(8,128)(2,1)S(1)}, u32[]{:S(2)}, u32[]{:S(2)}) collective-permute-start(bf16[1664,128]{1,0:T(8,128)(2,1)S(1)} %collective-permute-done.1.m1.refs_7_), channel_id=1, source_target_pairs={{0,7},{1,0},{2,1},{3,2},{4,3},{5,4},{6,5},{7,6},{8,15},{9,8},{10,9... | collective-permute-start | bytes 1277960 | tf_op jit(solution)/shard_map/ppermute | solution.py:370
  31.6 13.9 %collective-permute-start.6 = (bf16[1664,128]{1,0:T(8,128)(2,1)S(1)}, bf16[1664,128]{1,0:T(8,128)(2,1)S(1)}, u32[]{:S(2)}, u32[]{:S(2)}) collective-permute-start(bf16[1664,128]{1,0:T(8,128)(2,1)S(1)} %collective-permute-done.p1.refs_10_), channel_id=1, source_target_pairs={{0,1},{1,2},{2,3},{3,4},{4,5},{5,6},{6,7},{7,0},{8,9},{9,10},{10,1... | collective-permute-start | bytes 1277960 | tf_op jit(solution)/shard_map/ppermute | solution.py:370
  42.1 16.2 %copy-start.14 = (bf16[1664,128]{1,0:T(8,128)(2,1)}, bf16[1664,128]{1,0:T(8,128)(2,1)S(1)}, u32[]{:S(2)}) copy-start(bf16[1664,128]{1,0:T(8,128)(2,1)S(1)} %collective-permute-done.3.m2.refs_8_) | copy-start | bytes 1277956
  42.1 11.5 %collective-permute-start.4 = (bf16[1664,128]{1,0:T(8,128)(2,1)S(1)}, bf16[1664,128]{1,0:T(8,128)(2,1)S(1)}, u32[]{:S(2)}, u32[]{:S(2)}) collective-permute-start(bf16[1664,128]{1,0:T(8,128)(2,1)S(1)} %collective-permute-done.3.m2.refs_8_), channel_id=1, source_target_pairs={{0,7},{1,0},{2,1},{3,2},{4,3},{5,4},{6,5},{7,6},{8,15},{9,8},{10,9... | collective-permute-start | bytes 1277960 | tf_op jit(solution)/shard_map/ppermute | solution.py:370
  45.5 12.8 %copy-start.15 = (bf16[1664,128]{1,0:T(8,128)(2,1)}, bf16[1664,128]{1,0:T(8,128)(2,1)S(1)}, u32[]{:S(2)}) copy-start(bf16[1664,128]{1,0:T(8,128)(2,1)S(1)} %collective-permute-done.6.p2.refs_11_) | copy-start | bytes 1277956
  45.5 12.8 %collective-permute-start.7 = (bf16[1664,128]{1,0:T(8,128)(2,1)S(1)}, bf16[1664,128]{1,0:T(8,128)(2,1)S(1)}, u32[]{:S(2)}, u32[]{:S(2)}) collective-permute-start(bf16[1664,128]{1,0:T(8,128)(2,1)S(1)} %collective-permute-done.6.p2.refs_11_), channel_id=1, source_target_pairs={{0,1},{1,2},{2,3},{3,4},{4,5},{5,6},{6,7},{7,0},{8,9},{9,10},{10,1... | collective-permute-start | bytes 1277960 | tf_op jit(solution)/shard_map/ppermute | solution.py:370
  53.6 4.7 %copy-start.1 = (bf16[1664,128]{1,0:T(8,128)(2,1)}, bf16[1664,128]{1,0:T(8,128)(2,1)S(1)}, u32[]{:S(2)}) copy-start(bf16[1664,128]{1,0:T(8,128)(2,1)S(1)} %collective-permute-done.4.m3.refs_9_) | copy-start | bytes 1277956
  58.3 0.8 copy-start.3
  62.8 21.7 %collective-permute-start.10 = (bf16[1024,1024]{1,0:T(8,128)(2,1)}, bf16[1024,1024]{1,0:T(8,128)(2,1)S(1)}, u32[]{:S(2)}, u32[]{:S(2)}) collective-permute-start(bf16[1024,1024]{1,0:T(8,128)(2,1)} %shard_map.112.refs_4_), channel_id=1, source_target_pairs={{0,8},{8,0},{16,24},{24,16},{32,40},{40,32},{48,56},{56,48},{64,72... | collective-permute-start | bytes 6291464 | tf_op jit(solution)/shard_map/ppermute | solution.py:366
  68.2 8.3 %collective-permute-start.5 = (bf16[768,128]{1,0:T(8,128)(2,1)S(1)}, bf16[768,128]{1,0:T(8,128)(2,1)S(1)}, u32[]{:S(2)}, u32[]{:S(2)}) collective-permute-start(bf16[768,128]{1,0:T(8,128)(2,1)S(1)} %slice.53), channel_id=1, source_target_pairs={{0,7},{1,0},{2,1},{3,2},{4,3},{5,4},{6,5},{7,6},{8,15},{9,8},{10,9... | collective-permute-start | bytes 589832 | tf_op jit(solution)/shard_map/ppermute | solution.py:370
  71.1 9.5 %collective-permute-start.8 = (bf16[768,128]{1,0:T(8,128)(2,1)S(1)}, bf16[768,128]{1,0:T(8,128)(2,1)S(1)}, u32[]{:S(2)}, u32[]{:S(2)}) collective-permute-start(bf16[768,128]{1,0:T(8,128)(2,1)S(1)} %slice.55), channel_id=1, source_target_pairs={{0,1},{1,2},{2,3},{3,4},{4,5},{5,6},{6,7},{7,0},{8,9},{9,10},{10,1... | collective-permute-start | bytes 589832 | tf_op jit(solution)/shard_map/ppermute | solution.py:370
  76.5 7.9 %copy-start.19 = (bf16[768,128]{1,0:T(8,128)(2,1)}, bf16[768,128]{1,0:T(8,128)(2,1)S(1)}, u32[]{:S(2)}) copy-start(bf16[768,128]{1,0:T(8,128)(2,1)S(1)} %collective-permute-done.5.refs_13_) | copy-start | bytes 589828
  80.6 3.8 %copy-start.21 = (bf16[768,128]{1,0:T(8,128)(2,1)}, bf16[768,128]{1,0:T(8,128)(2,1)S(1)}, u32[]{:S(2)}) copy-start(bf16[768,128]{1,0:T(8,128)(2,1)S(1)} %collective-permute-done.8.refs_14_) | copy-start | bytes 589828
  80.7 3.8 %copy-start.17 = (bf16[512,128]{1,0:T(8,128)(2,1)}, bf16[512,128]{1,0:T(8,128)(2,1)S(1)}, u32[]{:S(2)}) copy-start(bf16[512,128]{1,0:T(8,128)(2,1)S(1)} %pad_maximum_fusion.1.last_own) | copy-start | bytes 393220
  80.7 3.8 %collective-permute-start.9 = (bf16[512,128]{1,0:T(8,128)(2,1)S(1)}, bf16[512,128]{1,0:T(8,128)(2,1)S(1)}, u32[]{:S(2)}, u32[]{:S(2)}) collective-permute-start(bf16[512,128]{1,0:T(8,128)(2,1)S(1)} %pad_maximum_fusion.1.last_own), channel_id=1, source_target_pairs={{0,8},{8,0},{16,24},{24,16},{32,40},{40,32},{48,56},{56,48},{64,72... | collective-permute-start | bytes 393224 | tf_op jit(solution)/shard_map/ppermute | solution.py:366
  84.4 0.7 copy-start.27
  85.1 1.4 copy-start.6
  95.9 3.6 %collective-permute-start.11 = (bf16[1040,128]{1,0:T(8,128)(2,1)}, bf16[1040,128]{1,0:T(8,128)(2,1)S(1)}, u32[]{:S(2)}, u32[]{:S(2)}) collective-permute-start(bf16[1040,128]{1,0:T(8,128)(2,1)} %get-tuple-element.58.out2.refs_1_), channel_id=1, source_target_pairs={{0,8},{8,0},{16,24},{24,16},{32,40},{40,32},{48,56},{56,48},{64,72... | collective-permute-start | bytes 798728 | tf_op jit(solution)/shard_map/ppermute | solution.py:366
  99.5 0.7 copy-start.4
  101.9 9.8 %collective-permute-start.12 = (bf16[1024,128]{1,0:T(8,128)(2,1)}, bf16[1024,128]{1,0:T(8,128)(2,1)S(1)}, u32[]{:S(2)}, u32[]{:S(2)}) collective-permute-start(bf16[1024,128]{1,0:T(8,128)(2,1)} %shard_map.114), channel_id=1, source_target_pairs={{0,16},{8,24},{16,0},{24,8},{32,48},{40,56},{48,32},{56,40},{64,80... | collective-permute-start | bytes 786440 | tf_op jit(solution)/shard_map/ppermute | solution.py:366
  111.7 0.7 copy-start.5
  114.2 8.9 %collective-permute-start.15 = (bf16[1040,128]{1,0:T(8,128)(2,1)S(1)}, bf16[1040,128]{1,0:T(8,128)(2,1)S(1)}, u32[]{:S(2)}, u32[]{:S(2)}) collective-permute-start(bf16[1040,128]{1,0:T(8,128)(2,1)S(1)} %pad_maximum_fusion), channel_id=1, source_target_pairs={{0,16},{8,24},{16,0},{24,8},{32,48},{40,56},{48,32},{56,40},{64,80... | collective-permute-start | bytes 798728 | tf_op jit(solution)/shard_map/ppermute | solution.py:366
  116.5 12.5 %collective-permute-start.14 = (bf16[1664,128]{1,0:T(8,128)(2,1)}, bf16[1664,128]{1,0:T(8,128)(2,1)S(1)}, u32[]{:S(2)}, u32[]{:S(2)}) collective-permute-start(bf16[1664,128]{1,0:T(8,128)(2,1)} %shard_map.115.refs_7_), channel_id=1, source_target_pairs={{0,7},{1,0},{2,1},{3,2},{4,3},{5,4},{6,5},{7,6},{8,15},{9,8},{10,9... | collective-permute-start | bytes 1277960 | tf_op jit(solution)/shard_map/ppermute | solution.py:370
  118.4 13.7 %collective-permute-start.13 = (bf16[1664,128]{1,0:T(8,128)(2,1)}, bf16[1664,128]{1,0:T(8,128)(2,1)S(1)}, u32[]{:S(2)}, u32[]{:S(2)}) collective-permute-start(bf16[1664,128]{1,0:T(8,128)(2,1)} %shard_map.115.refs_7_), channel_id=1, source_target_pairs={{0,1},{1,2},{2,3},{3,4},{4,5},{5,6},{6,7},{7,0},{8,9},{9,10},{10,1... | collective-permute-start | bytes 1277960 | tf_op jit(solution)/shard_map/ppermute | solution.py:370
  123.1 62.7 %copy-start.23 = (bf16[1040,128]{1,0:T(8,128)(2,1)}, bf16[1040,128]{1,0:T(8,128)(2,1)S(1)}, u32[]{:S(2)}) copy-start(bf16[1040,128]{1,0:T(8,128)(2,1)S(1)} %collective-permute-done.15.refs_4_) | copy-start | bytes 798724
  128.9 29.8 %copy-start.10 = (bf16[1664,128]{1,0:T(8,128)(2,1)}, bf16[1664,128]{1,0:T(8,128)(2,1)S(1)}, u32[]{:S(2)}) copy-start(bf16[1664,128]{1,0:T(8,128)(2,1)S(1)} %collective-permute-done.14.m1.refs_8_) | copy-start | bytes 1277956
  132.1 26.6 %copy-start.11 = (bf16[1664,128]{1,0:T(8,128)(2,1)}, bf16[1664,128]{1,0:T(8,128)(2,1)S(1)}, u32[]{:S(2)}) copy-start(bf16[1664,128]{1,0:T(8,128)(2,1)S(1)} %collective-permute-done.13.p1.refs_11_) | copy-start | bytes 1277956
  132.1 11.4 %collective-permute-start.16 = (bf16[1664,128]{1,0:T(8,128)(2,1)S(1)}, bf16[1664,128]{1,0:T(8,128)(2,1)S(1)}, u32[]{:S(2)}, u32[]{:S(2)}) collective-permute-start(bf16[1664,128]{1,0:T(8,128)(2,1)S(1)} %collective-permute-done.14.m1.refs_8_), channel_id=1, source_target_pairs={{0,7},{1,0},{2,1},{3,2},{4,3},{5,4},{6,5},{7,6},{8,15},{9,8},{10,9... | collective-permute-start | bytes 1277960 | tf_op jit(solution)/shard_map/ppermute | solution.py:370
  134.0 12.9 %collective-permute-start.19 = (bf16[1664,128]{1,0:T(8,128)(2,1)S(1)}, bf16[1664,128]{1,0:T(8,128)(2,1)S(1)}, u32[]{:S(2)}, u32[]{:S(2)}) collective-permute-start(bf16[1664,128]{1,0:T(8,128)(2,1)S(1)} %collective-permute-done.13.p1.refs_11_), channel_id=1, source_target_pairs={{0,1},{1,2},{2,3},{3,4},{4,5},{5,6},{6,7},{7,0},{8,9},{9,10},{10,1... | collective-permute-start | bytes 1277960 | tf_op jit(solution)/shard_map/ppermute | solution.py:370
  143.5 15.2 %copy-start.12 = (bf16[1664,128]{1,0:T(8,128)(2,1)}, bf16[1664,128]{1,0:T(8,128)(2,1)S(1)}, u32[]{:S(2)}) copy-start(bf16[1664,128]{1,0:T(8,128)(2,1)S(1)} %collective-permute-done.16.m2.refs_9_) | copy-start | bytes 1277956
  143.5 10.6 %collective-permute-start.17 = (bf16[1664,128]{1,0:T(8,128)(2,1)S(1)}, bf16[1664,128]{1,0:T(8,128)(2,1)S(1)}, u32[]{:S(2)}, u32[]{:S(2)}) collective-permute-start(bf16[1664,128]{1,0:T(8,128)(2,1)S(1)} %collective-permute-done.16.m2.refs_9_), channel_id=1, source_target_pairs={{0,7},{1,0},{2,1},{3,2},{4,3},{5,4},{6,5},{7,6},{8,15},{9,8},{10,9... | collective-permute-start | bytes 1277960 | tf_op jit(solution)/shard_map/ppermute | solution.py:370
  146.9 11.8 %copy-start.13 = (bf16[1664,128]{1,0:T(8,128)(2,1)}, bf16[1664,128]{1,0:T(8,128)(2,1)S(1)}, u32[]{:S(2)}) copy-start(bf16[1664,128]{1,0:T(8,128)(2,1)S(1)} %collective-permute-done.19.p2.refs_12_) | copy-start | bytes 1277956
  146.9 11.8 %collective-permute-start.20 = (bf16[1664,128]{1,0:T(8,128)(2,1)S(1)}, bf16[1664,128]{1,0:T(8,128)(2,1)S(1)}, u32[]{:S(2)}, u32[]{:S(2)}) collective-permute-start(bf16[1664,128]{1,0:T(8,128)(2,1)S(1)} %collective-permute-done.19.p2.refs_12_), channel_id=1, source_target_pairs={{0,1},{1,2},{2,3},{3,4},{4,5},{5,6},{6,7},{7,0},{8,9},{9,10},{10,1... | collective-permute-start | bytes 1277960 | tf_op jit(solution)/shard_map/ppermute | solution.py:370
  154.1 4.7 %copy-start = (bf16[1664,128]{1,0:T(8,128)(2,1)}, bf16[1664,128]{1,0:T(8,128)(2,1)S(1)}, u32[]{:S(2)}) copy-start(bf16[1664,128]{1,0:T(8,128)(2,1)S(1)} %collective-permute-done.17.m3.refs_10_) | copy-start | bytes 1277956
  158.7 0.8 copy-start.2
  163.4 22.4 %collective-permute-start.23 = (bf16[1024,1024]{1,0:T(8,128)(2,1)}, bf16[1024,1024]{1,0:T(8,128)(2,1)S(1)}, u32[]{:S(2)}, u32[]{:S(2)}) collective-permute-start(bf16[1024,1024]{1,0:T(8,128)(2,1)} %shard_map.116.refs_5_), channel_id=1, source_target_pairs={{0,8},{8,0},{16,24},{24,16},{32,40},{40,32},{48,56},{56,48},{64,72... | collective-permute-start | bytes 6291464 | tf_op jit(solution)/shard_map/ppermute | solution.py:366
  169.6 8.3 %collective-permute-start.18 = (bf16[768,128]{1,0:T(8,128)(2,1)S(1)}, bf16[768,128]{1,0:T(8,128)(2,1)S(1)}, u32[]{:S(2)}, u32[]{:S(2)}) collective-permute-start(bf16[768,128]{1,0:T(8,128)(2,1)S(1)} %slice.59), channel_id=1, source_target_pairs={{0,7},{1,0},{2,1},{3,2},{4,3},{5,4},{6,5},{7,6},{8,15},{9,8},{10,9... | collective-permute-start | bytes 589832 | tf_op jit(solution)/shard_map/ppermute | solution.py:370
  172.5 9.5 %collective-permute-start.21 = (bf16[768,128]{1,0:T(8,128)(2,1)S(1)}, bf16[768,128]{1,0:T(8,128)(2,1)S(1)}, u32[]{:S(2)}, u32[]{:S(2)}) collective-permute-start(bf16[768,128]{1,0:T(8,128)(2,1)S(1)} %slice.61), channel_id=1, source_target_pairs={{0,1},{1,2},{2,3},{3,4},{4,5},{5,6},{6,7},{7,0},{8,9},{9,10},{10,1... | collective-permute-start | bytes 589832 | tf_op jit(solution)/shard_map/ppermute | solution.py:370
  177.9 7.9 %copy-start.18 = (bf16[768,128]{1,0:T(8,128)(2,1)}, bf16[768,128]{1,0:T(8,128)(2,1)S(1)}, u32[]{:S(2)}) copy-start(bf16[768,128]{1,0:T(8,128)(2,1)S(1)} %collective-permute-done.18.refs_14_) | copy-start | bytes 589828
  182.0 3.8 %copy-start.20 = (bf16[768,128]{1,0:T(8,128)(2,1)}, bf16[768,128]{1,0:T(8,128)(2,1)S(1)}, u32[]{:S(2)}) copy-start(bf16[768,128]{1,0:T(8,128)(2,1)S(1)} %collective-permute-done.21.refs_15_) | copy-start | bytes 589828
  182.0 3.8 %copy-start.16 = (bf16[512,128]{1,0:T(8,128)(2,1)}, bf16[512,128]{1,0:T(8,128)(2,1)S(1)}, u32[]{:S(2)}) copy-start(bf16[512,128]{1,0:T(8,128)(2,1)S(1)} %pad_maximum_fusion.2.last_own) | copy-start | bytes 393220
  182.1 3.8 %collective-permute-start.22 = (bf16[512,128]{1,0:T(8,128)(2,1)S(1)}, bf16[512,128]{1,0:T(8,128)(2,1)S(1)}, u32[]{:S(2)}, u32[]{:S(2)}) collective-permute-start(bf16[512,128]{1,0:T(8,128)(2,1)S(1)} %pad_maximum_fusion.2.last_own), channel_id=1, source_target_pairs={{0,8},{8,0},{16,24},{24,16},{32,40},{40,32},{48,56},{56,48},{64,72... | collective-permute-start | bytes 393224 | tf_op jit(solution)/shard_map/ppermute | solution.py:366
  185.8 0.7 copy-start.26
  186.5 1.4 copy-start.7
  197.3 5.7 %collective-permute-start.25 = (bf16[1040,128]{1,0:T(8,128)(2,1)}, bf16[1040,128]{1,0:T(8,128)(2,1)S(1)}, u32[]{:S(2)}, u32[]{:S(2)}) collective-permute-start(bf16[1040,128]{1,0:T(8,128)(2,1)} %get-tuple-element.63.own2), channel_id=1, source_target_pairs={{0,8},{8,0},{16,24},{24,16},{32,40},{40,32},{48,56},{56,48},{64,72... | collective-permute-start | bytes 798728 | tf_op jit(solution)/shard_map/ppermute | solution.py:366
  199.2 3.8 %collective-permute-start.24 = (bf16[1024,128]{1,0:T(8,128)(2,1)}, bf16[1024,128]{1,0:T(8,128)(2,1)S(1)}, u32[]{:S(2)}, u32[]{:S(2)}) collective-permute-start(bf16[1024,128]{1,0:T(8,128)(2,1)} %get-tuple-element.62.own1), channel_id=1, source_target_pairs={{0,8},{8,0},{16,24},{24,16},{32,40},{40,32},{48,56},{56,48},{64,72... | collective-permute-start | bytes 786440 | tf_op jit(solution)/shard_map/ppermute | solution.py:366
  203.0 0.7 copy-start.25
  203.7 0.7 copy-start.24

commit v5 on v4

--- a/solution.py
+++ b/solution.py
@@ -12,7 +12,8 @@
 W = 128
 N = 8
 D = W * N
-RING = 1664
+UP = 1536
+DOWN = 1664
 HALF = 768
 INTERPRET = False
 
@@ -53,28 +54,32 @@
 
 
 def stream(pieces, buf, sems_in, sems_out):
-    ins = [
-        pltpu.make_async_copy(src.at[pl.ds(a, W)], buf.at[pl.ds(k * W, W)], sems_in.at[k])
-        for k, (src, a, _, _) in enumerate(pieces)
-    ]
-    outs = [
-        pltpu.make_async_copy(buf.at[pl.ds(k * W, W)], dst.at[pl.ds(b, W)], sems_out.at[k])
-        for k, (_, _, dst, b) in enumerate(pieces)
-    ]
+    ins, outs = [], []
+    for k, (src, a, targets) in enumerate(pieces):
+        part = buf.at[pl.ds(k * W, W)]
+        ins.append(pltpu.make_async_copy(src.at[pl.ds(a, W)], part, sems_in.at[k]))
+        outs.append(
+            [
+                pltpu.make_async_copy(part, dst.at[pl.ds(b, W)], sems_out.at[2 * k + i])
+                for i, (dst, b) in enumerate(targets)
+            ]
+        )
     for c in ins:
         c.start()
-    for c, o in zip(ins, outs):
+    for c, group in zip(ins, outs):
         c.wait()
-        o.start()
-    for o in outs:
-        o.wait()
+        for o in group:
+            o.start()
+    for group in outs:
+        for o in group:
+            o.wait()
 
 
 def streaming(pieces):
     return (
         pltpu.VMEM((pieces * W, W), bf16),
         pltpu.SemaphoreType.DMA((pieces,)),
-        pltpu.SemaphoreType.DMA((pieces,)),
+        pltpu.SemaphoreType.DMA((2 * pieces,)),
     )
 
 
@@ -118,13 +123,15 @@
 
 
 def ring_kernel(sources, *refs):
-    *inputs, msg, buf, sems_in, sems_out = refs
+    *inputs, up, down, buf, sems_in, sems_out = refs
     q = place()[2]
 
     def run(core, odd):
         x, a = (inputs[k] for k in sources(core, odd))
-        pieces = [(x, at((q + d) % N), msg, 512 + d * W if d < 4 else 1536) for d in range(5)]
-        pieces += [(a, k * W, msg, k * W if k < 4 else 512 + k * W) for k in range(N)]
+        spots = [(a, k * W, k * W if k < 4 else 512 + k * W) for k in range(N)]
+        spots += [(x, at((q + d) % N), 512 + d * W) for d in range(4)]
+        pieces = [(src, row, [(down, to), (up, to)]) for src, row, to in spots]
+        pieces += [(x, at((q + 4) % N), [(down, UP)])]
         stream(pieces, buf, sems_in, sems_out)
 
     each_state(run)
@@ -165,6 +172,11 @@
 
 def combine_kernel(own_is_cov, sides, count, last_own, last_far, vec_i, vec_j, *refs):
     side_refs = refs[:count]
+    joined = len(refs) == count + 22
+    if joined:
+        out1 = refs[count + 11].at[pl.ds(0, D)]
+        out2 = refs[count + 11].at[pl.ds(D, D + 2 * N)]
+        refs = refs[: count + 11] + (out1, out2) + refs[count + 12 :]
     (x_here, x_far, msg, m1, m2, m3, p1, p2, p3, m4, p4, out1, out2,
      x_own, x_other, a_full, r, t, base, vecs, ai, add, sems) = refs[count:]
     core, _, q = place()
@@ -325,31 +337,21 @@
         out2[D : D + 2 * N, :] = jnp.where(rows < N, 0.0, vecs[...]).astype(bf16)
 
 
-def pick_kernel(out1, out2, got2, msg, buf, sems_in, sems_out):
-    def run(core, odd):
-        src = out2 if (core, odd) == (1, 1) else got2 if (core, odd) == (0, 0) else out1
-        stream([(src, k * W, msg, k * W) for k in range(N)], buf, sems_in, sems_out)
-
-    each_state(run)
-
-
-def finish_kernel(
-    own1, own2, got1, got2, drift, belief, move, spread, weight, buf, sems_in, sems_out, vec, sems
-):
+def finish_kernel(own, got, drift, belief, move, spread, weight, buf, sems_in, sems_out, vec, sems):
     core = place()[0]
 
-    def put(first, moved, last, b, e):
+    def put(early, late):
         tails = [
             pltpu.make_async_copy(
-                src.at[pl.ds(D, 2 * N)], vec.at[pl.ds(k * 2 * N, 2 * N)], sems.at[k]
+                src.at[pl.ds(2 * D, 2 * N)], vec.at[pl.ds(k * 2 * N, 2 * N)], sems.at[k]
             )
-            for k, src in enumerate((b, e))
+            for k, src in enumerate((early, late))
         ]
         for c in tails:
             c.start()
         pieces = []
-        for src, dst in ((first, spread), (moved, move), (last, weight)):
-            pieces += [(src, k * W, dst, k * W) for k in range(N)]
+        for src, first, dst in ((early, 0, spread), (early, D, move), (late, 0, weight)):
+            pieces += [(src, first + k * W, [(dst, k * W)]) for k in range(N)]
         stream(pieces, buf, sems_in, sems_out)
         for c in tails:
             c.wait()
@@ -358,8 +360,8 @@
             drift[:, l * W : (l + 1) * W] = rows[l : l + 1, :].astype(bf16)
             belief[:, l * W : (l + 1) * W] = rows[3 * N + l : 3 * N + l + 1, :].astype(bf16)
 
-    pl.when(core == 1)(lambda: put(own1, own2, got1, own2, got2))
-    pl.when(core == 0)(lambda: put(got1, got2, own1, got2, own2))
+    pl.when(core == 1)(lambda: put(own, got))
+    pl.when(core == 0)(lambda: put(got, own))
 
 
 def swap(x, axis_bit):
@@ -370,18 +372,18 @@
     return lax.ppermute(x, "panel", [(i, (i + by) % N) for i in range(N)])
 
 
-def combined(own_is_cov, x_pair, x_pick, ring_refs, sources, gate, side, sides):
-    (msg,) = call(
+def combined(own_is_cov, outs, x_pair, x_pick, ring_refs, sources, gate, side, sides):
+    up, down = call(
         functools.partial(ring_kernel, sources),
-        [struct(RING, W)],
-        streaming(RING // W),
+        [struct(UP, W), struct(DOWN, W)],
+        streaming(DOWN // W),
         *ring_refs,
         vmem=0,
         vmem_out=False,
     )
-    msg, gate = lax.optimization_barrier((msg, gate))
-    p1 = shift(msg, 1)
-    m1 = shift(msg, -1)
+    up, down, gate = lax.optimization_barrier((up, down, gate))
+    p1 = shift(up, 1)
+    m1 = shift(down, -1)
     p1, m1, (vec_i, vec_j, side_refs) = lax.optimization_barrier((p1, m1, side(gate)))
     p2, m2 = shift(p1, 1), shift(m1, -1)
     p3, m3 = shift(p2, 1), shift(m2, -1)
@@ -404,7 +406,7 @@
     last_far = swap(last_own, 0)
     return call(
         functools.partial(combine_kernel, own_is_cov, sides, len(side_refs)),
-        [struct(D, W), struct(D + 2 * N, W)],
+        outs,
         (
             pltpu.VMEM((D, D), bf16),
             pltpu.VMEM((D, D), bf16),
@@ -424,7 +426,7 @@
         *side_refs,
         x_here,
         x_far,
-        msg,
+        down,
         m1,
         m2,
         m3,
@@ -461,6 +463,7 @@
 
     out1, out2 = combined(
         False,
+        [struct(D, W), struct(D + 2 * N, W)],
         (cov, info),
         lambda core, odd: core,
         (cov, info, move),
@@ -469,12 +472,14 @@
         side0,
         lambda core, odd: (core, 3 - core),
     )
+    far_a = lax.ppermute(
+        out2, "tm", [(i, i + 1 if i % 4 == 1 else i - 2) for i in range(1, lax.axis_size("tm"), 2)]
+    )
+    far_x = lax.ppermute(
+        out1, "tm", [(i, i ^ 2) for i in range(lax.axis_size("tm")) if i % 4 in (1, 2)]
+    )
     got2 = swap(out2, 0)
     own_vec = out2[D:] + got2[D:]
-    (panel,) = call(
-        pick_kernel, [struct(D, W)], streaming(N), out1, out2, got2, vmem=0, vmem_out=False
-    )
-    far = swap(panel, 1)
 
     def side1(own_vec):
         rest = jnp.where((core == 1) & near, out2[:D], out1)
@@ -482,32 +487,30 @@
         far_vec = bundle[D:]
         vec_i = jnp.where(near, own_vec, far_vec)
         vec_j = jnp.where(near, far_vec, own_vec)
-        return vec_i, vec_j, (out1, out2, got2, far, bundle)
-
-    sources = {(1, 0): (0, 3), (1, 1): (3, 1), (0, 0): (3, 2), (0, 1): (0, 3)}
+        return vec_i, vec_j, (out1, out2, got2, far_a, bundle)
+
+    sources = {(1, 0): (0, 3), (1, 1): (4, 1), (0, 0): (4, 2), (0, 1): (0, 3)}
     sides = {(1, 0): (1, 4), (1, 1): (4, 0), (0, 0): (2, 0), (0, 1): (3, 4)}
-    out1, out2 = combined(
+    (own,) = combined(
         True,
-        (out1, far),
+        [struct(2 * D + 2 * N, W)],
+        (out1, far_x),
         lambda core, odd: 1 ^ core ^ odd,
-        (out1, out2, got2, far),
+        (out1, out2, got2, far_a, far_x),
         lambda core, odd: sources[core, odd],
         own_vec,
         side1,
         lambda core, odd: sides[core, odd],
     )
-    got1 = swap(out1, 0)
-    got2 = swap(out2, 0)
+    got = swap(own, 0)
     panel = struct(D, W)
     row = struct(1, D)
     drift, belief, move, cov, info = call(
         finish_kernel,
         [row, row, panel, panel, panel],
         streaming(3 * N) + (pltpu.VMEM((4 * N, W), bf16), pltpu.SemaphoreType.DMA((2,))),
-        out1,
-        out2,
-        got1,
-        got2,
+        own,
+        got,
         vmem=0,
         vmem_out=[True, True, False, False, False],
     )

time: 209 us -> 206 us (0.986)
  waiting for transfers between devices: 77.1 us -> 67.6 us
  starting transfers between devices: 76.7 us -> 83.8 us
    ppermute x10 -> x8, waiting for transfers between devices: 12.6 us -> 4.03 us  [swap(): lax.ppermute(x, 'tm', [(i, i ^ 1 << axis_bit) for i in range(lax.axis_siz...]
    ppermute x0 -> x2, starting transfers between devices: none -> 5.31 us  [the longest x1 3.39 us: local(): lax.ppermute(out1, 'tm', [(i, i ^ 2) for i in range(lax.axis_size('tm'))...]
    ppermute x16, starting transfers between devices: 42.3 us -> 46.7 us  [shift(): return lax.ppermute(x, 'panel', [(i, (i + by) % N) for i in range(N)])]
    ppermute x16, waiting for transfers between devices: 64.5 us -> 61.6 us  [shift(): return lax.ppermute(x, 'panel', [(i, (i + by) % N) for i in range(N)])]
    ppermute x10 -> x8, starting transfers between devices: 34.4 us -> 31.8 us  [swap(): lax.ppermute(x, 'tm', [(i, i ^ 1 << axis_bit) for i in range(lax.axis_siz...]
    pallas_call x9 -> x8, Pallas kernels: 36.3 us -> 35.1 us  [call(): pl.pallas_call(kernel, out_shape=list(out_shape), in_specs=[vm] * staged...]
  transfers between devices with their start and end apart: 26 -> 26, of which waited for: 20 -> 14; matrix products, arithmetic and copies ran while one was open for 4% -> 4% of each run, Pallas kernels for 0% -> 0%
where the time goes in v5:
time: 206 us; the launch traced here: 205 us
  starting transfers between devices  83.8 us (41%)
  waiting for transfers between devices  67.6 us (33%)
  Pallas kernels  35.1 us (17%)
  local copies, waits for them, and re-layouts  13 us (6%)
  other arithmetic  3.72 us (2%)
    ppermute x16, waiting for transfers between devices, shift(): return lax.ppermute(x, 'panel', [(i, (i + by) % N) for i in range(N)])  61.6 us
    ppermute x16, starting transfers between devices, shift(): return lax.ppermute(x, 'panel', [(i, (i + by) % N) for i in range(N)])  46.7 us
    pallas_call x8, Pallas kernels, call(): pl.pallas_call(kernel, out_shape=list(out_shape), in_specs=[vm] * staged...  35.1 us
    ppermute x8, starting transfers between devices, swap(): lax.ppermute(x, 'tm', [(i, i ^ 1 << axis_bit) for i in range(lax.axis_siz...  31.8 us
    unnamed x56, local copies, waits for them, and re-layouts  9.23 us
  transfers between devices with their start and end apart: 26, of which 14 were waited for; matrix products, arithmetic and copies ran while one was open for 4% of the time, Pallas kernels for 0%

profile of v5, /device:TPU:1, one launch (start us, length us, event | category | flops | bytes accessed | tf_op | source)
XLA Modules:
  0.0 204.5 jit_solution(9135419940299011144)
XLA Ops:
  0.6 2.0 shard_map.110
  2.7 1.9 shard_map.111
  4.6 8.7 %collective-permute-start.2 = (bf16[1040,128]{1,0:T(8,128)(2,1)}, bf16[1040,128]{1,0:T(8,128)(2,1)S(1)}, u32[]{:S(2)}, u32[]{:S(2)}) collective-permute-start(bf16[1040,128]{1,0:T(8,128)(2,1)} %get-tuple-element.47), channel_id=1, source_target_pairs={{0,8},{8,0},{16,24},{24,16},{32,40},{40,32},{48,56},{56,48},{64,72... | collective-permute-start | bytes 798728 | tf_op jit(solution)/shard_map/ppermute | solution.py:368
  13.3 1.9 collective-permute-start.1
  15.2 3.4 %collective-permute-start = (bf16[1536,128]{1,0:T(8,128)(2,1)}, bf16[1536,128]{1,0:T(8,128)(2,1)S(1)}, u32[]{:S(2)}, u32[]{:S(2)}) collective-permute-start(bf16[1536,128]{1,0:T(8,128)(2,1)} %get-tuple-element.43), channel_id=1, source_target_pairs={{0,1},{1,2},{2,3},{3,4},{4,5},{5,6},{6,7},{7,0},{8,9},{9,10},{10,1... | collective-permute-start | bytes 1179656 | tf_op jit(solution)/shard_map/ppermute | solution.py:372
  18.6 1.3 broadcast_select_fusion.2
  20.0 9.2 %collective-permute-done.p1.refs_10_ = bf16[1536,128]{1,0:T(8,128)(2,1)S(1)} collective-permute-done((bf16[1536,128]{1,0:T(8,128)(2,1)}, bf16[1536,128]{1,0:T(8,128)(2,1)S(1)}, u32[]{:S(2)}, u32[]{:S(2)}) %collective-permute-start) | collective-permute-done | bytes 393248 | tf_op jit(solution)/shard_map/ppermute | solution.py:372
  29.2 1.9 collective-permute-start.3
  31.1 3.4 %collective-permute-start.6 = (bf16[1536,128]{1,0:T(8,128)(2,1)S(1)}, bf16[1536,128]{1,0:T(8,128)(2,1)S(1)}, u32[]{:S(2)}, u32[]{:S(2)}) collective-permute-start(bf16[1536,128]{1,0:T(8,128)(2,1)S(1)} %collective-permute-done.p1.refs_10_), channel_id=1, source_target_pairs={{0,1},{1,2},{2,3},{3,4},{4,5},{5,6},{6,7},{7,0},{8,9},{9,10},{10,1... | collective-permute-start | bytes 1179656 | tf_op jit(solution)/shard_map/ppermute | solution.py:372
  34.5 7.1 %collective-permute-done.3.m2.refs_8_ = bf16[1664,128]{1,0:T(8,128)(2,1)S(1)} collective-permute-done((bf16[1664,128]{1,0:T(8,128)(2,1)S(1)}, bf16[1664,128]{1,0:T(8,128)(2,1)S(1)}, u32[]{:S(2)}, u32[]{:S(2)}) %collective-permute-start.3) | collective-permute-done | bytes 426016 | tf_op jit(solution)/shard_map/ppermute | solution.py:372
  41.6 3.4 %collective-permute-start.4 = (bf16[1664,128]{1,0:T(8,128)(2,1)S(1)}, bf16[1664,128]{1,0:T(8,128)(2,1)S(1)}, u32[]{:S(2)}, u32[]{:S(2)}) collective-permute-start(bf16[1664,128]{1,0:T(8,128)(2,1)S(1)} %collective-permute-done.3.m2.refs_8_), channel_id=1, source_target_pairs={{0,7},{1,0},{2,1},{3,2},{4,3},{5,4},{6,5},{7,6},{8,15},{9,8},{10,9... | collective-permute-start | bytes 1277960 | tf_op jit(solution)/shard_map/ppermute | solution.py:372
  45.0 1.9 collective-permute-start.7
  47.0 10.1 %collective-permute-done.7.p3.refs_12_ = bf16[1536,128]{1,0:T(8,128)(2,1)S(1)} collective-permute-done((bf16[1536,128]{1,0:T(8,128)(2,1)S(1)}, bf16[1536,128]{1,0:T(8,128)(2,1)S(1)}, u32[]{:S(2)}, u32[]{:S(2)}) %collective-permute-start.7) | collective-permute-done | bytes 393248 | tf_op jit(solution)/shard_map/ppermute | solution.py:372
  57.1 0.7 copy-done.3
  57.8 0.8 copy-done.1
  58.6 3.6 %shard_map.112.refs_4_ = bf16[1024,1024]{1,0:T(8,128)(2,1)} custom-call(bf16[1024,128]{1,0:T(8,128)(2,1)} %bitcast.7, bf16[1024,128]{1,0:T(8,128)(2,1)} %bitcast.10, bf16[1664,128]{1,0:T(8,128)(2,1)} %copy-done.6, bf16[1664,128]{1,0:T(8,128)(2,1)} %copy-done.9, bf16[1664,128]{1,0:T(8,128)(2,1)} %copy-done.1, bf16[1536,128]{1,0:T(8,128)(2,1)} %copy-done.10, ...), custom_call_target="tpu_custom_call" | custom-call | tf_op jit(solution)/shard_map/pallas_call | solution.py:33
  62.3 4.5 %collective-permute-start.10 = (bf16[1024,1024]{1,0:T(8,128)(2,1)}, bf16[1024,1024]{1,0:T(8,128)(2,1)S(1)}, u32[]{:S(2)}, u32[]{:S(2)}) collective-permute-start(bf16[1024,1024]{1,0:T(8,128)(2,1)} %shard_map.112.refs_4_), channel_id=1, source_target_pairs={{0,8},{8,0},{16,24},{24,16},{32,40},{40,32},{48,56},{56,48},{64,72... | collective-permute-start | bytes 6291464 | tf_op jit(solution)/shard_map/ppermute | solution.py:368
  66.7 0.9 slice.55
  67.7 1.9 collective-permute-start.8
  69.6 0.9 slice.53
  70.6 4.6 %collective-permute-start.5 = (bf16[768,128]{1,0:T(8,128)(2,1)S(1)}, bf16[768,128]{1,0:T(8,128)(2,1)S(1)}, u32[]{:S(2)}, u32[]{:S(2)}) collective-permute-start(bf16[768,128]{1,0:T(8,128)(2,1)S(1)} %slice.53), channel_id=1, source_target_pairs={{0,7},{1,0},{2,1},{3,2},{4,3},{5,4},{6,5},{7,6},{8,15},{9,8},{10,9... | collective-permute-start | bytes 589832 | tf_op jit(solution)/shard_map/ppermute | solution.py:372
  75.1 2.1 %collective-permute-done.8.refs_14_ = bf16[768,128]{1,0:T(8,128)(2,1)S(1)} collective-permute-done((bf16[768,128]{1,0:T(8,128)(2,1)S(1)}, bf16[768,128]{1,0:T(8,128)(2,1)S(1)}, u32[]{:S(2)}, u32[]{:S(2)}) %collective-permute-start.8) | collective-permute-done | bytes 196640 | tf_op jit(solution)/shard_map/ppermute | solution.py:372
  77.2 1.8 collective-permute-done.5.refs_13_
  79.1 3.1 %collective-permute-start.9 = (bf16[512,128]{1,0:T(8,128)(2,1)S(1)}, bf16[512,128]{1,0:T(8,128)(2,1)S(1)}, u32[]{:S(2)}, u32[]{:S(2)}) collective-permute-start(bf16[512,128]{1,0:T(8,128)(2,1)S(1)} %pad_maximum_fusion.1.last_own), channel_id=1, source_target_pairs={{0,8},{8,0},{16,24},{24,16},{32,40},{40,32},{48,56},{56,48},{64,72... | collective-permute-start | bytes 393224 | tf_op jit(solution)/shard_map/ppermute | solution.py:368
  82.2 1.0 collective-permute-done.9.last_far
  83.8 1.4 copy-done.5
  85.2 9.5 %shard_map.113 = (bf16[1024,128]{1,0:T(8,128)(2,1)}, bf16[1040,128]{1,0:T(8,128)(2,1)}) custom-call(bf16[512,128]{1,0:T(8,128)(2,1)} %copy-done.19, bf16[512,128]{1,0:T(8,128)(2,1)} %copy-done.27, bf16[16,128]{1,0:T(8,128)(2,1)} %get-tuple-element.50.vec_i, bf16[16,128]{1,0:T(8,128)(2,1)} %get-tuple-element.51.vec_j, bf16[1024,128]{1,0:T(8,128)(2,1)} %bitcast.14, ...), custom_call_target="tpu_custom_call" | custom-call | tf_op jit(solution)/shard_map/pallas_call | solution.py:33
  94.6 1.9 collective-permute-start.11
  96.6 1.9 collective-permute-start.12
  98.5 3.4 %collective-permute-start.13 = (bf16[1024,128]{1,0:T(8,128)(2,1)}, bf16[1024,128]{1,0:T(8,128)(2,1)S(1)}, u32[]{:S(2)}, u32[]{:S(2)}) collective-permute-start(bf16[1024,128]{1,0:T(8,128)(2,1)} %get-tuple-element.67.refs_0_.xa), channel_id=1, source_target_pairs={{8,24},{16,0},{40,56},{48,32},{72,88},{80,64},{104,120},{112,96},{... | collective-permute-start | bytes 786440 | tf_op jit(solution)/shard_map/ppermute | solution.py:478
  101.9 1.0 slice_select_fusion
  102.9 0.7 slice_add_fusion
  103.6 1.9 collective-permute-done.13.refs_4_.xb
  105.5 0.7 copy-done.16
  106.2 0.7 copy-done.15
  106.9 2.0 shard_map.114
  109.0 3.7 %collective-permute-start.16 = (bf16[1040,128]{1,0:T(8,128)(2,1)S(1)}, bf16[1040,128]{1,0:T(8,128)(2,1)S(1)}, u32[]{:S(2)}, u32[]{:S(2)}) collective-permute-start(bf16[1040,128]{1,0:T(8,128)(2,1)S(1)} %pad_maximum_fusion), channel_id=1, source_target_pairs={{0,16},{8,24},{16,0},{24,8},{32,48},{40,56},{48,32},{56,40},{64,80... | collective-permute-start | bytes 798728 | tf_op jit(solution)/shard_map/ppermute | solution.py:368
  112.7 5.3 %collective-permute-start.15 = (bf16[1664,128]{1,0:T(8,128)(2,1)}, bf16[1664,128]{1,0:T(8,128)(2,1)S(1)}, u32[]{:S(2)}, u32[]{:S(2)}) collective-permute-start(bf16[1664,128]{1,0:T(8,128)(2,1)} %get-tuple-element.61.refs_7_), channel_id=1, source_target_pairs={{0,7},{1,0},{2,1},{3,2},{4,3},{5,4},{6,5},{7,6},{8,15},{9,8},{10,9... | collective-permute-start | bytes 1277960 | tf_op jit(solution)/shard_map/ppermute | solution.py:372
  118.0 1.9 collective-permute-start.14
  120.6 10.9 %collective-permute-done.14.p1.refs_11_ = bf16[1536,128]{1,0:T(8,128)(2,1)S(1)} collective-permute-done((bf16[1536,128]{1,0:T(8,128)(2,1)}, bf16[1536,128]{1,0:T(8,128)(2,1)S(1)}, u32[]{:S(2)}, u32[]{:S(2)}) %collective-permute-start.14) | collective-permute-done | bytes 393248 | tf_op jit(solution)/shard_map/ppermute | solution.py:372
  131.6 1.9 collective-permute-start.17
  133.5 3.4 %collective-permute-start.20 = (bf16[1536,128]{1,0:T(8,128)(2,1)S(1)}, bf16[1536,128]{1,0:T(8,128)(2,1)S(1)}, u32[]{:S(2)}, u32[]{:S(2)}) collective-permute-start(bf16[1536,128]{1,0:T(8,128)(2,1)S(1)} %collective-permute-done.14.p1.refs_11_), channel_id=1, source_target_pairs={{0,1},{1,2},{2,3},{3,4},{4,5},{5,6},{6,7},{7,0},{8,9},{9,10},{10,1... | collective-permute-start | bytes 1179656 | tf_op jit(solution)/shard_map/ppermute | solution.py:372
  136.9 6.7 %collective-permute-done.17.m2.refs_9_ = bf16[1664,128]{1,0:T(8,128)(2,1)S(1)} collective-permute-done((bf16[1664,128]{1,0:T(8,128)(2,1)S(1)}, bf16[1664,128]{1,0:T(8,128)(2,1)S(1)}, u32[]{:S(2)}, u32[]{:S(2)}) %collective-permute-start.17) | collective-permute-done | bytes 426016 | tf_op jit(solution)/shard_map/ppermute | solution.py:372
  143.5 3.4 %collective-permute-start.18 = (bf16[1664,128]{1,0:T(8,128)(2,1)S(1)}, bf16[1664,128]{1,0:T(8,128)(2,1)S(1)}, u32[]{:S(2)}, u32[]{:S(2)}) collective-permute-start(bf16[1664,128]{1,0:T(8,128)(2,1)S(1)} %collective-permute-done.17.m2.refs_9_), channel_id=1, source_target_pairs={{0,7},{1,0},{2,1},{3,2},{4,3},{5,4},{6,5},{7,6},{8,15},{9,8},{10,9... | collective-permute-start | bytes 1277960 | tf_op jit(solution)/shard_map/ppermute | solution.py:372
  147.0 1.9 collective-permute-start.21
  148.9 9.7 %collective-permute-done.21.p3.refs_13_ = bf16[1536,128]{1,0:T(8,128)(2,1)S(1)} collective-permute-done((bf16[1536,128]{1,0:T(8,128)(2,1)S(1)}, bf16[1536,128]{1,0:T(8,128)(2,1)S(1)}, u32[]{:S(2)}, u32[]{:S(2)}) %collective-permute-start.21) | collective-permute-done | bytes 393248 | tf_op jit(solution)/shard_map/ppermute | solution.py:372
  158.6 0.7 copy-done.2
  159.3 0.8 copy-done
  160.1 3.6 %shard_map.115.refs_5_ = bf16[1024,1024]{1,0:T(8,128)(2,1)} custom-call(bf16[1024,128]{1,0:T(8,128)(2,1)} %get-tuple-element.67.refs_0_.xa, bf16[1024,128]{1,0:T(8,128)(2,1)} %copy-done.16, bf16[1664,128]{1,0:T(8,128)(2,1)} %copy-done.7, bf16[1664,128]{1,0:T(8,128)(2,1)} %copy-done.8, bf16[1664,128]{1,0:T(8,128)(2,1)} %copy-done, ...), custom_call_target="tpu_custom_call" | custom-call | tf_op jit(solution)/shard_map/pallas_call | solution.py:33
  163.7 4.9 %collective-permute-start.24 = (bf16[1024,1024]{1,0:T(8,128)(2,1)}, bf16[1024,1024]{1,0:T(8,128)(2,1)S(1)}, u32[]{:S(2)}, u32[]{:S(2)}) collective-permute-start(bf16[1024,1024]{1,0:T(8,128)(2,1)} %shard_map.115.refs_5_), channel_id=1, source_target_pairs={{0,8},{8,0},{16,24},{24,16},{32,40},{40,32},{48,56},{56,48},{64,72... | collective-permute-start | bytes 6291464 | tf_op jit(solution)/shard_map/ppermute | solution.py:368
  168.6 0.9 slice.61
  169.6 1.9 collective-permute-start.22
  171.5 0.9 slice.59
  172.5 4.6 %collective-permute-start.19 = (bf16[768,128]{1,0:T(8,128)(2,1)S(1)}, bf16[768,128]{1,0:T(8,128)(2,1)S(1)}, u32[]{:S(2)}, u32[]{:S(2)}) collective-permute-start(bf16[768,128]{1,0:T(8,128)(2,1)S(1)} %slice.59), channel_id=1, source_target_pairs={{0,7},{1,0},{2,1},{3,2},{4,3},{5,4},{6,5},{7,6},{8,15},{9,8},{10,9... | collective-permute-start | bytes 589832 | tf_op jit(solution)/shard_map/ppermute | solution.py:372
  177.0 2.1 %collective-permute-done.22.refs_15_ = bf16[768,128]{1,0:T(8,128)(2,1)S(1)} collective-permute-done((bf16[768,128]{1,0:T(8,128)(2,1)S(1)}, bf16[768,128]{1,0:T(8,128)(2,1)S(1)}, u32[]{:S(2)}, u32[]{:S(2)}) %collective-permute-start.22) | collective-permute-done | bytes 196640 | tf_op jit(solution)/shard_map/ppermute | solution.py:372
  179.2 1.8 collective-permute-done.19.refs_14_
  181.0 3.1 %collective-permute-start.23 = (bf16[512,128]{1,0:T(8,128)(2,1)S(1)}, bf16[512,128]{1,0:T(8,128)(2,1)S(1)}, u32[]{:S(2)}, u32[]{:S(2)}) collective-permute-start(bf16[512,128]{1,0:T(8,128)(2,1)S(1)} %pad_maximum_fusion.2.last_own), channel_id=1, source_target_pairs={{0,8},{8,0},{16,24},{24,16},{32,40},{40,32},{48,56},{56,48},{64,72... | collective-permute-start | bytes 393224 | tf_op jit(solution)/shard_map/ppermute | solution.py:368
  184.1 1.0 collective-permute-done.23.last_far
  185.7 1.4 copy-done.4
  187.1 9.5 %shard_map.116.own = bf16[2064,128]{1,0:T(8,128)(2,1)} custom-call(bf16[512,128]{1,0:T(8,128)(2,1)} %copy-done.18, bf16[512,128]{1,0:T(8,128)(2,1)} %copy-done.26, bf16[16,128]{1,0:T(8,128)(2,1)} %get-tuple-element.65.vec_i, bf16[16,128]{1,0:T(8,128)(2,1)} %get-tuple-element.66.vec_j, bf16[1024,128]{1,0:T(8,128)(2,1)} %get-tuple-element.67.refs_0_.xa, ...), custom_call_target="tpu_custom_call" | custom-call | tf_op jit(solution)/shard_map/pallas_call | solution.py:33
  196.5 1.9 collective-permute-start.25
  198.5 2.1 %collective-permute-done.25.got = bf16[2064,128]{1,0:T(8,128)(2,1)S(1)} collective-permute-done((bf16[2064,128]{1,0:T(8,128)(2,1)}, bf16[2064,128]{1,0:T(8,128)(2,1)S(1)}, u32[]{:S(2)}, u32[]{:S(2)}) %collective-permute-start.25) | collective-permute-done | bytes 528416 | tf_op jit(solution)/shard_map/ppermute | solution.py:368
  200.6 0.8 copy-done.17
  201.4 3.0 %shard_map.117 = (bf16[1,1024]{1,0:T(2,128)(2,1)}, bf16[1,1024]{1,0:T(2,128)(2,1)}, bf16[1024,128]{1,0:T(8,128)(2,1)}, bf16[1024,128]{1,0:T(8,128)(2,1)}, bf16[1024,128]{1,0:T(8,128)(2,1)}) custom-call(bf16[2064,128]{1,0:T(8,128)(2,1)} %shard_map.116.own, bf16[2064,128]{1,0:T(8,128)(2,1)} %copy-done.17), custom_call_target="tpu_custom_call" | custom-call | tf_op jit(solution)/shard_map/pallas_call | solution.py:33
  (67 shorter events, 2.1 us)
Async XLA Ops:
  4.6 14.0 %collective-permute-start.2 = (bf16[1040,128]{1,0:T(8,128)(2,1)}, bf16[1040,128]{1,0:T(8,128)(2,1)S(1)}, u32[]{:S(2)}, u32[]{:S(2)}) collective-permute-start(bf16[1040,128]{1,0:T(8,128)(2,1)} %get-tuple-element.47), channel_id=1, source_target_pairs={{0,8},{8,0},{16,24},{24,16},{32,40},{40,32},{48,56},{56,48},{64,72... | collective-permute-start | bytes 798728 | tf_op jit(solution)/shard_map/ppermute | solution.py:368
  13.3 15.9 %collective-permute-start.1 = (bf16[1664,128]{1,0:T(8,128)(2,1)}, bf16[1664,128]{1,0:T(8,128)(2,1)S(1)}, u32[]{:S(2)}, u32[]{:S(2)}) collective-permute-start(bf16[1664,128]{1,0:T(8,128)(2,1)} %get-tuple-element.44.refs_6_), channel_id=1, source_target_pairs={{0,7},{1,0},{2,1},{3,2},{4,3},{5,4},{6,5},{7,6},{8,15},{9,8},{10,9... | collective-permute-start | bytes 1277960 | tf_op jit(solution)/shard_map/ppermute | solution.py:372
  15.2 14.0 %collective-permute-start = (bf16[1536,128]{1,0:T(8,128)(2,1)}, bf16[1536,128]{1,0:T(8,128)(2,1)S(1)}, u32[]{:S(2)}, u32[]{:S(2)}) collective-permute-start(bf16[1536,128]{1,0:T(8,128)(2,1)} %get-tuple-element.43), channel_id=1, source_target_pairs={{0,1},{1,2},{2,3},{3,4},{4,5},{5,6},{6,7},{7,0},{8,9},{9,10},{10,1... | collective-permute-start | bytes 1179656 | tf_op jit(solution)/shard_map/ppermute | solution.py:372
  18.6 64.5 %copy-start.25 = (bf16[1040,128]{1,0:T(8,128)(2,1)}, bf16[1040,128]{1,0:T(8,128)(2,1)S(1)}, u32[]{:S(2)}) copy-start(bf16[1040,128]{1,0:T(8,128)(2,1)S(1)} %collective-permute-done.2.refs_1_) | copy-start | bytes 798724
  29.2 27.9 %copy-start.10 = (bf16[1536,128]{1,0:T(8,128)(2,1)}, bf16[1536,128]{1,0:T(8,128)(2,1)S(1)}, u32[]{:S(2)}) copy-start(bf16[1536,128]{1,0:T(8,128)(2,1)S(1)} %collective-permute-done.p1.refs_10_) | copy-start | bytes 1179652
  29.2 27.9 %copy-start.6 = (bf16[1664,128]{1,0:T(8,128)(2,1)}, bf16[1664,128]{1,0:T(8,128)(2,1)S(1)}, u32[]{:S(2)}) copy-start(bf16[1664,128]{1,0:T(8,128)(2,1)S(1)} %collective-permute-done.1.m1.refs_7_) | copy-start | bytes 1277956
  29.2 12.4 %collective-permute-start.3 = (bf16[1664,128]{1,0:T(8,128)(2,1)S(1)}, bf16[1664,128]{1,0:T(8,128)(2,1)S(1)}, u32[]{:S(2)}, u32[]{:S(2)}) collective-permute-start(bf16[1664,128]{1,0:T(8,128)(2,1)S(1)} %collective-permute-done.1.m1.refs_7_), channel_id=1, source_target_pairs={{0,7},{1,0},{2,1},{3,2},{4,3},{5,4},{6,5},{7,6},{8,15},{9,8},{10,9... | collective-permute-start | bytes 1277960 | tf_op jit(solution)/shard_map/ppermute | solution.py:372
  31.1 13.9 %collective-permute-start.6 = (bf16[1536,128]{1,0:T(8,128)(2,1)S(1)}, bf16[1536,128]{1,0:T(8,128)(2,1)S(1)}, u32[]{:S(2)}, u32[]{:S(2)}) collective-permute-start(bf16[1536,128]{1,0:T(8,128)(2,1)S(1)} %collective-permute-done.p1.refs_10_), channel_id=1, source_target_pairs={{0,1},{1,2},{2,3},{3,4},{4,5},{5,6},{6,7},{7,0},{8,9},{9,10},{10,1... | collective-permute-start | bytes 1179656 | tf_op jit(solution)/shard_map/ppermute | solution.py:372
  41.6 15.5 %copy-start.9 = (bf16[1664,128]{1,0:T(8,128)(2,1)}, bf16[1664,128]{1,0:T(8,128)(2,1)S(1)}, u32[]{:S(2)}) copy-start(bf16[1664,128]{1,0:T(8,128)(2,1)S(1)} %collective-permute-done.3.m2.refs_8_) | copy-start | bytes 1277956
  41.6 15.5 %collective-permute-start.4 = (bf16[1664,128]{1,0:T(8,128)(2,1)S(1)}, bf16[1664,128]{1,0:T(8,128)(2,1)S(1)}, u32[]{:S(2)}, u32[]{:S(2)}) collective-permute-start(bf16[1664,128]{1,0:T(8,128)(2,1)S(1)} %collective-permute-done.3.m2.refs_8_), channel_id=1, source_target_pairs={{0,7},{1,0},{2,1},{3,2},{4,3},{5,4},{6,5},{7,6},{8,15},{9,8},{10,9... | collective-permute-start | bytes 1277960 | tf_op jit(solution)/shard_map/ppermute | solution.py:372
  45.0 12.1 %copy-start.13 = (bf16[1536,128]{1,0:T(8,128)(2,1)}, bf16[1536,128]{1,0:T(8,128)(2,1)S(1)}, u32[]{:S(2)}) copy-start(bf16[1536,128]{1,0:T(8,128)(2,1)S(1)} %collective-permute-done.6.p2.refs_11_) | copy-start | bytes 1179652
  45.0 12.1 %collective-permute-start.7 = (bf16[1536,128]{1,0:T(8,128)(2,1)S(1)}, bf16[1536,128]{1,0:T(8,128)(2,1)S(1)}, u32[]{:S(2)}, u32[]{:S(2)}) collective-permute-start(bf16[1536,128]{1,0:T(8,128)(2,1)S(1)} %collective-permute-done.6.p2.refs_11_), channel_id=1, source_target_pairs={{0,1},{1,2},{2,3},{3,4},{4,5},{5,6},{6,7},{7,0},{8,9},{9,10},{10,1... | collective-permute-start | bytes 1179656 | tf_op jit(solution)/shard_map/ppermute | solution.py:372
  57.1 0.8 copy-start.3
  57.8 0.8 copy-start.1
  62.3 20.9 %collective-permute-start.10 = (bf16[1024,1024]{1,0:T(8,128)(2,1)}, bf16[1024,1024]{1,0:T(8,128)(2,1)S(1)}, u32[]{:S(2)}, u32[]{:S(2)}) collective-permute-start(bf16[1024,1024]{1,0:T(8,128)(2,1)} %shard_map.112.refs_4_), channel_id=1, source_target_pairs={{0,8},{8,0},{16,24},{24,16},{32,40},{40,32},{48,56},{56,48},{64,72... | collective-permute-start | bytes 6291464 | tf_op jit(solution)/shard_map/ppermute | solution.py:368
  67.7 9.5 %collective-permute-start.8 = (bf16[768,128]{1,0:T(8,128)(2,1)S(1)}, bf16[768,128]{1,0:T(8,128)(2,1)S(1)}, u32[]{:S(2)}, u32[]{:S(2)}) collective-permute-start(bf16[768,128]{1,0:T(8,128)(2,1)S(1)} %slice.55), channel_id=1, source_target_pairs={{0,1},{1,2},{2,3},{3,4},{4,5},{5,6},{6,7},{7,0},{8,9},{9,10},{10,1... | collective-permute-start | bytes 589832 | tf_op jit(solution)/shard_map/ppermute | solution.py:372
  70.6 8.5 %collective-permute-start.5 = (bf16[768,128]{1,0:T(8,128)(2,1)S(1)}, bf16[768,128]{1,0:T(8,128)(2,1)S(1)}, u32[]{:S(2)}, u32[]{:S(2)}) collective-permute-start(bf16[768,128]{1,0:T(8,128)(2,1)S(1)} %slice.53), channel_id=1, source_target_pairs={{0,7},{1,0},{2,1},{3,2},{4,3},{5,4},{6,5},{7,6},{8,15},{9,8},{10,9... | collective-permute-start | bytes 589832 | tf_op jit(solution)/shard_map/ppermute | solution.py:372
  77.2 5.9 %copy-start.21 = (bf16[768,128]{1,0:T(8,128)(2,1)}, bf16[768,128]{1,0:T(8,128)(2,1)S(1)}, u32[]{:S(2)}) copy-start(bf16[768,128]{1,0:T(8,128)(2,1)S(1)} %collective-permute-done.8.refs_14_) | copy-start | bytes 589828
  79.1 4.1 %copy-start.23 = (bf16[768,128]{1,0:T(8,128)(2,1)}, bf16[768,128]{1,0:T(8,128)(2,1)S(1)}, u32[]{:S(2)}) copy-start(bf16[768,128]{1,0:T(8,128)(2,1)S(1)} %collective-permute-done.5.refs_13_) | copy-start | bytes 589828
  79.1 4.1 %copy-start.19 = (bf16[512,128]{1,0:T(8,128)(2,1)}, bf16[512,128]{1,0:T(8,128)(2,1)S(1)}, u32[]{:S(2)}) copy-start(bf16[512,128]{1,0:T(8,128)(2,1)S(1)} %pad_maximum_fusion.1.last_own) | copy-start | bytes 393220
  79.1 4.0 %collective-permute-start.9 = (bf16[512,128]{1,0:T(8,128)(2,1)S(1)}, bf16[512,128]{1,0:T(8,128)(2,1)S(1)}, u32[]{:S(2)}, u32[]{:S(2)}) collective-permute-start(bf16[512,128]{1,0:T(8,128)(2,1)S(1)} %pad_maximum_fusion.1.last_own), channel_id=1, source_target_pairs={{0,8},{8,0},{16,24},{24,16},{32,40},{40,32},{48,56},{56,48},{64,72... | collective-permute-start | bytes 393224 | tf_op jit(solution)/shard_map/ppermute | solution.py:368
  83.1 0.6 copy-start.27
  83.8 1.4 copy-start.5
  94.6 8.3 %collective-permute-start.11 = (bf16[1040,128]{1,0:T(8,128)(2,1)}, bf16[1040,128]{1,0:T(8,128)(2,1)S(1)}, u32[]{:S(2)}, u32[]{:S(2)}) collective-permute-start(bf16[1040,128]{1,0:T(8,128)(2,1)} %get-tuple-element.68.refs_1_), channel_id=1, source_target_pairs={{0,8},{8,0},{16,24},{24,16},{32,40},{40,32},{48,56},{56,48},{64,72... | collective-permute-start | bytes 798728 | tf_op jit(solution)/shard_map/ppermute | solution.py:368
  96.6 8.9 %collective-permute-start.12 = (bf16[1040,128]{1,0:T(8,128)(2,1)}, bf16[1040,128]{1,0:T(8,128)(2,1)S(1)}, u32[]{:S(2)}, u32[]{:S(2)}) collective-permute-start(bf16[1040,128]{1,0:T(8,128)(2,1)} %get-tuple-element.68.refs_1_), channel_id=1, source_target_pairs={{8,16},{24,8},{40,48},{56,40},{72,80},{88,72},{104,112},{120,104},... | collective-permute-start | bytes 798728 | tf_op jit(solution)/shard_map/ppermute | solution.py:475
  98.5 7.0 %collective-permute-start.13 = (bf16[1024,128]{1,0:T(8,128)(2,1)}, bf16[1024,128]{1,0:T(8,128)(2,1)S(1)}, u32[]{:S(2)}, u32[]{:S(2)}) collective-permute-start(bf16[1024,128]{1,0:T(8,128)(2,1)} %get-tuple-element.67.refs_0_.xa), channel_id=1, source_target_pairs={{8,24},{16,0},{40,56},{48,32},{72,88},{80,64},{104,120},{112,96},{... | collective-permute-start | bytes 786440 | tf_op jit(solution)/shard_map/ppermute | solution.py:478
  102.9 2.6 %copy-start.14 = (bf16[1040,128]{1,0:T(8,128)(2,1)}, bf16[1040,128]{1,0:T(8,128)(2,1)S(1)}, u32[]{:S(2)}) copy-start(bf16[1040,128]{1,0:T(8,128)(2,1)S(1)} %collective-permute-done.11.refs_2_) | copy-start | bytes 798724
  105.5 0.7 copy-start.16
  106.2 0.7 copy-start.15
  109.0 11.0 %collective-permute-start.16 = (bf16[1040,128]{1,0:T(8,128)(2,1)S(1)}, bf16[1040,128]{1,0:T(8,128)(2,1)S(1)}, u32[]{:S(2)}, u32[]{:S(2)}) collective-permute-start(bf16[1040,128]{1,0:T(8,128)(2,1)S(1)} %pad_maximum_fusion), channel_id=1, source_target_pairs={{0,16},{8,24},{16,0},{24,8},{32,48},{40,56},{48,32},{56,40},{64,80... | collective-permute-start | bytes 798728 | tf_op jit(solution)/shard_map/ppermute | solution.py:368
  112.7 18.9 %collective-permute-start.15 = (bf16[1664,128]{1,0:T(8,128)(2,1)}, bf16[1664,128]{1,0:T(8,128)(2,1)S(1)}, u32[]{:S(2)}, u32[]{:S(2)}) collective-permute-start(bf16[1664,128]{1,0:T(8,128)(2,1)} %get-tuple-element.61.refs_7_), channel_id=1, source_target_pairs={{0,7},{1,0},{2,1},{3,2},{4,3},{5,4},{6,5},{7,6},{8,15},{9,8},{10,9... | collective-permute-start | bytes 1277960 | tf_op jit(solution)/shard_map/ppermute | solution.py:372
  118.0 13.5 %collective-permute-start.14 = (bf16[1536,128]{1,0:T(8,128)(2,1)}, bf16[1536,128]{1,0:T(8,128)(2,1)S(1)}, u32[]{:S(2)}, u32[]{:S(2)}) collective-permute-start(bf16[1536,128]{1,0:T(8,128)(2,1)} %get-tuple-element.60), channel_id=1, source_target_pairs={{0,1},{1,2},{2,3},{3,4},{4,5},{5,6},{6,7},{7,0},{8,9},{9,10},{10,1... | collective-permute-start | bytes 1179656 | tf_op jit(solution)/shard_map/ppermute | solution.py:372
  120.0 65.1 %copy-start.24 = (bf16[1040,128]{1,0:T(8,128)(2,1)}, bf16[1040,128]{1,0:T(8,128)(2,1)S(1)}, u32[]{:S(2)}) copy-start(bf16[1040,128]{1,0:T(8,128)(2,1)S(1)} %collective-permute-done.16.refs_4_) | copy-start | bytes 798724
  131.6 27.0 %copy-start.11 = (bf16[1536,128]{1,0:T(8,128)(2,1)}, bf16[1536,128]{1,0:T(8,128)(2,1)S(1)}, u32[]{:S(2)}) copy-start(bf16[1536,128]{1,0:T(8,128)(2,1)S(1)} %collective-permute-done.14.p1.refs_11_) | copy-start | bytes 1179652
  131.6 27.0 %copy-start.7 = (bf16[1664,128]{1,0:T(8,128)(2,1)}, bf16[1664,128]{1,0:T(8,128)(2,1)S(1)}, u32[]{:S(2)}) copy-start(bf16[1664,128]{1,0:T(8,128)(2,1)S(1)} %collective-permute-done.15.m1.refs_8_) | copy-start | bytes 1277956
  131.6 12.0 %collective-permute-start.17 = (bf16[1664,128]{1,0:T(8,128)(2,1)S(1)}, bf16[1664,128]{1,0:T(8,128)(2,1)S(1)}, u32[]{:S(2)}, u32[]{:S(2)}) collective-permute-start(bf16[1664,128]{1,0:T(8,128)(2,1)S(1)} %collective-permute-done.15.m1.refs_8_), channel_id=1, source_target_pairs={{0,7},{1,0},{2,1},{3,2},{4,3},{5,4},{6,5},{7,6},{8,15},{9,8},{10,9... | collective-permute-start | bytes 1277960 | tf_op jit(solution)/shard_map/ppermute | solution.py:372
  133.5 13.5 %collective-permute-start.20 = (bf16[1536,128]{1,0:T(8,128)(2,1)S(1)}, bf16[1536,128]{1,0:T(8,128)(2,1)S(1)}, u32[]{:S(2)}, u32[]{:S(2)}) collective-permute-start(bf16[1536,128]{1,0:T(8,128)(2,1)S(1)} %collective-permute-done.14.p1.refs_11_), channel_id=1, source_target_pairs={{0,1},{1,2},{2,3},{3,4},{4,5},{5,6},{6,7},{7,0},{8,9},{9,10},{10,1... | collective-permute-start | bytes 1179656 | tf_op jit(solution)/shard_map/ppermute | solution.py:372
  143.5 15.1 %copy-start.8 = (bf16[1664,128]{1,0:T(8,128)(2,1)}, bf16[1664,128]{1,0:T(8,128)(2,1)S(1)}, u32[]{:S(2)}) copy-start(bf16[1664,128]{1,0:T(8,128)(2,1)S(1)} %collective-permute-done.17.m2.refs_9_) | copy-start | bytes 1277956
  143.5 15.1 %collective-permute-start.18 = (bf16[1664,128]{1,0:T(8,128)(2,1)S(1)}, bf16[1664,128]{1,0:T(8,128)(2,1)S(1)}, u32[]{:S(2)}, u32[]{:S(2)}) collective-permute-start(bf16[1664,128]{1,0:T(8,128)(2,1)S(1)} %collective-permute-done.17.m2.refs_9_), channel_id=1, source_target_pairs={{0,7},{1,0},{2,1},{3,2},{4,3},{5,4},{6,5},{7,6},{8,15},{9,8},{10,9... | collective-permute-start | bytes 1277960 | tf_op jit(solution)/shard_map/ppermute | solution.py:372
  147.0 11.7 %copy-start.12 = (bf16[1536,128]{1,0:T(8,128)(2,1)}, bf16[1536,128]{1,0:T(8,128)(2,1)S(1)}, u32[]{:S(2)}) copy-start(bf16[1536,128]{1,0:T(8,128)(2,1)S(1)} %collective-permute-done.20.p2.refs_12_) | copy-start | bytes 1179652
  147.0 11.6 %collective-permute-start.21 = (bf16[1536,128]{1,0:T(8,128)(2,1)S(1)}, bf16[1536,128]{1,0:T(8,128)(2,1)S(1)}, u32[]{:S(2)}, u32[]{:S(2)}) collective-permute-start(bf16[1536,128]{1,0:T(8,128)(2,1)S(1)} %collective-permute-done.20.p2.refs_12_), channel_id=1, source_target_pairs={{0,1},{1,2},{2,3},{3,4},{4,5},{5,6},{6,7},{7,0},{8,9},{9,10},{10,1... | collective-permute-start | bytes 1179656 | tf_op jit(solution)/shard_map/ppermute | solution.py:372
  158.6 0.7 copy-start.2
  159.3 0.8 copy-start
  163.7 21.3 %collective-permute-start.24 = (bf16[1024,1024]{1,0:T(8,128)(2,1)}, bf16[1024,1024]{1,0:T(8,128)(2,1)S(1)}, u32[]{:S(2)}, u32[]{:S(2)}) collective-permute-start(bf16[1024,1024]{1,0:T(8,128)(2,1)} %shard_map.115.refs_5_), channel_id=1, source_target_pairs={{0,8},{8,0},{16,24},{24,16},{32,40},{40,32},{48,56},{56,48},{64,72... | collective-permute-start | bytes 6291464 | tf_op jit(solution)/shard_map/ppermute | solution.py:368
  169.6 9.5 %collective-permute-start.22 = (bf16[768,128]{1,0:T(8,128)(2,1)S(1)}, bf16[768,128]{1,0:T(8,128)(2,1)S(1)}, u32[]{:S(2)}, u32[]{:S(2)}) collective-permute-start(bf16[768,128]{1,0:T(8,128)(2,1)S(1)} %slice.61), channel_id=1, source_target_pairs={{0,1},{1,2},{2,3},{3,4},{4,5},{5,6},{6,7},{7,0},{8,9},{9,10},{10,1... | collective-permute-start | bytes 589832 | tf_op jit(solution)/shard_map/ppermute | solution.py:372
  172.5 8.5 %collective-permute-start.19 = (bf16[768,128]{1,0:T(8,128)(2,1)S(1)}, bf16[768,128]{1,0:T(8,128)(2,1)S(1)}, u32[]{:S(2)}, u32[]{:S(2)}) collective-permute-start(bf16[768,128]{1,0:T(8,128)(2,1)S(1)} %slice.59), channel_id=1, source_target_pairs={{0,7},{1,0},{2,1},{3,2},{4,3},{5,4},{6,5},{7,6},{8,15},{9,8},{10,9... | collective-permute-start | bytes 589832 | tf_op jit(solution)/shard_map/ppermute | solution.py:372
  179.1 5.9 %copy-start.20 = (bf16[768,128]{1,0:T(8,128)(2,1)}, bf16[768,128]{1,0:T(8,128)(2,1)S(1)}, u32[]{:S(2)}) copy-start(bf16[768,128]{1,0:T(8,128)(2,1)S(1)} %collective-permute-done.22.refs_15_) | copy-start | bytes 589828
  181.0 4.1 %copy-start.22 = (bf16[768,128]{1,0:T(8,128)(2,1)}, bf16[768,128]{1,0:T(8,128)(2,1)S(1)}, u32[]{:S(2)}) copy-start(bf16[768,128]{1,0:T(8,128)(2,1)S(1)} %collective-permute-done.19.refs_14_) | copy-start | bytes 589828
  181.0 4.1 %copy-start.18 = (bf16[512,128]{1,0:T(8,128)(2,1)}, bf16[512,128]{1,0:T(8,128)(2,1)S(1)}, u32[]{:S(2)}) copy-start(bf16[512,128]{1,0:T(8,128)(2,1)S(1)} %pad_maximum_fusion.2.last_own) | copy-start | bytes 393220
  181.0 4.0 %collective-permute-start.23 = (bf16[512,128]{1,0:T(8,128)(2,1)S(1)}, bf16[512,128]{1,0:T(8,128)(2,1)S(1)}, u32[]{:S(2)}, u32[]{:S(2)}) collective-permute-start(bf16[512,128]{1,0:T(8,128)(2,1)S(1)} %pad_maximum_fusion.2.last_own), channel_id=1, source_target_pairs={{0,8},{8,0},{16,24},{24,16},{32,40},{40,32},{48,56},{56,48},{64,72... | collective-permute-start | bytes 393224 | tf_op jit(solution)/shard_map/ppermute | solution.py:368
  185.1 0.7 copy-start.26
  185.7 1.4 copy-start.4
  196.5 4.0 %collective-permute-start.25 = (bf16[2064,128]{1,0:T(8,128)(2,1)}, bf16[2064,128]{1,0:T(8,128)(2,1)S(1)}, u32[]{:S(2)}, u32[]{:S(2)}) collective-permute-start(bf16[2064,128]{1,0:T(8,128)(2,1)} %shard_map.116.own), channel_id=1, source_target_pairs={{0,8},{8,0},{16,24},{24,16},{32,40},{40,32},{48,56},{56,48},{64,72... | collective-permute-start | bytes 1585160 | tf_op jit(solution)/shard_map/ppermute | solution.py:368
  200.6 0.8 copy-start.17

commit v6 on v5

--- a/solution.py
+++ b/solution.py
@@ -12,8 +12,7 @@
 W = 128
 N = 8
 D = W * N
-UP = 1536
-DOWN = 1664
+RING = 1664
 HALF = 768
 INTERPRET = False
 
@@ -54,32 +53,28 @@
 
 
 def stream(pieces, buf, sems_in, sems_out):
-    ins, outs = [], []
-    for k, (src, a, targets) in enumerate(pieces):
-        part = buf.at[pl.ds(k * W, W)]
-        ins.append(pltpu.make_async_copy(src.at[pl.ds(a, W)], part, sems_in.at[k]))
-        outs.append(
-            [
-                pltpu.make_async_copy(part, dst.at[pl.ds(b, W)], sems_out.at[2 * k + i])
-                for i, (dst, b) in enumerate(targets)
-            ]
-        )
+    ins = [
+        pltpu.make_async_copy(src.at[pl.ds(a, W)], buf.at[pl.ds(k * W, W)], sems_in.at[k])
+        for k, (src, a, _, _) in enumerate(pieces)
+    ]
+    outs = [
+        pltpu.make_async_copy(buf.at[pl.ds(k * W, W)], dst.at[pl.ds(b, W)], sems_out.at[k])
+        for k, (_, _, dst, b) in enumerate(pieces)
+    ]
     for c in ins:
         c.start()
-    for c, group in zip(ins, outs):
+    for c, o in zip(ins, outs):
         c.wait()
-        for o in group:
-            o.start()
-    for group in outs:
-        for o in group:
-            o.wait()
+        o.start()
+    for o in outs:
+        o.wait()
 
 
 def streaming(pieces):
     return (
         pltpu.VMEM((pieces * W, W), bf16),
         pltpu.SemaphoreType.DMA((pieces,)),
-        pltpu.SemaphoreType.DMA((2 * pieces,)),
+        pltpu.SemaphoreType.DMA((pieces,)),
     )
 
 
@@ -123,16 +118,15 @@
 
 
 def ring_kernel(sources, *refs):
-    *inputs, up, down, buf, sems_in, sems_out = refs
+    *inputs, msg, buf, sems_in, sems_out = refs
     q = place()[2]
 
     def run(core, odd):
         x, a = (inputs[k] for k in sources(core, odd))
         spots = [(a, k * W, k * W if k < 4 else 512 + k * W) for k in range(N)]
         spots += [(x, at((q + d) % N), 512 + d * W) for d in range(4)]
-        pieces = [(src, row, [(down, to), (up, to)]) for src, row, to in spots]
-        pieces += [(x, at((q + 4) % N), [(down, UP)])]
-        stream(pieces, buf, sems_in, sems_out)
+        spots += [(x, at((q + 4) % N), 1536)]
+        stream([(src, row, msg, to) for src, row, to in spots], buf, sems_in, sems_out)
 
     each_state(run)
 
@@ -223,11 +217,19 @@
         for c in group:
             c.wait()
 
+    top_half = q < N // 2
+    halves = copies[0::2], copies[1::2]
+
+    def by_half(act, first):
+        pl.when(top_half)(lambda: act(halves[0 if first else 1]))
+        pl.when(jnp.logical_not(top_half))(lambda: act(halves[1 if first else 0]))
+
     @pl.when(core == 1)
     def _():
-        start(copies)
+        by_half(start, True)
         start(own_copies if own_is_cov else far_copies)
         start(far_copies if own_is_cov else own_copies)
+        by_half(start, False)
 
     @pl.when(core == 0)
     def _():
@@ -268,7 +270,7 @@
         side_copies[0].wait()
         rotated_move(base, W)
         r[W : W + 16, :] = as_rows(eta)
-        wait(copies)
+        by_half(wait, True)
         r[0:W, :] = a_full[blk(q), :]
         first_ready()
         out = dot(r[0 : W + 16, :], cov[...])
@@ -282,6 +284,7 @@
             out = dot(t[...], cov[...])
             r[0 : 2 * W, :] = (base[...].astype(f32) - out[0 : 2 * W]).astype(bf16)
             r[2 * W : 2 * W + 16, :] = as_rows(w - out[2 * W : 2 * W + 1])
+        by_half(wait, False)
         res = lax.dot_general(
             r[...], a_full[...], (((1,), (1,)), ((), ())), preferred_element_type=f32
         )
@@ -337,28 +340,18 @@
         out2[D : D + 2 * N, :] = jnp.where(rows < N, 0.0, vecs[...]).astype(bf16)
 
 
-def finish_kernel(own, got, drift, belief, move, spread, weight, buf, sems_in, sems_out, vec, sems):
+def finish_kernel(own, got, drift, belief, move, spread, weight):
     core = place()[0]
 
     def put(early, late):
-        tails = [
-            pltpu.make_async_copy(
-                src.at[pl.ds(2 * D, 2 * N)], vec.at[pl.ds(k * 2 * N, 2 * N)], sems.at[k]
-            )
-            for k, src in enumerate((early, late))
-        ]
-        for c in tails:
-            c.start()
-        pieces = []
-        for src, first, dst in ((early, 0, spread), (early, D, move), (late, 0, weight)):
-            pieces += [(src, first + k * W, [(dst, k * W)]) for k in range(N)]
-        stream(pieces, buf, sems_in, sems_out)
-        for c in tails:
-            c.wait()
-        rows = vec[...].astype(f32)
-        for l in range(N):
-            drift[:, l * W : (l + 1) * W] = rows[l : l + 1, :].astype(bf16)
-            belief[:, l * W : (l + 1) * W] = rows[3 * N + l : 3 * N + l + 1, :].astype(bf16)
+        spread[...] = early[0:D, :]
+        move[...] = early[D : 2 * D, :]
+        weight[...] = late[0:D, :]
+        b = early[2 * D : 2 * D + 2 * N, :].astype(f32)
+        e = late[2 * D : 2 * D + 2 * N, :].astype(f32)
+        for l in range(N):
+            drift[:, l * W : (l + 1) * W] = b[l : l + 1, :].astype(bf16)
+            belief[:, l * W : (l + 1) * W] = e[N + l : N + l + 1, :].astype(bf16)
 
     pl.when(core == 1)(lambda: put(own, got))
     pl.when(core == 0)(lambda: put(got, own))
@@ -373,19 +366,19 @@
 
 
 def combined(own_is_cov, outs, x_pair, x_pick, ring_refs, sources, gate, side, sides):
-    up, down = call(
+    (msg,) = call(
         functools.partial(ring_kernel, sources),
-        [struct(UP, W), struct(DOWN, W)],
-        streaming(DOWN // W),
+        [struct(RING, W)],
+        streaming(RING // W),
         *ring_refs,
         vmem=0,
         vmem_out=False,
     )
-    up, down, gate = lax.optimization_barrier((up, down, gate))
-    p1 = shift(up, 1)
-    m1 = shift(down, -1)
-    p1, m1, (vec_i, vec_j, side_refs) = lax.optimization_barrier((p1, m1, side(gate)))
+    msg, gate = lax.optimization_barrier((msg, gate))
+    p1 = shift(msg, 1)
+    m1 = shift(msg, -1)
     p2, m2 = shift(p1, 1), shift(m1, -1)
+    p2, (vec_i, vec_j, side_refs) = lax.optimization_barrier((p2, side(gate)))
     p3, m3 = shift(p2, 1), shift(m2, -1)
     p4 = shift(p3[HALF : 2 * HALF], 1)
     m4 = shift(m3[0:HALF], -1)
@@ -426,7 +419,7 @@
         *side_refs,
         x_here,
         x_far,
-        down,
+        msg,
         m1,
         m2,
         m3,
@@ -508,11 +501,9 @@
     drift, belief, move, cov, info = call(
         finish_kernel,
         [row, row, panel, panel, panel],
-        streaming(3 * N) + (pltpu.VMEM((4 * N, W), bf16), pltpu.SemaphoreType.DMA((2,))),
+        (),
         own,
         got,
-        vmem=0,
-        vmem_out=[True, True, False, False, False],
     )
     return move[None], drift, cov[None], belief, info[None]
 

time: 206 us -> 190 us (0.922)
  waiting for transfers between devices: 67.6 us -> 46.9 us
  starting transfers between devices: 83.8 us -> 90.4 us
    ppermute x16, waiting for transfers between devices: 61.6 us -> 40 us  [shift(): return lax.ppermute(x, 'panel', [(i, (i + by) % N) for i in range(N)])]
    ppermute x16, starting transfers between devices: 46.7 us -> 54.8 us  [shift(): return lax.ppermute(x, 'panel', [(i, (i + by) % N) for i in range(N)])]
  transfers between devices with their start and end apart: 26 -> 26, of which waited for: 14 -> 15; matrix products, arithmetic and copies ran while one was open for 4% -> 4% of each run, Pallas kernels for 0% -> 1%
where the time goes in v6:
time: 190 us; the launch traced here: 187 us
  starting transfers between devices  90.4 us (48%)
  waiting for transfers between devices  46.9 us (25%)
  Pallas kernels  33.7 us (18%)
  local copies, waits for them, and re-layouts  11.6 us (6%)
  other arithmetic  3.71 us (2%)
    ppermute x16, starting transfers between devices, shift(): return lax.ppermute(x, 'panel', [(i, (i + by) % N) for i in range(N)])  54.8 us
    ppermute x16, waiting for transfers between devices, shift(): return lax.ppermute(x, 'panel', [(i, (i + by) % N) for i in range(N)])  40 us
    pallas_call x8, Pallas kernels, call(): pl.pallas_call(kernel, out_shape=list(out_shape), in_specs=[vm] * staged...  33.7 us
    ppermute x8, starting transfers between devices, swap(): lax.ppermute(x, 'tm', [(i, i ^ 1 << axis_bit) for i in range(lax.axis_siz...  30.3 us
    unnamed x56, local copies, waits for them, and re-layouts  7.81 us
    ppermute x8, waiting for transfers between devices, swap(): lax.ppermute(x, 'tm', [(i, i ^ 1 << axis_bit) for i in range(lax.axis_siz...  4.03 us
  transfers between devices with their start and end apart: 26, of which 15 were waited for; matrix products, arithmetic and copies ran while one was open for 4% of the time, Pallas kernels for 1%

profile of v6, /device:TPU:1, one launch (start us, length us, event | category | flops | bytes accessed | tf_op | source)
XLA Modules:
  0.0 187.5 jit_solution(16791156895153210521)
XLA Ops:
  0.6 1.8 shard_map.110.refs_6_
  2.5 4.0 %collective-permute-start.4 = (bf16[1664,128]{1,0:T(8,128)(2,1)}, bf16[1664,128]{1,0:T(8,128)(2,1)S(1)}, u32[]{:S(2)}, u32[]{:S(2)}) collective-permute-start(bf16[1664,128]{1,0:T(8,128)(2,1)} %shard_map.110.refs_6_), channel_id=1, source_target_pairs={{0,1},{1,2},{2,3},{3,4},{4,5},{5,6},{6,7},{7,0},{8,9},{9,10},{10,1... | collective-permute-start | bytes 1277960 | tf_op jit(solution)/shard_map/ppermute | solution.py:365
  6.5 3.8 %collective-permute-start = (bf16[1664,128]{1,0:T(8,128)(2,1)}, bf16[1664,128]{1,0:T(8,128)(2,1)S(1)}, u32[]{:S(2)}, u32[]{:S(2)}) collective-permute-start(bf16[1664,128]{1,0:T(8,128)(2,1)} %shard_map.110.refs_6_), channel_id=1, source_target_pairs={{0,7},{1,0},{2,1},{3,2},{4,3},{5,4},{6,5},{7,6},{8,15},{9,8},{10,9... | collective-permute-start | bytes 1277960 | tf_op jit(solution)/shard_map/ppermute | solution.py:365
  10.3 1.9 %shard_map.111 = (bf16[1040,128]{1,0:T(8,128)(2,1)}, bf16[16,128]{1,0:T(8,128)(2,1)}) custom-call(bf16[1024,128]{1,0:T(8,128)(2,1)} %bitcast.13, bf16[1,1024]{1,0:T(2,128)(2,1)} %drift, bf16[1,1024]{1,0:T(2,128)(2,1)} %belief.1, s32[1,256]{1,0:T(1,128)} %hosts.1, f32[1,256]{1,0:T(1,128)} %values.1), custom_call_target="tpu_custom_call" | custom-call | tf_op jit(solution)/shard_map/pallas_call | solution.py:32
  12.2 7.9 %collective-permute-start.6 = (bf16[1040,128]{1,0:T(8,128)(2,1)}, bf16[1040,128]{1,0:T(8,128)(2,1)S(1)}, u32[]{:S(2)}, u32[]{:S(2)}) collective-permute-start(bf16[1040,128]{1,0:T(8,128)(2,1)} %get-tuple-element.36), channel_id=1, source_target_pairs={{0,8},{8,0},{16,24},{24,16},{32,40},{40,32},{48,56},{56,48},{64,72... | collective-permute-start | bytes 798728 | tf_op jit(solution)/shard_map/ppermute | solution.py:361
  20.2 1.9 %collective-permute-start.5 = (bf16[1664,128]{1,0:T(8,128)(2,1)S(1)}, bf16[1664,128]{1,0:T(8,128)(2,1)S(1)}, u32[]{:S(2)}, u32[]{:S(2)}) collective-permute-start(bf16[1664,128]{1,0:T(8,128)(2,1)S(1)} %collective-permute-done.4.p1.refs_10_), channel_id=1, source_target_pairs={{0,1},{1,2},{2,3},{3,4},{4,5},{5,6},{6,7},{7,0},{8,9},{9,10},{10,1... | collective-permute-start | bytes 1277960 | tf_op jit(solution)/shard_map/ppermute | solution.py:365
  22.1 4.6 %collective-permute-start.1 = (bf16[1664,128]{1,0:T(8,128)(2,1)S(1)}, bf16[1664,128]{1,0:T(8,128)(2,1)S(1)}, u32[]{:S(2)}, u32[]{:S(2)}) collective-permute-start(bf16[1664,128]{1,0:T(8,128)(2,1)S(1)} %collective-permute-done.m1.refs_7_), channel_id=1, source_target_pairs={{0,7},{1,0},{2,1},{3,2},{4,3},{5,4},{6,5},{7,6},{8,15},{9,8},{10,9... | collective-permute-start | bytes 1277960 | tf_op jit(solution)/shard_map/ppermute | solution.py:365
  26.7 1.3 broadcast_select_fusion.2
  28.1 6.0 %collective-permute-done.5.p2.refs_11_ = bf16[1664,128]{1,0:T(8,128)(2,1)S(1)} collective-permute-done((bf16[1664,128]{1,0:T(8,128)(2,1)S(1)}, bf16[1664,128]{1,0:T(8,128)(2,1)S(1)}, u32[]{:S(2)}, u32[]{:S(2)}) %collective-permute-start.5) | collective-permute-done | bytes 426016 | tf_op jit(solution)/shard_map/ppermute | solution.py:365
  34.1 1.9 %collective-permute-start.7 = (bf16[1664,128]{1,0:T(8,128)(2,1)S(1)}, bf16[1664,128]{1,0:T(8,128)(2,1)S(1)}, u32[]{:S(2)}, u32[]{:S(2)}) collective-permute-start(bf16[1664,128]{1,0:T(8,128)(2,1)S(1)} %collective-permute-done.5.p2.refs_11_), channel_id=1, source_target_pairs={{0,1},{1,2},{2,3},{3,4},{4,5},{5,6},{6,7},{7,0},{8,9},{9,10},{10,1... | collective-permute-start | bytes 1277960 | tf_op jit(solution)/shard_map/ppermute | solution.py:365
  36.1 4.6 %collective-permute-start.2 = (bf16[1664,128]{1,0:T(8,128)(2,1)S(1)}, bf16[1664,128]{1,0:T(8,128)(2,1)S(1)}, u32[]{:S(2)}, u32[]{:S(2)}) collective-permute-start(bf16[1664,128]{1,0:T(8,128)(2,1)S(1)} %collective-permute-done.1.m2.refs_8_), channel_id=1, source_target_pairs={{0,7},{1,0},{2,1},{3,2},{4,3},{5,4},{6,5},{7,6},{8,15},{9,8},{10,9... | collective-permute-start | bytes 1277960 | tf_op jit(solution)/shard_map/ppermute | solution.py:365
  40.6 6.6 %collective-permute-done.7.p3.refs_12_ = bf16[1664,128]{1,0:T(8,128)(2,1)S(1)} collective-permute-done((bf16[1664,128]{1,0:T(8,128)(2,1)S(1)}, bf16[1664,128]{1,0:T(8,128)(2,1)S(1)}, u32[]{:S(2)}, u32[]{:S(2)}) %collective-permute-start.7) | collective-permute-done | bytes 426016 | tf_op jit(solution)/shard_map/ppermute | solution.py:365
  47.2 0.9 collective-permute-done.2.m3.refs_9_
  48.1 0.8 copy-done.3
  48.9 3.7 %shard_map.112.refs_4_ = bf16[1024,1024]{1,0:T(8,128)(2,1)} custom-call(bf16[1024,128]{1,0:T(8,128)(2,1)} %bitcast.7, bf16[1024,128]{1,0:T(8,128)(2,1)} %bitcast.10, bf16[1664,128]{1,0:T(8,128)(2,1)} %copy-done.7, bf16[1664,128]{1,0:T(8,128)(2,1)} %copy-done.11, bf16[1664,128]{1,0:T(8,128)(2,1)} %copy-done.3, bf16[1664,128]{1,0:T(8,128)(2,1)} %copy-done.6, ...), custom_call_target="tpu_custom_call" | custom-call | tf_op jit(solution)/shard_map/pallas_call | solution.py:32
  52.6 4.4 %collective-permute-start.10 = (bf16[1024,1024]{1,0:T(8,128)(2,1)}, bf16[1024,1024]{1,0:T(8,128)(2,1)S(1)}, u32[]{:S(2)}, u32[]{:S(2)}) collective-permute-start(bf16[1024,1024]{1,0:T(8,128)(2,1)} %shard_map.112.refs_4_), channel_id=1, source_target_pairs={{0,8},{8,0},{16,24},{24,16},{32,40},{40,32},{48,56},{56,48},{64,72... | collective-permute-start | bytes 6291464 | tf_op jit(solution)/shard_map/ppermute | solution.py:361
  57.0 0.9 slice.55
  58.0 1.9 %collective-permute-start.8 = (bf16[768,128]{1,0:T(8,128)(2,1)S(1)}, bf16[768,128]{1,0:T(8,128)(2,1)S(1)}, u32[]{:S(2)}, u32[]{:S(2)}) collective-permute-start(bf16[768,128]{1,0:T(8,128)(2,1)S(1)} %slice.55), channel_id=1, source_target_pairs={{0,1},{1,2},{2,3},{3,4},{4,5},{5,6},{6,7},{7,0},{8,9},{9,10},{10,1... | collective-permute-start | bytes 589832 | tf_op jit(solution)/shard_map/ppermute | solution.py:365
  59.9 0.9 slice.52
  60.8 5.3 %collective-permute-start.3 = (bf16[768,128]{1,0:T(8,128)(2,1)S(1)}, bf16[768,128]{1,0:T(8,128)(2,1)S(1)}, u32[]{:S(2)}, u32[]{:S(2)}) collective-permute-start(bf16[768,128]{1,0:T(8,128)(2,1)S(1)} %slice.52), channel_id=1, source_target_pairs={{0,7},{1,0},{2,1},{3,2},{4,3},{5,4},{6,5},{7,6},{8,15},{9,8},{10,9... | collective-permute-start | bytes 589832 | tf_op jit(solution)/shard_map/ppermute | solution.py:365
  66.2 2.4 %collective-permute-done.8.refs_14_ = bf16[768,128]{1,0:T(8,128)(2,1)S(1)} collective-permute-done((bf16[768,128]{1,0:T(8,128)(2,1)S(1)}, bf16[768,128]{1,0:T(8,128)(2,1)S(1)}, u32[]{:S(2)}, u32[]{:S(2)}) %collective-permute-start.8) | collective-permute-done | bytes 196640 | tf_op jit(solution)/shard_map/ppermute | solution.py:365
  68.6 1.8 collective-permute-done.3.refs_13_
  70.4 2.8 %collective-permute-start.9 = (bf16[512,128]{1,0:T(8,128)(2,1)S(1)}, bf16[512,128]{1,0:T(8,128)(2,1)S(1)}, u32[]{:S(2)}, u32[]{:S(2)}) collective-permute-start(bf16[512,128]{1,0:T(8,128)(2,1)S(1)} %pad_maximum_fusion.1.last_own), channel_id=1, source_target_pairs={{0,8},{8,0},{16,24},{24,16},{32,40},{40,32},{48,56},{56,48},{64,72... | collective-permute-start | bytes 393224 | tf_op jit(solution)/shard_map/ppermute | solution.py:361
  73.2 1.0 collective-permute-done.9.last_far
  74.8 1.4 copy-done.5
  76.2 9.3 %shard_map.113 = (bf16[1024,128]{1,0:T(8,128)(2,1)}, bf16[1040,128]{1,0:T(8,128)(2,1)}) custom-call(bf16[512,128]{1,0:T(8,128)(2,1)} %copy-done.19, bf16[512,128]{1,0:T(8,128)(2,1)} %copy-done.27, bf16[16,128]{1,0:T(8,128)(2,1)} %get-tuple-element.38.vec_i, bf16[16,128]{1,0:T(8,128)(2,1)} %get-tuple-element.39.vec_j, bf16[1024,128]{1,0:T(8,128)(2,1)} %bitcast.14, ...), custom_call_target="tpu_custom_call" | custom-call | tf_op jit(solution)/shard_map/pallas_call | solution.py:32
  85.5 1.9 %collective-permute-start.11 = (bf16[1040,128]{1,0:T(8,128)(2,1)}, bf16[1040,128]{1,0:T(8,128)(2,1)S(1)}, u32[]{:S(2)}, u32[]{:S(2)}) collective-permute-start(bf16[1040,128]{1,0:T(8,128)(2,1)} %get-tuple-element.52.refs_1_), channel_id=1, source_target_pairs={{0,8},{8,0},{16,24},{24,16},{32,40},{40,32},{48,56},{56,48},{64,72... | collective-permute-start | bytes 798728 | tf_op jit(solution)/shard_map/ppermute | solution.py:361
  87.5 2.3 %collective-permute-start.12 = (bf16[1040,128]{1,0:T(8,128)(2,1)}, bf16[1040,128]{1,0:T(8,128)(2,1)S(1)}, u32[]{:S(2)}, u32[]{:S(2)}) collective-permute-start(bf16[1040,128]{1,0:T(8,128)(2,1)} %get-tuple-element.52.refs_1_), channel_id=1, source_target_pairs={{8,16},{24,8},{40,48},{56,40},{72,80},{88,72},{104,112},{120,104},... | collective-permute-start | bytes 798728 | tf_op jit(solution)/shard_map/ppermute | solution.py:468
  89.8 3.0 %collective-permute-start.13 = (bf16[1024,128]{1,0:T(8,128)(2,1)}, bf16[1024,128]{1,0:T(8,128)(2,1)S(1)}, u32[]{:S(2)}, u32[]{:S(2)}) collective-permute-start(bf16[1024,128]{1,0:T(8,128)(2,1)} %get-tuple-element.51.refs_0_.xa), channel_id=1, source_target_pairs={{8,24},{16,0},{40,56},{48,32},{72,88},{80,64},{104,120},{112,96},{... | collective-permute-start | bytes 786440 | tf_op jit(solution)/shard_map/ppermute | solution.py:471
  92.8 0.7 slice_add_fusion
  93.5 2.9 %collective-permute-done.13.refs_4_.xb = bf16[1024,128]{1,0:T(8,128)(2,1)S(1)} collective-permute-done((bf16[1024,128]{1,0:T(8,128)(2,1)}, bf16[1024,128]{1,0:T(8,128)(2,1)S(1)}, u32[]{:S(2)}, u32[]{:S(2)}) %collective-permute-start.13) | collective-permute-done | bytes 262176 | tf_op jit(solution)/shard_map/ppermute | solution.py:471
  96.4 0.7 copy-done.16
  97.1 0.7 copy-done.15
  97.8 1.8 shard_map.114.refs_7_
  99.6 4.4 %collective-permute-start.18 = (bf16[1664,128]{1,0:T(8,128)(2,1)}, bf16[1664,128]{1,0:T(8,128)(2,1)S(1)}, u32[]{:S(2)}, u32[]{:S(2)}) collective-permute-start(bf16[1664,128]{1,0:T(8,128)(2,1)} %shard_map.114.refs_7_), channel_id=1, source_target_pairs={{0,1},{1,2},{2,3},{3,4},{4,5},{5,6},{6,7},{7,0},{8,9},{9,10},{10,1... | collective-permute-start | bytes 1277960 | tf_op jit(solution)/shard_map/ppermute | solution.py:365
  104.1 2.8 %collective-permute-start.14 = (bf16[1664,128]{1,0:T(8,128)(2,1)}, bf16[1664,128]{1,0:T(8,128)(2,1)S(1)}, u32[]{:S(2)}, u32[]{:S(2)}) collective-permute-start(bf16[1664,128]{1,0:T(8,128)(2,1)} %shard_map.114.refs_7_), channel_id=1, source_target_pairs={{0,7},{1,0},{2,1},{3,2},{4,3},{5,4},{6,5},{7,6},{8,15},{9,8},{10,9... | collective-permute-start | bytes 1277960 | tf_op jit(solution)/shard_map/ppermute | solution.py:365
  106.9 1.0 slice_select_fusion
  107.9 3.8 %collective-permute-start.20 = (bf16[1040,128]{1,0:T(8,128)(2,1)S(1)}, bf16[1040,128]{1,0:T(8,128)(2,1)S(1)}, u32[]{:S(2)}, u32[]{:S(2)}) collective-permute-start(bf16[1040,128]{1,0:T(8,128)(2,1)S(1)} %pad_maximum_fusion), channel_id=1, source_target_pairs={{0,16},{8,24},{16,0},{24,8},{32,48},{40,56},{48,32},{56,40},{64,80... | collective-permute-start | bytes 798728 | tf_op jit(solution)/shard_map/ppermute | solution.py:361
  111.7 1.8 collective-permute-done.18.p1.refs_11_
  113.5 4.0 %collective-permute-start.19 = (bf16[1664,128]{1,0:T(8,128)(2,1)S(1)}, bf16[1664,128]{1,0:T(8,128)(2,1)S(1)}, u32[]{:S(2)}, u32[]{:S(2)}) collective-permute-start(bf16[1664,128]{1,0:T(8,128)(2,1)S(1)} %collective-permute-done.18.p1.refs_11_), channel_id=1, source_target_pairs={{0,1},{1,2},{2,3},{3,4},{4,5},{5,6},{6,7},{7,0},{8,9},{9,10},{10,1... | collective-permute-start | bytes 1277960 | tf_op jit(solution)/shard_map/ppermute | solution.py:365
  117.5 2.5 %collective-permute-start.15 = (bf16[1664,128]{1,0:T(8,128)(2,1)S(1)}, bf16[1664,128]{1,0:T(8,128)(2,1)S(1)}, u32[]{:S(2)}, u32[]{:S(2)}) collective-permute-start(bf16[1664,128]{1,0:T(8,128)(2,1)S(1)} %collective-permute-done.14.m1.refs_8_), channel_id=1, source_target_pairs={{0,7},{1,0},{2,1},{3,2},{4,3},{5,4},{6,5},{7,6},{8,15},{9,8},{10,9... | collective-permute-start | bytes 1277960 | tf_op jit(solution)/shard_map/ppermute | solution.py:365
  120.0 0.7 broadcast_select_fusion
  120.7 5.1 %collective-permute-done.19.p2.refs_12_ = bf16[1664,128]{1,0:T(8,128)(2,1)S(1)} collective-permute-done((bf16[1664,128]{1,0:T(8,128)(2,1)S(1)}, bf16[1664,128]{1,0:T(8,128)(2,1)S(1)}, u32[]{:S(2)}, u32[]{:S(2)}) %collective-permute-start.19) | collective-permute-done | bytes 426016 | tf_op jit(solution)/shard_map/ppermute | solution.py:365
  125.8 4.1 %collective-permute-start.21 = (bf16[1664,128]{1,0:T(8,128)(2,1)S(1)}, bf16[1664,128]{1,0:T(8,128)(2,1)S(1)}, u32[]{:S(2)}, u32[]{:S(2)}) collective-permute-start(bf16[1664,128]{1,0:T(8,128)(2,1)S(1)} %collective-permute-done.19.p2.refs_12_), channel_id=1, source_target_pairs={{0,1},{1,2},{2,3},{3,4},{4,5},{5,6},{6,7},{7,0},{8,9},{9,10},{10,1... | collective-permute-start | bytes 1277960 | tf_op jit(solution)/shard_map/ppermute | solution.py:365
  129.9 2.4 %collective-permute-start.16 = (bf16[1664,128]{1,0:T(8,128)(2,1)S(1)}, bf16[1664,128]{1,0:T(8,128)(2,1)S(1)}, u32[]{:S(2)}, u32[]{:S(2)}) collective-permute-start(bf16[1664,128]{1,0:T(8,128)(2,1)S(1)} %collective-permute-done.15.m2.refs_9_), channel_id=1, source_target_pairs={{0,7},{1,0},{2,1},{3,2},{4,3},{5,4},{6,5},{7,6},{8,15},{9,8},{10,9... | collective-permute-start | bytes 1277960 | tf_op jit(solution)/shard_map/ppermute | solution.py:365
  132.3 5.0 %collective-permute-done.21.p3.refs_13_ = bf16[1664,128]{1,0:T(8,128)(2,1)S(1)} collective-permute-done((bf16[1664,128]{1,0:T(8,128)(2,1)S(1)}, bf16[1664,128]{1,0:T(8,128)(2,1)S(1)}, u32[]{:S(2)}, u32[]{:S(2)}) %collective-permute-start.21) | collective-permute-done | bytes 426016 | tf_op jit(solution)/shard_map/ppermute | solution.py:365
  137.3 3.9 %collective-permute-done.16.m3.refs_10_ = bf16[1664,128]{1,0:T(8,128)(2,1)S(1)} collective-permute-done((bf16[1664,128]{1,0:T(8,128)(2,1)S(1)}, bf16[1664,128]{1,0:T(8,128)(2,1)S(1)}, u32[]{:S(2)}, u32[]{:S(2)}) %collective-permute-start.16) | collective-permute-done | bytes 426016 | tf_op jit(solution)/shard_map/ppermute | solution.py:365
  141.2 0.8 copy-done.2
  142.0 3.7 %shard_map.115.refs_5_ = bf16[1024,1024]{1,0:T(8,128)(2,1)} custom-call(bf16[1024,128]{1,0:T(8,128)(2,1)} %get-tuple-element.51.refs_0_.xa, bf16[1024,128]{1,0:T(8,128)(2,1)} %copy-done.16, bf16[1664,128]{1,0:T(8,128)(2,1)} %copy-done.9, bf16[1664,128]{1,0:T(8,128)(2,1)} %copy-done.13, bf16[1664,128]{1,0:T(8,128)(2,1)} %copy-done.2, ...), custom_call_target="tpu_custom_call" | custom-call | tf_op jit(solution)/shard_map/pallas_call | solution.py:32
  145.6 4.8 %collective-permute-start.24 = (bf16[1024,1024]{1,0:T(8,128)(2,1)}, bf16[1024,1024]{1,0:T(8,128)(2,1)S(1)}, u32[]{:S(2)}, u32[]{:S(2)}) collective-permute-start(bf16[1024,1024]{1,0:T(8,128)(2,1)} %shard_map.115.refs_5_), channel_id=1, source_target_pairs={{0,8},{8,0},{16,24},{24,16},{32,40},{40,32},{48,56},{56,48},{64,72... | collective-permute-start | bytes 6291464 | tf_op jit(solution)/shard_map/ppermute | solution.py:361
  150.4 0.9 slice.61
  151.4 3.4 %collective-permute-start.22 = (bf16[768,128]{1,0:T(8,128)(2,1)S(1)}, bf16[768,128]{1,0:T(8,128)(2,1)S(1)}, u32[]{:S(2)}, u32[]{:S(2)}) collective-permute-start(bf16[768,128]{1,0:T(8,128)(2,1)S(1)} %slice.61), channel_id=1, source_target_pairs={{0,1},{1,2},{2,3},{3,4},{4,5},{5,6},{6,7},{7,0},{8,9},{9,10},{10,1... | collective-permute-start | bytes 589832 | tf_op jit(solution)/shard_map/ppermute | solution.py:365
  154.7 0.9 slice.58
  155.7 3.1 %collective-permute-start.17 = (bf16[768,128]{1,0:T(8,128)(2,1)S(1)}, bf16[768,128]{1,0:T(8,128)(2,1)S(1)}, u32[]{:S(2)}, u32[]{:S(2)}) collective-permute-start(bf16[768,128]{1,0:T(8,128)(2,1)S(1)} %slice.58), channel_id=1, source_target_pairs={{0,7},{1,0},{2,1},{3,2},{4,3},{5,4},{6,5},{7,6},{8,15},{9,8},{10,9... | collective-permute-start | bytes 589832 | tf_op jit(solution)/shard_map/ppermute | solution.py:365
  158.8 2.1 %collective-permute-done.22.refs_15_ = bf16[768,128]{1,0:T(8,128)(2,1)S(1)} collective-permute-done((bf16[768,128]{1,0:T(8,128)(2,1)S(1)}, bf16[768,128]{1,0:T(8,128)(2,1)S(1)}, u32[]{:S(2)}, u32[]{:S(2)}) %collective-permute-start.22) | collective-permute-done | bytes 196640 | tf_op jit(solution)/shard_map/ppermute | solution.py:365
  160.9 4.4 %collective-permute-done.17.refs_14_ = bf16[768,128]{1,0:T(8,128)(2,1)S(1)} collective-permute-done((bf16[768,128]{1,0:T(8,128)(2,1)S(1)}, bf16[768,128]{1,0:T(8,128)(2,1)S(1)}, u32[]{:S(2)}, u32[]{:S(2)}) %collective-permute-start.17) | collective-permute-done | bytes 196640 | tf_op jit(solution)/shard_map/ppermute | solution.py:365
  165.4 2.8 %collective-permute-start.23 = (bf16[512,128]{1,0:T(8,128)(2,1)S(1)}, bf16[512,128]{1,0:T(8,128)(2,1)S(1)}, u32[]{:S(2)}, u32[]{:S(2)}) collective-permute-start(bf16[512,128]{1,0:T(8,128)(2,1)S(1)} %pad_maximum_fusion.2.last_own), channel_id=1, source_target_pairs={{0,8},{8,0},{16,24},{24,16},{32,40},{40,32},{48,56},{56,48},{64,72... | collective-permute-start | bytes 393224 | tf_op jit(solution)/shard_map/ppermute | solution.py:361
  168.2 1.0 collective-permute-done.23.last_far
  169.8 1.4 copy-done.4
  171.1 9.4 %shard_map.116.own = bf16[2064,128]{1,0:T(8,128)(2,1)} custom-call(bf16[512,128]{1,0:T(8,128)(2,1)} %copy-done.18, bf16[512,128]{1,0:T(8,128)(2,1)} %copy-done.26, bf16[16,128]{1,0:T(8,128)(2,1)} %get-tuple-element.49.vec_i, bf16[16,128]{1,0:T(8,128)(2,1)} %get-tuple-element.50.vec_j, bf16[1024,128]{1,0:T(8,128)(2,1)} %get-tuple-element.51.refs_0_.xa, ...), custom_call_target="tpu_custom_call" | custom-call | tf_op jit(solution)/shard_map/pallas_call | solution.py:32
  180.5 1.9 %collective-permute-start.25 = (bf16[2064,128]{1,0:T(8,128)(2,1)}, bf16[2064,128]{1,0:T(8,128)(2,1)S(1)}, u32[]{:S(2)}, u32[]{:S(2)}) collective-permute-start(bf16[2064,128]{1,0:T(8,128)(2,1)} %shard_map.116.own), channel_id=1, source_target_pairs={{0,8},{8,0},{16,24},{24,16},{32,40},{40,32},{48,56},{56,48},{64,72... | collective-permute-start | bytes 1585160 | tf_op jit(solution)/shard_map/ppermute | solution.py:361
  182.4 2.1 %collective-permute-done.25.got = bf16[2064,128]{1,0:T(8,128)(2,1)S(1)} collective-permute-done((bf16[2064,128]{1,0:T(8,128)(2,1)}, bf16[2064,128]{1,0:T(8,128)(2,1)S(1)}, u32[]{:S(2)}, u32[]{:S(2)}) %collective-permute-start.25) | collective-permute-done | bytes 528416 | tf_op jit(solution)/shard_map/ppermute | solution.py:361
  184.5 0.8 copy-done.17
  185.3 2.1 %shard_map.117 = (bf16[1,1024]{1,0:T(2,128)(2,1)}, bf16[1,1024]{1,0:T(2,128)(2,1)}, bf16[1024,128]{1,0:T(8,128)(2,1)}, bf16[1024,128]{1,0:T(8,128)(2,1)}, bf16[1024,128]{1,0:T(8,128)(2,1)}) custom-call(bf16[2064,128]{1,0:T(8,128)(2,1)} %shard_map.116.own, bf16[2064,128]{1,0:T(8,128)(2,1)} %copy-done.17), custom_call_target="tpu_custom_call" | custom-call | tf_op jit(solution)/shard_map/pallas_call | solution.py:32
  (67 shorter events, 1.4 us)
Async XLA Ops:
  2.5 17.7 %collective-permute-start.4 = (bf16[1664,128]{1,0:T(8,128)(2,1)}, bf16[1664,128]{1,0:T(8,128)(2,1)S(1)}, u32[]{:S(2)}, u32[]{:S(2)}) collective-permute-start(bf16[1664,128]{1,0:T(8,128)(2,1)} %shard_map.110.refs_6_), channel_id=1, source_target_pairs={{0,1},{1,2},{2,3},{3,4},{4,5},{5,6},{6,7},{7,0},{8,9},{9,10},{10,1... | collective-permute-start | bytes 1277960 | tf_op jit(solution)/shard_map/ppermute | solution.py:365
  6.5 15.6 %collective-permute-start = (bf16[1664,128]{1,0:T(8,128)(2,1)}, bf16[1664,128]{1,0:T(8,128)(2,1)S(1)}, u32[]{:S(2)}, u32[]{:S(2)}) collective-permute-start(bf16[1664,128]{1,0:T(8,128)(2,1)} %shard_map.110.refs_6_), channel_id=1, source_target_pairs={{0,7},{1,0},{2,1},{3,2},{4,3},{5,4},{6,5},{7,6},{8,15},{9,8},{10,9... | collective-permute-start | bytes 1277960 | tf_op jit(solution)/shard_map/ppermute | solution.py:365
  12.2 14.5 %collective-permute-start.6 = (bf16[1040,128]{1,0:T(8,128)(2,1)}, bf16[1040,128]{1,0:T(8,128)(2,1)S(1)}, u32[]{:S(2)}, u32[]{:S(2)}) collective-permute-start(bf16[1040,128]{1,0:T(8,128)(2,1)} %get-tuple-element.36), channel_id=1, source_target_pairs={{0,8},{8,0},{16,24},{24,16},{32,40},{40,32},{48,56},{56,48},{64,72... | collective-permute-start | bytes 798728 | tf_op jit(solution)/shard_map/ppermute | solution.py:361
  20.2 27.9 %copy-start.6 = (bf16[1664,128]{1,0:T(8,128)(2,1)}, bf16[1664,128]{1,0:T(8,128)(2,1)S(1)}, u32[]{:S(2)}) copy-start(bf16[1664,128]{1,0:T(8,128)(2,1)S(1)} %collective-permute-done.4.p1.refs_10_) | copy-start | bytes 1277956
  20.2 13.9 %collective-permute-start.5 = (bf16[1664,128]{1,0:T(8,128)(2,1)S(1)}, bf16[1664,128]{1,0:T(8,128)(2,1)S(1)}, u32[]{:S(2)}, u32[]{:S(2)}) collective-permute-start(bf16[1664,128]{1,0:T(8,128)(2,1)S(1)} %collective-permute-done.4.p1.refs_10_), channel_id=1, source_target_pairs={{0,1},{1,2},{2,3},{3,4},{4,5},{5,6},{6,7},{7,0},{8,9},{9,10},{10,1... | collective-permute-start | bytes 1277960 | tf_op jit(solution)/shard_map/ppermute | solution.py:365
  22.1 26.0 %copy-start.7 = (bf16[1664,128]{1,0:T(8,128)(2,1)}, bf16[1664,128]{1,0:T(8,128)(2,1)S(1)}, u32[]{:S(2)}) copy-start(bf16[1664,128]{1,0:T(8,128)(2,1)S(1)} %collective-permute-done.m1.refs_7_) | copy-start | bytes 1277956
  22.1 13.9 %collective-permute-start.1 = (bf16[1664,128]{1,0:T(8,128)(2,1)S(1)}, bf16[1664,128]{1,0:T(8,128)(2,1)S(1)}, u32[]{:S(2)}, u32[]{:S(2)}) collective-permute-start(bf16[1664,128]{1,0:T(8,128)(2,1)S(1)} %collective-permute-done.m1.refs_7_), channel_id=1, source_target_pairs={{0,7},{1,0},{2,1},{3,2},{4,3},{5,4},{6,5},{7,6},{8,15},{9,8},{10,9... | collective-permute-start | bytes 1277960 | tf_op jit(solution)/shard_map/ppermute | solution.py:365
  26.7 47.5 %copy-start.25 = (bf16[1040,128]{1,0:T(8,128)(2,1)}, bf16[1040,128]{1,0:T(8,128)(2,1)S(1)}, u32[]{:S(2)}) copy-start(bf16[1040,128]{1,0:T(8,128)(2,1)S(1)} %collective-permute-done.6.refs_1_) | copy-start | bytes 798724
  34.1 14.0 %copy-start.10 = (bf16[1664,128]{1,0:T(8,128)(2,1)}, bf16[1664,128]{1,0:T(8,128)(2,1)S(1)}, u32[]{:S(2)}) copy-start(bf16[1664,128]{1,0:T(8,128)(2,1)S(1)} %collective-permute-done.5.p2.refs_11_) | copy-start | bytes 1277956
  34.1 13.1 %collective-permute-start.7 = (bf16[1664,128]{1,0:T(8,128)(2,1)S(1)}, bf16[1664,128]{1,0:T(8,128)(2,1)S(1)}, u32[]{:S(2)}, u32[]{:S(2)}) collective-permute-start(bf16[1664,128]{1,0:T(8,128)(2,1)S(1)} %collective-permute-done.5.p2.refs_11_), channel_id=1, source_target_pairs={{0,1},{1,2},{2,3},{3,4},{4,5},{5,6},{6,7},{7,0},{8,9},{9,10},{10,1... | collective-permute-start | bytes 1277960 | tf_op jit(solution)/shard_map/ppermute | solution.py:365
  36.0 12.1 %copy-start.11 = (bf16[1664,128]{1,0:T(8,128)(2,1)}, bf16[1664,128]{1,0:T(8,128)(2,1)S(1)}, u32[]{:S(2)}) copy-start(bf16[1664,128]{1,0:T(8,128)(2,1)S(1)} %collective-permute-done.1.m2.refs_8_) | copy-start | bytes 1277956
  36.1 12.1 %collective-permute-start.2 = (bf16[1664,128]{1,0:T(8,128)(2,1)S(1)}, bf16[1664,128]{1,0:T(8,128)(2,1)S(1)}, u32[]{:S(2)}, u32[]{:S(2)}) collective-permute-start(bf16[1664,128]{1,0:T(8,128)(2,1)S(1)} %collective-permute-done.1.m2.refs_8_), channel_id=1, source_target_pairs={{0,7},{1,0},{2,1},{3,2},{4,3},{5,4},{6,5},{7,6},{8,15},{9,8},{10,9... | collective-permute-start | bytes 1277960 | tf_op jit(solution)/shard_map/ppermute | solution.py:365
  47.2 0.9 copy-start.1
  48.1 0.8 copy-start.3
  52.6 21.6 %collective-permute-start.10 = (bf16[1024,1024]{1,0:T(8,128)(2,1)}, bf16[1024,1024]{1,0:T(8,128)(2,1)S(1)}, u32[]{:S(2)}, u32[]{:S(2)}) collective-permute-start(bf16[1024,1024]{1,0:T(8,128)(2,1)} %shard_map.112.refs_4_), channel_id=1, source_target_pairs={{0,8},{8,0},{16,24},{24,16},{32,40},{40,32},{48,56},{56,48},{64,72... | collective-permute-start | bytes 6291464 | tf_op jit(solution)/shard_map/ppermute | solution.py:361
  58.0 10.6 %collective-permute-start.8 = (bf16[768,128]{1,0:T(8,128)(2,1)S(1)}, bf16[768,128]{1,0:T(8,128)(2,1)S(1)}, u32[]{:S(2)}, u32[]{:S(2)}) collective-permute-start(bf16[768,128]{1,0:T(8,128)(2,1)S(1)} %slice.55), channel_id=1, source_target_pairs={{0,1},{1,2},{2,3},{3,4},{4,5},{5,6},{6,7},{7,0},{8,9},{9,10},{10,1... | collective-permute-start | bytes 589832 | tf_op jit(solution)/shard_map/ppermute | solution.py:365
  60.8 9.6 %collective-permute-start.3 = (bf16[768,128]{1,0:T(8,128)(2,1)S(1)}, bf16[768,128]{1,0:T(8,128)(2,1)S(1)}, u32[]{:S(2)}, u32[]{:S(2)}) collective-permute-start(bf16[768,128]{1,0:T(8,128)(2,1)S(1)} %slice.52), channel_id=1, source_target_pairs={{0,7},{1,0},{2,1},{3,2},{4,3},{5,4},{6,5},{7,6},{8,15},{9,8},{10,9... | collective-permute-start | bytes 589832 | tf_op jit(solution)/shard_map/ppermute | solution.py:365
  68.5 5.6 %copy-start.21 = (bf16[768,128]{1,0:T(8,128)(2,1)}, bf16[768,128]{1,0:T(8,128)(2,1)S(1)}, u32[]{:S(2)}) copy-start(bf16[768,128]{1,0:T(8,128)(2,1)S(1)} %collective-permute-done.8.refs_14_) | copy-start | bytes 589828
  70.4 3.8 %copy-start.23 = (bf16[768,128]{1,0:T(8,128)(2,1)}, bf16[768,128]{1,0:T(8,128)(2,1)S(1)}, u32[]{:S(2)}) copy-start(bf16[768,128]{1,0:T(8,128)(2,1)S(1)} %collective-permute-done.3.refs_13_) | copy-start | bytes 589828
  70.4 3.8 %copy-start.19 = (bf16[512,128]{1,0:T(8,128)(2,1)}, bf16[512,128]{1,0:T(8,128)(2,1)S(1)}, u32[]{:S(2)}) copy-start(bf16[512,128]{1,0:T(8,128)(2,1)S(1)} %pad_maximum_fusion.1.last_own) | copy-start | bytes 393220
  70.4 3.8 %collective-permute-start.9 = (bf16[512,128]{1,0:T(8,128)(2,1)S(1)}, bf16[512,128]{1,0:T(8,128)(2,1)S(1)}, u32[]{:S(2)}, u32[]{:S(2)}) collective-permute-start(bf16[512,128]{1,0:T(8,128)(2,1)S(1)} %pad_maximum_fusion.1.last_own), channel_id=1, source_target_pairs={{0,8},{8,0},{16,24},{24,16},{32,40},{40,32},{48,56},{56,48},{64,72... | collective-permute-start | bytes 393224 | tf_op jit(solution)/shard_map/ppermute | solution.py:361
  74.2 0.7 copy-start.27
  74.8 1.4 copy-start.5
  85.5 7.3 %collective-permute-start.11 = (bf16[1040,128]{1,0:T(8,128)(2,1)}, bf16[1040,128]{1,0:T(8,128)(2,1)S(1)}, u32[]{:S(2)}, u32[]{:S(2)}) collective-permute-start(bf16[1040,128]{1,0:T(8,128)(2,1)} %get-tuple-element.52.refs_1_), channel_id=1, source_target_pairs={{0,8},{8,0},{16,24},{24,16},{32,40},{40,32},{48,56},{56,48},{64,72... | collective-permute-start | bytes 798728 | tf_op jit(solution)/shard_map/ppermute | solution.py:361
  87.5 8.9 %collective-permute-start.12 = (bf16[1040,128]{1,0:T(8,128)(2,1)}, bf16[1040,128]{1,0:T(8,128)(2,1)S(1)}, u32[]{:S(2)}, u32[]{:S(2)}) collective-permute-start(bf16[1040,128]{1,0:T(8,128)(2,1)} %get-tuple-element.52.refs_1_), channel_id=1, source_target_pairs={{8,16},{24,8},{40,48},{56,40},{72,80},{88,72},{104,112},{120,104},... | collective-permute-start | bytes 798728 | tf_op jit(solution)/shard_map/ppermute | solution.py:468
  89.8 6.6 %collective-permute-start.13 = (bf16[1024,128]{1,0:T(8,128)(2,1)}, bf16[1024,128]{1,0:T(8,128)(2,1)S(1)}, u32[]{:S(2)}, u32[]{:S(2)}) collective-permute-start(bf16[1024,128]{1,0:T(8,128)(2,1)} %get-tuple-element.51.refs_0_.xa), channel_id=1, source_target_pairs={{8,24},{16,0},{40,56},{48,32},{72,88},{80,64},{104,120},{112,96},{... | collective-permute-start | bytes 786440 | tf_op jit(solution)/shard_map/ppermute | solution.py:471
  92.8 3.6 %copy-start.14 = (bf16[1040,128]{1,0:T(8,128)(2,1)}, bf16[1040,128]{1,0:T(8,128)(2,1)S(1)}, u32[]{:S(2)}) copy-start(bf16[1040,128]{1,0:T(8,128)(2,1)S(1)} %collective-permute-done.11.refs_2_) | copy-start | bytes 798724
  96.4 0.7 copy-start.16
  97.1 0.7 copy-start.15
  99.6 13.9 %collective-permute-start.18 = (bf16[1664,128]{1,0:T(8,128)(2,1)}, bf16[1664,128]{1,0:T(8,128)(2,1)S(1)}, u32[]{:S(2)}, u32[]{:S(2)}) collective-permute-start(bf16[1664,128]{1,0:T(8,128)(2,1)} %shard_map.114.refs_7_), channel_id=1, source_target_pairs={{0,1},{1,2},{2,3},{3,4},{4,5},{5,6},{6,7},{7,0},{8,9},{9,10},{10,1... | collective-permute-start | bytes 1277960 | tf_op jit(solution)/shard_map/ppermute | solution.py:365
  104.1 13.4 %collective-permute-start.14 = (bf16[1664,128]{1,0:T(8,128)(2,1)}, bf16[1664,128]{1,0:T(8,128)(2,1)S(1)}, u32[]{:S(2)}, u32[]{:S(2)}) collective-permute-start(bf16[1664,128]{1,0:T(8,128)(2,1)} %shard_map.114.refs_7_), channel_id=1, source_target_pairs={{0,7},{1,0},{2,1},{3,2},{4,3},{5,4},{6,5},{7,6},{8,15},{9,8},{10,9... | collective-permute-start | bytes 1277960 | tf_op jit(solution)/shard_map/ppermute | solution.py:365
  107.9 12.1 %collective-permute-start.20 = (bf16[1040,128]{1,0:T(8,128)(2,1)S(1)}, bf16[1040,128]{1,0:T(8,128)(2,1)S(1)}, u32[]{:S(2)}, u32[]{:S(2)}) collective-permute-start(bf16[1040,128]{1,0:T(8,128)(2,1)S(1)} %pad_maximum_fusion), channel_id=1, source_target_pairs={{0,16},{8,24},{16,0},{24,8},{32,48},{40,56},{48,32},{56,40},{64,80... | collective-permute-start | bytes 798728 | tf_op jit(solution)/shard_map/ppermute | solution.py:361
  113.5 27.7 %copy-start.8 = (bf16[1664,128]{1,0:T(8,128)(2,1)}, bf16[1664,128]{1,0:T(8,128)(2,1)S(1)}, u32[]{:S(2)}) copy-start(bf16[1664,128]{1,0:T(8,128)(2,1)S(1)} %collective-permute-done.18.p1.refs_11_) | copy-start | bytes 1277956
  113.5 12.3 %collective-permute-start.19 = (bf16[1664,128]{1,0:T(8,128)(2,1)S(1)}, bf16[1664,128]{1,0:T(8,128)(2,1)S(1)}, u32[]{:S(2)}, u32[]{:S(2)}) collective-permute-start(bf16[1664,128]{1,0:T(8,128)(2,1)S(1)} %collective-permute-done.18.p1.refs_11_), channel_id=1, source_target_pairs={{0,1},{1,2},{2,3},{3,4},{4,5},{5,6},{6,7},{7,0},{8,9},{9,10},{10,1... | collective-permute-start | bytes 1277960 | tf_op jit(solution)/shard_map/ppermute | solution.py:365
  117.5 23.6 %copy-start.9 = (bf16[1664,128]{1,0:T(8,128)(2,1)}, bf16[1664,128]{1,0:T(8,128)(2,1)S(1)}, u32[]{:S(2)}) copy-start(bf16[1664,128]{1,0:T(8,128)(2,1)S(1)} %collective-permute-done.14.m1.refs_8_) | copy-start | bytes 1277956
  117.5 12.4 %collective-permute-start.15 = (bf16[1664,128]{1,0:T(8,128)(2,1)S(1)}, bf16[1664,128]{1,0:T(8,128)(2,1)S(1)}, u32[]{:S(2)}, u32[]{:S(2)}) collective-permute-start(bf16[1664,128]{1,0:T(8,128)(2,1)S(1)} %collective-permute-done.14.m1.refs_8_), channel_id=1, source_target_pairs={{0,7},{1,0},{2,1},{3,2},{4,3},{5,4},{6,5},{7,6},{8,15},{9,8},{10,9... | collective-permute-start | bytes 1277960 | tf_op jit(solution)/shard_map/ppermute | solution.py:365
  120.0 49.1 %copy-start.24 = (bf16[1040,128]{1,0:T(8,128)(2,1)}, bf16[1040,128]{1,0:T(8,128)(2,1)S(1)}, u32[]{:S(2)}) copy-start(bf16[1040,128]{1,0:T(8,128)(2,1)S(1)} %collective-permute-done.20.refs_4_) | copy-start | bytes 798724
  125.8 15.4 %copy-start.12 = (bf16[1664,128]{1,0:T(8,128)(2,1)}, bf16[1664,128]{1,0:T(8,128)(2,1)S(1)}, u32[]{:S(2)}) copy-start(bf16[1664,128]{1,0:T(8,128)(2,1)S(1)} %collective-permute-done.19.p2.refs_12_) | copy-start | bytes 1277956
  125.8 11.5 %collective-permute-start.21 = (bf16[1664,128]{1,0:T(8,128)(2,1)S(1)}, bf16[1664,128]{1,0:T(8,128)(2,1)S(1)}, u32[]{:S(2)}, u32[]{:S(2)}) collective-permute-start(bf16[1664,128]{1,0:T(8,128)(2,1)S(1)} %collective-permute-done.19.p2.refs_12_), channel_id=1, source_target_pairs={{0,1},{1,2},{2,3},{3,4},{4,5},{5,6},{6,7},{7,0},{8,9},{9,10},{10,1... | collective-permute-start | bytes 1277960 | tf_op jit(solution)/shard_map/ppermute | solution.py:365
  129.9 11.3 %copy-start.13 = (bf16[1664,128]{1,0:T(8,128)(2,1)}, bf16[1664,128]{1,0:T(8,128)(2,1)S(1)}, u32[]{:S(2)}) copy-start(bf16[1664,128]{1,0:T(8,128)(2,1)S(1)} %collective-permute-done.15.m2.refs_9_) | copy-start | bytes 1277956
  129.9 11.3 %collective-permute-start.16 = (bf16[1664,128]{1,0:T(8,128)(2,1)S(1)}, bf16[1664,128]{1,0:T(8,128)(2,1)S(1)}, u32[]{:S(2)}, u32[]{:S(2)}) collective-permute-start(bf16[1664,128]{1,0:T(8,128)(2,1)S(1)} %collective-permute-done.15.m2.refs_9_), channel_id=1, source_target_pairs={{0,7},{1,0},{2,1},{3,2},{4,3},{5,4},{6,5},{7,6},{8,15},{9,8},{10,9... | collective-permute-start | bytes 1277960 | tf_op jit(solution)/shard_map/ppermute | solution.py:365
  137.3 3.9 %copy-start = (bf16[1664,128]{1,0:T(8,128)(2,1)}, bf16[1664,128]{1,0:T(8,128)(2,1)S(1)}, u32[]{:S(2)}) copy-start(bf16[1664,128]{1,0:T(8,128)(2,1)S(1)} %collective-permute-done.21.p3.refs_13_) | copy-start | bytes 1277956
  141.2 0.8 copy-start.2
  145.6 23.5 %collective-permute-start.24 = (bf16[1024,1024]{1,0:T(8,128)(2,1)}, bf16[1024,1024]{1,0:T(8,128)(2,1)S(1)}, u32[]{:S(2)}, u32[]{:S(2)}) collective-permute-start(bf16[1024,1024]{1,0:T(8,128)(2,1)} %shard_map.115.refs_5_), channel_id=1, source_target_pairs={{0,8},{8,0},{16,24},{24,16},{32,40},{40,32},{48,56},{56,48},{64,72... | collective-permute-start | bytes 6291464 | tf_op jit(solution)/shard_map/ppermute | solution.py:361
  151.4 9.5 %collective-permute-start.22 = (bf16[768,128]{1,0:T(8,128)(2,1)S(1)}, bf16[768,128]{1,0:T(8,128)(2,1)S(1)}, u32[]{:S(2)}, u32[]{:S(2)}) collective-permute-start(bf16[768,128]{1,0:T(8,128)(2,1)S(1)} %slice.61), channel_id=1, source_target_pairs={{0,1},{1,2},{2,3},{3,4},{4,5},{5,6},{6,7},{7,0},{8,9},{9,10},{10,1... | collective-permute-start | bytes 589832 | tf_op jit(solution)/shard_map/ppermute | solution.py:365
  155.7 9.6 %collective-permute-start.17 = (bf16[768,128]{1,0:T(8,128)(2,1)S(1)}, bf16[768,128]{1,0:T(8,128)(2,1)S(1)}, u32[]{:S(2)}, u32[]{:S(2)}) collective-permute-start(bf16[768,128]{1,0:T(8,128)(2,1)S(1)} %slice.58), channel_id=1, source_target_pairs={{0,7},{1,0},{2,1},{3,2},{4,3},{5,4},{6,5},{7,6},{8,15},{9,8},{10,9... | collective-permute-start | bytes 589832 | tf_op jit(solution)/shard_map/ppermute | solution.py:365
  160.9 8.2 %copy-start.20 = (bf16[768,128]{1,0:T(8,128)(2,1)}, bf16[768,128]{1,0:T(8,128)(2,1)S(1)}, u32[]{:S(2)}) copy-start(bf16[768,128]{1,0:T(8,128)(2,1)S(1)} %collective-permute-done.22.refs_15_) | copy-start | bytes 589828
  165.3 3.8 %copy-start.22 = (bf16[768,128]{1,0:T(8,128)(2,1)}, bf16[768,128]{1,0:T(8,128)(2,1)S(1)}, u32[]{:S(2)}) copy-start(bf16[768,128]{1,0:T(8,128)(2,1)S(1)} %collective-permute-done.17.refs_14_) | copy-start | bytes 589828
  165.4 3.8 %copy-start.18 = (bf16[512,128]{1,0:T(8,128)(2,1)}, bf16[512,128]{1,0:T(8,128)(2,1)S(1)}, u32[]{:S(2)}) copy-start(bf16[512,128]{1,0:T(8,128)(2,1)S(1)} %pad_maximum_fusion.2.last_own) | copy-start | bytes 393220
  165.4 3.8 %collective-permute-start.23 = (bf16[512,128]{1,0:T(8,128)(2,1)S(1)}, bf16[512,128]{1,0:T(8,128)(2,1)S(1)}, u32[]{:S(2)}, u32[]{:S(2)}) collective-permute-start(bf16[512,128]{1,0:T(8,128)(2,1)S(1)} %pad_maximum_fusion.2.last_own), channel_id=1, source_target_pairs={{0,8},{8,0},{16,24},{24,16},{32,40},{40,32},{48,56},{56,48},{64,72... | collective-permute-start | bytes 393224 | tf_op jit(solution)/shard_map/ppermute | solution.py:361
  169.1 0.6 copy-start.26
  169.8 1.4 copy-start.4
  180.5 4.0 %collective-permute-start.25 = (bf16[2064,128]{1,0:T(8,128)(2,1)}, bf16[2064,128]{1,0:T(8,128)(2,1)S(1)}, u32[]{:S(2)}, u32[]{:S(2)}) collective-permute-start(bf16[2064,128]{1,0:T(8,128)(2,1)} %shard_map.116.own), channel_id=1, source_target_pairs={{0,8},{8,0},{16,24},{24,16},{32,40},{40,32},{48,56},{56,48},{64,72... | collective-permute-start | bytes 1585160 | tf_op jit(solution)/shard_map/ppermute | solution.py:361
  184.5 0.8 copy-start.17
